TPU v7x, 32 devices: a whole 2x2x4 slice. The times are simulated.
32 devices in a mesh: tower: 2 (over core), dp: 16 (over z, y, x).
Axes of the slice: x: 2, y: 2, z: 4, core: 2. Of those that a mesh axis runs over, the one named last changes fastest.
Arguments:
- embeddings: bfloat16 [2, 128, 128, 768], P('tower', 'dp'), may hold values from -6 to 6
- lengths: int32 [2, 128], P('tower', 'dp'), may hold values from 5 to 128, as said below
- labels: int32 [128], P('dp'), may hold values from 0 to 2
- qkv_weight: bfloat16 [768, 2304], P('dp'), may hold values from -0.21875 to 0.21875
- query_bias: bfloat16 [768], P('dp'), may hold values from -3 to 3
- value_bias: bfloat16 [768], P('dp'), may hold values from -3 to 3
- out_weight: bfloat16 [768, 768], P('dp'), may hold values from -0.625 to 0.625
- out_bias: bfloat16 [768], P('dp'), may hold values from -3 to 3
- attn_gain: bfloat16 [768], P('dp'), may hold values from 0.5 to 1.5
- attn_shift: bfloat16 [768], P('dp'), may hold values from -3 to 3
- up_weight: bfloat16 [768, 3072], P('dp'), may hold values from -0.21875 to 0.21875
- up_bias: bfloat16 [3072], P('dp'), may hold values from -3 to 3
- down_weight: bfloat16 [3072, 768], P('dp'), may hold values from -0.109375 to 0.109375
- down_bias: bfloat16 [768], P('dp'), may hold values from -3 to 3
- ffn_gain: bfloat16 [768], P('dp'), may hold values from 0.5 to 1.5
- ffn_shift: bfloat16 [768], P('dp'), may hold values from -3 to 3
- head_weight: bfloat16 [2304, 3], P('dp'), may hold values from -0.21875 to 0.21875
- head_bias: bfloat16 [3], replicated, may hold values from -3 to 3
Outputs:
- pooled: float32 [2, 128, 768], P('tower', 'dp')
- grad_embeddings: float32 [2, 128, 128, 768], P('tower', 'dp')
- grad_qkv_weight: float32 [768, 2304], P(('tower', 'dp'))
- grad_query_bias: float32 [768], P(('tower', 'dp'))
- grad_value_bias: float32 [768], P(('tower', 'dp'))
- grad_out_weight: float32 [768, 768], P(('tower', 'dp'))
- grad_out_bias: float32 [768], P(('tower', 'dp'))
- grad_attn_gain: float32 [768], P(('tower', 'dp'))
- grad_attn_shift: float32 [768], P(('tower', 'dp'))
- grad_up_weight: float32 [768, 3072], P(('tower', 'dp'))
- grad_up_bias: float32 [3072], P(('tower', 'dp'))
- grad_down_weight: float32 [3072, 768], P(('tower', 'dp'))
- grad_down_bias: float32 [768], P(('tower', 'dp'))
- grad_ffn_gain: float32 [768], P(('tower', 'dp'))
- grad_ffn_shift: float32 [768], P(('tower', 'dp'))
- grad_head_weight: float32 [2304, 3], P(('tower', 'dp'))
- grad_head_bias: float32 [3], replicated
Inputs may be any that keep to these rules, and one draw needn't show every extreme that they name: `lengths`: a sentence's real tokens fill its first slots, the rest are padding; some sentence has all 128.
All inputs are finite; a program needn't handle non-finite values.
Results may differ from a plain program's by a relative error of at most 0.008.
Values may be sent and summed in bfloat16 or wider, within the bound.
No kernel may reach another device: no remote copies, remote signals or barrier semaphores. Data moves between devices by JAX's collectives and lax.ppermute only.
A program may use at most 192 MiB of HBM per device.

v0:
```python
from functools import partial

import jax
import jax.numpy as jnp
from jax import lax
from jax.sharding import PartitionSpec as P

HEADS = 12
HEAD_DIM = 64
NCLASS = 3
MICRO = 2


eps_norm = 1e-12
gap_soft = 0.01
highest = lax.Precision.HIGHEST


def from_partner(array, axis, bit):
    return lax.ppermute(array, axis, [(i, i ^ 1 << bit) for i in range(lax.axis_size(axis))])


def contract_rows(left, right):
    return lax.dot_general(
        left, right, (((0,), (0,)), ((), ())), preferred_element_type=jnp.float32
    )


def contract_cols(left, right):
    return lax.dot_general(
        left, right, (((1,), (1,)), ((), ())), preferred_element_type=jnp.float32
    )


def norm_forward(hidden, gain, shift):
    center = hidden - jnp.mean(hidden, axis=-1, keepdims=True)
    inverse = lax.rsqrt(jnp.mean(center * center, axis=-1, keepdims=True) + eps_norm)
    normal = center * inverse
    return (normal * gain + shift, normal, inverse)


def norm_backward(upstream, normal, inverse, gain):
    scaled = upstream * gain
    inner = scaled - jnp.mean(scaled, axis=-1, keepdims=True)
    inner = inner - normal * jnp.mean(scaled * normal, axis=-1, keepdims=True)
    return (inverse * inner, jnp.sum(upstream * normal, axis=0), jnp.sum(upstream, axis=0))


def attention_probs(query_heads, key_heads, valid, total, scale):
    raw = jnp.einsum("bqhd,bkhd->bhqk", query_heads, key_heads, preferred_element_type=jnp.float32)
    scores = jnp.where(valid[:, None, None, :], raw * scale, -1000000000.0)
    return jnp.exp(scores - total)


def body(
    embeddings,
    lengths,
    labels,
    qkv_weight,
    query_bias,
    value_bias,
    out_weight,
    out_bias,
    attn_gain,
    attn_shift,
    up_weight,
    up_bias,
    down_weight,
    down_bias,
    ffn_gain,
    ffn_shift,
    head_weight,
    head_bias,
):
    width = embeddings.shape[-1]
    seq_len = embeddings.shape[2]
    sentences = embeddings.shape[1]
    per_micro = sentences // MICRO
    rows = per_micro * seq_len
    scale = HEAD_DIM ** (-0.5)
    heads_shape = (per_micro, seq_len, HEADS, HEAD_DIM)
    leading = lax.axis_index("tower") == 0
    gelu_exact = partial(jax.nn.gelu, approximate=False)
    shards = (
        qkv_weight,
        query_bias,
        value_bias,
        out_weight,
        out_bias,
        attn_gain,
        attn_shift,
        up_weight,
        up_bias,
        down_weight,
        down_bias,
        ffn_gain,
        ffn_shift,
        head_weight,
    )
    groups = lax.axis_size("dp")
    accum = tuple(
        (jnp.zeros((shard.shape[0] * groups,) + shard.shape[1:], jnp.float32) for shard in shards)
    )
    class_total = jnp.zeros((NCLASS,), jnp.float32)
    pooled_parts = []
    input_parts = []
    for micro_step in range(MICRO):
        start = micro_step * per_micro
        sent_len = lengths[0, start : start + per_micro]
        proj_qkv = lax.all_gather(qkv_weight, "dp", axis=0, tiled=True)
        bias_query = lax.all_gather(query_bias, "dp", axis=0, tiled=True)
        bias_value = lax.all_gather(value_bias, "dp", axis=0, tiled=True)
        proj_out = lax.all_gather(out_weight, "dp", axis=0, tiled=True)
        bias_out = lax.all_gather(out_bias, "dp", axis=0, tiled=True)
        gain_attn = lax.all_gather(attn_gain, "dp", axis=0, tiled=True)
        shift_attn = lax.all_gather(attn_shift, "dp", axis=0, tiled=True)
        proj_up = lax.all_gather(up_weight, "dp", axis=0, tiled=True)
        bias_up = lax.all_gather(up_bias, "dp", axis=0, tiled=True)
        proj_down = lax.all_gather(down_weight, "dp", axis=0, tiled=True)
        bias_down = lax.all_gather(down_bias, "dp", axis=0, tiled=True)
        gain_ffn = lax.all_gather(ffn_gain, "dp", axis=0, tiled=True)
        shift_ffn = lax.all_gather(ffn_shift, "dp", axis=0, tiled=True)
        proj_head = lax.all_gather(head_weight, "dp", axis=0, tiled=True)
        gain_one = gain_attn.astype(jnp.float32)
        gain_two = gain_ffn.astype(jnp.float32)
        flat = embeddings[0, start : start + per_micro].reshape(rows, width)
        joined = jnp.dot(flat, proj_qkv, preferred_element_type=jnp.float32)
        queries = (joined[:, :width] + bias_query.astype(jnp.float32)).astype(jnp.bfloat16)
        key_rows = joined[:, width : 2 * width].astype(jnp.bfloat16)
        values = (joined[:, 2 * width :] + bias_value.astype(jnp.float32)).astype(jnp.bfloat16)
        query_heads = queries.reshape(heads_shape)
        key_heads = key_rows.reshape(heads_shape)
        value_heads = values.reshape(heads_shape)
        valid = jnp.arange(seq_len)[None, :] < sent_len[:, None]
        raw = jnp.einsum(
            "bqhd,bkhd->bhqk", query_heads, key_heads, preferred_element_type=jnp.float32
        )
        scores = jnp.where(valid[:, None, None, :], raw * scale, -1000000000.0)
        top = jnp.max(scores, axis=-1, keepdims=True)
        total = jnp.log(jnp.sum(jnp.exp(scores - top), axis=-1, keepdims=True)) + top
        probs_low = jnp.exp(scores - total).astype(jnp.bfloat16)
        context = jnp.einsum(
            "bhqk,bkhd->bqhd", probs_low, value_heads, preferred_element_type=jnp.float32
        )
        context = context.reshape(rows, width).astype(jnp.bfloat16)
        attended = jnp.dot(context, proj_out, preferred_element_type=jnp.float32) + bias_out.astype(
            jnp.float32
        )
        first, first_norm, first_inv = norm_forward(
            flat.astype(jnp.float32) + attended, gain_one, shift_attn.astype(jnp.float32)
        )
        first_low = first.astype(jnp.bfloat16)
        pre_act = jnp.dot(first_low, proj_up, preferred_element_type=jnp.float32) + bias_up.astype(
            jnp.float32
        )
        activated = gelu_exact(pre_act).astype(jnp.bfloat16)
        second = jnp.dot(
            activated, proj_down, preferred_element_type=jnp.float32
        ) + bias_down.astype(jnp.float32)
        output, second_norm, second_inv = norm_forward(
            first + second, gain_two, shift_ffn.astype(jnp.float32)
        )
        mask = valid.astype(jnp.float32)
        length_f = sent_len.astype(jnp.float32)[:, None]
        pooled = (
            jnp.sum(output.reshape(per_micro, seq_len, width) * mask[:, :, None], axis=1) / length_f
        )
        partner = from_partner(pooled, "tower", 0)
        left = jnp.where(leading, pooled, partner)
        right = jnp.where(leading, partner, pooled)
        gap = left - right
        soft_gap = jnp.sqrt(gap * gap + gap_soft)
        feats = jnp.concatenate([left, right, soft_gap], axis=1)
        head_full = proj_head.astype(jnp.float32)
        logits = jnp.dot(feats, head_full, precision=highest) + head_bias.astype(jnp.float32)
        onehot = (labels[start : start + per_micro][:, None] == jnp.arange(NCLASS)[None, :]).astype(
            jnp.float32
        )
        logit_grad = jax.nn.softmax(logits, axis=-1) - onehot
        head_grad = 0.5 * jnp.dot(feats.T, logit_grad, precision=highest)
        class_grad = jnp.where(leading, jnp.sum(logit_grad, axis=0), 0.0)
        feat_grad = jnp.dot(logit_grad, head_full.T, precision=highest)
        slope = gap / soft_gap
        left_grad = feat_grad[:, :width] + slope * feat_grad[:, 2 * width :]
        right_grad = feat_grad[:, width : 2 * width] - slope * feat_grad[:, 2 * width :]
        pooled_grad = jnp.where(leading, left_grad, right_grad)
        output_grad = ((pooled_grad / length_f)[:, None, :] * mask[:, :, None]).reshape(rows, width)
        sum_grad, gain_two_grad, shift_two_grad = norm_backward(
            output_grad, second_norm, second_inv, gain_two
        )
        down_bias_grad = jnp.sum(sum_grad, axis=0)
        sum_low = sum_grad.astype(jnp.bfloat16)
        down_grad = contract_rows(activated, sum_low)
        act_grad = contract_cols(sum_low, proj_down)
        pre_grad = jax.vjp(gelu_exact, pre_act)[1](act_grad)[0]
        up_bias_grad = jnp.sum(pre_grad, axis=0)
        pre_low = pre_grad.astype(jnp.bfloat16)
        up_grad = contract_rows(first_low, pre_low)
        first_grad = sum_grad + contract_cols(pre_low, proj_up)
        mid_grad, gain_one_grad, shift_one_grad = norm_backward(
            first_grad, first_norm, first_inv, gain_one
        )
        out_bias_grad = jnp.sum(mid_grad, axis=0)
        mid_low = mid_grad.astype(jnp.bfloat16)
        out_grad = contract_rows(context, mid_low)
        context_grad = contract_cols(mid_low, proj_out).astype(jnp.bfloat16).reshape(heads_shape)
        probs = attention_probs(query_heads, key_heads, valid, total, scale)
        probs_again = probs.astype(jnp.bfloat16)
        prob_grad = jnp.einsum(
            "bqhd,bkhd->bhqk", context_grad, value_heads, preferred_element_type=jnp.float32
        )
        value_grad = jnp.einsum(
            "bhqk,bqhd->bkhd", probs_again, context_grad, preferred_element_type=jnp.float32
        )
        score_grad = (
            probs * (prob_grad - jnp.sum(prob_grad * probs, axis=-1, keepdims=True)) * scale
        )
        score_low = score_grad.astype(jnp.bfloat16)
        query_grad = jnp.einsum(
            "bhqk,bkhd->bqhd", score_low, key_heads, preferred_element_type=jnp.float32
        )
        key_grad = jnp.einsum(
            "bhqk,bqhd->bkhd", score_low, query_heads, preferred_element_type=jnp.float32
        )
        qkv_grad = jnp.concatenate(
            [
                query_grad.reshape(rows, width),
                key_grad.reshape(rows, width),
                value_grad.reshape(rows, width),
            ],
            axis=1,
        ).astype(jnp.bfloat16)
        query_bias_grad = jnp.sum(qkv_grad[:, :width].astype(jnp.float32), axis=0)
        value_bias_grad = jnp.sum(qkv_grad[:, 2 * width :].astype(jnp.float32), axis=0)
        qkv_full_grad = contract_rows(flat, qkv_grad)
        input_grad = contract_cols(qkv_grad, proj_qkv) + mid_grad
        grads = (
            qkv_full_grad,
            query_bias_grad,
            value_bias_grad,
            out_grad,
            out_bias_grad,
            gain_one_grad,
            shift_one_grad,
            up_grad,
            up_bias_grad,
            down_grad,
            down_bias_grad,
            gain_two_grad,
            shift_two_grad,
            head_grad,
        )
        grads, class_grad, pooled, input_grad = (
            grads,
            class_grad,
            pooled,
            input_grad.reshape(per_micro, seq_len, width),
        )
        accum = jax.tree.map(jnp.add, accum, grads)
        class_total = class_total + class_grad
        pooled_parts.append(pooled)
        input_parts.append(input_grad)
    accum = (
        lax.psum_scatter(accum[0], ("tower", "dp"), scatter_dimension=0, tiled=True),
        lax.psum_scatter(accum[1], ("tower", "dp"), scatter_dimension=0, tiled=True),
        lax.psum_scatter(accum[2], ("tower", "dp"), scatter_dimension=0, tiled=True),
        lax.psum_scatter(accum[3], ("tower", "dp"), scatter_dimension=0, tiled=True),
        lax.psum_scatter(accum[4], ("tower", "dp"), scatter_dimension=0, tiled=True),
        lax.psum_scatter(accum[5], ("tower", "dp"), scatter_dimension=0, tiled=True),
        lax.psum_scatter(accum[6], ("tower", "dp"), scatter_dimension=0, tiled=True),
        lax.psum_scatter(accum[7], ("tower", "dp"), scatter_dimension=0, tiled=True),
        lax.psum_scatter(accum[8], ("tower", "dp"), scatter_dimension=0, tiled=True),
        lax.psum_scatter(accum[9], ("tower", "dp"), scatter_dimension=0, tiled=True),
        lax.psum_scatter(accum[10], ("tower", "dp"), scatter_dimension=0, tiled=True),
        lax.psum_scatter(accum[11], ("tower", "dp"), scatter_dimension=0, tiled=True),
        lax.psum_scatter(accum[12], ("tower", "dp"), scatter_dimension=0, tiled=True),
        lax.psum_scatter(accum[13], ("tower", "dp"), scatter_dimension=0, tiled=True),
    )
    class_sum = lax.psum(class_total, ("tower", "dp"))
    pooled_all = jnp.concatenate(pooled_parts, axis=0)[None]
    input_all = jnp.concatenate(input_parts, axis=0)[None]
    return (
        pooled_all,
        input_all,
        accum[0],
        accum[1],
        accum[2],
        accum[3],
        accum[4],
        accum[5],
        accum[6],
        accum[7],
        accum[8],
        accum[9],
        accum[10],
        accum[11],
        accum[12],
        accum[13],
        class_sum,
    )


def solution(mesh):
    return jax.shard_map(
        body,
        mesh=mesh,
        in_specs=(
            P("tower", "dp", None, None),
            P("tower", "dp"),
            P("dp"),
            P("dp", None),
            P("dp"),
            P("dp"),
            P("dp", None),
            P("dp"),
            P("dp"),
            P("dp"),
            P("dp", None),
            P("dp"),
            P("dp", None),
            P("dp"),
            P("dp"),
            P("dp"),
            P("dp", None),
            P(),
        ),
        out_specs=(
            P("tower", "dp", None),
            P("tower", "dp", None, None),
            P(("tower", "dp"), None),
            P(("tower", "dp")),
            P(("tower", "dp")),
            P(("tower", "dp"), None),
            P(("tower", "dp")),
            P(("tower", "dp")),
            P(("tower", "dp")),
            P(("tower", "dp"), None),
            P(("tower", "dp")),
            P(("tower", "dp"), None),
            P(("tower", "dp")),
            P(("tower", "dp")),
            P(("tower", "dp")),
            P(("tower", "dp"), None),
            P(),
        ),
        check_vma=False,
    )
```

profile of v0, /device:TPU:0, one launch (start us, length us, event | category | flops | bytes accessed | tf_op | source)
XLA Modules:
  0.0 913.4 jit_solution(18266142529048585072)
XLA Ops:
  22.4 79.4 %all-reduce.20 = (bf16[768]{0:T(1024)(128)(2,1)S(1)}, bf16[768]{0:T(1024)(128)(2,1)S(1)}, bf16[768]{0:T(1024)(128)(2,1)S(1)}, bf16[768]{0:T(1024)(128)(2,1)S(1)}...) all-reduce(bf16[768]{0:T(1024)(128)(2,1)S(1)} %dynamic-update-slice, ...), channel_id=1, replica_groups=mesh['tower'=2,'dp'=16] {'dp'}, use_global_device_ids=true, to_apply=%add.2 | all-reduce | flops 9216 | bytes 36864
  101.8 36.6 %all-gather = bf16[16,144,3]{1,2,0:T(4,128)(2,1)S(1)} all-gather(bf16[1,144,3]{1,2,0:T(4,128)(2,1)} %bitcast.232), channel_id=1, replica_groups=mesh['tower'=2,'dp'=16] {'dp'}, dimensions={0}, use_global_device_ids=true | all-gather | bytes 14688 | tf_op jit(solution)/shard_map/all_gather | solution.py:123
  140.2 4.5 fusion.225
  144.6 2.1 copy-done.13
  148.2 4.0 fusion.224
  152.2 2.2 copy-done.14
  155.9 4.5 fusion.37
  166.9 2.3 fusion.21
  171.8 2.5 fusion.216
  180.8 44.5 %all-gather.10.cloned.1.call-done = bf16[768,3072]{1,0:T(8,128)(2,1)} async-done(((bf16[48,3072]{1,0:T(8,128)(2,1)}), bf16[768,3072]{1,0:T(8,128)(2,1)}) %all-gather.10.cloned.1.call-update) | async-done | bytes 4718608 | tf_op jit(solution)/shard_map/all_gather | solution.py:117
  225.2 4.8 fusion.199
  230.1 2.7 copy-done.61
  232.8 34.9 %multiply_convert_fusion.1 = (bf16[512,3072]{1,0:T(8,128)(2,1)}, f32[512,3072]{1,0:T(8,128)}, bf16[512,3072]{1,0:T(8,128)(2,1)}, f32[512,3072]{1,0:T(8,128)}, f32[512,3072]{1,0:T(8,128)}) fusion(f32[3072]{0:T(1024)S(1)} %convert_element_type.203, f32[512,3072]{1,0:T(8,128)S(1)} %fusion.199, bf16[768,3072]{1,0:T(8,128)(2,1)S(1)} %copy-done.55, ...), kind=kOutput, calls=%fused_computation.22 | convolution fusion | flops 2625503232 | bytes 37771264 | tf_op jit(solution)/shard_map/dot_general | solution.py:153
  267.7 39.3 %all-gather.12.cloned.1.call-done = bf16[3072,768]{1,0:T(8,128)(2,1)} async-done(((bf16[192,768]{1,0:T(8,128)(2,1)}), bf16[3072,768]{1,0:T(8,128)(2,1)}) %all-gather.12.cloned.1.call-update) | async-done | bytes 4718608 | tf_op jit(solution)/shard_map/all_gather | solution.py:119
  307.0 6.2 fusion.218
  313.5 2.8 fusion.219
  323.5 10.1 %fusion.222 = (f32[3072]{0:T(1024)S(1)}, bf16[512,3072]{1,0:T(8,128)(2,1)}) fusion(f32[512,3072]{1,0:T(8,128)} %get-tuple-element.123, bf16[3072,768]{1,0:T(8,128)(2,1)S(1)} %copy-done.56, f32[512,768]{1,0:T(8,128)S(1)} %get-tuple-element.111, f32[512,3072]{1,0:T(8,128)} %get-tuple-element.168, f32[3072]{0:T(1024)S(1)} %convert_element_type.203), kind=kOutput, calls=%fused_computation.312 | convolution fusion | flops 2441475072 | bytes 22044672 | tf_op jit(solution)/shard_map/dot_general | solution.py:30
  333.6 6.1 multiply_reduce_fusion.5
  339.7 7.6 fusion.223
  347.4 6.6 fusion.211
  357.2 2.2 reshape.380
  359.4 4.1 fusion.102
  363.5 2.3 fusion.119
  365.8 7.7 fusion.91
  373.5 7.6 fusion.88
  381.1 2.0 fusion.210
  384.9 2.3 copy.131
  387.2 2.4 reshape.385
  389.7 4.4 fusion.103
  394.1 2.3 fusion.116
  397.6 2.2 convolution_add_fusion.3
  400.0 7.9 fusion.94
  407.9 1.9 copy.142
  415.1 7.9 fusion.97
  428.6 2.0 fusion.228
  430.6 5.2 add_bitcast_fusion
  435.8 8.0 copy.152
  443.9 5.4 fusion.60
  449.3 5.8 convolution_add_fusion.1
  455.2 5.3 fusion.144
  460.5 5.3 convolution_add_fusion
  471.3 41.2 %all-reduce.19 = (f32[768]{0:T(1024)S(1)}, f32[768]{0:T(1024)S(1)}, f32[768]{0:T(1024)S(1)}, f32[768]{0:T(1024)S(1)}, f32[768]{0:T(1024)S(1)}, /*index=5*/f32[30...) all-reduce(f32[768]{0:T(1024)S(1)} %add.319, ...), channel_id=3, replica_groups=mesh['tower'=2,'dp'=16] {'tower','dp'}, use_global_device_ids=true, to_apply=%region_31.32.clone | all-reduce | flops 16131 | bytes 129048
  518.5 4.8 convolution_add_fusion.4
  523.6 2.0 convolution_add_fusion.5
  525.7 2.0 maximum_bitcast_fusion
  527.7 95.2 %reduce-scatter.14.cloned.1.call-done = f32[24,2304]{1,0:T(8,128)} async-done(((f32[768,2304]{1,0:T(8,128)}), f32[24,2304]{1,0:T(8,128)}) %reduce-scatter.14.cloned.1.call-update) | async-done | bytes 221200
  622.9 141.2 %reduce-scatter.10.cloned.1.call-done = f32[24,3072]{1,0:T(8,128)} async-done(((f32[768,3072]{1,0:T(8,128)}), f32[24,3072]{1,0:T(8,128)}) %reduce-scatter.10.cloned.1.call-update) | async-done | bytes 294928 | tf_op jit(solution)/shard_map/reduce_scatter | solution.py:271
  764.1 142.2 %reduce-scatter.12.cloned.1.call-done = f32[96,768]{1,0:T(8,128)} async-done(((f32[3072,768]{1,0:T(8,128)}), f32[96,768]{1,0:T(8,128)}) %reduce-scatter.12.cloned.1.call-update) | async-done | bytes 294928 | tf_op jit(solution)/shard_map/reduce_scatter | solution.py:273
  (290 shorter events, 69.8 us)
Async XLA Ops:
  7.2 133.0 %all-gather.6.cloned.1.call-start = ((), (), s32[]{:S(2)}) async-start(), calls=%async_computation.4 | async-start | bytes 3760128 | tf_op jit(solution)/shard_map/all_gather | solution.py:110
  7.9 163.8 %all-gather.8.cloned.1.call-start = ((), (), s32[]{:S(2)}) async-start(), calls=%async_computation.5 | async-start | bytes 1253376 | tf_op jit(solution)/shard_map/all_gather | solution.py:113
  8.7 216.6 %all-gather.10.cloned.1.call-start = ((), (), s32[]{:S(2)}) async-start(), calls=%async_computation.6 | async-start | bytes 5013504 | tf_op jit(solution)/shard_map/all_gather | solution.py:117
  9.4 297.6 %all-gather.12.cloned.1.call-start = ((), (), s32[]{:S(2)}) async-start(), calls=%async_computation.7 | async-start | bytes 5013504 | tf_op jit(solution)/shard_map/all_gather | solution.py:119
  10.0 517.7 %reduce-scatter.8.cloned.1.call-start = ((), (), s32[]{:S(2)}) async-start(), calls=%async_computation.8 | async-start | bytes 2433024 | tf_op jit(solution)/shard_map/reduce_scatter | solution.py:267
  140.0 8.2 copy-start.32
  140.0 39.4 %copy-start.15 = (bf16[1,4,128,768]{3,2,1,0:T(8,128)(2,1)}, bf16[1,4,128,768]{3,2,1,0:T(8,128)(2,1)S(1)}, u32[]{:S(2)}) copy-start(bf16[1,4,128,768]{3,2,1,0:T(8,128)(2,1)S(1)} %get-tuple-element.131) | copy-start | bytes 2359300
  140.1 30.0 %copy-start.53 = (pred[4,128]{1,0:T(4,128)(4,1)}, pred[4,128]{1,0:T(4,128)(4,1)S(1)}, u32[]{:S(2)}) copy-start(pred[4,128]{1,0:T(4,128)(4,1)S(1)} %get-tuple-element.183) | copy-start | bytes 1540
  140.1 37.7 %copy-start.51 = (pred[4,128]{1,0:T(4,128)(4,1)}, pred[4,128]{1,0:T(4,128)(4,1)S(1)}, u32[]{:S(2)}) copy-start(pred[4,128]{1,0:T(4,128)(4,1)S(1)} %get-tuple-element.155) | copy-start | bytes 1540
  162.2 15.7 %copy-start.19 = (bf16[4,128,12,64]{1,0,3,2:T(4,128)(2,1)}, bf16[4,128,12,64]{1,0,3,2:T(4,128)(2,1)S(1)}, u32[]{:S(2)}) copy-start(bf16[4,128,12,64]{1,0,3,2:T(4,128)(2,1)S(1)} %reshape.376) | copy-start | bytes 2359300
  164.1 6.0 copy-start.23
  171.8 3.7 copy-start.40
  180.8 52.0 %copy-start.36 = (f32[512,768]{1,0:T(8,128)S(1)}, f32[512,768]{1,0:T(8,128)}, u32[]{:S(2)}) copy-start(f32[512,768]{1,0:T(8,128)} %copy-done.35) | copy-start | bytes 4718596
  225.2 7.5 copy-start.55
  307.0 6.5 copy-start.5
  307.0 6.5 copy-start.56
  317.4 1.2 collective-permute-start
  317.7 1.7 collective-permute-start.1
  322.2 11.4 %slice-start = ((s8[4718592]{0:T(1024)(128)(4,1)}), s8[4194304]{0:T(1024)(128)(4,1)S(1)}, s32[]{:S(2)}) async-start(s8[4718592]{0:T(1024)(128)(4,1)} %bitcast.233), calls=%async_computation.12 | async-start | bytes 8388608
  323.5 10.1 %copy-start.10 = (f32[512,768]{1,0:T(8,128)}, f32[512,768]{1,0:T(8,128)S(1)}, u32[]{:S(2)}) copy-start(f32[512,768]{1,0:T(8,128)S(1)} %get-tuple-element.111) | copy-start | bytes 4718596
  323.5 23.9 %copy-start.7 = (f32[512,768]{1,0:T(8,128)}, f32[512,768]{1,0:T(8,128)S(1)}, u32[]{:S(2)}) copy-start(f32[512,768]{1,0:T(8,128)S(1)} %get-tuple-element.143) | copy-start | bytes 4718596
  323.5 10.1 %slice-start.1 = ((s8[4718592]{0:T(1024)(128)(4,1)}), s8[524288]{0:T(1024)(128)(4,1)S(1)}, s32[]{:S(2)}) async-start(s8[4718592]{0:T(1024)(128)(4,1)} %bitcast.233), calls=%async_computation.13 | async-start | bytes 1048576
  347.3 6.6 copy-start.17
  347.4 7.8 copy-start.59
  355.1 4.3 copy-start.50
  355.1 4.3 copy-start.54
  357.2 6.3 copy-start.24
  365.8 7.7 copy-start.42
  383.2 14.1 %copy-start.9 = (f32[512,768]{1,0:T(8,128)}, f32[512,768]{1,0:T(8,128)S(1)}, u32[]{:S(2)}) copy-start(f32[512,768]{1,0:T(8,128)S(1)} %get-tuple-element.113) | copy-start | bytes 4718596
  383.2 6.5 copy-start.48
  383.2 6.5 copy-start.52
  389.7 4.4 copy-start.20
  389.7 4.4 copy-start.27
  399.8 10.1 %copy-start.43 = (bf16[4,128,12,64]{1,3,2,0:T(8,128)(2,1)S(1)}, bf16[4,128,12,64]{1,3,2,0:T(8,128)(2,1)}, u32[]{:S(2)}) copy-start(bf16[4,128,12,64]{1,3,2,0:T(8,128)(2,1)} %fusion.102) | copy-start | bytes 2359300
  399.8 223.1 %reduce-scatter.14.cloned.1.call-start = ((), (), s32[]{:S(2)}) async-start(), calls=%async_computation.11 | async-start | bytes 7299072
  407.9 5.0 copy-start.44
  407.9 5.6 copy-start.46
  409.9 15.4 %copy-start.2 = (bf16[4,128,12,64]{1,0,3,2:T(4,128)(2,1)}, bf16[4,128,12,64]{1,0,3,2:T(4,128)(2,1)S(1)}, u32[]{:S(2)}) copy-start(bf16[4,128,12,64]{1,0,3,2:T(4,128)(2,1)S(1)} %copy.142) | copy-start | bytes 2359300
  425.4 5.2 copy-start
  443.8 320.3 %reduce-scatter.10.cloned.1.call-start = ((), (), s32[]{:S(2)}) async-start(), calls=%async_computation.9 | async-start | bytes 9732096 | tf_op jit(solution)/shard_map/reduce_scatter | solution.py:271
  443.9 5.4 copy-start.18
  455.1 5.4 copy-start.8
  455.1 451.1 %reduce-scatter.12.cloned.1.call-start = ((), (), s32[]{:S(2)}) async-start(), calls=%async_computation.10 | async-start | bytes 9732096 | tf_op jit(solution)/shard_map/reduce_scatter | solution.py:273
  455.2 5.3 copy-start.6
  465.9 52.6 %copy-start.1 = (bf16[512,2304]{0,1:T(8,128)(2,1)S(1)}, bf16[512,2304]{0,1:T(8,128)(2,1)}, u32[]{:S(2)}) copy-start(bf16[512,2304]{0,1:T(8,128)(2,1)} %copy-done) | copy-start | bytes 7077892
  518.5 4.9 copy-start.12
  518.5 4.9 copy-start.39
  518.5 5.1 copy-start.57
  (26 other events, 51.4 us)
Sparse Core Ops, SparseCore 0:
  10.8 74.5 all-gather.5
  88.2 54.8 all-gather.7
  145.9 79.3 all-gather.9
  227.9 79.0 all-gather.11
  399.9 97.6 reduce-scatter.7
  504.7 118.1 reduce-scatter.13
  629.4 134.7 reduce-scatter.9
  771.6 134.6 reduce-scatter.11
where the time goes:
time: 917 us; the launch traced here: 913 us
  waiting for transfers between devices  466 us (51%)
  matrix products  184 us (20%)
  blocking collectives  157 us (17%)
  local copies, waits for them, and re-layouts  66.2 us (7%)
  other arithmetic  23 us (3%)
  between operations  17 us (2%)
    reduce_scatter x1, waiting for transfers between devices, body(): lax.psum_scatter(accum[9], ('tower', 'dp'), scatter_dimension=0, tiled=True)  142 us
    reduce_scatter x1, waiting for transfers between devices, body(): lax.psum_scatter(accum[7], ('tower', 'dp'), scatter_dimension=0, tiled=True)  141 us
    unnamed x2, blocking collectives  121 us
    unnamed x9, waiting for transfers between devices  97.9 us
    all_gather x1, waiting for transfers between devices, body(): proj_up = lax.all_gather(up_weight, 'dp', axis=0, tiled=True)  44.5 us
    dot_general x8, matrix products, contract_cols(): lax.dot_general(left, right, (((1,), (1,)), ((), ())), preferred_element_...  39.8 us
    dot_general x2, matrix products, body(): jnp.dot(first_low, proj_up, preferred_element_type=jnp.float32)  39.7 us
    all_gather x1, waiting for transfers between devices, body(): proj_down = lax.all_gather(down_weight, 'dp', axis=0, tiled=True)  39.3 us
  transfers between devices with their start and end apart: 10, of which 6 were waited for; matrix products, arithmetic and copies ran while one was open for 19% of the time, Pallas kernels for 0%

commit v1 on v0

v1 whole, which is shorter than its diff:
```python
from functools import partial

import jax
import jax.numpy as jnp
from jax import lax
from jax.sharding import PartitionSpec as P

HEADS = 12
HEAD_DIM = 64
NCLASS = 3
CHUNK = 384
FAR = 4

eps_norm = 1e-12
gap_soft = 0.01
highest = lax.Precision.HIGHEST
f32 = jnp.float32
b16 = jnp.bfloat16


def swap(x, axis, k):
    return lax.ppermute(x, axis, [(i, i ^ k) for i in range(lax.axis_size(axis))])


def places():
    low = lax.axis_size("dp") // FAR
    me = lax.axis_index("dp")
    return low, me // low, me % low


def in_order(pieces, me, axis):
    stack = jnp.stack(pieces, axis)
    return jnp.concatenate(
        [lax.dynamic_index_in_dim(stack, me ^ j, axis) for j in range(len(pieces))], axis
    )


def gather_rows(part):
    low, far, near = places()
    block = in_order([part] + [swap(part, "dp", j * low) for j in range(1, FAR)], far, 0)
    if low == 4:
        half = FAR // 2
        by_one, by_two = swap(block, "dp", 1), swap(block, "dp", 2)
        both = jnp.concatenate(
            [swap(by_one[:half], "dp", 2), swap(by_two[half:], "dp", 1)], 0
        )
        pieces = [block, by_one, by_two, both]
    else:
        pieces, bit = [block], 1
        while bit < low:
            pieces = pieces + [swap(p, "dp", bit) for p in pieces]
            bit *= 2
    return in_order(pieces, near, 1)


def to_chunks(shard):
    rows, cols = shard.shape
    half = cols // 2
    mine = lax.dynamic_slice_in_dim(shard, lax.axis_index("tower") * half, half, 1)
    return mine.reshape(rows, half // CHUNK, CHUNK).transpose(1, 0, 2).reshape(-1, CHUNK)


def from_chunks(mine, other, rows):
    low_half = lax.axis_index("tower") == 0
    a, b = jnp.where(low_half, mine, other), jnp.where(low_half, other, mine)
    both = jnp.stack([a, b])
    far, low, total = mine.shape[:3]
    n = total // rows
    both = both.reshape(2, far, low, n, rows, CHUNK).transpose(1, 2, 4, 0, 3, 5)
    return both.reshape(far * low * rows, 2 * n * CHUNK)


def tower_half(grad):
    tower = lax.axis_index("tower")
    low, _, _ = places()
    halves = grad.reshape((2, FAR, low, -1) + grad.shape[1:])
    got = swap(lax.dynamic_index_in_dim(halves, 1 - tower, 0, keepdims=False), "tower", 1)
    mine = lax.dynamic_index_in_dim(halves, tower, 0, keepdims=False)
    return (mine.astype(f32) + got.astype(f32)).astype(b16)


def add_low(a, b):
    return (a.astype(f32) + b.astype(f32)).astype(b16)


def scatter_rows(data):
    low, far, near = places()

    def at(k):
        return lax.dynamic_index_in_dim(data, near ^ k, 1, keepdims=False)

    if low == 4:
        half = FAR // 2
        corner = at(3)
        got_one, got_two = swap(corner[:half], "dp", 1), swap(corner[half:], "dp", 2)
        one, two = at(1), at(2)
        one = jnp.concatenate([one[:half], add_low(one[half:], got_two)], 0)
        two = jnp.concatenate([add_low(two[:half], got_one), two[half:]], 0)
        own = at(0).astype(f32) + swap(one, "dp", 1).astype(f32) + swap(two, "dp", 2).astype(f32)
    else:
        blocks, bit = [at(k) for k in range(low)], low // 2
        while bit:
            blocks = [
                add_low(blocks[k], swap(blocks[k + bit], "dp", bit)) for k in range(bit)
            ]
            bit //= 2
        own = blocks[0].astype(f32)
    total = lax.dynamic_index_in_dim(own, far, 0, keepdims=False)
    for j in range(1, FAR):
        sent = lax.dynamic_index_in_dim(own, far ^ j, 0, keepdims=False).astype(b16)
        total = total + swap(sent, "dp", j * low).astype(f32)
    return total


def sum_all(x):
    x = x + swap(x, "tower", 1)
    bit = 1
    while bit < lax.axis_size("dp"):
        x = x + swap(x, "dp", bit)
        bit *= 2
    return x


def contract_rows(left, right):
    return lax.dot_general(left, right, (((0,), (0,)), ((), ())), preferred_element_type=f32)


def contract_cols(left, right):
    return lax.dot_general(left, right, (((1,), (1,)), ((), ())), preferred_element_type=f32)


def norm_forward(hidden, gain, shift):
    center = hidden - jnp.mean(hidden, axis=-1, keepdims=True)
    inverse = lax.rsqrt(jnp.mean(center * center, axis=-1, keepdims=True) + eps_norm)
    normal = center * inverse
    return (normal * gain + shift, normal, inverse)


def norm_backward(upstream, normal, inverse, gain):
    scaled = upstream * gain
    inner = scaled - jnp.mean(scaled, axis=-1, keepdims=True)
    inner = inner - normal * jnp.mean(scaled * normal, axis=-1, keepdims=True)
    return (inverse * inner, jnp.sum(upstream * normal, axis=0), jnp.sum(upstream, axis=0))


def body(
    embeddings, lengths, labels, qkv_weight, query_bias, value_bias, out_weight, out_bias, attn_gain,
    attn_shift, up_weight, up_bias, down_weight, down_bias, ffn_gain, ffn_shift, head_weight, head_bias,
):
    width = embeddings.shape[-1]
    seq_len = embeddings.shape[2]
    count = embeddings.shape[1]
    rows = count * seq_len
    scale = HEAD_DIM ** (-0.5)
    heads_shape = (count, seq_len, HEADS, HEAD_DIM)
    leading = lax.axis_index("tower") == 0
    gelu_exact = partial(jax.nn.gelu, approximate=False)
    groups = lax.axis_size("dp")

    small = (
        query_bias, value_bias, out_bias, attn_gain, attn_shift, down_bias, ffn_gain, ffn_shift, up_bias,
        head_weight.reshape(-1),
    )
    small_sizes = [s.shape[0] for s in small]
    packed = jnp.concatenate(small)
    pad_rows = -(-packed.shape[0] // (8 * CHUNK)) * 8
    packed = jnp.pad(packed, (0, pad_rows * CHUNK - packed.shape[0])).reshape(pad_rows, CHUNK)
    shard_rows = qkv_weight.shape[0]
    first_part = jnp.concatenate([to_chunks(qkv_weight), to_chunks(out_weight), packed], 0)
    cut = first_part.shape[0] - pad_rows
    near_first = gather_rows(first_part)
    other_first = swap(near_first[:, :, :cut], "tower", 1)
    near_up = gather_rows(to_chunks(up_weight))
    other_up = swap(near_up, "tower", 1)
    proj_down = lax.all_gather(
        lax.dynamic_slice_in_dim(
            down_weight, lax.axis_index("tower") * (down_weight.shape[0] // 2), down_weight.shape[0] // 2, 0
        ),
        ("dp", "tower"), axis=0, tiled=True,
    )
    n_qkv = qkv_weight.shape[1] // 2 // CHUNK * shard_rows
    proj_qkv = from_chunks(near_first[:, :, :n_qkv], other_first[:, :, :n_qkv], shard_rows)
    proj_out = from_chunks(near_first[:, :, n_qkv:cut], other_first[:, :, n_qkv:cut], shard_rows)
    proj_up = from_chunks(near_up, other_up, shard_rows)
    flat_small = near_first[:, :, cut:].reshape(groups, pad_rows * CHUNK)
    whole, at = [], 0
    for size in small_sizes:
        whole.append(flat_small[:, at : at + size].reshape(-1).astype(f32))
        at += size
    (bias_query, bias_value, bias_out, gain_one, shift_one, bias_down, gain_two, shift_two, bias_up, head_full) = whole
    head_full = head_full.reshape(-1, NCLASS)

    flat = embeddings[0].reshape(rows, width)
    sent_len = lengths[0]
    joined = jnp.dot(flat, proj_qkv, preferred_element_type=f32)
    query_heads = (joined[:, :width] + bias_query).astype(b16).reshape(heads_shape)
    key_heads = joined[:, width : 2 * width].astype(b16).reshape(heads_shape)
    value_heads = (joined[:, 2 * width :] + bias_value).astype(b16).reshape(heads_shape)
    valid = jnp.arange(seq_len)[None, :] < sent_len[:, None]
    raw = jnp.einsum("bqhd,bkhd->bhqk", query_heads, key_heads, preferred_element_type=f32)
    scores = jnp.where(valid[:, None, None, :], raw * scale, -1000000000.0)
    top = jnp.max(scores, axis=-1, keepdims=True)
    total = jnp.log(jnp.sum(jnp.exp(scores - top), axis=-1, keepdims=True)) + top
    probs = jnp.exp(scores - total)
    probs_low = probs.astype(b16)
    context = jnp.einsum("bhqk,bkhd->bqhd", probs_low, value_heads, preferred_element_type=f32)
    context = context.reshape(rows, width).astype(b16)
    attended = jnp.dot(context, proj_out, preferred_element_type=f32) + bias_out
    first, first_norm, first_inv = norm_forward(flat.astype(f32) + attended, gain_one, shift_one)
    first_low = first.astype(b16)
    pre_act = jnp.dot(first_low, proj_up, preferred_element_type=f32) + bias_up
    activated = gelu_exact(pre_act).astype(b16)
    second = jnp.dot(activated, proj_down, preferred_element_type=f32) + bias_down
    output, second_norm, second_inv = norm_forward(first + second, gain_two, shift_two)
    mask = valid.astype(f32)
    length_f = sent_len.astype(f32)[:, None]
    pooled = jnp.sum(output.reshape(count, seq_len, width) * mask[:, :, None], axis=1) / length_f

    partner = swap(pooled, "tower", 1)
    left = jnp.where(leading, pooled, partner)
    right = jnp.where(leading, partner, pooled)
    gap = left - right
    soft_gap = jnp.sqrt(gap * gap + gap_soft)
    feats = jnp.concatenate([left, right, soft_gap], axis=1)
    logits = jnp.dot(feats, head_full, precision=highest) + head_bias.astype(f32)
    onehot = (labels[:, None] == jnp.arange(NCLASS)[None, :]).astype(f32)
    logit_grad = jax.nn.softmax(logits, axis=-1) - onehot
    head_grad = 0.5 * jnp.dot(feats.T, logit_grad, precision=highest)
    class_grad = 0.5 * jnp.sum(logit_grad, axis=0)
    feat_grad = jnp.dot(logit_grad, head_full.T, precision=highest)
    slope = gap / soft_gap
    left_grad = feat_grad[:, :width] + slope * feat_grad[:, 2 * width :]
    right_grad = feat_grad[:, width : 2 * width] - slope * feat_grad[:, 2 * width :]
    pooled_grad = jnp.where(leading, left_grad, right_grad)

    output_grad = ((pooled_grad / length_f)[:, None, :] * mask[:, :, None]).reshape(rows, width)
    sum_grad, gain_two_grad, shift_two_grad = norm_backward(output_grad, second_norm, second_inv, gain_two)
    down_bias_grad = jnp.sum(sum_grad, axis=0)
    sum_low = sum_grad.astype(b16)
    down_grad = contract_rows(activated, sum_low).astype(b16)
    down_out = scatter_rows(tower_half(down_grad))
    act_grad = contract_cols(sum_low, proj_down)
    pre_grad = jax.vjp(gelu_exact, pre_act)[1](act_grad)[0]
    up_bias_grad = jnp.sum(pre_grad, axis=0)
    pre_low = pre_grad.astype(b16)
    up_grad = contract_rows(first_low, pre_low).astype(b16)
    up_out = scatter_rows(tower_half(up_grad))
    first_grad = sum_grad + contract_cols(pre_low, proj_up)
    mid_grad, gain_one_grad, shift_one_grad = norm_backward(first_grad, first_norm, first_inv, gain_one)
    out_bias_grad = jnp.sum(mid_grad, axis=0)
    mid_low = mid_grad.astype(b16)
    out_grad = contract_rows(context, mid_low).astype(b16)
    context_grad = contract_cols(mid_low, proj_out).astype(b16).reshape(heads_shape)
    prob_grad = jnp.einsum("bqhd,bkhd->bhqk", context_grad, value_heads, preferred_element_type=f32)
    value_grad = jnp.einsum("bhqk,bqhd->bkhd", probs_low, context_grad, preferred_element_type=f32)
    score_grad = probs * (prob_grad - jnp.sum(prob_grad * probs, axis=-1, keepdims=True)) * scale
    score_low = score_grad.astype(b16)
    query_grad = jnp.einsum("bhqk,bkhd->bqhd", score_low, key_heads, preferred_element_type=f32)
    key_grad = jnp.einsum("bhqk,bqhd->bkhd", score_low, query_heads, preferred_element_type=f32)
    qkv_grad = jnp.concatenate(
        [query_grad.reshape(rows, width), key_grad.reshape(rows, width), value_grad.reshape(rows, width)], axis=1
    ).astype(b16)
    query_bias_grad = jnp.sum(qkv_grad[:, :width].astype(f32), axis=0)
    value_bias_grad = jnp.sum(qkv_grad[:, 2 * width :].astype(f32), axis=0)
    qkv_full_grad = contract_rows(flat, qkv_grad).astype(b16)
    last_out = scatter_rows(tower_half(jnp.concatenate([qkv_full_grad, out_grad], 1)))
    input_grad = contract_cols(qkv_grad, proj_qkv) + mid_grad

    vectors = (
        query_bias_grad, value_bias_grad, out_bias_grad, gain_one_grad, shift_one_grad, up_bias_grad, down_bias_grad,
        gain_two_grad, shift_two_grad, head_grad.reshape(-1), class_grad,
    )
    sizes = [v.shape[0] for v in vectors]
    flat_vec = jnp.concatenate(vectors)
    padded = -(-flat_vec.shape[0] // 1024) * 1024
    summed = sum_all(jnp.pad(flat_vec, (0, padded - flat_vec.shape[0])).reshape(-1, 128)).reshape(-1)
    place = lax.axis_index("tower") * groups + lax.axis_index("dp")
    outs, at = [], 0
    for size in sizes[:-1]:
        mine = size // (2 * groups)
        outs.append(lax.dynamic_slice_in_dim(summed, at + place * mine, mine))
        at += size
    class_sum = summed[at : at + NCLASS]
    n_qkv_cols = 3 * width
    return (
        pooled[None],
        input_grad.reshape(embeddings.shape),
        last_out[:, :n_qkv_cols],
        outs[0], outs[1],
        last_out[:, n_qkv_cols:],
        outs[2], outs[3], outs[4],
        up_out,
        outs[5],
        down_out,
        outs[6], outs[7], outs[8],
        outs[9].reshape(-1, NCLASS),
        class_sum,
    )


def solution(mesh):
    rows, vec = P("dp", None), P("dp")
    out_rows, out_vec = P(("tower", "dp"), None), P(("tower", "dp"))
    return jax.shard_map(
        body,
        mesh=mesh,
        in_specs=(
            P("tower", "dp", None, None), P("tower", "dp"), vec,
            rows, vec, vec, rows, vec, vec, vec, rows, vec, rows, vec, vec, vec, rows, P(),
        ),
        out_specs=(
            P("tower", "dp", None), P("tower", "dp", None, None),
            out_rows, out_vec, out_vec, out_rows, out_vec, out_vec, out_vec, out_rows, out_vec, out_rows, out_vec,
            out_vec, out_vec, out_rows, P(),
        ),
        check_vma=False,
    )
```

time: 917 us -> 459 us (0.50)
  waiting for transfers between devices: 466 us -> 87.3 us
  blocking collectives: 157 us -> 0 us
  starting transfers between devices: 1 us -> 56.4 us
  other arithmetic: 23 us -> 51.4 us
  matrix products: 184 us -> 157 us
  local copies, waits for them, and re-layouts: 66.2 us -> 84.4 us
    reduce_scatter x3 -> x0, waiting for transfers between devices: 283 us -> none  [the longest x1 142 us: body(): lax.psum_scatter(accum[9], ('tower', 'dp'), scatter_dimension=0, tiled=True)]
    unnamed x2 -> x0, blocking collectives: 121 us -> none
    unnamed x9 -> x1, waiting for transfers between devices: 97.9 us -> 0.02 us
    ppermute x2 -> x46, waiting for transfers between devices: 0.39 us -> 87.3 us  [swap(): lax.ppermute(x, axis, [(i, i ^ k) for i in range(lax.axis_size(axis))])]
    all_gather x4 -> x1, waiting for transfers between devices: 83.8 us -> 0.01 us  [body(): lax.all_gather(lax.dynamic_slice_in_dim(down_weight, lax.axis_index('towe...]
    ppermute x2 -> x46, starting transfers between devices: 0.51 us -> 56.3 us  [swap(): lax.ppermute(x, axis, [(i, i ^ k) for i in range(lax.axis_size(axis))])]
    all_gather x1 -> x0, blocking collectives: 36.6 us -> none  [body(): proj_head = lax.all_gather(head_weight, 'dp', axis=0, tiled=True)]
    unnamed x163 -> x135, local copies, waits for them, and re-layouts: 36 us -> 11.9 us
  transfers between devices with their start and end apart: 10 -> 47, of which waited for: 6 -> 13; matrix products, arithmetic and copies ran while one was open for 19% -> 39% of each run, Pallas kernels for 0% -> 0%
where the time goes in v1:
time: 459 us; the launch traced here: 452 us
  matrix products  157 us (34%)
  waiting for transfers between devices  87.3 us (19%)
  local copies, waits for them, and re-layouts  84.4 us (18%)
  starting transfers between devices  56.4 us (12%)
  other arithmetic  51.4 us (11%)
  between operations  15.7 us (3%)
    ppermute x46, waiting for transfers between devices, swap(): lax.ppermute(x, axis, [(i, i ^ k) for i in range(lax.axis_size(axis))])  87.3 us
    ppermute x46, starting transfers between devices, swap(): lax.ppermute(x, axis, [(i, i ^ k) for i in range(lax.axis_size(axis))])  56.3 us
    dot_general x4, matrix products, contract_cols(): lax.dot_general(left, right, (((1,), (1,)), ((), ())), preferred_element_...  36.8 us
    dot_general x1, matrix products, body(): pre_act = jnp.dot(first_low, proj_up, preferred_element_type=f32) + bias_up  35.1 us
    dot_general x4, matrix products, contract_rows(): lax.dot_general(left, right, (((0,), (0,)), ((), ())), preferred_element_...  25.5 us
    reshape x2, local copies, waits for them, and re-layouts, from_chunks(): return both.reshape(far * low * rows, 2 * n * CHUNK)  18.8 us
    dot_general x1, matrix products, body(): jnp.einsum('bhqk,bqhd->bkhd', score_low, query_heads, preferred_element_t...  13.5 us
    dot_general x1, matrix products, body(): jnp.einsum('bhqk,bkhd->bqhd', score_low, key_heads, preferred_element_typ...  12.9 us
  transfers between devices with their start and end apart: 47, of which 13 were waited for; matrix products, arithmetic and copies ran while one was open for 39% of the time, Pallas kernels for 0%

profile of v1, /device:TPU:0, one launch (start us, length us, event | category | flops | bytes accessed | tf_op | source)
XLA Modules:
  0.0 452.4 jit_solution(3822002038029970471)
XLA Ops:
  8.2 3.1 collective-permute-start.8
  11.3 2.6 collective-permute-start.9
  16.7 6.1 %concatenate.57 = bf16[1008]{0:T(1024)(128)(2,1)S(1)} concatenate(bf16[48]{0:T(256)(128)(2,1)} %param.22, bf16[48]{0:T(256)(128)(2,1)} %param.23, bf16[48]{0:T(256)(128)(2,1)} %param.25, bf16[48]{0:T(256)(128)(2,1)} %param.26, bf16[48]{0:T(256)(128)(2,1)} %param.27, bf16[48]{0:T(256)(128)(2,1)} %param.31, bf16[48]{0:T(256)(128)(2,1)} %param.32, bf16[48]{0:T(256)(128)(2,1)} %param.33, ...), dimensions={0} | concatenate | bytes 4032 | tf_op jit(solution)/shard_map/concatenate | solution.py:165
  23.8 3.5 collective-permute-start.1
  30.9 7.5 %collective-permute-done.1 = bf16[200,384]{1,0:T(8,128)(2,1)S(1)} collective-permute-done((bf16[200,384]{1,0:T(8,128)(2,1)S(1)}, bf16[200,384]{1,0:T(8,128)(2,1)S(1)}, u32[]{:S(2)}, u32[]{:S(2)}) %collective-permute-start.1) | collective-permute-done | bytes 153632 | tf_op jit(solution)/shard_map/ppermute | solution.py:22
  48.9 8.3 %collective-permute-done.3 = bf16[4,200,384]{2,1,0:T(8,128)(2,1)S(1)} collective-permute-done((bf16[4,200,384]{2,1,0:T(8,128)(2,1)}, bf16[4,200,384]{2,1,0:T(8,128)(2,1)S(1)}, u32[]{:S(2)}, u32[]{:S(2)}) %collective-permute-start.3) | collective-permute-done | bytes 614432 | tf_op jit(solution)/shard_map/ppermute | solution.py:22
  60.6 4.4 collective-permute-done.13
  79.0 2.9 broadcast_select_fusion.1
  84.2 5.3 %maximum_bitcast_fusion.1 = bf16[4,4,48,2,4,384]{5,4,3,2,1,0:T(4,128)(2,1)} fusion(bf16[1,4,4,4,48,384]{5,3,0,4,2,1:T(4,128)(2,1)S(1)} %copy.108, bf16[1,4,4,4,48,384]{5,3,0,4,2,1:T(4,128)(2,1)S(1)} %copy.107), kind=kLoop, calls=%fused_computation.30 | loop fusion | flops 2359296 | bytes 9437184 | tf_op jit(solution)/shard_map/transpose | solution.py:69
  89.5 8.7 %reshape.432 = bf16[768,3072]{1,0:T(8,128)(2,1)} reshape(bf16[4,4,48,2,4,384]{5,4,3,2,1,0:T(4,128)(2,1)} %maximum_bitcast_fusion.1) | data formatting | bytes 9437184 | tf_op jit(solution)/shard_map/reshape | solution.py:70
  102.3 5.3 %maximum_bitcast_fusion = bf16[4,4,48,2,3,384]{5,4,3,2,1,0:T(4,128)(2,1)} fusion(bf16[1,4,4,3,48,384]{5,3,0,4,2,1:T(4,128)(2,1)S(1)} %copy.97, bf16[1,4,4,3,48,384]{5,3,0,4,2,1:T(4,128)(2,1)S(1)} %copy.96), kind=kLoop, calls=%fused_computation.29 | loop fusion | flops 1769472 | bytes 7077888 | tf_op jit(solution)/shard_map/transpose | solution.py:69
  107.6 10.0 %reshape.423 = bf16[768,2304]{1,0:T(8,128)(2,1)} reshape(bf16[4,4,48,2,3,384]{5,4,3,2,1,0:T(4,128)(2,1)} %maximum_bitcast_fusion) | data formatting | bytes 7077888 | tf_op jit(solution)/shard_map/reshape | solution.py:70
  117.6 6.7 %convolution_bitcast_fusion = f32[1024,2304]{0,1:T(8,128)S(1)} fusion(bf16[768,2304]{1,0:T(8,128)(2,1)} %reshape.423, bf16[1024,768]{1,0:T(8,128)(2,1)S(1)} %bitcast.367), kind=kOutput, calls=%fused_computation.18 | convolution fusion | flops 3623878656 | bytes 14548992 | tf_op jit(solution)/shard_map/dot_general | solution.py:195
  141.7 35.1 %multiply_convert_fusion = (bf16[1024,3072]{1,0:T(8,128)(2,1)}, f32[1024,3072]{1,0:T(8,128)}, f32[1024,3072]{1,0:T(8,128)}) fusion(f32[3072]{0:T(1024)S(1)} %reshape.452, bf16[768,3072]{1,0:T(8,128)(2,1)S(1)} %bitcast.331, f32[1024,768]{1,0:T(8,128)S(1)} %get-tuple-element.151, f32[768]{0:T(1024)S(1)} %reshape.451, f32[768]{0:T(1024)S(1)} %reshape.450, ...), kind=kOutput, calls=%fused_computation.4 | convolution fusion | flops 5043388416 | bytes 39348224 | tf_op jit(solution)/shard_map/dot_general | solution.py:211
  176.8 9.2 %fusion.141 = (f32[1024]{0:T(1024)S(1)}, f32[1024,768]{1,0:T(8,128)S(1)}) fusion(f32[768]{0:T(1024)S(1)} %reshape.453, bf16[1024,3072]{1,0:T(8,128)(2,1)} %get-tuple-element.68, bf16[3072,768]{1,0:T(8,128)(2,1)} %all-gather.2.cloned.1.call-done, f32[768]{0:T(1024)S(1)} %reshape.451, f32[768]{0:T(1024)S(1)} %reshape.450, f32[1024]{0:T(1024)S(1)} %add_rsqrt_fusion.1, ...), kind=kOutput, calls=%fused_computation.310 | convolution fusion | flops 4837342208 | bytes 17323008 | tf_op jit(solution)/shard_map/dot_general | solution.py:213
  194.1 7.1 %convolution_convert_fusion = bf16[3072,768]{1,0:T(8,128)(2,1)} fusion(bf16[1024,3072]{1,0:T(8,128)(2,1)S(1)} %bitcast.372, f32[1024,768]{1,0:T(8,128)S(1)} %get-tuple-element.62), kind=kOutput, calls=%fused_computation.25 | convolution fusion | flops 4834983936 | bytes 14155776 | tf_op jit(solution)/shard_map/dot_general | solution.py:125
  201.2 18.6 %fusion.143 = (f32[3072]{0:T(1024)S(1)}, bf16[1024,3072]{1,0:T(8,128)(2,1)}) fusion(f32[1024,3072]{1,0:T(8,128)} %get-tuple-element.69, bf16[3072,768]{1,0:T(8,128)(2,1)} %all-gather.2.cloned.1.call-done, f32[1024,768]{1,0:T(8,128)} %copy-done.19, f32[1024,3072]{1,0:T(8,128)} %get-tuple-element.152, f32[3072]{0:T(1024)S(1)} %reshape.452), kind=kOutput, calls=%fused_computation.312 | convolution fusion | flops 4882953216 | bytes 39346176 | tf_op jit(solution)/shard_map/dot_general | solution.py:129
  219.8 10.2 %convolution_convert_fusion.1 = bf16[768,3072]{1,0:T(8,128)(2,1)} fusion(bf16[1024,3072]{1,0:T(8,128)(2,1)} %get-tuple-element.159, f32[1024,768]{1,0:T(8,128)S(1)} %get-tuple-element.151, f32[768]{0:T(1024)S(1)} %reshape.451, f32[768]{0:T(1024)S(1)} %reshape.450, f32[1024]{0:T(1024)S(1)} %add_rsqrt_fusion.1, f32[1024]{0:T(1024)S(1)} %broadcast_multiply_fusion.4), kind=kOutput, calls=%fused_computation.26 | convolution fusion | flops 4838129664 | bytes 14170112 | tf_op jit(solution)/shard_map/dot_general | solution.py:125
  230.1 8.4 %multiply_reduce_fusion.2 = (f32[768]{0:T(1024)S(1)}, f32[1024]{0:T(1024)S(1)}, f32[1024]{0:T(1024)S(1)}, f32[768]{0:T(1024)S(1)}, f32[1024,768]{1,0:T(8,128)S(1)}) fusion(f32[1024,768]{1,0:T(8,128)S(1)} %get-tuple-element.151, f32[1024]{0:T(1024)S(1)} %add_rsqrt_fusion.1, f32[1024]{0:T(1024)S(1)} %broadcast_multiply_fusion.4, f32[768]{0:T(1024)S(1)} %reshape.450, ...), kind=kOutput, calls=%fused_computation.59 | convolution fusion | flops 4839698432 | bytes 20472832 | tf_op jit(solution)/shard_map/dot_general | solution.py:129
  244.0 6.5 %fusion.64 = bf16[8,128,12,64]{1,3,2,0:T(8,128)(2,1)} fusion(bf16[8,128,12,64]{1,0,3,2:T(8,128)(2,1)S(1)} %bitcast.326, f32[8,12,128]{2,1,0:T(8,128)S(1)} %copy-done.35, f32[8,12,128,128]{2,3,1,0:T(8,128)} %copy-done.10, pred[8,128]{1,0:T(8,128)(4,1)S(1)} %copy-done.40), kind=kOutput, calls=%fused_computation.114 | convolution fusion | flops 208404480 | bytes 9487360 | tf_op jit(solution)/shard_map/bhqk,bqhd->bkhd/dot_general | solution.py:255
  250.5 3.7 fusion.68
  254.2 12.9 %fusion.60 = bf16[8,128,12,64]{1,3,2,0:T(8,128)(2,1)} fusion(f32[8,12,128,128]{2,3,1,0:T(8,128)} %fusion.68, f32[8,12,128]{2,1,0:T(8,128)S(1)} %copy-done.35, f32[8,12,128,128]{2,3,1,0:T(8,128)} %copy-done.10, pred[8,128]{1,0:T(8,128)(4,1)S(1)} %copy-done.40, bf16[8,128,12,64]{1,0,3,2:T(8,128)(2,1)S(1)} %bitcast.342), kind=kOutput, calls=%fused_computation.112 | convolution fusion | flops 219426944 | bytes 15778816 | tf_op jit(solution)/shard_map/bhqk,bkhd->bqhd/dot_general | solution.py:258
  267.1 13.5 %fusion.57 = bf16[8,128,12,64]{1,3,2,0:T(8,128)(2,1)} fusion(f32[8,12,128,128]{2,3,1,0:T(8,128)} %fusion.68, f32[8,12,128]{2,1,0:T(8,128)S(1)} %copy-done.35, f32[8,12,128,128]{2,3,1,0:T(8,128)} %copy-done.10, pred[8,128]{1,0:T(8,128)(4,1)S(1)} %copy-done.40, bf16[8,128,12,64]{1,0,3,2:T(8,128)(2,1)S(1)} %bitcast.340), kind=kOutput, calls=%fused_computation.111 | convolution fusion | flops 219426944 | bytes 15778816 | tf_op jit(solution)/shard_map/bhqk,bqhd->bkhd/dot_general | solution.py:259
  283.5 4.3 constant_dynamic-slice_fusion.1
  293.2 2.1 reshape.441
  295.3 2.8 copy.120
  303.1 6.7 %fusion.12 = bf16[768,2304]{0,1:T(8,128)(2,1)S(1)} fusion(bf16[1024,2304]{0,1:T(8,128)(2,1)} %bitcast_dynamic-update-slice_fusion, bf16[1024,768]{1,0:T(8,128)(2,1)S(1)} %bitcast.369), kind=kOutput, calls=%fused_computation.40 | convolution fusion | flops 3625648128 | bytes 9830400 | tf_op jit(solution)/shard_map/dot_general | solution.py:125
  311.4 2.8 collective-permute-done.26
  315.7 2.5 pad_maximum_fusion
  318.1 6.6 %copy.121 = bf16[768,3072]{1,0:T(8,128)(2,1)} copy(bf16[768,3072]{0,1:T(8,128)(2,1)} %pad_maximum_fusion) | data formatting | bytes 9437184 | tf_op jit(solution)/shard_map/concatenate | solution.py:266
  324.8 2.1 collective-permute-start.28
  326.9 3.3 dynamic-slice_bitcast_fusion
  330.3 2.2 collective-permute-start.29
  332.5 8.4 %convolution_add_fusion = f32[1024,768]{1,0:T(8,128)} fusion(f32[1024,768]{1,0:T(8,128)} %copy-done.17, bf16[1024,2304]{0,1:T(8,128)(2,1)} %bitcast_dynamic-update-slice_fusion, bf16[768,2304]{1,0:T(8,128)(2,1)S(1)} %copy-done.16), kind=kOutput, calls=%fused_computation.95 | convolution fusion | flops 3624665088 | bytes 14548992 | tf_op jit(solution)/shard_map/dot_general | solution.py:129
  343.5 3.1 fusion.9
  347.5 2.7 fusion.10
  353.7 2.6 fusion.11
  359.5 3.5 collective-permute-done.31
  364.0 5.3 %collective-permute-done.18 = bf16[2,24,3072]{2,1,0:T(8,128)(2,1)S(1)} collective-permute-done((bf16[2,24,3072]{2,1,0:T(8,128)(2,1)S(1)}, bf16[2,24,3072]{2,1,0:T(8,128)(2,1)S(1)}, u32[]{:S(2)}, u32[]{:S(2)}) %collective-permute-start.18) | collective-permute-done | bytes 294944 | tf_op jit(solution)/shard_map/ppermute | solution.py:22
  371.6 10.8 %collective-permute-done.40 = bf16[4,96,768]{2,1,0:T(8,128)(2,1)S(1)} collective-permute-done((bf16[4,96,768]{2,1,0:T(8,128)(2,1)S(1)}, bf16[4,96,768]{2,1,0:T(8,128)(2,1)S(1)}, u32[]{:S(2)}, u32[]{:S(2)}) %collective-permute-start.40) | collective-permute-done | bytes 589856 | tf_op jit(solution)/shard_map/ppermute | solution.py:22
  385.3 21.4 %collective-permute-done.19 = bf16[4,24,3072]{2,1,0:T(8,128)(2,1)S(1)} collective-permute-done((bf16[4,24,3072]{2,1,0:T(8,128)(2,1)S(1)}, bf16[4,24,3072]{2,1,0:T(8,128)(2,1)S(1)}, u32[]{:S(2)}, u32[]{:S(2)}) %collective-permute-start.19) | collective-permute-done | bytes 589856 | tf_op jit(solution)/shard_map/ppermute | solution.py:22
  408.3 2.6 collective-permute-start.23
  412.5 2.5 collective-permute-done.22
  414.9 2.6 collective-permute-start.45
  417.5 11.3 %collective-permute-done.23 = bf16[24,3072]{1,0:T(8,128)(2,1)S(1)} collective-permute-done((bf16[24,3072]{1,0:T(8,128)(2,1)S(1)}, bf16[24,3072]{1,0:T(8,128)(2,1)S(1)}, u32[]{:S(2)}, u32[]{:S(2)}) %collective-permute-start.23) | collective-permute-done | bytes 147488 | tf_op jit(solution)/shard_map/ppermute | solution.py:22
  428.8 3.5 collective-permute-start.36
  433.7 2.6 collective-permute-start.37
  437.1 7.5 %collective-permute-done.36 = bf16[24,3072]{1,0:T(8,128)(2,1)S(1)} collective-permute-done((bf16[24,3072]{1,0:T(8,128)(2,1)S(1)}, bf16[24,3072]{1,0:T(8,128)(2,1)S(1)}, u32[]{:S(2)}, u32[]{:S(2)}) %collective-permute-start.36) | collective-permute-done | bytes 147488 | tf_op jit(solution)/shard_map/ppermute | solution.py:22
  (352 shorter events, 111.2 us)
Async XLA Ops:
  7.2 169.6 %all-gather.2.cloned.1.call-start = ((), (), s32[]{:S(2)}) async-start(), calls=%async_computation | async-start | bytes 4866048 | tf_op jit(solution)/shard_map/all_gather | solution.py:175
  8.2 19.1 %collective-permute-start.8 = (bf16[192,384]{1,0:T(8,128)(2,1)S(1)}, bf16[192,384]{1,0:T(8,128)(2,1)S(1)}, u32[]{:S(2)}, u32[]{:S(2)}) collective-permute-start(bf16[192,384]{1,0:T(8,128)(2,1)S(1)} %bitcast.349), channel_id=1, source_target_pairs={{0,4},{1,5},{2,6},{3,7},{4,0},{5,1},{6,2},{7,3},{8,12},{9,13},{10,... | collective-permute-start | bytes 442376 | tf_op jit(solution)/shard_map/ppermute | solution.py:22
  11.3 16.0 %collective-permute-start.9 = (bf16[192,384]{1,0:T(8,128)(2,1)S(1)}, bf16[192,384]{1,0:T(8,128)(2,1)S(1)}, u32[]{:S(2)}, u32[]{:S(2)}) collective-permute-start(bf16[192,384]{1,0:T(8,128)(2,1)S(1)} %bitcast.350), channel_id=1, source_target_pairs={{0,8},{1,9},{2,10},{3,11},{4,12},{5,13},{6,14},{7,15},{8,0},{9,1},... | collective-permute-start | bytes 442376 | tf_op jit(solution)/shard_map/ppermute | solution.py:22
  13.9 13.4 %collective-permute-start.10 = (bf16[192,384]{1,0:T(8,128)(2,1)S(1)}, bf16[192,384]{1,0:T(8,128)(2,1)S(1)}, u32[]{:S(2)}, u32[]{:S(2)}) collective-permute-start(bf16[192,384]{1,0:T(8,128)(2,1)S(1)} %bitcast.351), channel_id=1, source_target_pairs={{0,12},{1,13},{2,14},{3,15},{4,8},{5,9},{6,10},{7,11},{8,4},{9,5},... | collective-permute-start | bytes 442376 | tf_op jit(solution)/shard_map/ppermute | solution.py:22
  22.9 8.1 %collective-permute-start = (bf16[200,384]{1,0:T(8,128)(2,1)S(1)}, bf16[200,384]{1,0:T(8,128)(2,1)S(1)}, u32[]{:S(2)}, u32[]{:S(2)}) collective-permute-start(bf16[200,384]{1,0:T(8,128)(2,1)S(1)} %get-tuple-element.128), channel_id=1, source_target_pairs={{0,4},{1,5},{2,6},{3,7},{4,0},{5,1},{6,2},{7,3},{8,12},{9,13},{10,... | collective-permute-start | bytes 460808 | tf_op jit(solution)/shard_map/ppermute | solution.py:22
  23.8 14.6 %collective-permute-start.1 = (bf16[200,384]{1,0:T(8,128)(2,1)S(1)}, bf16[200,384]{1,0:T(8,128)(2,1)S(1)}, u32[]{:S(2)}, u32[]{:S(2)}) collective-permute-start(bf16[200,384]{1,0:T(8,128)(2,1)S(1)} %get-tuple-element.128), channel_id=1, source_target_pairs={{0,8},{1,9},{2,10},{3,11},{4,12},{5,13},{6,14},{7,15},{8,0},{9,1},... | collective-permute-start | bytes 460808 | tf_op jit(solution)/shard_map/ppermute | solution.py:22
  27.3 11.1 %collective-permute-start.2 = (bf16[200,384]{1,0:T(8,128)(2,1)S(1)}, bf16[200,384]{1,0:T(8,128)(2,1)S(1)}, u32[]{:S(2)}, u32[]{:S(2)}) collective-permute-start(bf16[200,384]{1,0:T(8,128)(2,1)S(1)} %get-tuple-element.128), channel_id=1, source_target_pairs={{0,12},{1,13},{2,14},{3,15},{4,8},{5,9},{6,10},{7,11},{8,4},{9,5},... | collective-permute-start | bytes 460808 | tf_op jit(solution)/shard_map/ppermute | solution.py:22
  27.7 16.3 %collective-permute-start.11 = (bf16[4,192,384]{2,1,0:T(8,128)(2,1)S(1)}, bf16[4,192,384]{2,1,0:T(8,128)(2,1)S(1)}, u32[]{:S(2)}, u32[]{:S(2)}) collective-permute-start(bf16[4,192,384]{2,1,0:T(8,128)(2,1)S(1)} %get-tuple-element.122), channel_id=1, source_target_pairs={{0,1},{1,0},{2,3},{3,2},{4,5},{5,4},{6,7},{7,6},{8,9},{9,8},{10,11... | collective-permute-start | bytes 1769480 | tf_op jit(solution)/shard_map/ppermute | solution.py:22
  29.4 16.4 %collective-permute-start.12 = (bf16[4,192,384]{2,1,0:T(8,128)(2,1)S(1)}, bf16[4,192,384]{2,1,0:T(8,128)(2,1)S(1)}, u32[]{:S(2)}, u32[]{:S(2)}) collective-permute-start(bf16[4,192,384]{2,1,0:T(8,128)(2,1)S(1)} %get-tuple-element.122), channel_id=1, source_target_pairs={{0,2},{1,3},{2,0},{3,1},{4,6},{5,7},{6,4},{7,5},{8,10},{9,11},{10,... | collective-permute-start | bytes 1769480 | tf_op jit(solution)/shard_map/ppermute | solution.py:22
  39.6 17.6 %collective-permute-start.3 = (bf16[4,200,384]{2,1,0:T(8,128)(2,1)}, bf16[4,200,384]{2,1,0:T(8,128)(2,1)S(1)}, u32[]{:S(2)}, u32[]{:S(2)}) collective-permute-start(bf16[4,200,384]{2,1,0:T(8,128)(2,1)} %get-tuple-element.116), channel_id=1, source_target_pairs={{0,1},{1,0},{2,3},{3,2},{4,5},{5,4},{6,7},{7,6},{8,9},{9,8},{10,11... | collective-permute-start | bytes 1843208 | tf_op jit(solution)/shard_map/ppermute | solution.py:22
  41.1 17.9 %collective-permute-start.4 = (bf16[4,200,384]{2,1,0:T(8,128)(2,1)}, bf16[4,200,384]{2,1,0:T(8,128)(2,1)S(1)}, u32[]{:S(2)}, u32[]{:S(2)}) collective-permute-start(bf16[4,200,384]{2,1,0:T(8,128)(2,1)} %get-tuple-element.116), channel_id=1, source_target_pairs={{0,2},{1,3},{2,0},{3,1},{4,6},{5,7},{6,4},{7,5},{8,10},{9,11},{10,... | collective-permute-start | bytes 1843208 | tf_op jit(solution)/shard_map/ppermute | solution.py:22
  44.0 21.0 %collective-permute-start.13 = (bf16[2,192,384]{2,1,0:T(8,128)(2,1)S(1)}, bf16[2,192,384]{2,1,0:T(8,128)(2,1)}, u32[]{:S(2)}, u32[]{:S(2)}) collective-permute-start(bf16[2,192,384]{2,1,0:T(8,128)(2,1)S(1)} %slice.260), channel_id=1, source_target_pairs={{0,2},{1,3},{2,0},{3,1},{4,6},{5,7},{6,4},{7,5},{8,10},{9,11},{10,... | collective-permute-start | bytes 884744 | tf_op jit(solution)/shard_map/ppermute | solution.py:22
  47.4 17.6 %collective-permute-start.14 = (bf16[2,192,384]{2,1,0:T(8,128)(2,1)}, bf16[2,192,384]{2,1,0:T(8,128)(2,1)}, u32[]{:S(2)}, u32[]{:S(2)}) collective-permute-start(bf16[2,192,384]{2,1,0:T(8,128)(2,1)} %slice.261), channel_id=1, source_target_pairs={{0,1},{1,0},{2,3},{3,2},{4,5},{5,4},{6,7},{7,6},{8,9},{9,8},{10,11... | collective-permute-start | bytes 884744 | tf_op jit(solution)/shard_map/ppermute | solution.py:22
  57.2 12.8 %collective-permute-start.5 = (bf16[2,200,384]{2,1,0:T(8,128)(2,1)S(1)}, bf16[2,200,384]{2,1,0:T(8,128)(2,1)S(1)}, u32[]{:S(2)}, u32[]{:S(2)}) collective-permute-start(bf16[2,200,384]{2,1,0:T(8,128)(2,1)S(1)} %slice.246), channel_id=1, source_target_pairs={{0,2},{1,3},{2,0},{3,1},{4,6},{5,7},{6,4},{7,5},{8,10},{9,11},{10,... | collective-permute-start | bytes 921608 | tf_op jit(solution)/shard_map/ppermute | solution.py:22
  59.0 10.9 %collective-permute-start.6 = (bf16[2,200,384]{2,1,0:T(8,128)(2,1)S(1)}, bf16[2,200,384]{2,1,0:T(8,128)(2,1)S(1)}, u32[]{:S(2)}, u32[]{:S(2)}) collective-permute-start(bf16[2,200,384]{2,1,0:T(8,128)(2,1)S(1)} %slice.247), channel_id=1, source_target_pairs={{0,1},{1,0},{2,3},{3,2},{4,5},{5,4},{6,7},{7,6},{8,9},{9,8},{10,11... | collective-permute-start | bytes 921608 | tf_op jit(solution)/shard_map/ppermute | solution.py:22
  70.0 9.1 %collective-permute-start.15 = (bf16[4,4,192,384]{3,2,0,1:T(8,128)(2,1)}, bf16[4,4,192,384]{3,2,0,1:T(8,128)(2,1)}, u32[]{:S(2)}, u32[]{:S(2)}) collective-permute-start(bf16[4,4,192,384]{3,2,0,1:T(8,128)(2,1)} %pad_maximum_fusion.4), channel_id=1, source_target_pairs={{0,16},{16,0},{1,17},{17,1},{2,18},{18,2},{3,19},{19,3},{4,20},{20... | collective-permute-start | bytes 7077896 | tf_op jit(solution)/shard_map/ppermute | solution.py:22
  73.0 25.3 %collective-permute-start.7 = (bf16[4,4,192,384]{3,2,0,1:T(8,128)(2,1)}, bf16[4,4,192,384]{3,2,0,1:T(8,128)(2,1)}, u32[]{:S(2)}, u32[]{:S(2)}) collective-permute-start(bf16[4,4,192,384]{3,2,0,1:T(8,128)(2,1)} %slice.249), channel_id=1, source_target_pairs={{0,16},{16,0},{1,17},{17,1},{2,18},{18,2},{3,19},{19,3},{4,20},{20... | collective-permute-start | bytes 7077896 | tf_op jit(solution)/shard_map/ppermute | solution.py:22
  76.0 54.4 %copy-start.39 = (pred[8,128]{1,0:T(8,128)(4,1)}, pred[8,128]{1,0:T(8,128)(4,1)S(1)}, u32[]{:S(2)}) copy-start(pred[8,128]{1,0:T(8,128)(4,1)S(1)} %get-tuple-element.147) | copy-start | bytes 3076
  187.7 1.2 collective-permute-start.16
  289.3 54.2 %collective-permute-start.38 = (bf16[4,4,96,768]{3,2,0,1:T(8,128)(2,1)}, bf16[4,4,96,768]{3,2,0,1:T(8,128)(2,1)}, u32[]{:S(2)}, u32[]{:S(2)}) collective-permute-start(bf16[4,4,96,768]{3,2,0,1:T(8,128)(2,1)} %bitcast.310), channel_id=1, source_target_pairs={{0,16},{16,0},{1,17},{17,1},{2,18},{18,2},{3,19},{19,3},{4,20},{20... | collective-permute-start | bytes 7077896 | tf_op jit(solution)/shard_map/ppermute | solution.py:22
  291.4 56.1 %collective-permute-start.30 = (bf16[4,4,24,3072]{3,2,0,1:T(8,128)(2,1)}, bf16[4,4,24,3072]{3,2,0,1:T(8,128)(2,1)}, u32[]{:S(2)}, u32[]{:S(2)}) collective-permute-start(bf16[4,4,24,3072]{3,2,0,1:T(8,128)(2,1)} %bitcast.311), channel_id=1, source_target_pairs={{0,16},{16,0},{1,17},{17,1},{2,18},{18,2},{3,19},{19,3},{4,20},{20... | collective-permute-start | bytes 7077896 | tf_op jit(solution)/shard_map/ppermute | solution.py:22
  298.4 11.3 %collective-permute-start.25 = (f32[128,128]{1,0:T(8,128)S(1)}, f32[128,128]{1,0:T(8,128)S(1)}, u32[]{:S(2)}, u32[]{:S(2)}) collective-permute-start(f32[128,128]{1,0:T(8,128)S(1)} %pad_bitcast_fusion), channel_id=1, source_target_pairs={{0,16},{16,0},{1,17},{17,1},{2,18},{18,2},{3,19},{19,3},{4,20},{20... | collective-permute-start | bytes 196616 | tf_op jit(solution)/shard_map/ppermute | solution.py:22
  309.8 4.4 collective-permute-start.26
  314.2 10.6 %collective-permute-start.27 = (f32[128,128]{1,0:T(8,128)S(1)}, f32[128,128]{1,0:T(8,128)S(1)}, u32[]{:S(2)}, u32[]{:S(2)}) collective-permute-start(f32[128,128]{1,0:T(8,128)S(1)} %fusion.165), channel_id=1, source_target_pairs={{0,2},{1,3},{2,0},{3,1},{4,6},{5,7},{6,4},{7,5},{8,10},{9,11},{10,... | collective-permute-start | bytes 196616 | tf_op jit(solution)/shard_map/ppermute | solution.py:22
  324.8 5.5 %collective-permute-start.28 = (f32[128,128]{1,0:T(8,128)S(1)}, f32[128,128]{1,0:T(8,128)S(1)}, u32[]{:S(2)}, u32[]{:S(2)}) collective-permute-start(f32[128,128]{1,0:T(8,128)S(1)} %add.412), channel_id=1, source_target_pairs={{0,4},{1,5},{2,6},{3,7},{4,0},{5,1},{6,2},{7,3},{8,12},{9,13},{10,... | collective-permute-start | bytes 196616 | tf_op jit(solution)/shard_map/ppermute | solution.py:22
  330.3 23.4 %collective-permute-start.17 = (bf16[4,4,24,3072]{3,2,1,0:T(8,128)(2,1)}, bf16[4,4,24,3072]{3,2,1,0:T(8,128)(2,1)}, u32[]{:S(2)}, u32[]{:S(2)}) collective-permute-start(bf16[4,4,24,3072]{3,2,1,0:T(8,128)(2,1)} %dynamic-slice_bitcast_fusion), channel_id=1, source_target_pairs={{0,16},{16,0},{1,17},{17,1},{2,18},{18,2},{3,19},{19,3},{4,20},{20... | collective-permute-start | bytes 7077896 | tf_op jit(solution)/shard_map/ppermute | solution.py:22
  330.3 10.6 %collective-permute-start.29 = (f32[128,128]{1,0:T(8,128)S(1)}, f32[128,128]{1,0:T(8,128)S(1)}, u32[]{:S(2)}, u32[]{:S(2)}) collective-permute-start(f32[128,128]{1,0:T(8,128)S(1)} %add.413), channel_id=1, source_target_pairs={{0,8},{1,9},{2,10},{3,11},{4,12},{5,13},{6,14},{7,15},{8,0},{9,1},... | collective-permute-start | bytes 196616 | tf_op jit(solution)/shard_map/ppermute | solution.py:22
  346.7 10.3 %collective-permute-start.39 = (bf16[2,96,768]{2,1,0:T(8,128)(2,1)S(1)}, bf16[2,96,768]{2,1,0:T(8,128)(2,1)S(1)}, u32[]{:S(2)}, u32[]{:S(2)}) collective-permute-start(bf16[2,96,768]{2,1,0:T(8,128)(2,1)S(1)} %get-tuple-element.87), channel_id=1, source_target_pairs={{0,2},{1,3},{2,0},{3,1},{4,6},{5,7},{6,4},{7,5},{8,10},{9,11},{10,... | collective-permute-start | bytes 884744 | tf_op jit(solution)/shard_map/ppermute | solution.py:22
  347.3 10.2 %collective-permute-start.41 = (bf16[2,96,768]{2,1,0:T(8,128)(2,1)S(1)}, bf16[2,96,768]{2,1,0:T(8,128)(2,1)S(1)}, u32[]{:S(2)}, u32[]{:S(2)}) collective-permute-start(bf16[2,96,768]{2,1,0:T(8,128)(2,1)S(1)} %get-tuple-element.89), channel_id=1, source_target_pairs={{0,1},{1,0},{2,3},{3,2},{4,5},{5,4},{6,7},{7,6},{8,9},{9,8},{10,11... | collective-permute-start | bytes 884744 | tf_op jit(solution)/shard_map/ppermute | solution.py:22
  350.4 12.6 %collective-permute-start.31 = (bf16[2,24,3072]{2,1,0:T(8,128)(2,1)S(1)}, bf16[2,24,3072]{2,1,0:T(8,128)(2,1)S(1)}, u32[]{:S(2)}, u32[]{:S(2)}) collective-permute-start(bf16[2,24,3072]{2,1,0:T(8,128)(2,1)S(1)} %get-tuple-element.93), channel_id=1, source_target_pairs={{0,2},{1,3},{2,0},{3,1},{4,6},{5,7},{6,4},{7,5},{8,10},{9,11},{10,... | collective-permute-start | bytes 884744 | tf_op jit(solution)/shard_map/ppermute | solution.py:22
  352.0 11.5 %collective-permute-start.33 = (bf16[2,24,3072]{2,1,0:T(8,128)(2,1)S(1)}, bf16[2,24,3072]{2,1,0:T(8,128)(2,1)S(1)}, u32[]{:S(2)}, u32[]{:S(2)}) collective-permute-start(bf16[2,24,3072]{2,1,0:T(8,128)(2,1)S(1)} %get-tuple-element.95), channel_id=1, source_target_pairs={{0,1},{1,0},{2,3},{3,2},{4,5},{5,4},{6,7},{7,6},{8,9},{9,8},{10,11... | collective-permute-start | bytes 884744 | tf_op jit(solution)/shard_map/ppermute | solution.py:22
  356.4 12.8 %collective-permute-start.18 = (bf16[2,24,3072]{2,1,0:T(8,128)(2,1)S(1)}, bf16[2,24,3072]{2,1,0:T(8,128)(2,1)S(1)}, u32[]{:S(2)}, u32[]{:S(2)}) collective-permute-start(bf16[2,24,3072]{2,1,0:T(8,128)(2,1)S(1)} %get-tuple-element.100), channel_id=1, source_target_pairs={{0,2},{1,3},{2,0},{3,1},{4,6},{5,7},{6,4},{7,5},{8,10},{9,11},{10,... | collective-permute-start | bytes 884744 | tf_op jit(solution)/shard_map/ppermute | solution.py:22
  357.0 12.7 %collective-permute-start.20 = (bf16[2,24,3072]{2,1,0:T(8,128)(2,1)S(1)}, bf16[2,24,3072]{2,1,0:T(8,128)(2,1)S(1)}, u32[]{:S(2)}, u32[]{:S(2)}) collective-permute-start(bf16[2,24,3072]{2,1,0:T(8,128)(2,1)S(1)} %get-tuple-element.101), channel_id=1, source_target_pairs={{0,1},{1,0},{2,3},{3,2},{4,5},{5,4},{6,7},{7,6},{8,9},{9,8},{10,11... | collective-permute-start | bytes 884744 | tf_op jit(solution)/shard_map/ppermute | solution.py:22
  357.6 24.8 %collective-permute-start.40 = (bf16[4,96,768]{2,1,0:T(8,128)(2,1)S(1)}, bf16[4,96,768]{2,1,0:T(8,128)(2,1)S(1)}, u32[]{:S(2)}, u32[]{:S(2)}) collective-permute-start(bf16[4,96,768]{2,1,0:T(8,128)(2,1)S(1)} %pad_maximum_fusion.14), channel_id=1, source_target_pairs={{0,1},{1,0},{2,3},{3,2},{4,5},{5,4},{6,7},{7,6},{8,9},{9,8},{10,11... | collective-permute-start | bytes 1769480 | tf_op jit(solution)/shard_map/ppermute | solution.py:22
  362.9 21.0 %collective-permute-start.42 = (bf16[4,96,768]{2,1,0:T(8,128)(2,1)S(1)}, bf16[4,96,768]{2,1,0:T(8,128)(2,1)S(1)}, u32[]{:S(2)}, u32[]{:S(2)}) collective-permute-start(bf16[4,96,768]{2,1,0:T(8,128)(2,1)S(1)} %pad_maximum_fusion.15), channel_id=1, source_target_pairs={{0,2},{1,3},{2,0},{3,1},{4,6},{5,7},{6,4},{7,5},{8,10},{9,11},{10,... | collective-permute-start | bytes 1769480 | tf_op jit(solution)/shard_map/ppermute | solution.py:22
  363.7 44.7 %collective-permute-start.32 = (bf16[4,24,3072]{2,1,0:T(8,128)(2,1)S(1)}, bf16[4,24,3072]{2,1,0:T(8,128)(2,1)S(1)}, u32[]{:S(2)}, u32[]{:S(2)}) collective-permute-start(bf16[4,24,3072]{2,1,0:T(8,128)(2,1)S(1)} %pad_maximum_fusion.12), channel_id=1, source_target_pairs={{0,1},{1,0},{2,3},{3,2},{4,5},{5,4},{6,7},{7,6},{8,9},{9,8},{10,11... | collective-permute-start | bytes 1769480 | tf_op jit(solution)/shard_map/ppermute | solution.py:22
  369.4 37.3 %collective-permute-start.19 = (bf16[4,24,3072]{2,1,0:T(8,128)(2,1)S(1)}, bf16[4,24,3072]{2,1,0:T(8,128)(2,1)S(1)}, u32[]{:S(2)}, u32[]{:S(2)}) collective-permute-start(bf16[4,24,3072]{2,1,0:T(8,128)(2,1)S(1)} %pad_maximum_fusion.10), channel_id=1, source_target_pairs={{0,1},{1,0},{2,3},{3,2},{4,5},{5,4},{6,7},{7,6},{8,9},{9,8},{10,11... | collective-permute-start | bytes 1769480 | tf_op jit(solution)/shard_map/ppermute | solution.py:22
  369.9 37.5 %collective-permute-start.21 = (bf16[4,24,3072]{2,1,0:T(8,128)(2,1)S(1)}, bf16[4,24,3072]{2,1,0:T(8,128)(2,1)S(1)}, u32[]{:S(2)}, u32[]{:S(2)}) collective-permute-start(bf16[4,24,3072]{2,1,0:T(8,128)(2,1)S(1)} %pad_maximum_fusion.11), channel_id=1, source_target_pairs={{0,2},{1,3},{2,0},{3,1},{4,6},{5,7},{6,4},{7,5},{8,10},{9,11},{10,... | collective-permute-start | bytes 1769480 | tf_op jit(solution)/shard_map/ppermute | solution.py:22
  382.4 28.5 %collective-permute-start.34 = (bf16[4,24,3072]{2,1,0:T(8,128)(2,1)S(1)}, bf16[4,24,3072]{2,1,0:T(8,128)(2,1)S(1)}, u32[]{:S(2)}, u32[]{:S(2)}) collective-permute-start(bf16[4,24,3072]{2,1,0:T(8,128)(2,1)S(1)} %pad_maximum_fusion.13), channel_id=1, source_target_pairs={{0,2},{1,3},{2,0},{3,1},{4,6},{5,7},{6,4},{7,5},{8,10},{9,11},{10,... | collective-permute-start | bytes 1769480 | tf_op jit(solution)/shard_map/ppermute | solution.py:22
  384.2 49.5 %collective-permute-start.43 = (bf16[96,768]{1,0:T(8,128)(2,1)S(1)}, bf16[96,768]{1,0:T(8,128)(2,1)S(1)}, u32[]{:S(2)}, u32[]{:S(2)}) collective-permute-start(bf16[96,768]{1,0:T(8,128)(2,1)S(1)} %get-tuple-element.106), channel_id=1, source_target_pairs={{0,4},{1,5},{2,6},{3,7},{4,0},{5,1},{6,2},{7,3},{8,12},{9,13},{10,... | collective-permute-start | bytes 442376 | tf_op jit(solution)/shard_map/ppermute | solution.py:22
  406.7 29.6 %collective-permute-start.44 = (bf16[96,768]{1,0:T(8,128)(2,1)S(1)}, bf16[96,768]{1,0:T(8,128)(2,1)S(1)}, u32[]{:S(2)}, u32[]{:S(2)}) collective-permute-start(bf16[96,768]{1,0:T(8,128)(2,1)S(1)} %get-tuple-element.108), channel_id=1, source_target_pairs={{0,8},{1,9},{2,10},{3,11},{4,12},{5,13},{6,14},{7,15},{8,0},{9,1},... | collective-permute-start | bytes 442376 | tf_op jit(solution)/shard_map/ppermute | solution.py:22
  407.7 7.2 %collective-permute-start.22 = (bf16[24,3072]{1,0:T(8,128)(2,1)S(1)}, bf16[24,3072]{1,0:T(8,128)(2,1)S(1)}, u32[]{:S(2)}, u32[]{:S(2)}) collective-permute-start(bf16[24,3072]{1,0:T(8,128)(2,1)S(1)} %get-tuple-element.112), channel_id=1, source_target_pairs={{0,4},{1,5},{2,6},{3,7},{4,0},{5,1},{6,2},{7,3},{8,12},{9,13},{10,... | collective-permute-start | bytes 442376 | tf_op jit(solution)/shard_map/ppermute | solution.py:22
  408.3 20.5 %collective-permute-start.23 = (bf16[24,3072]{1,0:T(8,128)(2,1)S(1)}, bf16[24,3072]{1,0:T(8,128)(2,1)S(1)}, u32[]{:S(2)}, u32[]{:S(2)}) collective-permute-start(bf16[24,3072]{1,0:T(8,128)(2,1)S(1)} %get-tuple-element.114), channel_id=1, source_target_pairs={{0,8},{1,9},{2,10},{3,11},{4,12},{5,13},{6,14},{7,15},{8,0},{9,1},... | collective-permute-start | bytes 442376 | tf_op jit(solution)/shard_map/ppermute | solution.py:22
  410.9 17.9 %collective-permute-start.24 = (bf16[24,3072]{1,0:T(8,128)(2,1)S(1)}, bf16[24,3072]{1,0:T(8,128)(2,1)S(1)}, u32[]{:S(2)}, u32[]{:S(2)}) collective-permute-start(bf16[24,3072]{1,0:T(8,128)(2,1)S(1)} %get-tuple-element.113), channel_id=1, source_target_pairs={{0,12},{1,13},{2,14},{3,15},{4,8},{5,9},{6,10},{7,11},{8,4},{9,5},... | collective-permute-start | bytes 442376 | tf_op jit(solution)/shard_map/ppermute | solution.py:22
  414.9 21.4 %collective-permute-start.45 = (bf16[96,768]{1,0:T(8,128)(2,1)S(1)}, bf16[96,768]{1,0:T(8,128)(2,1)S(1)}, u32[]{:S(2)}, u32[]{:S(2)}) collective-permute-start(bf16[96,768]{1,0:T(8,128)(2,1)S(1)} %get-tuple-element.107), channel_id=1, source_target_pairs={{0,12},{1,13},{2,14},{3,15},{4,8},{5,9},{6,10},{7,11},{8,4},{9,5},... | collective-permute-start | bytes 442376 | tf_op jit(solution)/shard_map/ppermute | solution.py:22
  428.8 8.3 %collective-permute-start.35 = (bf16[24,3072]{1,0:T(8,128)(2,1)S(1)}, bf16[24,3072]{1,0:T(8,128)(2,1)S(1)}, u32[]{:S(2)}, u32[]{:S(2)}) collective-permute-start(bf16[24,3072]{1,0:T(8,128)(2,1)S(1)} %get-tuple-element.109), channel_id=1, source_target_pairs={{0,4},{1,5},{2,6},{3,7},{4,0},{5,1},{6,2},{7,3},{8,12},{9,13},{10,... | collective-permute-start | bytes 442376 | tf_op jit(solution)/shard_map/ppermute | solution.py:22
  428.8 15.8 %collective-permute-start.36 = (bf16[24,3072]{1,0:T(8,128)(2,1)S(1)}, bf16[24,3072]{1,0:T(8,128)(2,1)S(1)}, u32[]{:S(2)}, u32[]{:S(2)}) collective-permute-start(bf16[24,3072]{1,0:T(8,128)(2,1)S(1)} %get-tuple-element.111), channel_id=1, source_target_pairs={{0,8},{1,9},{2,10},{3,11},{4,12},{5,13},{6,14},{7,15},{8,0},{9,1},... | collective-permute-start | bytes 442376 | tf_op jit(solution)/shard_map/ppermute | solution.py:22
  433.7 10.9 %collective-permute-start.37 = (bf16[24,3072]{1,0:T(8,128)(2,1)S(1)}, bf16[24,3072]{1,0:T(8,128)(2,1)S(1)}, u32[]{:S(2)}, u32[]{:S(2)}) collective-permute-start(bf16[24,3072]{1,0:T(8,128)(2,1)S(1)} %get-tuple-element.110), channel_id=1, source_target_pairs={{0,12},{1,13},{2,14},{3,15},{4,8},{5,9},{6,10},{7,11},{8,4},{9,5},... | collective-permute-start | bytes 442376 | tf_op jit(solution)/shard_map/ppermute | solution.py:22
  (56 other events, 256.2 us)
Sparse Core Ops, SparseCore 0:
  74.4 63.8 all-gather.1

commit v2 on v1

v2 whole, which is shorter than its diff:
```python
from functools import partial
import math

import jax
import jax.numpy as jnp
from jax import lax
from jax.experimental import pallas as pl
from jax.experimental.pallas import tpu as pltpu
from jax.sharding import PartitionSpec as P

HEADS = 12
HEAD_DIM = 64
NCLASS = 3
CHUNK = 384
FAR = 4

eps_norm = 1e-12
gap_soft = 0.01
f32 = jnp.float32
b16 = jnp.bfloat16


def swap(x, axis, k):
    return lax.ppermute(x, axis, [(i, i ^ k) for i in range(lax.axis_size(axis))])


def places():
    low = lax.axis_size("dp") // FAR
    me = lax.axis_index("dp")
    return low, me // low, me % low


def in_order(pieces, me, axis):
    stack = jnp.stack(pieces, axis)
    return jnp.concatenate(
        [lax.dynamic_index_in_dim(stack, me ^ j, axis) for j in range(len(pieces))], axis
    )


def far_pieces(part):
    low, _, _ = places()
    return [part] + [swap(part, "dp", j * low) for j in range(1, FAR)]


def after(x, *deps):
    return lax.optimization_barrier((x, *deps))[0]


def gather_near(block, *ready):
    half = FAR // 2
    by_one, by_two = after((swap(block, "dp", 1), swap(block, "dp", 2)), *ready)
    return [block, by_one, by_two, swap(by_one[:half], "dp", 2), swap(by_two[half:], "dp", 1)]


def gather_any(block):
    low, _, near = places()
    pieces, bit = [block], 1
    while bit < low:
        pieces = pieces + [swap(p, "dp", bit) for p in pieces]
        bit *= 2
    return in_order(pieces, near, 1)


def to_chunks(shard):
    rows, cols = shard.shape
    half = cols // 2
    mine = lax.dynamic_slice_in_dim(shard, lax.axis_index("tower") * half, half, 1)
    return mine.reshape(rows, half // CHUNK, CHUNK).transpose(1, 0, 2).reshape(-1, CHUNK)


def from_chunks(mine, rows):
    other = swap(mine, "tower", 1)
    low_half = lax.axis_index("tower") == 0
    both = jnp.stack([jnp.where(low_half, mine, other), jnp.where(low_half, other, mine)])
    far, low, total = mine.shape[:3]
    n = total // rows
    both = both.reshape(2, far, low, n, rows, CHUNK).transpose(1, 2, 4, 0, 3, 5)
    return both.reshape(far, low * rows, 2 * n * CHUNK)


def add_low(a, b):
    return (a.astype(f32) + b.astype(f32)).astype(b16)


class Scatter:
    def __init__(self, parts):
        self.mine, *others = parts
        self.first = swap(others[0], "tower", 1)
        self.rest = swap(after(others[1], self.first), "tower", 1)
        self.corner = self.side = self.far = None

    def both(self, k, part=slice(None)):
        got = self.first[part] if k == 3 else self.rest[k, part]
        return self.mine[k, part].astype(f32) + got.astype(f32)

    def corners(self):
        if self.corner is None:
            half = FAR // 2
            self.corner = (
                swap(self.both(3, slice(0, half)).astype(b16), "dp", 1),
                swap(self.both(3, slice(half, FAR)).astype(b16), "dp", 2),
            )
        return self.corner

    def sides(self):
        if self.side is None:
            half = FAR // 2
            first, second = slice(0, half), slice(half, FAR)
            for_one, for_two = self.corners()
            one = [self.both(1, first).astype(b16), (self.both(1, second) + for_two.astype(f32)).astype(b16)]
            two = [(self.both(2, first) + for_one.astype(f32)).astype(b16), self.both(2, second).astype(b16)]
            self.sent = jnp.concatenate(one, 0), jnp.concatenate(two, 0)
            self.side = swap(self.sent[0], "dp", 1), swap(self.sent[1], "dp", 2)
        return self.side

    def fars(self):
        if self.far is None:
            low = lax.axis_size("dp") // FAR
            one, two = self.sides()
            self.own = self.both(0) + one.astype(f32) + two.astype(f32)
            self.far = [swap(self.own[j].astype(b16), "dp", j * low) for j in range(1, FAR)]
        return self.far

    def sum(self):
        far = self.fars()
        return self.own[0] + far[0].astype(f32) + far[1].astype(f32) + far[2].astype(f32)


def scatter_any(grad):
    low, far, near = places()
    tower = lax.axis_index("tower")
    halves = grad.reshape((2, FAR, low, -1) + grad.shape[1:])
    got = swap(lax.dynamic_index_in_dim(halves, 1 - tower, 0, keepdims=False), "tower", 1)
    data = add_low(lax.dynamic_index_in_dim(halves, tower, 0, keepdims=False), got)
    blocks = [lax.dynamic_index_in_dim(data, near ^ k, 1, keepdims=False) for k in range(low)]
    bit = low // 2
    while bit:
        blocks = [add_low(blocks[k], swap(blocks[k + bit], "dp", bit)) for k in range(bit)]
        bit //= 2
    own = [lax.dynamic_index_in_dim(blocks[0], far ^ j, 0, keepdims=False) for j in range(FAR)]
    total = own[0].astype(f32)
    for j in range(1, FAR):
        total = total + swap(own[j], "dp", j * low).astype(f32)
    return total


def add_from(x, axis, k):
    return x + swap(x, axis, k)


TILE = 192
PACK = 16
PAIR = 2 * HEAD_DIM
GROUP = 3
Q_BIAS, V_BIAS, O_BIAS, GAIN_1, SHIFT_1, D_BIAS, GAIN_2, SHIFT_2 = range(8)


def dot(a, b):
    return jnp.dot(a, b, preferred_element_type=f32)


def dot_nt(a, b):
    return lax.dot_general(a, b, (((1,), (1,)), ((), ())), preferred_element_type=f32)


def dot_tn(a, b):
    return lax.dot_general(a, b, (((0,), (0,)), ((), ())), preferred_element_type=f32)


def tile_at(t):
    return pl.ds(pl.multiple_of(t * TILE, TILE), TILE)


def sentence_rows(offs, b, seq):
    return pl.ds(pl.multiple_of(offs[b], PACK), seq)


def split_heads(x):
    left = lax.broadcasted_iota(jnp.int32, x.shape, 1) < HEAD_DIM
    zero = jnp.zeros_like(x)
    return jnp.concatenate([jnp.where(left, x, zero), jnp.where(left, zero, x)], 0)


def join_heads(x):
    seq = x.shape[0] // 2
    left = lax.broadcasted_iota(jnp.int32, (seq, PAIR), 1) < HEAD_DIM
    return jnp.where(left, x[:seq], x[seq:])


def by_head(fn, x):
    half = x.shape[0] // 2
    return jnp.concatenate([fn(x[:half]), fn(x[half:])], 0)


def by_length(lens, count, seq, step):
    def one(b, _):
        @pl.when(lens[b] > seq // 2)
        def _():
            step(b, seq)

        @pl.when(lens[b] <= seq // 2)
        def _():
            step(b, seq // 2)

        return 0

    lax.fori_loop(0, count, one, 0)


def norm_rows(hidden):
    center = hidden - jnp.mean(hidden, axis=-1, keepdims=True)
    inverse = lax.rsqrt(jnp.mean(center * center, axis=-1, keepdims=True) + eps_norm)
    return center * inverse, inverse


def norm_back(upstream, normal, inverse, gain):
    scaled = upstream * gain
    inner = scaled - jnp.mean(scaled, axis=-1, keepdims=True)
    return inverse * (inner - normal * jnp.mean(scaled * normal, axis=-1, keepdims=True))


def row_of(vec, i):
    return vec[i : i + 1, :].astype(f32)


def add_row(sums, i, x):
    sums[i : i + 1, :] += jnp.sum(x, axis=0, keepdims=True)


def parts_kernel(place, wqkv, wout, wup, wdown, packed, first, second, third):
    def put(src, dst, at):
        rows, half = src.shape[0], src.shape[1] // 2
        for c in range(half // CHUNK):
            dst[at : at + rows, :] = src[:, pl.ds(pl.multiple_of(place[0] * half + c * CHUNK, 128), CHUNK)]
            at += rows
        return at

    at = put(wout, first, put(wqkv, first, 0))
    first[at:, :] = packed[...]
    put(wup, second, 0)
    put(wdown, third, 0)


def fetch(place, pieces, targets, sems):
    copies = []
    for side in range(2):
        tower = place[0] if side == 0 else 1 - place[0]
        block, by_one, by_two, low, high = pieces[5 * side : 5 * side + 5]
        half = FAR // 2
        spots = ((block, 0, 0, FAR), (by_one, 1, 0, FAR), (by_two, 2, 0, FAR), (low, 3, 0, half), (high, 3, half, half))
        for piece, k, far, size in spots:
            at = 0
            for weight, rows in targets:
                cols = weight.shape[2] // 2
                for c in range(cols // CHUNK):
                    row = pl.multiple_of((place[1] ^ k) * rows, PACK)
                    col = pl.multiple_of(tower * cols + c * CHUNK, 128)
                    copies.append(
                        pltpu.make_async_copy(
                            piece.at[:, pl.ds(at, rows), :],
                            weight.at[pl.ds(far, size), pl.ds(row, rows), pl.ds(col, CHUNK)],
                            sems.at[len(copies)],
                        )
                    )
                    at += rows
    for copy in copies:
        copy.start()
    return copies


def deal(place, acc, outs, base=0):
    cols = acc.shape[1]
    if len(outs) == 1:
        outs[0][:, base : base + cols] = acc[...].astype(b16)
        return
    mine, first, rest = outs
    rows = first.shape[1]
    for own in (False, True):
        side = place[0] if own else 1 - place[0]
        for k in range(4):
            target = mine.at[k] if own else first if k == 3 else rest.at[k]
            for j in range(FAR):
                at = (side * 4 * FAR + (place[2] ^ j) * 4 + (place[1] ^ k)) * rows
                target[j, :, base : base + cols] = acc[pl.ds(pl.multiple_of(at, 8), rows), :].astype(b16)


def flat_of(weight, cols=slice(None)):
    block = weight[:, :, cols]
    return block.reshape(block.shape[0] * block.shape[1], block.shape[2])


def attend_kernel(n_pieces, lens, offs, tiles, place, x_ref, vec, *refs):
    pieces, refs = refs[:n_pieces], refs[n_pieces:]
    if n_pieces:
        sinks, refs = refs[:8], refs[8:]
        wqkv, wout, xs, qkv, probs, ctx, n1, inv1, got, sent = refs
        copies = fetch(place, pieces, ((wqkv, wqkv.shape[1] // 4), (wout, wout.shape[1] // 4)), got)
    else:
        wqkv, wout = refs[:2]
        sinks, refs = refs[2:8], refs[8:]
        xs, qkv, probs, ctx, n1, inv1, sent = refs
        copies = []
    held = (wqkv, wout, xs, qkv, probs, ctx, n1, inv1)[8 - len(sinks) :]
    count, seq, width = x_ref.shape
    leaving = []

    def leave(*which):
        for ref in which:
            for i, own in enumerate(held):
                if own is ref:
                    copy = pltpu.make_async_copy(ref, sinks[i], sent.at[i])
                    copy.start()
                    leaving.append(copy)

    xs[...] = jnp.zeros_like(xs)
    ctx[...] = jnp.zeros_like(ctx)

    def pack(b, _):
        def block(i, _):
            at = pl.multiple_of(offs[b] + i * PACK, PACK)
            xs[pl.ds(at, PACK), :] = x_ref[b, pl.ds(pl.multiple_of(i * PACK, PACK), PACK), :]
            return 0

        return lax.fori_loop(0, (lens[b] + PACK - 1) // PACK, block, 0)

    lax.fori_loop(0, count, pack, 0)
    for copy in copies:
        copy.wait()
    leave(wqkv, wout, xs)

    def project(t, _):
        x = xs[tile_at(t), :]
        for c in range(3):
            cols = slice(c * width, (c + 1) * width)
            joined = dot(x, flat_of(wqkv, cols))
            if c == 0:
                joined = (joined + row_of(vec, Q_BIAS)) * (HEAD_DIM ** -0.5)
            if c == 2:
                joined = joined + row_of(vec, V_BIAS)
            qkv[tile_at(t), cols] = joined.astype(b16)
        return 0

    lax.fori_loop(0, tiles[0], project, 0)
    qkv[pl.ds(pl.multiple_of(tiles[0] * TILE, TILE), seq), :] = jnp.zeros((seq, 3 * width), b16)
    leave(qkv)

    def attend(b, size):
        rows, key_rows = sentence_rows(offs, b, seq), sentence_rows(offs, b, size)
        valid = lax.broadcasted_iota(jnp.int32, (size, seq), 0) < lens[b]

        def softmax(s):
            s = jnp.where(valid, s, -1000000000.0)
            e = jnp.exp(s - jnp.max(s, axis=0, keepdims=True))
            return (e * (1.0 / jnp.sum(e, axis=0, keepdims=True))).astype(b16)

        for group in range(0, width // PAIR, GROUP):
            pairs = range(group, group + GROUP)
            cols = [slice(p * PAIR, (p + 1) * PAIR) for p in pairs]
            queries = [qkv[rows, c] for c in cols]
            keys = [split_heads(qkv[key_rows, width + c.start : width + c.stop]) for c in cols]
            vals = [split_heads(qkv[key_rows, 2 * width + c.start : 2 * width + c.stop]) for c in cols]
            scores = [dot_nt(k, q) for k, q in zip(keys, queries)]
            lows = [by_head(softmax, s) for s in scores]
            outs = [dot_tn(low, v).astype(b16) for low, v in zip(lows, vals)]
            for p, c, low, out in zip(pairs, cols, lows, outs):
                probs[b, p * 2 * size : (p + 1) * 2 * size, :] = low
                ctx[rows, c] = out

    by_length(lens, count, seq, attend)
    leave(probs, ctx)

    def out(t, _):
        rows = tile_at(t)
        attended = dot(ctx[rows, :], flat_of(wout)) + row_of(vec, O_BIAS)
        normal, inverse = norm_rows(xs[rows, :].astype(f32) + attended)
        n1[rows, :] = normal
        inv1[rows, :] = jnp.broadcast_to(inverse, (TILE, 128))
        return 0

    lax.fori_loop(0, tiles[0], out, 0)
    leave(n1, inv1)
    for copy in leaving:
        copy.wait()


def inside(offs, lens, b, t):
    row = t * TILE + lax.broadcasted_iota(jnp.int32, (TILE, 1), 0)
    return (row >= offs[b]) & (row < offs[b] + lens[b])


def take_weight(step, tiles, place, pieces, refs, rows_of):
    if not pieces:
        return refs[0], refs[1:], lambda: None
    sink, refs = refs[0], refs[1:]
    weight, got, sent, refs = refs[-3], refs[-2], refs[-1], refs[:-3]
    leave = pltpu.make_async_copy(weight, sink, sent.at[0])

    @pl.when(step == 0)
    def _():
        for copy in fetch(place, pieces, ((weight, rows_of),), got):
            copy.wait()
        leave.start()

    def finish():
        @pl.when(step == pl.num_programs(0) - 1)
        def _():
            leave.wait()

    return weight, refs, finish


def up_kernel(n_pieces, lens, offs, tiles, place, n1, vec, ups, *refs):
    t = pl.program_id(0)
    pieces, refs = refs[:n_pieces], refs[n_pieces:]
    rows_of = pieces[0].shape[1] * CHUNK * 2 // (ups.shape[0] * ups.shape[1]) if n_pieces else 0
    wup, (act, slope), finish = take_weight(t, tiles, place, pieces, refs, rows_of)
    width = n1.shape[1]

    @pl.when(t < tiles[0])
    def _():
        low = (n1[...] * row_of(vec, GAIN_1) + row_of(vec, SHIFT_1)).astype(b16)
        for c in range(ups.shape[0]):
            cols = slice(c * width, (c + 1) * width)
            pre = dot(low, flat_of(wup, cols)) + row_of(ups, c)
            half = 0.5 * (1.0 + lax.erf(pre * (0.5 ** 0.5)))
            act[:, cols] = (pre * half).astype(b16)
            slope[:, cols] = (half + pre * (jnp.exp(-0.5 * pre * pre) * 0.3989422804014327)).astype(b16)

    finish()


def down_kernel(n_pieces, lens, offs, tiles, place, n1, act, vec, *refs):
    t = pl.program_id(0)
    pieces, refs = refs[:n_pieces], refs[n_pieces:]
    rows_of = pieces[0].shape[1] if n_pieces else 0
    wdown, (n2, inv2, pooled), finish = take_weight(t, tiles, place, pieces, refs, rows_of)
    width = n1.shape[1]
    count = pooled.shape[0]

    @pl.when(t == 0)
    def _():
        pooled[...] = jnp.zeros_like(pooled)

    @pl.when(t < tiles[0])
    def _():
        total = n1[...] * row_of(vec, GAIN_1) + row_of(vec, SHIFT_1) + row_of(vec, D_BIAS)
        total = total + dot(act[...], flat_of(wdown))
        normal, inverse = norm_rows(total)
        n2[...] = normal
        inv2[...] = jnp.broadcast_to(inverse, (TILE, 128))
        for b in range(count):
            add_row(pooled, b, jnp.where(inside(offs, lens, b, t), normal, 0.0))

    @pl.when(t == pl.num_programs(0) - 1)
    def _():
        for b in range(count):
            size = jnp.full((1, width), lens[b], jnp.int32).astype(f32)
            pooled[b : b + 1, :] = pooled[b : b + 1, :] / size * row_of(vec, GAIN_2) + row_of(vec, SHIFT_2)

    finish()


def accumulate(t, acc, cols, left, right):
    @pl.when(t == 0)
    def _():
        acc[:, cols] = dot_tn(left, right)

    @pl.when(t > 0)
    def _():
        acc[:, cols] += dot_tn(left, right)


def pair_head(lens, place, labels, bias, pooled, partner, head, tops):
    count, width = pooled.shape
    mine, other = pooled[...], partner[...]
    first = place[0] == 0
    left, right = jnp.where(first, mine, other), jnp.where(first, other, mine)
    gap = left - right
    soft = jnp.sqrt(gap * gap + gap_soft)
    feats = (left, right, soft)
    row = lax.broadcasted_iota(jnp.int32, (count, 1), 0)
    label = jnp.zeros((count, 1), jnp.int32)
    size = jnp.zeros((count, 1), jnp.int32)
    for b in range(count):
        label = jnp.where(row == b, labels[b], label)
        size = jnp.where(row == b, lens[b], size)
    logits = []
    for c in range(NCLASS):
        terms = [
            jnp.sum(feats[i] * head[c : c + 1, i * width : (i + 1) * width], axis=-1, keepdims=True) for i in range(3)
        ]
        logits.append(terms[0] + terms[1] + terms[2] + bias[c])
    top = jnp.maximum(jnp.maximum(logits[0], logits[1]), logits[2])
    exps = [jnp.exp(x - top) for x in logits]
    norm = exps[0] + exps[1] + exps[2]
    grads = [exps[c] / norm - jnp.where(label == c, 1.0, 0.0) for c in range(NCLASS)]
    back = []
    tops[...] = jnp.zeros_like(tops)
    for i in range(3):
        cols = slice(i * width, (i + 1) * width)
        back.append(sum(grads[c] * head[c : c + 1, cols] for c in range(NCLASS)))
        for c in range(NCLASS):
            tops[c : c + 1, cols] = 0.5 * jnp.sum(grads[c] * feats[i], axis=0, keepdims=True)
    for c in range(NCLASS):
        tops[NCLASS + c : NCLASS + c + 1, 0:128] = jnp.broadcast_to(0.5 * jnp.sum(grads[c], axis=0, keepdims=True), (1, 128))
    slope = gap / soft
    pooled_grad = jnp.where(first, back[0] + slope * back[2], back[1] - slope * back[2])
    return pooled_grad / size.astype(f32)


def down_back_kernel(
    lens, offs, tiles, place, labels, bias, pooled, partner, head, act, n2, inv2, vec, sum_grad, *refs
):
    *outs, sums, tops, acc, per_row = refs
    t = pl.program_id(0)
    count, width = pooled.shape

    @pl.when(t == 0)
    def _():
        per_row[...] = pair_head(lens, place, labels, bias, pooled, partner, head, tops)
        sums[...] = jnp.zeros_like(sums)

    @pl.when(t < tiles[0])
    def _():
        up = jnp.zeros((TILE, width), f32)
        for b in range(count):
            up = jnp.where(inside(offs, lens, b, t), per_row[b : b + 1, :], up)
        normal = n2[...]
        grad = norm_back(up, normal, inv2[:, 0:1], row_of(vec, GAIN_2))
        sum_grad[...] = grad
        add_row(sums, 0, up * normal)
        add_row(sums, 1, up)
        add_row(sums, 2, grad)
        low = grad.astype(b16)

        accumulate(t, acc, slice(None), act[...], low)

    @pl.when(t == pl.num_programs(0) - 1)
    def _():
        deal(place, acc, outs)


def pre_back_kernel(lens, offs, tiles, place, sum_grad, slope, wdown, pre_low, sums):
    t = pl.program_id(0)
    width = sum_grad.shape[1]
    chunks = slope.shape[1] // width
    split = wdown.shape[0] // chunks

    @pl.when(t == 0)
    def _():
        sums[...] = jnp.zeros_like(sums)

    @pl.when(t < tiles[0])
    def _():
        low = sum_grad[...].astype(b16)
        for c in range(chunks):
            cols = slice(c * width, (c + 1) * width)
            pre = dot_nt(low, flat_of(wdown[c * split : (c + 1) * split])) * slope[:, cols].astype(f32)
            add_row(sums, c, pre)
            pre_low[:, cols] = pre.astype(b16)


def mid_back_kernel(
    lens, offs, tiles, place, sum_grad, pre_low, n1, inv1, ctx, wup, wout, vec, mid, ctx_grad, *refs
):
    *outs, sums, acc = refs
    t = pl.program_id(0)
    hidden = pre_low.shape[1]

    @pl.when(t == 0)
    def _():
        sums[...] = jnp.zeros_like(sums)

    @pl.when(t < tiles[0])
    def _():
        pre = pre_low[...]
        grad = sum_grad[...] + dot_nt(pre, flat_of(wup))
        normal = n1[...]
        add_row(sums, 0, grad * normal)
        add_row(sums, 1, grad)
        middle = norm_back(grad, normal, inv1[:, 0:1], row_of(vec, GAIN_1))
        add_row(sums, 2, middle)
        mid[...] = middle
        low = middle.astype(b16)
        ctx_grad[...] = dot_nt(low, flat_of(wout)).astype(b16)
        first_low = (normal * row_of(vec, GAIN_1) + row_of(vec, SHIFT_1)).astype(b16)
        accumulate(t, acc, slice(0, hidden), first_low, pre)
        accumulate(t, acc, slice(hidden, None), ctx[...], low)

    @pl.when(t == pl.num_programs(0) - 1)
    def _():
        deal(place, acc, outs)


def attend_back_kernel(lens, offs, tiles, place, qkv_h, probs_h, ctx_grad_h, grad, sums, qkv, probs, ctx_grad, sems):
    width = ctx_grad.shape[1]
    count, seq = probs.shape[0], probs.shape[2]
    pairs = ((qkv_h, qkv), (probs_h, probs), (ctx_grad_h, ctx_grad))
    copies = [pltpu.make_async_copy(a, b, sems.at[i]) for i, (a, b) in enumerate(pairs)]
    for copy in copies:
        copy.start()
    grad[...] = jnp.zeros_like(grad)
    sums[...] = jnp.zeros_like(sums)
    for copy in copies:
        copy.wait()

    def attend(b, size):
        rows, key_rows = sentence_rows(offs, b, seq), sentence_rows(offs, b, size)
        real = lax.broadcasted_iota(jnp.int32, (seq, 1), 0) < lens[b]
        def spread(x):
            return jnp.broadcast_to(jnp.sum(x, axis=0, keepdims=True), x.shape)

        for group in range(0, width // PAIR, GROUP):
            pairs = range(group, group + GROUP)
            cols = [slice(p * PAIR, (p + 1) * PAIR) for p in pairs]
            ups = [jnp.where(real, ctx_grad[rows, c], jnp.zeros((), b16)) for c in cols]
            queries = [qkv[rows, c] for c in cols]
            keys = [split_heads(qkv[key_rows, width + c.start : width + c.stop]) for c in cols]
            vals = [split_heads(qkv[key_rows, 2 * width + c.start : 2 * width + c.stop]) for c in cols]
            lows = [probs[b, p * 2 * size : (p + 1) * 2 * size, :] for p in pairs]
            prob_grads = [dot_nt(v, up) for v, up in zip(vals, ups)]
            val_grads = [join_heads(dot(low, up)).astype(b16) for low, up in zip(lows, ups)]
            scores = []
            for low, pg in zip(lows, prob_grads):
                pr = low.astype(f32)
                scores.append((pr * (pg - by_head(spread, pg * pr))).astype(b16))
            query_grads = [(dot_tn(s, k) * (HEAD_DIM ** -0.5)).astype(b16) for s, k in zip(scores, keys)]
            key_grads = [join_heads(dot(s, q)).astype(b16) for s, q in zip(scores, queries)]
            for i, c in enumerate(cols):
                grad[rows, c] = query_grads[i]
                grad[key_rows, width + c.start : width + c.stop] = key_grads[i]
                grad[key_rows, 2 * width + c.start : 2 * width + c.stop] = val_grads[i]

    by_length(lens, count, seq, attend)

    def total(t, _):
        for c in (0, 2):
            add_row(sums, c // 2, grad[tile_at(t), c * width : (c + 1) * width].astype(f32))
        return 0

    lax.fori_loop(0, tiles[0], total, 0)

def qkv_back_kernel(lens, offs, tiles, place, xs, grad, *refs):
    *outs, acc = refs
    t = pl.program_id(0)

    @pl.when(t < tiles[0])
    def _():
        accumulate(t, acc, slice(None), xs[...], grad[...])

    @pl.when(t == pl.num_programs(0) - 1)
    def _():
        deal(place, acc, outs)


def input_kernel(lens, offs, tiles, place, grad, mid, wqkv, gx, buf):
    count, seq, width = gx.shape
    t = pl.program_id(0)

    @pl.when(t == 0)
    def _():
        gx[...] = jnp.zeros_like(gx)

    @pl.when(t < tiles[0])
    def _():
        buf[tile_at(t), :] = dot_nt(grad[...], flat_of(wqkv)) + mid[...]

    @pl.when(t == pl.num_programs(0) - 1)
    def _():
        def unpack(b, _):
            def block(i, _):
                at = pl.multiple_of(offs[b] + i * PACK, PACK)
                gx[b, pl.ds(pl.multiple_of(i * PACK, PACK), PACK), :] = buf[pl.ds(at, PACK), :]
                return 0

            return lax.fori_loop(0, (lens[b] + PACK - 1) // PACK, block, 0)

        lax.fori_loop(0, count, unpack, 0)


def small_kernel(spot, sums, *outs):
    width = sums.shape[1] // 4
    *plain, ups, head, classes = outs
    mine = plain[0].shape[1]

    def share(x, size):
        return pltpu.roll(x, lax.rem(x.shape[1] - spot[0] * size, x.shape[1]), axis=1)[:, 0:size]

    blocks = [share(sums[0:8, p * width : (p + 1) * width], mine) for p in (0, 2, 3)]
    for out, (block, row) in zip(plain, ((2, 0), (2, 1), (1, 2), (1, 0), (1, 1), (0, 2), (0, 0), (0, 1))):
        out[...] = blocks[block][row : row + 1]
    flat = jnp.concatenate([sums[r : r + 1, width : 2 * width] for r in range(4)], 1)
    ups[...] = share(jnp.broadcast_to(flat, (8, 4 * width)), 4 * mine)[0:1]
    head[...] = jnp.transpose(share(sums[8:16, 0 : 3 * width], 3 * mine))[:, 0:NCLASS]
    classes[...] = jnp.transpose(sums[8:16, 0:128])[0:1, NCLASS : 2 * NCLASS]


class Tiled:
    def __init__(self, array):
        self.array = array


class Flat:
    def __init__(self, array):
        self.array = array


class Scalars:
    def __init__(self, array):
        self.array = array


def spec_of(x):
    if isinstance(x, Scalars):
        return pl.BlockSpec(memory_space=pltpu.SMEM)
    if isinstance(x, Flat):
        return pl.BlockSpec(memory_space=pl.ANY)
    if isinstance(x, Tiled):
        return pl.BlockSpec((TILE, x.array.shape[1]), lambda i, lens, offs, tiles, place: (jnp.minimum(i, tiles[0] - 1), 0))
    return pl.BlockSpec(x.shape, lambda *_: (0,) * len(x.shape), pipeline_mode=pl.Buffered(1))


def bare(x):
    return x.array if isinstance(x, (Tiled, Flat, Scalars)) else x


def shape(dtype, *dims):
    return jax.ShapeDtypeStruct(dims, dtype)


def call(kernel, meta, args, outs, scratch=(), steps=1, micros=0):
    moved = sum(bare(a).size * bare(a).dtype.itemsize for a in (*args, *outs))
    return pl.pallas_call(
        kernel,
        out_shape=[bare(o) for o in outs],
        grid_spec=pltpu.PrefetchScalarGridSpec(
            num_scalar_prefetch=len(meta),
            grid=(steps,),
            in_specs=[spec_of(a) for a in args],
            out_specs=[spec_of(o) for o in outs],
            scratch_shapes=list(scratch),
        ),
        cost_estimate=pl.CostEstimate(flops=int(micros * 1.15e9), transcendentals=0, bytes_accessed=moved),
        compiler_params=pltpu.CompilerParams(vmem_limit_bytes=58 << 20),
    )(*meta, *[bare(a) for a in args])


def pack_small(vectors):
    total = sum(v.shape[0] for v in vectors)
    rows = -(-total // (8 * CHUNK)) * 8
    at, flat = 0, 0.0
    for v in vectors:
        flat = flat + jnp.pad(v.astype(f32), (at, rows * CHUNK - at - v.shape[0]))
        at += v.shape[0]
    return flat.astype(b16).reshape(rows, CHUNK)


def body(
    embeddings, lengths, labels, qkv_weight, query_bias, value_bias, out_weight, out_bias, attn_gain,
    attn_shift, up_weight, up_bias, down_weight, down_bias, ffn_gain, ffn_shift, head_weight, head_bias,
):
    width = embeddings.shape[-1]
    seq_len = embeddings.shape[2]
    count = embeddings.shape[1]
    rows = -(-count * seq_len // TILE) * TILE
    hidden = up_weight.shape[1]
    groups = lax.axis_size("dp")
    low, far, near = places()
    tower = lax.axis_index("tower")
    shard_rows = qkv_weight.shape[0]
    quick = low == 4 and shard_rows % PACK == 0

    sent_len = lengths[0]
    taken = (sent_len + PACK - 1) // PACK * PACK
    before = jnp.arange(count)[None, :] < jnp.arange(count)[:, None]
    offs = jnp.sum(jnp.where(before, taken[None, :], 0), axis=1)
    tiles = (jnp.sum(taken)[None] + TILE - 1) // TILE
    place = jnp.stack([tower, near, far]).astype(jnp.int32)
    meta = (sent_len, offs, tiles, place)
    steps = rows // TILE

    packed = pack_small((
        query_bias, value_bias, out_bias, attn_gain, attn_shift, down_bias, ffn_gain, ffn_shift, up_bias,
        head_weight.reshape(-1),
    ))
    weights = (qkv_weight, out_weight, up_weight, down_weight)
    if quick:
        sizes = [w.size // 2 // CHUNK for w in weights]
        first_part, up_part, down_part = call(
            parts_kernel, (place,), (*weights, packed),
            (
                shape(b16, sizes[0] + sizes[1] + packed.shape[0], CHUNK), shape(b16, sizes[2], CHUNK),
                shape(b16, sizes[3], CHUNK),
            ),
        )
    else:
        first_part = jnp.concatenate([to_chunks(qkv_weight), to_chunks(out_weight), packed], 0)
        up_part, down_part = to_chunks(up_weight), to_chunks(down_weight)
    cut = first_part.shape[0] - packed.shape[0]
    low_far = far_pieces(first_part)
    block_first = in_order(low_far, far, 0)
    far_up = far_pieces(after(up_part, *low_far))
    full = [(FAR, w.shape[0] * low, w.shape[1]) for w in weights]
    if quick:
        near_first = gather_near(block_first)
        far_up = after(far_up, *near_first[3:])
        block_up = in_order(far_up, far, 0)
        far_down = far_pieces(after(down_part, *far_up))
        pieces_first = near_first + [swap(p, "tower", 1) for p in near_first]
        tails = [p[:, cut:] for p in near_first]
        packs = in_order(tails[:3] + [jnp.concatenate(tails[3:], 0)], near, 1)
    else:
        block_up = in_order(far_up, far, 0)
        far_down = far_pieces(down_part)
        whole_first = gather_any(block_first)
        n_qkv = qkv_weight.shape[1] // 2 // CHUNK * shard_rows
        pieces_first = [
            from_chunks(whole_first[:, :, :n_qkv], shard_rows), from_chunks(whole_first[:, :, n_qkv:cut], shard_rows)
        ]
        packs = whole_first[:, :, cut:]
    packs = packs.reshape(groups, -1).astype(f32)
    cuts = [8 * shard_rows, 8 * shard_rows + up_bias.shape[0]]
    cuts.append(cuts[1] + head_weight.size)
    vec = packs[:, : cuts[0]].reshape(groups, 8, shard_rows).transpose(1, 0, 2).reshape(8, width)
    ups = packs[:, cuts[0] : cuts[1]].reshape(-1, width)
    head_rows = packs[:, cuts[1] : cuts[2]].reshape(-1, NCLASS).T

    ext = rows + seq_len
    dense = 2 * rows * width
    sinks = [
        Flat(shape(b16, ext, width)), Flat(shape(b16, ext, 3 * width)),
        Flat(shape(b16, count, HEADS * seq_len, seq_len)), Flat(shape(b16, ext, width)), Flat(shape(f32, rows, width)),
        Flat(shape(f32, rows, 128)),
    ]
    both = [Flat(shape(b16, *full[0])), Flat(shape(b16, *full[1]))]
    if quick:
        pieces_first = after(pieces_first, block_up)
        proj_qkv, proj_out, xs, qkv, probs, ctx, n1, inv1 = call(
            partial(attend_kernel, 10), meta, (embeddings[0], vec, *map(Flat, pieces_first)), both + sinks,
            [pltpu.VMEM(o.array.shape, o.array.dtype) for o in both + sinks]
            + [pltpu.SemaphoreType.DMA((40,)), pltpu.SemaphoreType.DMA((8,))],
            micros=20,
        )
    else:
        proj_qkv, proj_out = pieces_first
        xs, qkv, probs, ctx, n1, inv1 = call(
            partial(attend_kernel, 0), meta, (embeddings[0], vec, proj_qkv, proj_out), sinks,
            [pltpu.VMEM(o.array.shape, o.array.dtype) for o in sinks] + [pltpu.SemaphoreType.DMA((8,))],
            micros=20,
        )

    wide, slim = shape(b16, rows, hidden), shape(f32, rows, width)
    if quick:
        near_up = gather_near(block_up, n1)
        pieces_up = near_up + [swap(p, "tower", 1) for p in near_up]
        proj_up, act, slope = call(
            partial(up_kernel, 10), meta, (Tiled(n1), vec, ups, *map(Flat, pieces_up)),
            [Flat(shape(b16, *full[2])), Tiled(wide), Tiled(wide)],
            [pltpu.VMEM(full[2], b16), pltpu.SemaphoreType.DMA((40,)), pltpu.SemaphoreType.DMA((1,))],
            steps=steps, micros=12,
        )
    else:
        proj_up = from_chunks(gather_any(block_up), shard_rows)
        act, slope = call(
            partial(up_kernel, 0), meta, (Tiled(n1), vec, ups, proj_up), [Tiled(wide), Tiled(wide)], steps=steps,
            micros=12,
        )
    outs = [Tiled(slim), Tiled(shape(f32, rows, 128)), shape(f32, count, width)]
    if quick:
        block_down = in_order(after(far_down, n1), far, 0)
        near_down = gather_near(block_down, act)
        pieces_down = near_down + [swap(p, "tower", 1) for p in near_down]
        proj_down, n2, inv2, pooled = call(
            partial(down_kernel, 10), meta, (Tiled(n1), Tiled(act), vec, *map(Flat, pieces_down)),
            [Flat(shape(b16, *full[3]))] + outs,
            [pltpu.VMEM(full[3], b16), pltpu.SemaphoreType.DMA((10,)), pltpu.SemaphoreType.DMA((1,))],
            steps=steps, micros=10,
        )
    else:
        proj_down = from_chunks(gather_any(in_order(far_down, far, 0)), down_weight.shape[0])
        n2, inv2, pooled = call(
            partial(down_kernel, 0), meta, (Tiled(n1), Tiled(act), vec, proj_down), outs, steps=steps, micros=10,
        )

    def dealt(full_rows, cols):
        if quick:
            block = FAR, full_rows // (8 * FAR), cols
            return [shape(b16, 4, *block), shape(b16, *block), shape(b16, 3, *block)]
        return [shape(b16, full_rows, cols)]

    partner = swap(pooled, "tower", 1)
    sums_of = shape(f32, 8, width)
    sum_grad, *down_parts, sums_two, tops = call(
        down_back_kernel, meta,
        (
            Scalars(labels), Scalars(head_bias.astype(f32)), pooled, partner, head_rows, Tiled(act), Tiled(n2),
            Tiled(inv2), vec,
        ),
        [Tiled(slim)] + dealt(hidden, width) + [sums_of, shape(f32, 8, hidden)],
        [pltpu.VMEM((hidden, width), f32), pltpu.VMEM((count, width), f32)], steps=steps, micros=11,
    )
    if quick:
        down = Scatter(down_parts)
        sum_grad = after(sum_grad, down.first)
    pre_low, sums_up = call(
        pre_back_kernel, meta, (Tiled(sum_grad), Tiled(slope), proj_down), [Tiled(wide), sums_of], steps=steps,
        micros=8,
    )
    if quick:
        pre_low = after(pre_low, down.corners(), down.rest)
    mid, ctx_grad, *up_parts, sums_one = call(
        mid_back_kernel, meta,
        (Tiled(sum_grad), Tiled(pre_low), Tiled(n1), Tiled(inv1), Tiled(ctx), proj_up, proj_out, vec),
        [Tiled(slim), Tiled(shape(b16, ext, width))] + dealt(width, hidden + width) + [sums_of],
        [pltpu.VMEM((width, hidden + width), f32)], steps=steps, micros=20,
    )
    if quick:
        up = Scatter(after(up_parts, down.sides()))
        ctx_grad = after(ctx_grad, up.first, up.rest)
    qkv_grad, sums_in = call(
        attend_back_kernel, meta, (Flat(qkv), Flat(probs), Flat(ctx_grad)), [shape(b16, ext, 3 * width), sums_of],
        [
            pltpu.VMEM(qkv.shape, b16), pltpu.VMEM(probs.shape, b16), pltpu.VMEM(ctx_grad.shape, b16),
            pltpu.SemaphoreType.DMA((3,)),
        ],
        micros=14,
    )
    if quick:
        up.sides()
        down.far = after(down.fars(), qkv_grad)
        xs = after(xs, qkv_grad, *up.corner, *up.sent, *down.far)
    last_parts = call(
        qkv_back_kernel, meta, (Tiled(xs), Tiled(qkv_grad)), dealt(width, 3 * width),
        [pltpu.VMEM((width, 3 * width), f32)], steps=steps, micros=8,
    )
    summed = jnp.concatenate([jnp.concatenate([sums_two, sums_up, sums_one, sums_in], 1), tops], 0)
    summed = add_from(after(summed, *last_parts), "tower", 1)
    if quick:
        last = Scatter(last_parts)
        mid = after(mid, last.first, summed)
    came = swap(summed, "dp", low)
    (grad_in,) = call(
        input_kernel, meta, (Tiled(qkv_grad), Tiled(mid), proj_qkv), [shape(f32, count, seq_len, width)],
        [pltpu.VMEM((rows, width), f32)], steps=steps, micros=8,
    )
    if quick:
        last.corner = after(last.corners(), grad_in)
        last.sides()
        up.side = after(up.sides(), grad_in, *last.sent)
        came = after(came, grad_in, *last.sent)
        down_out, up_out, last_out = down.sum(), up.sum(), last.sum()
    else:
        down_out, up_out, last_out = (scatter_any(*p) for p in (down_parts, up_parts, last_parts))

    summed, bit = add_from(summed + came, "dp", 2 * low), 1
    while bit < low:
        summed = add_from(summed, "dp", bit)
        bit *= 2
    spot = (tower * groups + lax.axis_index("dp")).astype(jnp.int32)[None]
    mine = width // (2 * groups)
    *plain, up_bias_sum, head_sum, class_sum = pl.pallas_call(
        small_kernel,
        out_shape=[shape(f32, 1, mine)] * 8
        + [shape(f32, 1, 4 * mine), shape(f32, 3 * mine, NCLASS), shape(f32, 1, NCLASS)],
        in_specs=[pl.BlockSpec(memory_space=pltpu.SMEM), pl.BlockSpec(memory_space=pltpu.VMEM)],
        out_specs=[pl.BlockSpec(memory_space=pltpu.VMEM)] * 11,
    )(spot, summed)
    q_sum, v_sum, o_sum, gain_one, shift_one, d_sum, gain_two, shift_two = [x.reshape(-1) for x in plain]
    return (
        pooled[None],
        grad_in[None],
        last_out,
        q_sum, v_sum,
        up_out[:, hidden:],
        o_sum, gain_one, shift_one,
        up_out[:, :hidden],
        up_bias_sum.reshape(-1),
        down_out,
        d_sum, gain_two, shift_two,
        head_sum,
        class_sum.reshape(-1),
    )


def solution(mesh):
    rows, vec = P("dp", None), P("dp")
    out_rows, out_vec = P(("tower", "dp"), None), P(("tower", "dp"))
    return jax.shard_map(
        body,
        mesh=mesh,
        in_specs=(
            P("tower", "dp", None, None), P("tower", "dp"), vec,
            rows, vec, vec, rows, vec, vec, vec, rows, vec, rows, vec, vec, vec, rows, P(),
        ),
        out_specs=(
            P("tower", "dp", None), P("tower", "dp", None, None),
            out_rows, out_vec, out_vec, out_rows, out_vec, out_vec, out_vec, out_rows, out_vec, out_rows, out_vec,
            out_vec, out_vec, out_rows, P(),
        ),
        check_vma=False,
    )
```

time: 459 us -> 290 us (0.63); the launches traced: 452 us -> 291 us
  matrix products: 157 us -> 0 us
  Pallas kernels: 0 us -> 106 us
  local copies, waits for them, and re-layouts: 84.4 us -> 12 us
  other arithmetic: 51.4 us -> 22.6 us
  starting transfers between devices: 56.4 us -> 73 us
  between operations: 15.7 us -> 2.22 us
  waiting for transfers between devices: 87.3 us -> 74.8 us
    dot_general x21 -> x0, matrix products: 157 us -> none  [the longest x4 36.8 us: contract_cols(): lax.dot_general(left, right, (((1,), (1,)), ((), ())), preferred_element_...]
    pallas_call x0 -> x11, Pallas kernels: none -> 106 us  [the longest x10 105 us: call(): pl.pallas_call(kernel, out_shape=[bare(o) for o in outs], grid_spec=pltpu...]
    reshape x10 -> x6, local copies, waits for them, and re-layouts: 22.7 us -> 3.49 us  [the longest x2 1.43 us: body(): head_rows = packs[:, cuts[1]:cuts[2]].reshape(-1, NCLASS).T]
    ppermute x46 -> x69, starting transfers between devices: 56.3 us -> 73 us  [swap(): lax.ppermute(x, axis, [(i, i ^ k) for i in range(lax.axis_size(axis))])]
    concatenate x3 -> x0, local copies, waits for them, and re-layouts: 14.3 us -> none  [the longest x1 6.65 us: body(): jnp.concatenate([qkv_full_grad, out_grad], 1)]
    ppermute x46 -> x69, waiting for transfers between devices: 87.3 us -> 74.8 us  [swap(): lax.ppermute(x, axis, [(i, i ^ k) for i in range(lax.axis_size(axis))])]
    dynamic_slice x12 -> x0, local copies, waits for them, and re-layouts: 11.4 us -> none  [the longest x2 4.58 us: tower_half(): mine = lax.dynamic_index_in_dim(halves, tower, 0, keepdims=False)]
    transpose x3 -> x0, other arithmetic: 10.7 us -> none  [from_chunks(): both = both.reshape(2, far, low, n, rows, CHUNK).transpose(1, 2, 4, 0, 3, 5)]
  transfers between devices with their start and end apart: 47 -> 69, of which waited for: 13 -> 21; matrix products, arithmetic and copies ran while one was open for 39% -> 8% of each run, Pallas kernels for 0% -> 28%
where the time goes in v2:
time: 290 us; the launch traced here: 291 us
  Pallas kernels  106 us (37%)
  waiting for transfers between devices  74.8 us (26%)
  starting transfers between devices  73 us (25%)
  other arithmetic  22.6 us (8%)
  local copies, waits for them, and re-layouts  12 us (4%)
    pallas_call x10, Pallas kernels, call(): pl.pallas_call(kernel, out_shape=[bare(o) for o in outs], grid_spec=pltpu...  105 us
    ppermute x69, waiting for transfers between devices, swap(): lax.ppermute(x, axis, [(i, i ^ k) for i in range(lax.axis_size(axis))])  74.8 us
    ppermute x69, starting transfers between devices, swap(): lax.ppermute(x, axis, [(i, i ^ k) for i in range(lax.axis_size(axis))])  73 us
  transfers between devices with their start and end apart: 69, of which 21 were waited for; matrix products, arithmetic and copies ran while one was open for 8% of the time, Pallas kernels for 28%

profile of v2, /device:TPU:0, one launch (start us, length us, event | category | flops | bytes accessed | tf_op | source)
XLA Modules:
  0.0 291.0 jit_solution(1767393056810459780)
XLA Ops:
  3.8 2.7 shard_map.305
  6.4 5.0 %collective-permute-start.2 = (bf16[200,384]{1,0:T(8,128)(2,1)}, bf16[200,384]{1,0:T(8,128)(2,1)S(1)}, u32[]{:S(2)}, u32[]{:S(2)}) collective-permute-start(bf16[200,384]{1,0:T(8,128)(2,1)} %get-tuple-element.111), channel_id=1, source_target_pairs={{0,12},{1,13},{2,14},{3,15},{4,8},{5,9},{6,10},{7,11},{8,4},{9,5},... | collective-permute-start | bytes 460808 | tf_op jit(solution)/shard_map/ppermute | solution.py:24
  12.1 4.6 %collective-permute-done.2 = bf16[200,384]{1,0:T(8,128)(2,1)S(1)} collective-permute-done((bf16[200,384]{1,0:T(8,128)(2,1)}, bf16[200,384]{1,0:T(8,128)(2,1)S(1)}, u32[]{:S(2)}, u32[]{:S(2)}) %collective-permute-start.2) | collective-permute-done | bytes 153632 | tf_op jit(solution)/shard_map/ppermute | solution.py:24
  16.6 8.1 %collective-permute-done.1 = bf16[200,384]{1,0:T(8,128)(2,1)S(1)} collective-permute-done((bf16[200,384]{1,0:T(8,128)(2,1)}, bf16[200,384]{1,0:T(8,128)(2,1)S(1)}, u32[]{:S(2)}, u32[]{:S(2)}) %collective-permute-start.1) | collective-permute-done | bytes 153632 | tf_op jit(solution)/shard_map/ppermute | solution.py:24
  31.0 2.5 collective-permute-start.14
  33.5 1.9 collective-permute-start.12
  35.4 5.5 %collective-permute-done.4.refs_2_ = bf16[4,200,384]{2,1,0:T(8,128)(2,1)S(1)} collective-permute-done((bf16[4,200,384]{2,1,0:T(8,128)(2,1)S(1)}, bf16[4,200,384]{2,1,0:T(8,128)(2,1)S(1)}, u32[]{:S(2)}, u32[]{:S(2)}) %collective-permute-start.4) | collective-permute-done | bytes 614432 | tf_op jit(solution)/shard_map/ppermute | solution.py:24
  44.4 5.1 %collective-permute-done.6.refs_4_ = bf16[2,200,384]{2,1,0:T(8,128)(2,1)S(1)} collective-permute-done((bf16[2,200,384]{2,1,0:T(8,128)(2,1)S(1)}, bf16[2,200,384]{2,1,0:T(8,128)(2,1)S(1)}, u32[]{:S(2)}, u32[]{:S(2)}) %collective-permute-start.6) | collective-permute-done | bytes 307232 | tf_op jit(solution)/shard_map/ppermute | solution.py:24
  53.9 2.3 collective-permute-start.26
  56.3 2.1 collective-permute-start.24
  59.5 16.3 %shard_map.306 = (bf16[4,192,2304]{2,1,0:T(8,128)(2,1)}, bf16[4,192,768]{2,1,0:T(8,128)(2,1)}, bf16[1280,768]{1,0:T(8,128)(2,1)}, bf16[1280,2304]{1,0:T(8,128)(2...) custom-call(s32[8]{0:T(128)} %bitcast.179, ...), custom_call_target="tpu_custom_call" | custom-call | flops 23000000512 | bytes 28336128 | tf_op jit(solution)/shard_map/pallas_call | solution.py:733
  75.8 3.2 %collective-permute-start.18 = (bf16[2,192,384]{2,1,0:T(8,128)(2,1)S(1)}, bf16[2,192,384]{2,1,0:T(8,128)(2,1)}, u32[]{:S(2)}, u32[]{:S(2)}) collective-permute-start(bf16[2,192,384]{2,1,0:T(8,128)(2,1)S(1)} %slice.229), channel_id=1, source_target_pairs={{0,1},{1,0},{2,3},{3,2},{4,5},{5,4},{6,7},{7,6},{8,9},{9,8},{10,11... | collective-permute-start | bytes 884744 | tf_op jit(solution)/shard_map/ppermute | solution.py:24
  79.0 1.7 collective-permute-start.17
  82.0 2.9 %collective-permute-done.18.refs_4_ = bf16[2,192,384]{2,1,0:T(8,128)(2,1)} collective-permute-done((bf16[2,192,384]{2,1,0:T(8,128)(2,1)S(1)}, bf16[2,192,384]{2,1,0:T(8,128)(2,1)}, u32[]{:S(2)}, u32[]{:S(2)}) %collective-permute-start.18) | collective-permute-done | bytes 294944 | tf_op jit(solution)/shard_map/ppermute | solution.py:24
  86.8 1.6 collective-permute-start.28
  89.3 10.3 %shard_map.307 = (bf16[4,192,3072]{2,1,0:T(8,128)(2,1)}, bf16[1152,3072]{1,0:T(8,128)(2,1)}, bf16[1152,3072]{1,0:T(8,128)(2,1)}) custom-call(s32[8]{0:T(128)} %bitcast.180, s32[8]{0:T(128)} %select_reduce_fusion.offs, s32[1]{0:T(128)S(6)} %select_n.66.tiles, s32[3]{0:T(128)} %pad_add_fusion.place, f32[1152,768]{1,0:T(8,128)} %get-tuple-element.130.n1, ...), custom_call_target="tpu_custom_call" | custom-call | flops 13799999488 | bytes 27168768 | tf_op jit(solution)/shard_map/pallas_call | solution.py:733
  99.6 2.5 collective-permute-done.28.refs_2_
  105.9 5.6 %collective-permute-done.30.refs_4_ = bf16[2,192,384]{2,1,0:T(8,128)(2,1)S(1)} collective-permute-done((bf16[2,192,384]{2,1,0:T(8,128)(2,1)S(1)}, bf16[2,192,384]{2,1,0:T(8,128)(2,1)S(1)}, u32[]{:S(2)}, u32[]{:S(2)}) %collective-permute-start.30) | collective-permute-done | bytes 294944 | tf_op jit(solution)/shard_map/ppermute | solution.py:24
  115.5 9.4 %shard_map.308 = (bf16[4,768,768]{2,1,0:T(8,128)(2,1)}, f32[1152,768]{1,0:T(8,128)}, f32[1152,128]{1,0:T(8,128)}, f32[8,768]{1,0:T(8,128)}) custom-call(s32[8]{0:T(128)} %bitcast.181, s32[8]{0:T(128)} %select_reduce_fusion.offs, s32[1]{0:T(128)S(6)} %select_n.66.tiles, s32[3]{0:T(128)} %pad_add_fusion.place, f32[1152,768]{1,0:T(8,128)} %get-tuple-element.130.n1, ...), custom_call_target="tpu_custom_call" | custom-call | flops 11500000256 | bytes 24231936 | tf_op jit(solution)/shard_map/pallas_call | solution.py:733
  124.9 1.9 collective-permute-start.36
  129.4 10.2 %shard_map.309 = (f32[1152,768]{1,0:T(8,128)}, bf16[4,4,96,768]{3,2,1,0:T(8,128)(2,1)}, bf16[4,96,768]{2,1,0:T(8,128)(2,1)}, bf16[3,4,96,768]{3,2,1,0:T(8,128)(2...) custom-call(s32[8]{0:T(128)} %bitcast.182, s32[8]{0:T(128)} %select_reduce_fusion.offs, s32[1]{0:T(128)S(6)} %select_n.66.tiles, ...), custom_call_target="tpu_custom_call" | custom-call | flops 12650000384 | bytes 19688492 | tf_op jit(solution)/shard_map/pallas_call | solution.py:733
  139.6 2.2 collective-permute-start.37
  141.8 1.8 collective-permute-done.37
  145.3 2.8 collective-permute-start.38
  148.2 8.4 %shard_map.310 = (bf16[1152,3072]{1,0:T(8,128)(2,1)}, f32[8,768]{1,0:T(8,128)}) custom-call(s32[8]{0:T(128)} %bitcast.183, s32[8]{0:T(128)} %select_reduce_fusion.offs, s32[1]{0:T(128)S(6)} %select_n.66.tiles, s32[3]{0:T(128)} %pad_add_fusion.place, f32[1152,768]{1,0:T(8,128)} %get-tuple-element.149.sum_grad, bf16[1152,3072]{1,0:T(8,128)(2,1)} %get-tuple-element.150.slope, ...), custom_call_target="tpu_custom_call" | custom-call | flops 9200000000 | bytes 22437888 | tf_op jit(solution)/shard_map/pallas_call | solution.py:733
  158.0 1.9 collective-permute-start.41
  161.2 18.1 %shard_map.311 = (f32[1152,768]{1,0:T(8,128)}, bf16[1280,768]{1,0:T(8,128)(2,1)}, bf16[4,4,24,3840]{3,2,1,0:T(8,128)(2,1)}, bf16[4,24,3840]{2,1,0:T(8,128)(2,1)}...) custom-call(s32[8]{0:T(128)} %bitcast.184, s32[8]{0:T(128)} %select_reduce_fusion.offs, s32[1]{0:T(128)S(6)} %select_n.66.tiles, ...), custom_call_target="tpu_custom_call" | custom-call | flops 23000000512 | bytes 34062336 | tf_op jit(solution)/shard_map/pallas_call | solution.py:733
  179.3 3.5 %collective-permute-start.43 = (bf16[4,24,3840]{2,1,0:T(8,128)(2,1)}, bf16[4,24,3840]{2,1,0:T(8,128)(2,1)S(1)}, u32[]{:S(2)}, u32[]{:S(2)}) collective-permute-start(bf16[4,24,3840]{2,1,0:T(8,128)(2,1)} %get-tuple-element.165), channel_id=1, source_target_pairs={{0,16},{16,0},{1,17},{17,1},{2,18},{18,2},{3,19},{19,3},{4,20},{20... | collective-permute-start | bytes 2211848 | tf_op jit(solution)/shard_map/ppermute | solution.py:24
  182.8 2.1 collective-permute-done.43
  185.2 2.9 %fusion.34 = (bf16[4,96,768]{2,1,0:T(8,128)(2,1)S(1)}, f32[4,96,768]{2,1,0:T(8,128)}) fusion(bf16[4,96,768]{2,1,0:T(8,128)(2,1)} %copy-done.9, bf16[4,96,768]{2,1,0:T(8,128)(2,1)} %copy-done.8, bf16[3,4,96,768]{3,2,1,0:T(8,128)(2,1)} %copy-done.3, bf16[4,4,96,768]{3,2,1,0:T(8,128)(2,1)S(1)} %copy-done.1), kind=kLoop, calls=%fused_computation.114 | loop fusion | flops 2359296 | bytes 4128768 | tf_op jit(solution)/shard_map/convert.36
  188.3 4.3 %collective-permute-start.47 = (bf16[96,768]{1,0:T(8,128)(2,1)S(1)}, bf16[96,768]{1,0:T(8,128)(2,1)S(1)}, u32[]{:S(2)}, u32[]{:S(2)}) collective-permute-start(bf16[96,768]{1,0:T(8,128)(2,1)S(1)} %get-tuple-element.289), channel_id=1, source_target_pairs={{0,4},{1,5},{2,6},{3,7},{4,0},{5,1},{6,2},{7,3},{8,12},{9,13},{10,... | collective-permute-start | bytes 442376 | tf_op jit(solution)/shard_map/ppermute | solution.py:24
  193.5 2.0 collective-permute-start.45
  195.5 13.6 %shard_map.312 = (bf16[1280,2304]{1,0:T(8,128)(2,1)}, f32[8,768]{1,0:T(8,128)}) custom-call(s32[8]{0:T(128)} %bitcast.185, s32[8]{0:T(128)} %select_reduce_fusion.offs, s32[1]{0:T(128)S(6)} %select_n.66.tiles, s32[3]{0:T(128)} %pad_add_fusion.place, bf16[1280,2304]{1,0:T(8,128)(2,1)} %get-tuple-element.143.qkv_h, ...), custom_call_target="tpu_custom_call" | custom-call | flops 16099999744 | bytes 16932864 | tf_op jit(solution)/shard_map/pallas_call | solution.py:733
  214.5 1.6 collective-permute-start.65
  216.1 7.3 %shard_map.313 = (bf16[4,4,24,2304]{3,2,1,0:T(8,128)(2,1)}, bf16[4,24,2304]{2,1,0:T(8,128)(2,1)}, bf16[3,4,24,2304]{3,2,1,0:T(8,128)(2,1)}) custom-call(s32[8]{0:T(128)} %bitcast.186, s32[8]{0:T(128)} %select_reduce_fusion.offs, s32[1]{0:T(128)S(6)} %select_n.66.tiles, s32[3]{0:T(128)} %pad_add_fusion.place, bf16[1280,768]{1,0:T(8,128)(2,1)} %get-tuple-element.176.xs, ...), custom_call_target="tpu_custom_call" | custom-call | flops 9200000000 | bytes 11403264 | tf_op jit(solution)/shard_map/pallas_call | solution.py:733
  224.0 1.7 fusion.24
  227.7 2.5 collective-permute-start.53
  230.2 8.3 %shard_map.314 = f32[8,128,768]{2,1,0:T(8,128)} custom-call(s32[8]{0:T(128)} %bitcast.187, s32[8]{0:T(128)} %select_reduce_fusion.offs, s32[1]{0:T(128)S(6)} %select_n.66.tiles, s32[3]{0:T(128)} %pad_add_fusion.place, bf16[1280,2304]{1,0:T(8,128)(2,1)} %get-tuple-element.169.grad, f32[1152,768]{1,0:T(8,128)} %get-tuple-element.186.mid, ...), custom_call_target="tpu_custom_call" | custom-call | flops 9200000000 | bytes 16121856 | tf_op jit(solution)/shard_map/pallas_call | solution.py:733
  240.5 3.3 %collective-permute-start.56 = (bf16[4,24,2304]{2,1,0:T(8,128)(2,1)S(1)}, bf16[4,24,2304]{2,1,0:T(8,128)(2,1)S(1)}, u32[]{:S(2)}, u32[]{:S(2)}) collective-permute-start(bf16[4,24,2304]{2,1,0:T(8,128)(2,1)S(1)} %pad_maximum_fusion.11), channel_id=1, source_target_pairs={{0,2},{1,3},{2,0},{3,1},{4,6},{5,7},{6,4},{7,5},{8,10},{9,11},{10,... | collective-permute-start | bytes 1327112 | tf_op jit(solution)/shard_map/ppermute | solution.py:24
  244.1 2.1 collective-permute-done.60
  246.3 1.9 fusion.30
  249.2 3.5 %collective-permute-start.68 = (bf16[24,3840]{1,0:T(8,128)(2,1)S(1)}, bf16[24,3840]{1,0:T(8,128)(2,1)S(1)}, u32[]{:S(2)}, u32[]{:S(2)}) collective-permute-start(bf16[24,3840]{1,0:T(8,128)(2,1)S(1)} %get-tuple-element.281), channel_id=1, source_target_pairs={{0,12},{1,13},{2,14},{3,15},{4,8},{5,9},{6,10},{7,11},{8,4},{9,5},... | collective-permute-start | bytes 552968 | tf_op jit(solution)/shard_map/ppermute | solution.py:24
  252.7 13.9 %collective-permute-done.61 = f32[16,3072]{1,0:T(8,128)S(1)} collective-permute-done((f32[16,3072]{1,0:T(8,128)S(1)}, f32[16,3072]{1,0:T(8,128)S(1)}, u32[]{:S(2)}, u32[]{:S(2)}) %collective-permute-start.61) | collective-permute-done | bytes 196640 | tf_op jit(solution)/shard_map/ppermute | solution.py:24
  267.4 4.0 %collective-permute-start.59 = (bf16[24,2304]{1,0:T(8,128)(2,1)S(1)}, bf16[24,2304]{1,0:T(8,128)(2,1)S(1)}, u32[]{:S(2)}, u32[]{:S(2)}) collective-permute-start(bf16[24,2304]{1,0:T(8,128)(2,1)S(1)} %get-tuple-element.299), channel_id=1, source_target_pairs={{0,12},{1,13},{2,14},{3,15},{4,8},{5,9},{6,10},{7,11},{8,4},{9,5},... | collective-permute-start | bytes 331784 | tf_op jit(solution)/shard_map/ppermute | solution.py:24
  271.5 8.4 %collective-permute-done.67 = bf16[24,3840]{1,0:T(8,128)(2,1)S(1)} collective-permute-done((bf16[24,3840]{1,0:T(8,128)(2,1)S(1)}, bf16[24,3840]{1,0:T(8,128)(2,1)S(1)}, u32[]{:S(2)}, u32[]{:S(2)}) %collective-permute-start.67) | collective-permute-done | bytes 184352 | tf_op jit(solution)/shard_map/ppermute | solution.py:24
  281.5 2.5 collective-permute-done.58
  284.7 2.4 collective-permute-done.63
  287.8 1.8 shard_map.315
  (247 shorter events, 54.6 us)
Async XLA Ops:
  6.4 10.2 %collective-permute-start.2 = (bf16[200,384]{1,0:T(8,128)(2,1)}, bf16[200,384]{1,0:T(8,128)(2,1)S(1)}, u32[]{:S(2)}, u32[]{:S(2)}) collective-permute-start(bf16[200,384]{1,0:T(8,128)(2,1)} %get-tuple-element.111), channel_id=1, source_target_pairs={{0,12},{1,13},{2,14},{3,15},{4,8},{5,9},{6,10},{7,11},{8,4},{9,5},... | collective-permute-start | bytes 460808 | tf_op jit(solution)/shard_map/ppermute | solution.py:24
  11.5 13.2 %collective-permute-start.1 = (bf16[200,384]{1,0:T(8,128)(2,1)}, bf16[200,384]{1,0:T(8,128)(2,1)S(1)}, u32[]{:S(2)}, u32[]{:S(2)}) collective-permute-start(bf16[200,384]{1,0:T(8,128)(2,1)} %get-tuple-element.111), channel_id=1, source_target_pairs={{0,8},{1,9},{2,10},{3,11},{4,12},{5,13},{6,14},{7,15},{8,0},{9,1},... | collective-permute-start | bytes 460808 | tf_op jit(solution)/shard_map/ppermute | solution.py:24
  11.5 13.2 %collective-permute-start = (bf16[200,384]{1,0:T(8,128)(2,1)}, bf16[200,384]{1,0:T(8,128)(2,1)S(1)}, u32[]{:S(2)}, u32[]{:S(2)}) collective-permute-start(bf16[200,384]{1,0:T(8,128)(2,1)} %get-tuple-element.111), channel_id=1, source_target_pairs={{0,4},{1,5},{2,6},{3,7},{4,0},{5,1},{6,2},{7,3},{8,12},{9,13},{10,... | collective-permute-start | bytes 460808 | tf_op jit(solution)/shard_map/ppermute | solution.py:24
  26.0 15.0 %collective-permute-start.4 = (bf16[4,200,384]{2,1,0:T(8,128)(2,1)S(1)}, bf16[4,200,384]{2,1,0:T(8,128)(2,1)S(1)}, u32[]{:S(2)}, u32[]{:S(2)}) collective-permute-start(bf16[4,200,384]{2,1,0:T(8,128)(2,1)S(1)} %pad_maximum_fusion.3.refs_0_), channel_id=1, source_target_pairs={{0,2},{1,3},{2,0},{3,1},{4,6},{5,7},{6,4},{7,5},{8,10},{9,11},{10,... | collective-permute-start | bytes 1843208 | tf_op jit(solution)/shard_map/ppermute | solution.py:24
  27.6 14.6 %collective-permute-start.3 = (bf16[4,200,384]{2,1,0:T(8,128)(2,1)S(1)}, bf16[4,200,384]{2,1,0:T(8,128)(2,1)S(1)}, u32[]{:S(2)}, u32[]{:S(2)}) collective-permute-start(bf16[4,200,384]{2,1,0:T(8,128)(2,1)S(1)} %pad_maximum_fusion.3.refs_0_), channel_id=1, source_target_pairs={{0,1},{1,0},{2,3},{3,2},{4,5},{5,4},{6,7},{7,6},{8,9},{9,8},{10,11... | collective-permute-start | bytes 1843208 | tf_op jit(solution)/shard_map/ppermute | solution.py:24
  31.0 20.5 %collective-permute-start.14 = (bf16[192,384]{1,0:T(8,128)(2,1)S(1)}, bf16[192,384]{1,0:T(8,128)(2,1)S(1)}, u32[]{:S(2)}, u32[]{:S(2)}) collective-permute-start(bf16[192,384]{1,0:T(8,128)(2,1)S(1)} %copy-done.13), channel_id=1, source_target_pairs={{0,12},{1,13},{2,14},{3,15},{4,8},{5,9},{6,10},{7,11},{8,4},{9,5},... | collective-permute-start | bytes 442376 | tf_op jit(solution)/shard_map/ppermute | solution.py:24
  33.5 18.6 %collective-permute-start.13 = (bf16[192,384]{1,0:T(8,128)(2,1)S(1)}, bf16[192,384]{1,0:T(8,128)(2,1)S(1)}, u32[]{:S(2)}, u32[]{:S(2)}) collective-permute-start(bf16[192,384]{1,0:T(8,128)(2,1)S(1)} %copy-done.13), channel_id=1, source_target_pairs={{0,8},{1,9},{2,10},{3,11},{4,12},{5,13},{6,14},{7,15},{8,0},{9,1},... | collective-permute-start | bytes 442376 | tf_op jit(solution)/shard_map/ppermute | solution.py:24
  33.5 18.6 %collective-permute-start.12 = (bf16[192,384]{1,0:T(8,128)(2,1)S(1)}, bf16[192,384]{1,0:T(8,128)(2,1)S(1)}, u32[]{:S(2)}, u32[]{:S(2)}) collective-permute-start(bf16[192,384]{1,0:T(8,128)(2,1)S(1)} %copy-done.13), channel_id=1, source_target_pairs={{0,4},{1,5},{2,6},{3,7},{4,0},{5,1},{6,2},{7,3},{8,12},{9,13},{10,... | collective-permute-start | bytes 442376 | tf_op jit(solution)/shard_map/ppermute | solution.py:24
  53.9 26.8 %collective-permute-start.26 = (bf16[192,384]{1,0:T(8,128)(2,1)S(1)}, bf16[192,384]{1,0:T(8,128)(2,1)S(1)}, u32[]{:S(2)}, u32[]{:S(2)}) collective-permute-start(bf16[192,384]{1,0:T(8,128)(2,1)S(1)} %copy-done.12), channel_id=1, source_target_pairs={{0,12},{1,13},{2,14},{3,15},{4,8},{5,9},{6,10},{7,11},{8,4},{9,5},... | collective-permute-start | bytes 442376 | tf_op jit(solution)/shard_map/ppermute | solution.py:24
  56.3 24.5 %collective-permute-start.25 = (bf16[192,384]{1,0:T(8,128)(2,1)S(1)}, bf16[192,384]{1,0:T(8,128)(2,1)S(1)}, u32[]{:S(2)}, u32[]{:S(2)}) collective-permute-start(bf16[192,384]{1,0:T(8,128)(2,1)S(1)} %copy-done.12), channel_id=1, source_target_pairs={{0,8},{1,9},{2,10},{3,11},{4,12},{5,13},{6,14},{7,15},{8,0},{9,1},... | collective-permute-start | bytes 442376 | tf_op jit(solution)/shard_map/ppermute | solution.py:24
  56.3 25.0 %collective-permute-start.24 = (bf16[192,384]{1,0:T(8,128)(2,1)S(1)}, bf16[192,384]{1,0:T(8,128)(2,1)S(1)}, u32[]{:S(2)}, u32[]{:S(2)}) collective-permute-start(bf16[192,384]{1,0:T(8,128)(2,1)S(1)} %copy-done.12), channel_id=1, source_target_pairs={{0,4},{1,5},{2,6},{3,7},{4,0},{5,1},{6,2},{7,3},{8,12},{9,13},{10,... | collective-permute-start | bytes 442376 | tf_op jit(solution)/shard_map/ppermute | solution.py:24
  58.4 17.4 %collective-permute-start.16 = (bf16[4,192,384]{2,1,0:T(8,128)(2,1)S(1)}, bf16[4,192,384]{2,1,0:T(8,128)(2,1)S(1)}, u32[]{:S(2)}, u32[]{:S(2)}) collective-permute-start(bf16[4,192,384]{2,1,0:T(8,128)(2,1)S(1)} %pad_maximum_fusion.5.refs_0_), channel_id=1, source_target_pairs={{0,2},{1,3},{2,0},{3,1},{4,6},{5,7},{6,4},{7,5},{8,10},{9,11},{10,... | collective-permute-start | bytes 1769480 | tf_op jit(solution)/shard_map/ppermute | solution.py:24
  58.9 16.8 %collective-permute-start.15 = (bf16[4,192,384]{2,1,0:T(8,128)(2,1)S(1)}, bf16[4,192,384]{2,1,0:T(8,128)(2,1)S(1)}, u32[]{:S(2)}, u32[]{:S(2)}) collective-permute-start(bf16[4,192,384]{2,1,0:T(8,128)(2,1)S(1)} %pad_maximum_fusion.5.refs_0_), channel_id=1, source_target_pairs={{0,1},{1,0},{2,3},{3,2},{4,5},{5,4},{6,7},{7,6},{8,9},{9,8},{10,11... | collective-permute-start | bytes 1769480 | tf_op jit(solution)/shard_map/ppermute | solution.py:24
  75.8 9.1 %collective-permute-start.18 = (bf16[2,192,384]{2,1,0:T(8,128)(2,1)S(1)}, bf16[2,192,384]{2,1,0:T(8,128)(2,1)}, u32[]{:S(2)}, u32[]{:S(2)}) collective-permute-start(bf16[2,192,384]{2,1,0:T(8,128)(2,1)S(1)} %slice.229), channel_id=1, source_target_pairs={{0,1},{1,0},{2,3},{3,2},{4,5},{5,4},{6,7},{7,6},{8,9},{9,8},{10,11... | collective-permute-start | bytes 884744 | tf_op jit(solution)/shard_map/ppermute | solution.py:24
  80.7 8.5 %collective-permute-start.20 = (bf16[4,192,384]{2,1,0:T(8,128)(2,1)S(1)}, bf16[4,192,384]{2,1,0:T(8,128)(2,1)}, u32[]{:S(2)}, u32[]{:S(2)}) collective-permute-start(bf16[4,192,384]{2,1,0:T(8,128)(2,1)S(1)} %collective-permute-done.15.refs_1_), channel_id=1, source_target_pairs={{0,16},{16,0},{1,17},{17,1},{2,18},{18,2},{3,19},{19,3},{4,20},{20... | collective-permute-start | bytes 1769480 | tf_op jit(solution)/shard_map/ppermute | solution.py:24
  81.2 8.0 %collective-permute-start.21 = (bf16[4,192,384]{2,1,0:T(8,128)(2,1)S(1)}, bf16[4,192,384]{2,1,0:T(8,128)(2,1)}, u32[]{:S(2)}, u32[]{:S(2)}) collective-permute-start(bf16[4,192,384]{2,1,0:T(8,128)(2,1)S(1)} %collective-permute-done.16.refs_2_), channel_id=1, source_target_pairs={{0,16},{16,0},{1,17},{17,1},{2,18},{18,2},{3,19},{19,3},{4,20},{20... | collective-permute-start | bytes 1769480 | tf_op jit(solution)/shard_map/ppermute | solution.py:24
  86.2 26.0 %collective-permute-start.31 = (bf16[4,192,384]{2,1,0:T(8,128)(2,1)S(1)}, bf16[4,192,384]{2,1,0:T(8,128)(2,1)S(1)}, u32[]{:S(2)}, u32[]{:S(2)}) collective-permute-start(bf16[4,192,384]{2,1,0:T(8,128)(2,1)S(1)} %pad_maximum_fusion.7.refs_0_), channel_id=1, source_target_pairs={{0,16},{16,0},{1,17},{17,1},{2,18},{18,2},{3,19},{19,3},{4,20},{20... | collective-permute-start | bytes 1769480 | tf_op jit(solution)/shard_map/ppermute | solution.py:24
  86.8 15.3 %collective-permute-start.28 = (bf16[4,192,384]{2,1,0:T(8,128)(2,1)S(1)}, bf16[4,192,384]{2,1,0:T(8,128)(2,1)S(1)}, u32[]{:S(2)}, u32[]{:S(2)}) collective-permute-start(bf16[4,192,384]{2,1,0:T(8,128)(2,1)S(1)} %pad_maximum_fusion.7.refs_0_), channel_id=1, source_target_pairs={{0,2},{1,3},{2,0},{3,1},{4,6},{5,7},{6,4},{7,5},{8,10},{9,11},{10,... | collective-permute-start | bytes 1769480 | tf_op jit(solution)/shard_map/ppermute | solution.py:24
  88.4 15.0 %collective-permute-start.27 = (bf16[4,192,384]{2,1,0:T(8,128)(2,1)S(1)}, bf16[4,192,384]{2,1,0:T(8,128)(2,1)S(1)}, u32[]{:S(2)}, u32[]{:S(2)}) collective-permute-start(bf16[4,192,384]{2,1,0:T(8,128)(2,1)S(1)} %pad_maximum_fusion.7.refs_0_), channel_id=1, source_target_pairs={{0,1},{1,0},{2,3},{3,2},{4,5},{5,4},{6,7},{7,6},{8,9},{9,8},{10,11... | collective-permute-start | bytes 1769480 | tf_op jit(solution)/shard_map/ppermute | solution.py:24
  103.5 7.9 %collective-permute-start.30 = (bf16[2,192,384]{2,1,0:T(8,128)(2,1)S(1)}, bf16[2,192,384]{2,1,0:T(8,128)(2,1)S(1)}, u32[]{:S(2)}, u32[]{:S(2)}) collective-permute-start(bf16[2,192,384]{2,1,0:T(8,128)(2,1)S(1)} %slice.231), channel_id=1, source_target_pairs={{0,1},{1,0},{2,3},{3,2},{4,5},{5,4},{6,7},{7,6},{8,9},{9,8},{10,11... | collective-permute-start | bytes 884744 | tf_op jit(solution)/shard_map/ppermute | solution.py:24
  105.4 8.4 %collective-permute-start.32 = (bf16[4,192,384]{2,1,0:T(8,128)(2,1)S(1)}, bf16[4,192,384]{2,1,0:T(8,128)(2,1)S(1)}, u32[]{:S(2)}, u32[]{:S(2)}) collective-permute-start(bf16[4,192,384]{2,1,0:T(8,128)(2,1)S(1)} %collective-permute-done.27.refs_1_), channel_id=1, source_target_pairs={{0,16},{16,0},{1,17},{17,1},{2,18},{18,2},{3,19},{19,3},{4,20},{20... | collective-permute-start | bytes 1769480 | tf_op jit(solution)/shard_map/ppermute | solution.py:24
  105.4 8.4 %collective-permute-start.33 = (bf16[4,192,384]{2,1,0:T(8,128)(2,1)S(1)}, bf16[4,192,384]{2,1,0:T(8,128)(2,1)S(1)}, u32[]{:S(2)}, u32[]{:S(2)}) collective-permute-start(bf16[4,192,384]{2,1,0:T(8,128)(2,1)S(1)} %collective-permute-done.28.refs_2_), channel_id=1, source_target_pairs={{0,16},{16,0},{1,17},{17,1},{2,18},{18,2},{3,19},{19,3},{4,20},{20... | collective-permute-start | bytes 1769480 | tf_op jit(solution)/shard_map/ppermute | solution.py:24
  143.7 12.9 %collective-permute-start.40 = (bf16[3,4,96,768]{3,2,1,0:T(8,128)(2,1)}, bf16[3,4,96,768]{3,2,1,0:T(8,128)(2,1)S(1)}, u32[]{:S(2)}, u32[]{:S(2)}) collective-permute-start(bf16[3,4,96,768]{3,2,1,0:T(8,128)(2,1)} %get-tuple-element.155), channel_id=1, source_target_pairs={{0,16},{16,0},{1,17},{17,1},{2,18},{18,2},{3,19},{19,3},{4,20},{20... | collective-permute-start | bytes 5308424 | tf_op jit(solution)/shard_map/ppermute | solution.py:24
  145.2 11.4 %collective-permute-start.39 = (bf16[2,96,768]{2,1,0:T(8,128)(2,1)S(1)}, bf16[2,96,768]{2,1,0:T(8,128)(2,1)S(1)}, u32[]{:S(2)}, u32[]{:S(2)}) collective-permute-start(bf16[2,96,768]{2,1,0:T(8,128)(2,1)S(1)} %get-tuple-element.276), channel_id=1, source_target_pairs={{0,2},{1,3},{2,0},{3,1},{4,6},{5,7},{6,4},{7,5},{8,10},{9,11},{10,... | collective-permute-start | bytes 884744 | tf_op jit(solution)/shard_map/ppermute | solution.py:24
  145.3 11.3 %collective-permute-start.38 = (bf16[2,96,768]{2,1,0:T(8,128)(2,1)S(1)}, bf16[2,96,768]{2,1,0:T(8,128)(2,1)S(1)}, u32[]{:S(2)}, u32[]{:S(2)}) collective-permute-start(bf16[2,96,768]{2,1,0:T(8,128)(2,1)S(1)} %get-tuple-element.277), channel_id=1, source_target_pairs={{0,1},{1,0},{2,3},{3,2},{4,5},{5,4},{6,7},{7,6},{8,9},{9,8},{10,11... | collective-permute-start | bytes 884744 | tf_op jit(solution)/shard_map/ppermute | solution.py:24
  158.0 21.3 %collective-permute-start.41 = (bf16[4,96,768]{2,1,0:T(8,128)(2,1)S(1)}, bf16[4,96,768]{2,1,0:T(8,128)(2,1)S(1)}, u32[]{:S(2)}, u32[]{:S(2)}) collective-permute-start(bf16[4,96,768]{2,1,0:T(8,128)(2,1)S(1)} %pad_maximum_fusion.8), channel_id=1, source_target_pairs={{0,1},{1,0},{2,3},{3,2},{4,5},{5,4},{6,7},{7,6},{8,9},{9,8},{10,11... | collective-permute-start | bytes 1769480 | tf_op jit(solution)/shard_map/ppermute | solution.py:24
  159.9 19.4 %collective-permute-start.42 = (bf16[4,96,768]{2,1,0:T(8,128)(2,1)S(1)}, bf16[4,96,768]{2,1,0:T(8,128)(2,1)S(1)}, u32[]{:S(2)}, u32[]{:S(2)}) collective-permute-start(bf16[4,96,768]{2,1,0:T(8,128)(2,1)S(1)} %pad_maximum_fusion.9), channel_id=1, source_target_pairs={{0,2},{1,3},{2,0},{3,1},{4,6},{5,7},{6,4},{7,5},{8,10},{9,11},{10,... | collective-permute-start | bytes 1769480 | tf_op jit(solution)/shard_map/ppermute | solution.py:24
  184.9 8.6 %collective-permute-start.44 = (bf16[3,4,24,3840]{3,2,1,0:T(8,128)(2,1)}, bf16[3,4,24,3840]{3,2,1,0:T(8,128)(2,1)}, u32[]{:S(2)}, u32[]{:S(2)}) collective-permute-start(bf16[3,4,24,3840]{3,2,1,0:T(8,128)(2,1)} %get-tuple-element.167), channel_id=1, source_target_pairs={{0,16},{16,0},{1,17},{17,1},{2,18},{18,2},{3,19},{19,3},{4,20},{20... | collective-permute-start | bytes 6635528 | tf_op jit(solution)/shard_map/ppermute | solution.py:24
  188.2 22.2 %collective-permute-start.49 = (bf16[96,768]{1,0:T(8,128)(2,1)S(1)}, bf16[96,768]{1,0:T(8,128)(2,1)S(1)}, u32[]{:S(2)}, u32[]{:S(2)}) collective-permute-start(bf16[96,768]{1,0:T(8,128)(2,1)S(1)} %get-tuple-element.287), channel_id=1, source_target_pairs={{0,12},{1,13},{2,14},{3,15},{4,8},{5,9},{6,10},{7,11},{8,4},{9,5},... | collective-permute-start | bytes 442376 | tf_op jit(solution)/shard_map/ppermute | solution.py:24
  188.3 22.1 %collective-permute-start.48 = (bf16[96,768]{1,0:T(8,128)(2,1)S(1)}, bf16[96,768]{1,0:T(8,128)(2,1)S(1)}, u32[]{:S(2)}, u32[]{:S(2)}) collective-permute-start(bf16[96,768]{1,0:T(8,128)(2,1)S(1)} %get-tuple-element.288), channel_id=1, source_target_pairs={{0,8},{1,9},{2,10},{3,11},{4,12},{5,13},{6,14},{7,15},{8,0},{9,1},... | collective-permute-start | bytes 442376 | tf_op jit(solution)/shard_map/ppermute | solution.py:24
  188.3 22.0 %collective-permute-start.47 = (bf16[96,768]{1,0:T(8,128)(2,1)S(1)}, bf16[96,768]{1,0:T(8,128)(2,1)S(1)}, u32[]{:S(2)}, u32[]{:S(2)}) collective-permute-start(bf16[96,768]{1,0:T(8,128)(2,1)S(1)} %get-tuple-element.289), channel_id=1, source_target_pairs={{0,4},{1,5},{2,6},{3,7},{4,0},{5,1},{6,2},{7,3},{8,12},{9,13},{10,... | collective-permute-start | bytes 442376 | tf_op jit(solution)/shard_map/ppermute | solution.py:24
  192.8 17.6 %collective-permute-start.46 = (bf16[2,24,3840]{2,1,0:T(8,128)(2,1)S(1)}, bf16[2,24,3840]{2,1,0:T(8,128)(2,1)S(1)}, u32[]{:S(2)}, u32[]{:S(2)}) collective-permute-start(bf16[2,24,3840]{2,1,0:T(8,128)(2,1)S(1)} %get-tuple-element.270), channel_id=1, source_target_pairs={{0,2},{1,3},{2,0},{3,1},{4,6},{5,7},{6,4},{7,5},{8,10},{9,11},{10,... | collective-permute-start | bytes 1105928 | tf_op jit(solution)/shard_map/ppermute | solution.py:24
  193.5 16.9 %collective-permute-start.45 = (bf16[2,24,3840]{2,1,0:T(8,128)(2,1)S(1)}, bf16[2,24,3840]{2,1,0:T(8,128)(2,1)S(1)}, u32[]{:S(2)}, u32[]{:S(2)}) collective-permute-start(bf16[2,24,3840]{2,1,0:T(8,128)(2,1)S(1)} %get-tuple-element.271), channel_id=1, source_target_pairs={{0,1},{1,0},{2,3},{3,2},{4,5},{5,4},{6,7},{7,6},{8,9},{9,8},{10,11... | collective-permute-start | bytes 1105928 | tf_op jit(solution)/shard_map/ppermute | solution.py:24
  212.8 31.3 %collective-permute-start.64 = (bf16[4,24,3840]{2,1,0:T(8,128)(2,1)}, bf16[4,24,3840]{2,1,0:T(8,128)(2,1)}, u32[]{:S(2)}, u32[]{:S(2)}) collective-permute-start(bf16[4,24,3840]{2,1,0:T(8,128)(2,1)} %pad_maximum_fusion), channel_id=1, source_target_pairs={{0,1},{1,0},{2,3},{3,2},{4,5},{5,4},{6,7},{7,6},{8,9},{9,8},{10,11... | collective-permute-start | bytes 2211848 | tf_op jit(solution)/shard_map/ppermute | solution.py:24
  214.5 29.6 %collective-permute-start.65 = (bf16[4,24,3840]{2,1,0:T(8,128)(2,1)}, bf16[4,24,3840]{2,1,0:T(8,128)(2,1)}, u32[]{:S(2)}, u32[]{:S(2)}) collective-permute-start(bf16[4,24,3840]{2,1,0:T(8,128)(2,1)} %pad_maximum_fusion.1), channel_id=1, source_target_pairs={{0,2},{1,3},{2,0},{3,1},{4,6},{5,7},{6,4},{7,5},{8,10},{9,11},{10,... | collective-permute-start | bytes 2211848 | tf_op jit(solution)/shard_map/ppermute | solution.py:24
  226.5 12.6 %collective-permute-start.52 = (bf16[3,4,24,2304]{3,2,1,0:T(8,128)(2,1)}, bf16[3,4,24,2304]{3,2,1,0:T(8,128)(2,1)S(1)}, u32[]{:S(2)}, u32[]{:S(2)}) collective-permute-start(bf16[3,4,24,2304]{3,2,1,0:T(8,128)(2,1)} %get-tuple-element.188), channel_id=1, source_target_pairs={{0,16},{16,0},{1,17},{17,1},{2,18},{18,2},{3,19},{19,3},{4,20},{20... | collective-permute-start | bytes 3981320 | tf_op jit(solution)/shard_map/ppermute | solution.py:24
  227.4 11.1 %collective-permute-start.54 = (bf16[2,24,2304]{2,1,0:T(8,128)(2,1)}, bf16[2,24,2304]{2,1,0:T(8,128)(2,1)}, u32[]{:S(2)}, u32[]{:S(2)}) collective-permute-start(bf16[2,24,2304]{2,1,0:T(8,128)(2,1)} %get-tuple-element.278), channel_id=1, source_target_pairs={{0,2},{1,3},{2,0},{3,1},{4,6},{5,7},{6,4},{7,5},{8,10},{9,11},{10,... | collective-permute-start | bytes 663560 | tf_op jit(solution)/shard_map/ppermute | solution.py:24
  227.7 11.4 %collective-permute-start.53 = (bf16[2,24,2304]{2,1,0:T(8,128)(2,1)}, bf16[2,24,2304]{2,1,0:T(8,128)(2,1)}, u32[]{:S(2)}, u32[]{:S(2)}) collective-permute-start(bf16[2,24,2304]{2,1,0:T(8,128)(2,1)} %get-tuple-element.279), channel_id=1, source_target_pairs={{0,1},{1,0},{2,3},{3,2},{4,5},{5,4},{6,7},{7,6},{8,9},{9,8},{10,11... | collective-permute-start | bytes 663560 | tf_op jit(solution)/shard_map/ppermute | solution.py:24
  240.5 26.2 %collective-permute-start.56 = (bf16[4,24,2304]{2,1,0:T(8,128)(2,1)S(1)}, bf16[4,24,2304]{2,1,0:T(8,128)(2,1)S(1)}, u32[]{:S(2)}, u32[]{:S(2)}) collective-permute-start(bf16[4,24,2304]{2,1,0:T(8,128)(2,1)S(1)} %pad_maximum_fusion.11), channel_id=1, source_target_pairs={{0,2},{1,3},{2,0},{3,1},{4,6},{5,7},{6,4},{7,5},{8,10},{9,11},{10,... | collective-permute-start | bytes 1327112 | tf_op jit(solution)/shard_map/ppermute | solution.py:24
  243.8 22.9 %collective-permute-start.55 = (bf16[4,24,2304]{2,1,0:T(8,128)(2,1)S(1)}, bf16[4,24,2304]{2,1,0:T(8,128)(2,1)S(1)}, u32[]{:S(2)}, u32[]{:S(2)}) collective-permute-start(bf16[4,24,2304]{2,1,0:T(8,128)(2,1)S(1)} %pad_maximum_fusion.10), channel_id=1, source_target_pairs={{0,1},{1,0},{2,3},{3,2},{4,5},{5,4},{6,7},{7,6},{8,9},{9,8},{10,11... | collective-permute-start | bytes 1327112 | tf_op jit(solution)/shard_map/ppermute | solution.py:24
  246.2 20.4 %collective-permute-start.61 = (f32[16,3072]{1,0:T(8,128)S(1)}, f32[16,3072]{1,0:T(8,128)S(1)}, u32[]{:S(2)}, u32[]{:S(2)}) collective-permute-start(f32[16,3072]{1,0:T(8,128)S(1)} %add.341), channel_id=1, source_target_pairs={{0,8},{1,9},{2,10},{3,11},{4,12},{5,13},{6,14},{7,15},{8,0},{9,1},... | collective-permute-start | bytes 589832 | tf_op jit(solution)/shard_map/ppermute | solution.py:24
  248.3 19.1 %collective-permute-start.66 = (bf16[24,3840]{1,0:T(8,128)(2,1)S(1)}, bf16[24,3840]{1,0:T(8,128)(2,1)S(1)}, u32[]{:S(2)}, u32[]{:S(2)}) collective-permute-start(bf16[24,3840]{1,0:T(8,128)(2,1)S(1)} %get-tuple-element.280), channel_id=1, source_target_pairs={{0,4},{1,5},{2,6},{3,7},{4,0},{5,1},{6,2},{7,3},{8,12},{9,13},{10,... | collective-permute-start | bytes 552968 | tf_op jit(solution)/shard_map/ppermute | solution.py:24
  249.2 22.2 %collective-permute-start.68 = (bf16[24,3840]{1,0:T(8,128)(2,1)S(1)}, bf16[24,3840]{1,0:T(8,128)(2,1)S(1)}, u32[]{:S(2)}, u32[]{:S(2)}) collective-permute-start(bf16[24,3840]{1,0:T(8,128)(2,1)S(1)} %get-tuple-element.281), channel_id=1, source_target_pairs={{0,12},{1,13},{2,14},{3,15},{4,8},{5,9},{6,10},{7,11},{8,4},{9,5},... | collective-permute-start | bytes 552968 | tf_op jit(solution)/shard_map/ppermute | solution.py:24
  266.6 13.3 %collective-permute-start.67 = (bf16[24,3840]{1,0:T(8,128)(2,1)S(1)}, bf16[24,3840]{1,0:T(8,128)(2,1)S(1)}, u32[]{:S(2)}, u32[]{:S(2)}) collective-permute-start(bf16[24,3840]{1,0:T(8,128)(2,1)S(1)} %get-tuple-element.282), channel_id=1, source_target_pairs={{0,8},{1,9},{2,10},{3,11},{4,12},{5,13},{6,14},{7,15},{8,0},{9,1},... | collective-permute-start | bytes 552968 | tf_op jit(solution)/shard_map/ppermute | solution.py:24
  266.7 14.7 %collective-permute-start.62 = (f32[16,3072]{1,0:T(8,128)S(1)}, f32[16,3072]{1,0:T(8,128)S(1)}, u32[]{:S(2)}, u32[]{:S(2)}) collective-permute-start(f32[16,3072]{1,0:T(8,128)S(1)} %add.342), channel_id=1, source_target_pairs={{0,1},{1,0},{2,3},{3,2},{4,5},{5,4},{6,7},{7,6},{8,9},{9,8},{10,11... | collective-permute-start | bytes 589832 | tf_op jit(solution)/shard_map/ppermute | solution.py:24
  267.0 14.5 %collective-permute-start.57 = (bf16[24,2304]{1,0:T(8,128)(2,1)S(1)}, bf16[24,2304]{1,0:T(8,128)(2,1)S(1)}, u32[]{:S(2)}, u32[]{:S(2)}) collective-permute-start(bf16[24,2304]{1,0:T(8,128)(2,1)S(1)} %get-tuple-element.298), channel_id=1, source_target_pairs={{0,4},{1,5},{2,6},{3,7},{4,0},{5,1},{6,2},{7,3},{8,12},{9,13},{10,... | collective-permute-start | bytes 331784 | tf_op jit(solution)/shard_map/ppermute | solution.py:24
  267.4 14.0 %collective-permute-start.59 = (bf16[24,2304]{1,0:T(8,128)(2,1)S(1)}, bf16[24,2304]{1,0:T(8,128)(2,1)S(1)}, u32[]{:S(2)}, u32[]{:S(2)}) collective-permute-start(bf16[24,2304]{1,0:T(8,128)(2,1)S(1)} %get-tuple-element.299), channel_id=1, source_target_pairs={{0,12},{1,13},{2,14},{3,15},{4,8},{5,9},{6,10},{7,11},{8,4},{9,5},... | collective-permute-start | bytes 331784 | tf_op jit(solution)/shard_map/ppermute | solution.py:24
  271.5 12.5 %collective-permute-start.58 = (bf16[24,2304]{1,0:T(8,128)(2,1)S(1)}, bf16[24,2304]{1,0:T(8,128)(2,1)S(1)}, u32[]{:S(2)}, u32[]{:S(2)}) collective-permute-start(bf16[24,2304]{1,0:T(8,128)(2,1)S(1)} %get-tuple-element.300), channel_id=1, source_target_pairs={{0,8},{1,9},{2,10},{3,11},{4,12},{5,13},{6,14},{7,15},{8,0},{9,1},... | collective-permute-start | bytes 331784 | tf_op jit(solution)/shard_map/ppermute | solution.py:24
  (56 other events, 358.0 us)

commit v3 on v2

--- a/solution.py
+++ b/solution.py
@@ -105,11 +105,11 @@
     def sides(self):
         if self.side is None:
             half = FAR // 2
-            first, second = slice(0, half), slice(half, FAR)
-            for_one, for_two = self.corners()
-            one = [self.both(1, first).astype(b16), (self.both(1, second) + for_two.astype(f32)).astype(b16)]
-            two = [(self.both(2, first) + for_one.astype(f32)).astype(b16), self.both(2, second).astype(b16)]
-            self.sent = jnp.concatenate(one, 0), jnp.concatenate(two, 0)
+            for_one, for_two = (x.astype(f32) for x in self.corners())
+            none = ((0, 0), (0, 0))
+            one = self.both(1) + jnp.pad(for_two, ((half, 0), *none))
+            two = self.both(2) + jnp.pad(for_one, ((0, half), *none))
+            self.sent = one.astype(b16), two.astype(b16)
             self.side = swap(self.sent[0], "dp", 1), swap(self.sent[1], "dp", 2)
         return self.side
 
@@ -117,7 +117,7 @@
         if self.far is None:
             low = lax.axis_size("dp") // FAR
             one, two = self.sides()
-            self.own = self.both(0) + one.astype(f32) + two.astype(f32)
+            self.own = [self.both(0, j) + one[j].astype(f32) + two[j].astype(f32) for j in range(FAR)]
             self.far = [swap(self.own[j].astype(b16), "dp", j * low) for j in range(1, FAR)]
         return self.far
 
@@ -148,7 +148,7 @@
     return x + swap(x, axis, k)
 
 
-TILE = 192
+TILE = 256
 PACK = 16
 PAIR = 2 * HEAD_DIM
 GROUP = 3
@@ -235,9 +235,8 @@
             at += rows
         return at
 
-    at = put(wout, first, put(wqkv, first, 0))
-    first[at:, :] = packed[...]
-    put(wup, second, 0)
+    first[put(wqkv, first, 0) :, :] = packed[...]
+    put(wup, second, put(wout, second, 0))
     put(wdown, third, 0)
 
 
@@ -289,18 +288,18 @@
     return block.reshape(block.shape[0] * block.shape[1], block.shape[2])
 
 
-def attend_kernel(n_pieces, lens, offs, tiles, place, x_ref, vec, *refs):
+def attend_kernel(n_pieces, lens, offs, tiles, place, homes, x_ref, y_ref, vec, *refs):
     pieces, refs = refs[:n_pieces], refs[n_pieces:]
     if n_pieces:
-        sinks, refs = refs[:8], refs[8:]
-        wqkv, wout, xs, qkv, probs, ctx, n1, inv1, got, sent = refs
-        copies = fetch(place, pieces, ((wqkv, wqkv.shape[1] // 4), (wout, wout.shape[1] // 4)), got)
+        sinks, refs = refs[:5], refs[5:]
+        wqkv, xs, qkv, probs, ctx, got, sent = refs
+        copies = fetch(place, pieces, ((wqkv, wqkv.shape[1] // 4),), got)
     else:
-        wqkv, wout = refs[:2]
-        sinks, refs = refs[2:8], refs[8:]
-        xs, qkv, probs, ctx, n1, inv1, sent = refs
+        wqkv = refs[0]
+        sinks, refs = refs[1:5], refs[5:]
+        xs, qkv, probs, ctx, sent = refs
         copies = []
-    held = (wqkv, wout, xs, qkv, probs, ctx, n1, inv1)[8 - len(sinks) :]
+    held = (wqkv, xs, qkv, probs, ctx)[5 - len(sinks) :]
     count, seq, width = x_ref.shape
     leaving = []
 
@@ -316,17 +315,21 @@
     ctx[...] = jnp.zeros_like(ctx)
 
     def pack(b, _):
-        def block(i, _):
-            at = pl.multiple_of(offs[b] + i * PACK, PACK)
-            xs[pl.ds(at, PACK), :] = x_ref[b, pl.ds(pl.multiple_of(i * PACK, PACK), PACK), :]
-            return 0
-
-        return lax.fori_loop(0, (lens[b] + PACK - 1) // PACK, block, 0)
+        blocks = (lens[b] + PACK - 1) // PACK
+        for side, source in enumerate((x_ref, y_ref)):
+
+            def block(i, _):
+                at = pl.multiple_of(offs[b] + i * PACK, PACK)
+                xs[pl.ds(at, PACK), :] = source[homes[count + b], pl.ds(pl.multiple_of(i * PACK, PACK), PACK), :]
+                return 0
+
+            lax.fori_loop(0, jnp.where(homes[b] == side, blocks, 0), block, 0)
+        return 0
 
     lax.fori_loop(0, count, pack, 0)
     for copy in copies:
         copy.wait()
-    leave(wqkv, wout, xs)
+    leave(wqkv, xs)
 
     def project(t, _):
         x = xs[tile_at(t), :]
@@ -369,16 +372,6 @@
     by_length(lens, count, seq, attend)
     leave(probs, ctx)
 
-    def out(t, _):
-        rows = tile_at(t)
-        attended = dot(ctx[rows, :], flat_of(wout)) + row_of(vec, O_BIAS)
-        normal, inverse = norm_rows(xs[rows, :].astype(f32) + attended)
-        n1[rows, :] = normal
-        inv1[rows, :] = jnp.broadcast_to(inverse, (TILE, 128))
-        return 0
-
-    lax.fori_loop(0, tiles[0], out, 0)
-    leave(n1, inv1)
     for copy in leaving:
         copy.wait()
 
@@ -388,37 +381,42 @@
     return (row >= offs[b]) & (row < offs[b] + lens[b])
 
 
-def take_weight(step, tiles, place, pieces, refs, rows_of):
+def take_weights(step, place, pieces, refs, count, rows):
     if not pieces:
-        return refs[0], refs[1:], lambda: None
-    sink, refs = refs[0], refs[1:]
-    weight, got, sent, refs = refs[-3], refs[-2], refs[-1], refs[:-3]
-    leave = pltpu.make_async_copy(weight, sink, sent.at[0])
+        return refs[:count], refs[count:], lambda: None
+    sinks, refs = refs[:count], refs[count:]
+    held, got, sent, refs = refs[-count - 2 : -2], refs[-2], refs[-1], refs[: -count - 2]
+    leave = [pltpu.make_async_copy(a, b, sent.at[i]) for i, (a, b) in enumerate(zip(held, sinks))]
 
     @pl.when(step == 0)
     def _():
-        for copy in fetch(place, pieces, ((weight, rows_of),), got):
+        for copy in fetch(place, pieces, [(weight, rows) for weight in held], got):
             copy.wait()
-        leave.start()
+        for copy in leave:
+            copy.start()
 
     def finish():
         @pl.when(step == pl.num_programs(0) - 1)
         def _():
-            leave.wait()
-
-    return weight, refs, finish
-
-
-def up_kernel(n_pieces, lens, offs, tiles, place, n1, vec, ups, *refs):
+            for copy in leave:
+                copy.wait()
+
+    return held, refs, finish
+
+
+def up_kernel(n_pieces, rows, lens, offs, tiles, place, ctx, xs, vec, ups, *refs):
     t = pl.program_id(0)
     pieces, refs = refs[:n_pieces], refs[n_pieces:]
-    rows_of = pieces[0].shape[1] * CHUNK * 2 // (ups.shape[0] * ups.shape[1]) if n_pieces else 0
-    wup, (act, slope), finish = take_weight(t, tiles, place, pieces, refs, rows_of)
+    (wout, wup), (act, slope, n1, inv1), finish = take_weights(t, place, pieces, refs, 2, rows)
     width = n1.shape[1]
 
     @pl.when(t < tiles[0])
     def _():
-        low = (n1[...] * row_of(vec, GAIN_1) + row_of(vec, SHIFT_1)).astype(b16)
+        attended = dot(ctx[...], flat_of(wout)) + row_of(vec, O_BIAS)
+        normal, inverse = norm_rows(xs[...].astype(f32) + attended)
+        n1[...] = normal
+        inv1[...] = jnp.broadcast_to(inverse, (TILE, 128))
+        low = (normal * row_of(vec, GAIN_1) + row_of(vec, SHIFT_1)).astype(b16)
         for c in range(ups.shape[0]):
             cols = slice(c * width, (c + 1) * width)
             pre = dot(low, flat_of(wup, cols)) + row_of(ups, c)
@@ -429,11 +427,10 @@
     finish()
 
 
-def down_kernel(n_pieces, lens, offs, tiles, place, n1, act, vec, *refs):
+def down_kernel(n_pieces, rows, lens, offs, tiles, place, n1, act, vec, *refs):
     t = pl.program_id(0)
     pieces, refs = refs[:n_pieces], refs[n_pieces:]
-    rows_of = pieces[0].shape[1] if n_pieces else 0
-    wdown, (n2, inv2, pooled), finish = take_weight(t, tiles, place, pieces, refs, rows_of)
+    (wdown,), (n2, inv2, pooled), finish = take_weights(t, place, pieces, refs, 1, rows)
     width = n1.shape[1]
     count = pooled.shape[0]
 
@@ -470,20 +467,24 @@
         acc[:, cols] += dot_tn(left, right)
 
 
-def pair_head(lens, place, labels, bias, pooled, partner, head, tops):
+def pair_head(lens, place, homes, labels, bias, pooled, partner, head, tops, own, ends):
     count, width = pooled.shape
-    mine, other = pooled[...], partner[...]
-    first = place[0] == 0
-    left, right = jnp.where(first, mine, other), jnp.where(first, other, mine)
+
+    for side in range(2):
+        for i in range(count):
+            at = side * count + i
+            away, slot = homes[2 * count + at], homes[4 * count + at]
+            row = jnp.where(away == 0, pooled[pl.ds(slot, 1), :], partner[pl.ds(slot, 1), :])
+            ends[side, i : i + 1, :] = row
+    left, right = ends[0], ends[1]
+    own[...] = jnp.where(place[0] == 0, left, right)
     gap = left - right
     soft = jnp.sqrt(gap * gap + gap_soft)
     feats = (left, right, soft)
     row = lax.broadcasted_iota(jnp.int32, (count, 1), 0)
     label = jnp.zeros((count, 1), jnp.int32)
-    size = jnp.zeros((count, 1), jnp.int32)
     for b in range(count):
         label = jnp.where(row == b, labels[b], label)
-        size = jnp.where(row == b, lens[b], size)
     logits = []
     for c in range(NCLASS):
         terms = [
@@ -504,27 +505,32 @@
     for c in range(NCLASS):
         tops[NCLASS + c : NCLASS + c + 1, 0:128] = jnp.broadcast_to(0.5 * jnp.sum(grads[c], axis=0, keepdims=True), (1, 128))
     slope = gap / soft
-    pooled_grad = jnp.where(first, back[0] + slope * back[2], back[1] - slope * back[2])
-    return pooled_grad / size.astype(f32)
+    ends[0] = back[0] + slope * back[2]
+    ends[1] = back[1] - slope * back[2]
+    for b in range(count):
+        side = jnp.where(homes[b] == 0, place[0], 1 - place[0])
+        row = ends[side, pl.ds(homes[count + b], 1), :]
+        size = jnp.full((1, width), lens[b], jnp.int32).astype(f32)
+        ends[2, b : b + 1, :] = row / size
 
 
 def down_back_kernel(
-    lens, offs, tiles, place, labels, bias, pooled, partner, head, act, n2, inv2, vec, sum_grad, *refs
+    lens, offs, tiles, place, homes, labels, bias, pooled, partner, head, act, n2, inv2, vec, sum_grad, *refs
 ):
-    *outs, sums, tops, acc, per_row = refs
+    *outs, sums, tops, own, acc, ends = refs
     t = pl.program_id(0)
     count, width = pooled.shape
 
     @pl.when(t == 0)
     def _():
-        per_row[...] = pair_head(lens, place, labels, bias, pooled, partner, head, tops)
+        pair_head(lens, place, homes, labels, bias, pooled, partner, head, tops, own, ends)
         sums[...] = jnp.zeros_like(sums)
 
     @pl.when(t < tiles[0])
     def _():
         up = jnp.zeros((TILE, width), f32)
         for b in range(count):
-            up = jnp.where(inside(offs, lens, b, t), per_row[b : b + 1, :], up)
+            up = jnp.where(inside(offs, lens, b, t), ends[2, b : b + 1, :], up)
         normal = n2[...]
         grad = norm_back(up, normal, inv2[:, 0:1], row_of(vec, GAIN_2))
         sum_grad[...] = grad
@@ -538,6 +544,20 @@
     @pl.when(t == pl.num_programs(0) - 1)
     def _():
         deal(place, acc, outs)
+
+
+def early(t, copies):
+    @pl.when(t == 0)
+    def _():
+        for copy in copies:
+            copy.start()
+
+    def ready(i):
+        @pl.when(t == 0)
+        def _():
+            copies[i].wait()
+
+    return ready
 
 
 def pre_back_kernel(lens, offs, tiles, place, sum_grad, slope, wdown, pre_low, sums):
@@ -595,18 +615,32 @@
 def attend_back_kernel(lens, offs, tiles, place, qkv_h, probs_h, ctx_grad_h, grad, sums, qkv, probs, ctx_grad, sems):
     width = ctx_grad.shape[1]
     count, seq = probs.shape[0], probs.shape[2]
-    pairs = ((qkv_h, qkv), (probs_h, probs), (ctx_grad_h, ctx_grad))
-    copies = [pltpu.make_async_copy(a, b, sems.at[i]) for i, (a, b) in enumerate(pairs)]
-    for copy in copies:
-        copy.start()
+    blocks = qkv.shape[0] // seq
+
+    def rows_in_use(do):
+        for i in range(blocks):
+
+            @pl.when(i * seq < tiles[0] * TILE + seq)
+            def _():
+                at = pl.ds(i * seq, seq)
+                do(pltpu.make_async_copy(qkv_h.at[at], qkv.at[at], sems.at[i]))
+                do(pltpu.make_async_copy(ctx_grad_h.at[at], ctx_grad.at[at], sems.at[blocks + i]))
+
+    def probs_of(b, size):
+        at = pl.ds(0, HEADS * size)
+        return pltpu.make_async_copy(probs_h.at[b, at], probs.at[b, at], sems.at[2 * blocks + b])
+
+    rows_in_use(lambda copy: copy.start())
+    by_length(lens, count, seq, lambda b, size: probs_of(b, size).start())
     grad[...] = jnp.zeros_like(grad)
     sums[...] = jnp.zeros_like(sums)
-    for copy in copies:
-        copy.wait()
+    rows_in_use(lambda copy: copy.wait())
 
     def attend(b, size):
         rows, key_rows = sentence_rows(offs, b, seq), sentence_rows(offs, b, size)
         real = lax.broadcasted_iota(jnp.int32, (seq, 1), 0) < lens[b]
+        probs_of(b, size).wait()
+
         def spread(x):
             return jnp.broadcast_to(jnp.sum(x, axis=0, keepdims=True), x.shape)
 
@@ -640,58 +674,71 @@
 
     lax.fori_loop(0, tiles[0], total, 0)
 
-def qkv_back_kernel(lens, offs, tiles, place, xs, grad, *refs):
-    *outs, acc = refs
-    t = pl.program_id(0)
-
-    @pl.when(t < tiles[0])
-    def _():
-        accumulate(t, acc, slice(None), xs[...], grad[...])
-
-    @pl.when(t == pl.num_programs(0) - 1)
-    def _():
-        deal(place, acc, outs)
-
-
-def input_kernel(lens, offs, tiles, place, grad, mid, wqkv, gx, buf):
+def input_kernel(lens, offs, tiles, place, homes, grad, mid, xs, biases, wqkv_h, gx, gy, *refs):
+    *outs, buf, acc, tail, wqkv, sems = refs
     count, seq, width = gx.shape
     t = pl.program_id(0)
+    ready = early(t, [pltpu.make_async_copy(wqkv_h, wqkv, sems.at[0])])
 
     @pl.when(t == 0)
     def _():
         gx[...] = jnp.zeros_like(gx)
+        gy[...] = jnp.zeros_like(gy)
 
     @pl.when(t < tiles[0])
     def _():
+        accumulate(t, acc, slice(None), xs[...], grad[...])
+        ready(0)
         buf[tile_at(t), :] = dot_nt(grad[...], flat_of(wqkv)) + mid[...]
 
     @pl.when(t == pl.num_programs(0) - 1)
     def _():
         def unpack(b, _):
-            def block(i, _):
-                at = pl.multiple_of(offs[b] + i * PACK, PACK)
-                gx[b, pl.ds(pl.multiple_of(i * PACK, PACK), PACK), :] = buf[pl.ds(at, PACK), :]
-                return 0
-
-            return lax.fori_loop(0, (lens[b] + PACK - 1) // PACK, block, 0)
+            blocks = (lens[b] + PACK - 1) // PACK
+            for side, target in enumerate((gx, gy)):
+
+                def block(i, _):
+                    at = pl.multiple_of(offs[b] + i * PACK, PACK)
+                    rows = pl.ds(pl.multiple_of(i * PACK, PACK), PACK)
+                    target[homes[count + b], rows, :] = buf[pl.ds(at, PACK), :].astype(target.dtype)
+                    return 0
+
+                lax.fori_loop(0, jnp.where(homes[b] == side, blocks, 0), block, 0)
+            return 0
 
         lax.fori_loop(0, count, unpack, 0)
-
-
-def small_kernel(spot, sums, *outs):
-    width = sums.shape[1] // 4
+        deal(place, acc, outs)
+        if len(outs) > 1:
+            cols, lanes = acc.shape[1], tail.shape[1]
+            each = biases.shape[1] // lanes
+            tail[...] = jnp.zeros_like(tail)
+            for r in range(2 * each):
+                tail[r : r + 1, :] = biases[r // each : r // each + 1, r % each * lanes : (r % each + 1) * lanes]
+            block = tail[...].astype(b16)
+            mine, first, rest = outs
+            for target in [mine.at[k] for k in range(4)] + [first] + [rest.at[k] for k in range(3)]:
+                for spot in range(FAR):
+                    target[spot, :, cols : cols + lanes] = block
+
+
+def small_kernel(spot, sums, tail, *outs):
+    width = sums.shape[1] // 3
     *plain, ups, head, classes = outs
     mine = plain[0].shape[1]
 
     def share(x, size):
+        x = jnp.broadcast_to(x, (8, x.shape[1])) if x.shape[0] == 1 else x
         return pltpu.roll(x, lax.rem(x.shape[1] - spot[0] * size, x.shape[1]), axis=1)[:, 0:size]
 
-    blocks = [share(sums[0:8, p * width : (p + 1) * width], mine) for p in (0, 2, 3)]
-    for out, (block, row) in zip(plain, ((2, 0), (2, 1), (1, 2), (1, 0), (1, 1), (0, 2), (0, 0), (0, 1))):
+    count = width // tail.shape[1]
+    for p in range(2):
+        row = jnp.concatenate([tail[p * count + r : p * count + r + 1, :] for r in range(count)], 1)
+        plain[p][...] = share(row, mine)[0:1]
+    blocks = [share(sums[0:8, p * width : (p + 1) * width], mine) for p in (0, 2)]
+    for out, (block, row) in zip(plain[2:], ((1, 2), (1, 0), (1, 1), (0, 2), (0, 0), (0, 1))):
         out[...] = blocks[block][row : row + 1]
-    flat = jnp.concatenate([sums[r : r + 1, width : 2 * width] for r in range(4)], 1)
-    ups[...] = share(jnp.broadcast_to(flat, (8, 4 * width)), 4 * mine)[0:1]
-    head[...] = jnp.transpose(share(sums[8:16, 0 : 3 * width], 3 * mine))[:, 0:NCLASS]
+    ups[...] = share(jnp.concatenate([sums[r : r + 1, width : 2 * width] for r in range(4)], 1), 4 * mine)[0:1]
+    head[...] = share(sums[8:16, :], 3 * mine)[0:NCLASS]
     classes[...] = jnp.transpose(sums[8:16, 0:128])[0:1, NCLASS : 2 * NCLASS]
 
 
@@ -770,7 +817,23 @@
     shard_rows = qkv_weight.shape[0]
     quick = low == 4 and shard_rows % PACK == 0
 
-    sent_len = lengths[0]
+    other_len = swap(lengths[0].astype(f32), "tower", 1).astype(jnp.int32)
+    first_here = tower == 0
+    all_len = jnp.where(
+        first_here, jnp.concatenate([lengths[0], other_len]), jnp.concatenate([other_len, lengths[0]])
+    )
+    ids = jnp.arange(2 * count)
+    ahead = (all_len[None, :] > all_len[:, None]) | (
+        (all_len[None, :] == all_len[:, None]) & (ids[None, :] < ids[:, None])
+    )
+    rank = jnp.sum(ahead.astype(jnp.int32), axis=1)
+    away = (((rank + 1) // 2) % 2 != tower).astype(jnp.int32)
+    picked = (away[None, :] == 0) & (rank[None, :] // 2 == jnp.arange(count)[:, None])
+    source = jnp.sum(jnp.where(picked, ids[None, :], 0), axis=1)
+    sent_len = jnp.sum(jnp.where(picked, all_len[None, :], 0), axis=1)
+    homes = jnp.concatenate([(source // count != tower).astype(jnp.int32), source % count, away, rank // 2])
+    homes = homes.astype(jnp.int32)
+
     taken = (sent_len + PACK - 1) // PACK * PACK
     before = jnp.arange(count)[None, :] < jnp.arange(count)[:, None]
     offs = jnp.sum(jnp.where(before, taken[None, :], 0), axis=1)
@@ -789,15 +852,17 @@
         first_part, up_part, down_part = call(
             parts_kernel, (place,), (*weights, packed),
             (
-                shape(b16, sizes[0] + sizes[1] + packed.shape[0], CHUNK), shape(b16, sizes[2], CHUNK),
+                shape(b16, sizes[0] + packed.shape[0], CHUNK), shape(b16, sizes[1] + sizes[2], CHUNK),
                 shape(b16, sizes[3], CHUNK),
             ),
         )
     else:
-        first_part = jnp.concatenate([to_chunks(qkv_weight), to_chunks(out_weight), packed], 0)
-        up_part, down_part = to_chunks(up_weight), to_chunks(down_weight)
+        first_part = jnp.concatenate([to_chunks(qkv_weight), packed], 0)
+        up_part, down_part = jnp.concatenate([to_chunks(out_weight), to_chunks(up_weight)], 0), to_chunks(down_weight)
     cut = first_part.shape[0] - packed.shape[0]
     low_far = far_pieces(first_part)
+    other_tokens = swap(embeddings[0], "tower", 1)
+    low_far = after(low_far, other_tokens, homes)
     block_first = in_order(low_far, far, 0)
     far_up = far_pieces(after(up_part, *low_far))
     full = [(FAR, w.shape[0] * low, w.shape[1]) for w in weights]
@@ -813,10 +878,7 @@
         block_up = in_order(far_up, far, 0)
         far_down = far_pieces(down_part)
         whole_first = gather_any(block_first)
-        n_qkv = qkv_weight.shape[1] // 2 // CHUNK * shard_rows
-        pieces_first = [
-            from_chunks(whole_first[:, :, :n_qkv], shard_rows), from_chunks(whole_first[:, :, n_qkv:cut], shard_rows)
-        ]
+        pieces_first = [from_chunks(whole_first[:, :, :cut], shard_rows)]
         packs = whole_first[:, :, cut:]
     packs = packs.reshape(groups, -1).astype(f32)
     cuts = [8 * shard_rows, 8 * shard_rows + up_bias.shape[0]]
@@ -829,49 +891,56 @@
     dense = 2 * rows * width
     sinks = [
         Flat(shape(b16, ext, width)), Flat(shape(b16, ext, 3 * width)),
-        Flat(shape(b16, count, HEADS * seq_len, seq_len)), Flat(shape(b16, ext, width)), Flat(shape(f32, rows, width)),
-        Flat(shape(f32, rows, 128)),
+        Flat(shape(b16, count, HEADS * seq_len, seq_len)), Flat(shape(b16, ext, width)),
     ]
-    both = [Flat(shape(b16, *full[0])), Flat(shape(b16, *full[1]))]
     if quick:
+        both = [Flat(shape(b16, *full[0]))] + sinks
         pieces_first = after(pieces_first, block_up)
-        proj_qkv, proj_out, xs, qkv, probs, ctx, n1, inv1 = call(
-            partial(attend_kernel, 10), meta, (embeddings[0], vec, *map(Flat, pieces_first)), both + sinks,
-            [pltpu.VMEM(o.array.shape, o.array.dtype) for o in both + sinks]
-            + [pltpu.SemaphoreType.DMA((40,)), pltpu.SemaphoreType.DMA((8,))],
-            micros=20,
+        proj_qkv, xs, qkv, probs, ctx = call(
+            partial(attend_kernel, 10), meta,
+            (Scalars(homes), embeddings[0], other_tokens, vec, *map(Flat, pieces_first)), both,
+            [pltpu.VMEM(o.array.shape, o.array.dtype) for o in both]
+            + [pltpu.SemaphoreType.DMA((30,)), pltpu.SemaphoreType.DMA((5,))],
+            micros=16,
         )
     else:
-        proj_qkv, proj_out = pieces_first
-        xs, qkv, probs, ctx, n1, inv1 = call(
-            partial(attend_kernel, 0), meta, (embeddings[0], vec, proj_qkv, proj_out), sinks,
-            [pltpu.VMEM(o.array.shape, o.array.dtype) for o in sinks] + [pltpu.SemaphoreType.DMA((8,))],
-            micros=20,
+        (proj_qkv,) = pieces_first
+        xs, qkv, probs, ctx = call(
+            partial(attend_kernel, 0), meta, (Scalars(homes), embeddings[0], other_tokens, vec, proj_qkv), sinks,
+            [pltpu.VMEM(o.array.shape, o.array.dtype) for o in sinks] + [pltpu.SemaphoreType.DMA((5,))],
+            micros=16,
         )
 
-    wide, slim = shape(b16, rows, hidden), shape(f32, rows, width)
+    wide, slim, thin = shape(b16, rows, hidden), shape(f32, rows, width), shape(f32, rows, 128)
+    outs = [Tiled(wide), Tiled(wide), Tiled(slim), Tiled(thin)]
+    args = Tiled(ctx), Tiled(xs), vec, ups
     if quick:
-        near_up = gather_near(block_up, n1)
+        near_up = gather_near(block_up, ctx)
+        block_down = in_order(after(far_down, ctx), far, 0)
         pieces_up = near_up + [swap(p, "tower", 1) for p in near_up]
-        proj_up, act, slope = call(
-            partial(up_kernel, 10), meta, (Tiled(n1), vec, ups, *map(Flat, pieces_up)),
-            [Flat(shape(b16, *full[2])), Tiled(wide), Tiled(wide)],
-            [pltpu.VMEM(full[2], b16), pltpu.SemaphoreType.DMA((40,)), pltpu.SemaphoreType.DMA((1,))],
-            steps=steps, micros=12,
+        proj_out, proj_up, act, slope, n1, inv1 = call(
+            partial(up_kernel, 10, shard_rows), meta, (*args, *map(Flat, pieces_up)),
+            [Flat(shape(b16, *full[1])), Flat(shape(b16, *full[2]))] + outs,
+            [
+                pltpu.VMEM(full[1], b16), pltpu.VMEM(full[2], b16), pltpu.SemaphoreType.DMA((50,)),
+                pltpu.SemaphoreType.DMA((2,)),
+            ],
+            steps=steps, micros=14,
         )
     else:
-        proj_up = from_chunks(gather_any(block_up), shard_rows)
-        act, slope = call(
-            partial(up_kernel, 0), meta, (Tiled(n1), vec, ups, proj_up), [Tiled(wide), Tiled(wide)], steps=steps,
-            micros=12,
+        whole_up = gather_any(block_up)
+        cut = out_weight.size // 2 // CHUNK
+        proj_out = from_chunks(whole_up[:, :, :cut], shard_rows)
+        proj_up = from_chunks(whole_up[:, :, cut:], shard_rows)
+        act, slope, n1, inv1 = call(
+            partial(up_kernel, 0, 0), meta, (*args, proj_out, proj_up), outs, steps=steps, micros=14,
         )
-    outs = [Tiled(slim), Tiled(shape(f32, rows, 128)), shape(f32, count, width)]
+    outs = [Tiled(slim), Tiled(thin), shape(f32, count, width)]
     if quick:
-        block_down = in_order(after(far_down, n1), far, 0)
         near_down = gather_near(block_down, act)
         pieces_down = near_down + [swap(p, "tower", 1) for p in near_down]
         proj_down, n2, inv2, pooled = call(
-            partial(down_kernel, 10), meta, (Tiled(n1), Tiled(act), vec, *map(Flat, pieces_down)),
+            partial(down_kernel, 10, down_weight.shape[0]), meta, (Tiled(n1), Tiled(act), vec, *map(Flat, pieces_down)),
             [Flat(shape(b16, *full[3]))] + outs,
             [pltpu.VMEM(full[3], b16), pltpu.SemaphoreType.DMA((10,)), pltpu.SemaphoreType.DMA((1,))],
             steps=steps, micros=10,
@@ -879,7 +948,7 @@
     else:
         proj_down = from_chunks(gather_any(in_order(far_down, far, 0)), down_weight.shape[0])
         n2, inv2, pooled = call(
-            partial(down_kernel, 0), meta, (Tiled(n1), Tiled(act), vec, proj_down), outs, steps=steps, micros=10,
+            partial(down_kernel, 0, 0), meta, (Tiled(n1), Tiled(act), vec, proj_down), outs, steps=steps, micros=10,
         )
 
     def dealt(full_rows, cols):
@@ -890,14 +959,14 @@
 
     partner = swap(pooled, "tower", 1)
     sums_of = shape(f32, 8, width)
-    sum_grad, *down_parts, sums_two, tops = call(
+    sum_grad, *down_parts, sums_two, tops, own_pooled = call(
         down_back_kernel, meta,
         (
-            Scalars(labels), Scalars(head_bias.astype(f32)), pooled, partner, head_rows, Tiled(act), Tiled(n2),
+            Scalars(homes), Scalars(labels), Scalars(head_bias.astype(f32)), pooled, partner, head_rows, Tiled(act), Tiled(n2),
             Tiled(inv2), vec,
         ),
-        [Tiled(slim)] + dealt(hidden, width) + [sums_of, shape(f32, 8, hidden)],
-        [pltpu.VMEM((hidden, width), f32), pltpu.VMEM((count, width), f32)], steps=steps, micros=11,
+        [Tiled(slim)] + dealt(hidden, width) + [sums_of, shape(f32, 8, 3 * width), shape(f32, count, width)],
+        [pltpu.VMEM((hidden, width), f32), pltpu.VMEM((3, count, width), f32)], steps=steps, micros=11,
     )
     if quick:
         down = Scatter(down_parts)
@@ -914,60 +983,71 @@
         [Tiled(slim), Tiled(shape(b16, ext, width))] + dealt(width, hidden + width) + [sums_of],
         [pltpu.VMEM((width, hidden + width), f32)], steps=steps, micros=20,
     )
+    summed = jnp.concatenate([jnp.concatenate([sums_two, sums_up, sums_one], 1), tops], 0)
+    came = swap(summed, "tower", 1)
     if quick:
         up = Scatter(after(up_parts, down.sides()))
-        ctx_grad = after(ctx_grad, up.first, up.rest)
+        up.sides()
+        ctx_grad = after(ctx_grad, came, *up.corner, *up.sent)
     qkv_grad, sums_in = call(
         attend_back_kernel, meta, (Flat(qkv), Flat(probs), Flat(ctx_grad)), [shape(b16, ext, 3 * width), sums_of],
         [
             pltpu.VMEM(qkv.shape, b16), pltpu.VMEM(probs.shape, b16), pltpu.VMEM(ctx_grad.shape, b16),
-            pltpu.SemaphoreType.DMA((3,)),
+            pltpu.SemaphoreType.DMA((2 * (ext // seq_len) + count,)),
         ],
         micros=14,
     )
+    summed = after(summed + came, qkv_grad)
+    came = swap(summed, "dp", low)
     if quick:
-        up.sides()
-        down.far = after(down.fars(), qkv_grad)
-        xs = after(xs, qkv_grad, *up.corner, *up.sent, *down.far)
-    last_parts = call(
-        qkv_back_kernel, meta, (Tiled(xs), Tiled(qkv_grad)), dealt(width, 3 * width),
-        [pltpu.VMEM((width, 3 * width), f32)], steps=steps, micros=8,
+        mid = after(mid, qkv_grad, *up.side, *down.fars())
+        up.fars()
+    lanes = 128
+    last_cols = 3 * width + (lanes if quick else 0)
+    grad_in, grad_away, *last_parts = call(
+        input_kernel, meta, (Scalars(homes), Tiled(qkv_grad), Tiled(mid), Tiled(xs), sums_in, Flat(proj_qkv)),
+        [shape(f32, count, seq_len, width), shape(b16, count, seq_len, width)] + dealt(width, last_cols),
+        [pltpu.VMEM((rows, width), f32), pltpu.VMEM((width, 3 * width), f32), pltpu.VMEM((24, lanes), f32),
+         pltpu.VMEM(full[0], b16), pltpu.SemaphoreType.DMA((1,))],
+        steps=steps, micros=16,
     )
-    summed = jnp.concatenate([jnp.concatenate([sums_two, sums_up, sums_one, sums_in], 1), tops], 0)
-    summed = add_from(after(summed, *last_parts), "tower", 1)
+    if quick:
+        last_parts, up.far, came = after((last_parts, up.far, came))
+    summed = summed + came
+    came = swap(summed, "dp", 2 * low)
     if quick:
         last = Scatter(last_parts)
-        mid = after(mid, last.first, summed)
-    came = swap(summed, "dp", low)
-    (grad_in,) = call(
-        input_kernel, meta, (Tiled(qkv_grad), Tiled(mid), proj_qkv), [shape(f32, count, seq_len, width)],
-        [pltpu.VMEM((rows, width), f32)], steps=steps, micros=8,
-    )
-    if quick:
-        last.corner = after(last.corners(), grad_in)
         last.sides()
-        up.side = after(up.sides(), grad_in, *last.sent)
-        came = after(came, grad_in, *last.sent)
+        came = after(came, *last.sent)
+        grad_in = grad_in + swap(after(grad_away, *last.corner), "tower", 1).astype(f32)
+        last.far = after(last.fars(), grad_in)
         down_out, up_out, last_out = down.sum(), up.sum(), last.sum()
+        tail, last_out = last_out[:, 3 * width :], last_out[:, : 3 * width]
     else:
+        grad_in = grad_in + swap(grad_away, "tower", 1).astype(f32)
         down_out, up_out, last_out = (scatter_any(*p) for p in (down_parts, up_parts, last_parts))
-
-    summed, bit = add_from(summed + came, "dp", 2 * low), 1
+        tail, bit = add_from(sums_in[0:2].reshape(-1, lanes), "tower", 1), 1
+        while bit < groups:
+            tail = add_from(tail, "dp", bit)
+            bit *= 2
+    summed, bit = summed + came, 1
     while bit < low:
-        summed = add_from(summed, "dp", bit)
-        bit *= 2
+        came = swap(summed, "dp", bit)
+        if quick and bit == 1:
+            came = after(came, *last.side)
+        summed, bit = summed + came, 2 * bit
     spot = (tower * groups + lax.axis_index("dp")).astype(jnp.int32)[None]
     mine = width // (2 * groups)
     *plain, up_bias_sum, head_sum, class_sum = pl.pallas_call(
         small_kernel,
         out_shape=[shape(f32, 1, mine)] * 8
-        + [shape(f32, 1, 4 * mine), shape(f32, 3 * mine, NCLASS), shape(f32, 1, NCLASS)],
-        in_specs=[pl.BlockSpec(memory_space=pltpu.SMEM), pl.BlockSpec(memory_space=pltpu.VMEM)],
+        + [shape(f32, 1, 4 * mine), shape(f32, NCLASS, 3 * mine), shape(f32, 1, NCLASS)],
+        in_specs=[pl.BlockSpec(memory_space=pltpu.SMEM)] + [pl.BlockSpec(memory_space=pltpu.VMEM)] * 2,
         out_specs=[pl.BlockSpec(memory_space=pltpu.VMEM)] * 11,
-    )(spot, summed)
+    )(spot, summed, tail)
     q_sum, v_sum, o_sum, gain_one, shift_one, d_sum, gain_two, shift_two = [x.reshape(-1) for x in plain]
     return (
-        pooled[None],
+        own_pooled[None],
         grad_in[None],
         last_out,
         q_sum, v_sum,
@@ -977,7 +1057,7 @@
         up_bias_sum.reshape(-1),
         down_out,
         d_sum, gain_two, shift_two,
-        head_sum,
+        head_sum.T,
         class_sum.reshape(-1),
     )
 

time: 290 us -> 279 us (0.962); the launches traced: 291 us -> 274 us
  starting transfers between devices: 73 us -> 59.7 us
  waiting for transfers between devices: 74.8 us -> 66 us
  other arithmetic: 22.6 us -> 27.3 us
    ppermute x69 -> x72, starting transfers between devices: 73 us -> 59.7 us  [swap(): lax.ppermute(x, axis, [(i, i ^ k) for i in range(lax.axis_size(axis))])]
    ppermute x69 -> x72, waiting for transfers between devices: 74.8 us -> 66 us  [swap(): lax.ppermute(x, axis, [(i, i ^ k) for i in range(lax.axis_size(axis))])]
    another operation x3 -> x0, other arithmetic: 5.07 us -> none
    convert_element_type x6 -> x9, other arithmetic: 4.34 us -> 7.35 us  [the longest x3 4.39 us: fars(): self.own[j].astype(b16)]
    pallas_call x10 -> x9, Pallas kernels: 105 us -> 105 us  [call(): pl.pallas_call(kernel, out_shape=[bare(o) for o in outs], grid_spec=pltpu...]
  transfers between devices with their start and end apart: 69 -> 72, of which waited for: 21 -> 27; matrix products, arithmetic and copies ran while one was open for 8% -> 12% of each run, Pallas kernels for 28% -> 30%
where the time goes in v3:
time: 279 us; the launch traced here: 274 us
  Pallas kernels  106 us (38%)
  waiting for transfers between devices  66 us (24%)
  starting transfers between devices  59.7 us (21%)
  other arithmetic  27.3 us (10%)
  local copies, waits for them, and re-layouts  12.6 us (5%)
    pallas_call x9, Pallas kernels, call(): pl.pallas_call(kernel, out_shape=[bare(o) for o in outs], grid_spec=pltpu...  105 us
    ppermute x72, waiting for transfers between devices, swap(): lax.ppermute(x, axis, [(i, i ^ k) for i in range(lax.axis_size(axis))])  66 us
    ppermute x72, starting transfers between devices, swap(): lax.ppermute(x, axis, [(i, i ^ k) for i in range(lax.axis_size(axis))])  59.7 us
    unnamed x96, local copies, waits for them, and re-layouts  5.62 us
  transfers between devices with their start and end apart: 72, of which 27 were waited for; matrix products, arithmetic and copies ran while one was open for 12% of the time, Pallas kernels for 30%

profile of v3, /device:TPU:0, one launch (start us, length us, event | category | flops | bytes accessed | tf_op | source)
XLA Modules:
  0.0 274.2 jit_solution(6670890491266947678)
XLA Ops:
  4.3 2.7 shard_map.305
  7.0 4.6 %collective-permute-start.4 = (bf16[152,384]{1,0:T(8,128)(2,1)}, bf16[152,384]{1,0:T(8,128)(2,1)S(1)}, u32[]{:S(2)}, u32[]{:S(2)}) collective-permute-start(bf16[152,384]{1,0:T(8,128)(2,1)} %get-tuple-element.123), channel_id=1, source_target_pairs={{0,12},{1,13},{2,14},{3,15},{4,8},{5,9},{6,10},{7,11},{8,4},{9,5},... | collective-permute-start | bytes 350216 | tf_op jit(solution)/shard_map/ppermute | solution.py:24
  15.9 6.3 %collective-permute-done.3 = bf16[152,384]{1,0:T(8,128)(2,1)S(1)} collective-permute-done((bf16[152,384]{1,0:T(8,128)(2,1)}, bf16[152,384]{1,0:T(8,128)(2,1)S(1)}, u32[]{:S(2)}, u32[]{:S(2)}) %collective-permute-start.3) | collective-permute-done | bytes 116768 | tf_op jit(solution)/shard_map/ppermute | solution.py:24
  23.6 1.6 collective-permute-start.6
  25.2 1.5 collective-permute-start.5
  28.6 2.5 collective-permute-start.16
  31.1 1.9 collective-permute-start.14
  33.0 2.9 %collective-permute-done.6.refs_2_ = bf16[4,152,384]{2,1,0:T(8,128)(2,1)S(1)} collective-permute-done((bf16[4,152,384]{2,1,0:T(8,128)(2,1)S(1)}, bf16[4,152,384]{2,1,0:T(8,128)(2,1)S(1)}, u32[]{:S(2)}, u32[]{:S(2)}) %collective-permute-start.6) | collective-permute-done | bytes 466976 | tf_op jit(solution)/shard_map/ppermute | solution.py:24
  35.9 1.2 collective-permute-done.5.refs_1_
  37.2 1.6 collective-permute-start.8
  39.4 6.3 %collective-permute-done.15 = bf16[240,384]{1,0:T(8,128)(2,1)S(1)} collective-permute-done((bf16[240,384]{1,0:T(8,128)(2,1)S(1)}, bf16[240,384]{1,0:T(8,128)(2,1)S(1)}, u32[]{:S(2)}, u32[]{:S(2)}) %collective-permute-start.15) | collective-permute-done | bytes 184352 | tf_op jit(solution)/shard_map/ppermute | solution.py:24
  50.0 3.2 %collective-permute-start.26 = (bf16[192,384]{1,0:T(8,128)(2,1)S(1)}, bf16[192,384]{1,0:T(8,128)(2,1)S(1)}, u32[]{:S(2)}, u32[]{:S(2)}) collective-permute-start(bf16[192,384]{1,0:T(8,128)(2,1)S(1)} %copy-done.16), channel_id=1, source_target_pairs={{0,4},{1,5},{2,6},{3,7},{4,0},{5,1},{6,2},{7,3},{8,12},{9,13},{10,... | collective-permute-start | bytes 442376 | tf_op jit(solution)/shard_map/ppermute | solution.py:24
  54.3 16.0 %shard_map.306 = (bf16[4,192,2304]{2,1,0:T(8,128)(2,1)}, bf16[1152,768]{1,0:T(8,128)(2,1)}, bf16[1152,2304]{1,0:T(8,128)(2,1)}, bf16[8,1536,128]{2,1,0:T(8,128)(2,1)}, bf16[1152,768]{1,0:T(8,128)(2,1)}) custom-call(s32[8]{0:T(128)} %copy-done.32, s32[8]{0:T(128)} %select_reduce_fusion.1.offs, s32[1]{0:T(128)S(6)} %select_n.135.tiles, s32[3]{0:T(128)} %pad_add_fusion.place, ...), custom_call_target="tpu_custom_call" | custom-call | flops 18400000000 | bytes 22438080 | tf_op jit(solution)/shard_map/pallas_call | solution.py:780
  72.0 1.6 collective-permute-start.19
  75.6 4.2 %collective-permute-done.20.refs_4_ = bf16[2,240,384]{2,1,0:T(8,128)(2,1)} collective-permute-done((bf16[2,240,384]{2,1,0:T(8,128)(2,1)S(1)}, bf16[2,240,384]{2,1,0:T(8,128)(2,1)}, u32[]{:S(2)}, u32[]{:S(2)}) %collective-permute-start.20) | collective-permute-done | bytes 368672 | tf_op jit(solution)/shard_map/ppermute | solution.py:24
  79.8 1.3 collective-permute-done.19.refs_3_
  85.1 13.7 %shard_map.307 = (bf16[4,192,768]{2,1,0:T(8,128)(2,1)}, bf16[4,192,3072]{2,1,0:T(8,128)(2,1)}, bf16[1024,3072]{1,0:T(8,128)(2,1)}, bf16[1024,3072]{1,0:T(8,128)(...) custom-call(s32[8]{0:T(128)} %copy-done.32, s32[8]{0:T(128)} %select_reduce_fusion.1.offs, s32[1]{0:T(128)S(6)} %select_n.135.tiles, ...), custom_call_target="tpu_custom_call" | custom-call | flops 16099999744 | bytes 31625216 | tf_op jit(solution)/shard_map/pallas_call | solution.py:780
  101.3 7.5 %collective-permute-done.32.refs_4_ = bf16[2,192,384]{2,1,0:T(8,128)(2,1)S(1)} collective-permute-done((bf16[2,192,384]{2,1,0:T(8,128)(2,1)S(1)}, bf16[2,192,384]{2,1,0:T(8,128)(2,1)S(1)}, u32[]{:S(2)}, u32[]{:S(2)}) %collective-permute-start.32) | collective-permute-done | bytes 294944 | tf_op jit(solution)/shard_map/ppermute | solution.py:24
  112.1 10.7 %shard_map.308 = (bf16[4,768,768]{2,1,0:T(8,128)(2,1)}, f32[1024,768]{1,0:T(8,128)}, f32[1024,128]{1,0:T(8,128)}, f32[8,768]{1,0:T(8,128)}) custom-call(s32[8]{0:T(128)} %copy-done.32, s32[8]{0:T(128)} %select_reduce_fusion.1.offs, s32[1]{0:T(128)S(6)} %select_n.135.tiles, s32[3]{0:T(128)} %pad_add_fusion.place, f32[1024,768]{1,0:T(8,128)} %get-tuple-element.149.n1, ...), custom_call_target="tpu_custom_call" | custom-call | flops 11500000256 | bytes 22593536 | tf_op jit(solution)/shard_map/pallas_call | solution.py:780
  125.6 11.0 %shard_map.309 = (f32[1024,768]{1,0:T(8,128)}, bf16[4,4,96,768]{3,2,1,0:T(8,128)(2,1)}, bf16[4,96,768]{2,1,0:T(8,128)(2,1)}, bf16[3,4,96,768]{3,2,1,0:T(8,128)(2...) custom-call(s32[8]{0:T(128)} %copy-done.32, s32[8]{0:T(128)} %select_reduce_fusion.1.offs, ...), custom_call_target="tpu_custom_call" | custom-call | flops 12650000384 | bytes 18050284 | tf_op jit(solution)/shard_map/pallas_call | solution.py:780
  137.0 1.8 collective-permute-done.39
  142.5 8.1 %shard_map.310 = (bf16[1024,3072]{1,0:T(8,128)(2,1)}, f32[8,768]{1,0:T(8,128)}) custom-call(s32[8]{0:T(128)} %copy-done.32, s32[8]{0:T(128)} %select_reduce_fusion.1.offs, s32[1]{0:T(128)S(6)} %select_n.135.tiles, s32[3]{0:T(128)} %pad_add_fusion.place, f32[1024,768]{1,0:T(8,128)} %get-tuple-element.167.sum_grad, ...), custom_call_target="tpu_custom_call" | custom-call | flops 9200000000 | bytes 20471808 | tf_op jit(solution)/shard_map/pallas_call | solution.py:780
  153.9 17.9 %shard_map.311 = (f32[1024,768]{1,0:T(8,128)}, bf16[1152,768]{1,0:T(8,128)(2,1)}, bf16[4,4,24,3840]{3,2,1,0:T(8,128)(2,1)}, bf16[4,24,3840]{2,1,0:T(8,128)(2,1)}...) custom-call(s32[8]{0:T(128)} %copy-done.32, s32[8]{0:T(128)} %select_reduce_fusion.1.offs, s32[1]{0:T(128)S(6)} %select_n.135.tiles, ...), custom_call_target="tpu_custom_call" | custom-call | flops 23000000512 | bytes 31637504 | tf_op jit(solution)/shard_map/pallas_call | solution.py:780
  171.9 2.4 collective-permute-done.46
  175.7 1.4 fusion.6
  179.2 1.6 fusion.21
  180.8 1.2 collective-permute-start.54
  182.6 5.2 %collective-permute-done.48 = bf16[2,24,3840]{2,1,0:T(8,128)(2,1)S(1)} collective-permute-done((bf16[2,24,3840]{2,1,0:T(8,128)(2,1)S(1)}, bf16[2,24,3840]{2,1,0:T(8,128)(2,1)S(1)}, u32[]{:S(2)}, u32[]{:S(2)}) %collective-permute-start.48) | collective-permute-done | bytes 368672 | tf_op jit(solution)/shard_map/ppermute | solution.py:24
  192.1 11.8 %shard_map.312 = (bf16[1152,2304]{1,0:T(8,128)(2,1)}, f32[8,768]{1,0:T(8,128)}) custom-call(s32[8]{0:T(128)} %copy-done.32, s32[8]{0:T(128)} %select_reduce_fusion.1.offs, s32[1]{0:T(128)S(6)} %select_n.135.tiles, s32[3]{0:T(128)} %pad_add_fusion.place, bf16[1152,2304]{1,0:T(8,128)(2,1)} %get-tuple-element.163.qkv_h, ...), custom_call_target="tpu_custom_call" | custom-call | flops 16099999744 | bytes 15556608 | tf_op jit(solution)/shard_map/pallas_call | solution.py:780
  204.9 2.4 collective-permute-done.51
  208.3 1.6 fusion.15
  209.9 1.5 collective-permute-start.57
  212.5 1.8 collective-permute-start.55
  214.3 12.7 %shard_map.313 = (f32[8,128,768]{2,1,0:T(8,128)}, bf16[8,128,768]{2,1,0:T(8,128)(2,1)}, bf16[4,4,24,2432]{3,2,1,0:T(8,128)(2,1)}, bf16[4,24,2432]{2,1,0:T(8,128)(2,1)}, bf16[3,4,24,2432]{3,2,1,0:T(8,128)(2,1)}) custom-call(s32[8]{0:T(128)} %copy-done.32, s32[8]{0:T(128)} %select_reduce_fusion.1.offs, s32[1]{0:T(128)S(6)} %select_n.135.tiles, ...), custom_call_target="tpu_custom_call" | custom-call | flops 18400000000 | bytes 22241472 | tf_op jit(solution)/shard_map/pallas_call | solution.py:780
  227.7 2.2 collective-permute-done.59
  230.0 1.5 fusion.10
  233.6 2.1 fusion.20
  236.5 3.1 %collective-permute-done.61 = bf16[2,24,2432]{2,1,0:T(8,128)(2,1)S(1)} collective-permute-done((bf16[2,24,2432]{2,1,0:T(8,128)(2,1)S(1)}, bf16[2,24,2432]{2,1,0:T(8,128)(2,1)S(1)}, u32[]{:S(2)}, u32[]{:S(2)}) %collective-permute-start.61) | collective-permute-done | bytes 233504 | tf_op jit(solution)/shard_map/ppermute | solution.py:24
  240.2 1.5 fusion.5
  242.8 1.2 collective-permute-start.65
  244.0 1.5 fusion.14
  247.9 7.4 %collective-permute-done.64 = bf16[4,24,2432]{2,1,0:T(8,128)(2,1)S(1)} collective-permute-done((bf16[4,24,2432]{2,1,0:T(8,128)(2,1)S(1)}, bf16[4,24,2432]{2,1,0:T(8,128)(2,1)S(1)}, u32[]{:S(2)}, u32[]{:S(2)}) %collective-permute-start.64) | collective-permute-done | bytes 466976 | tf_op jit(solution)/shard_map/ppermute | solution.py:24
  256.8 1.9 collective-permute-start.68
  259.0 2.3 collective-permute-start.66
  261.3 2.0 convert_add_fusion
  263.3 1.3 collective-permute-start.71
  264.8 4.5 %collective-permute-done.67 = bf16[24,2432]{1,0:T(8,128)(2,1)S(1)} collective-permute-done((bf16[24,2432]{1,0:T(8,128)(2,1)S(1)}, bf16[24,2432]{1,0:T(8,128)(2,1)S(1)}, u32[]{:S(2)}, u32[]{:S(2)}) %collective-permute-start.67) | collective-permute-done | bytes 116768 | tf_op jit(solution)/shard_map/ppermute | solution.py:24
  272.3 1.7 shard_map.314
  (275 shorter events, 63.8 us)
Async XLA Ops:
  0.7 21.6 %collective-permute-start.1 = (bf16[8,128,768]{2,1,0:T(8,128)(2,1)}, bf16[8,128,768]{2,1,0:T(8,128)(2,1)S(1)}, u32[]{:S(2)}, u32[]{:S(2)}) collective-permute-start(bf16[8,128,768]{2,1,0:T(8,128)(2,1)} %bitcast.252), channel_id=1, source_target_pairs={{0,16},{16,0},{1,17},{17,1},{2,18},{18,2},{3,19},{19,3},{4,20},{20... | collective-permute-start | bytes 4718600 | tf_op jit(solution)/shard_map/ppermute | solution.py:24
  11.6 10.7 %collective-permute-start.3 = (bf16[152,384]{1,0:T(8,128)(2,1)}, bf16[152,384]{1,0:T(8,128)(2,1)S(1)}, u32[]{:S(2)}, u32[]{:S(2)}) collective-permute-start(bf16[152,384]{1,0:T(8,128)(2,1)} %get-tuple-element.123), channel_id=1, source_target_pairs={{0,8},{1,9},{2,10},{3,11},{4,12},{5,13},{6,14},{7,15},{8,0},{9,1},... | collective-permute-start | bytes 350216 | tf_op jit(solution)/shard_map/ppermute | solution.py:24
  11.6 10.7 %collective-permute-start.2 = (bf16[152,384]{1,0:T(8,128)(2,1)}, bf16[152,384]{1,0:T(8,128)(2,1)S(1)}, u32[]{:S(2)}, u32[]{:S(2)}) collective-permute-start(bf16[152,384]{1,0:T(8,128)(2,1)} %get-tuple-element.123), channel_id=1, source_target_pairs={{0,4},{1,5},{2,6},{3,7},{4,0},{5,1},{6,2},{7,3},{8,12},{9,13},{10,... | collective-permute-start | bytes 350216 | tf_op jit(solution)/shard_map/ppermute | solution.py:24
  23.6 12.4 %collective-permute-start.6 = (bf16[4,152,384]{2,1,0:T(8,128)(2,1)S(1)}, bf16[4,152,384]{2,1,0:T(8,128)(2,1)S(1)}, u32[]{:S(2)}, u32[]{:S(2)}) collective-permute-start(bf16[4,152,384]{2,1,0:T(8,128)(2,1)S(1)} %pad_maximum_fusion.5.refs_0_), channel_id=1, source_target_pairs={{0,2},{1,3},{2,0},{3,1},{4,6},{5,7},{6,4},{7,5},{8,10},{9,11},{10,... | collective-permute-start | bytes 1400840 | tf_op jit(solution)/shard_map/ppermute | solution.py:24
  25.2 12.0 %collective-permute-start.5 = (bf16[4,152,384]{2,1,0:T(8,128)(2,1)S(1)}, bf16[4,152,384]{2,1,0:T(8,128)(2,1)S(1)}, u32[]{:S(2)}, u32[]{:S(2)}) collective-permute-start(bf16[4,152,384]{2,1,0:T(8,128)(2,1)S(1)} %pad_maximum_fusion.5.refs_0_), channel_id=1, source_target_pairs={{0,1},{1,0},{2,3},{3,2},{4,5},{5,4},{6,7},{7,6},{8,9},{9,8},{10,11... | collective-permute-start | bytes 1400840 | tf_op jit(solution)/shard_map/ppermute | solution.py:24
  28.6 10.7 %collective-permute-start.16 = (bf16[240,384]{1,0:T(8,128)(2,1)S(1)}, bf16[240,384]{1,0:T(8,128)(2,1)S(1)}, u32[]{:S(2)}, u32[]{:S(2)}) collective-permute-start(bf16[240,384]{1,0:T(8,128)(2,1)S(1)} %copy-done.15), channel_id=1, source_target_pairs={{0,12},{1,13},{2,14},{3,15},{4,8},{5,9},{6,10},{7,11},{8,4},{9,5},... | collective-permute-start | bytes 552968 | tf_op jit(solution)/shard_map/ppermute | solution.py:24
  31.1 14.7 %collective-permute-start.15 = (bf16[240,384]{1,0:T(8,128)(2,1)S(1)}, bf16[240,384]{1,0:T(8,128)(2,1)S(1)}, u32[]{:S(2)}, u32[]{:S(2)}) collective-permute-start(bf16[240,384]{1,0:T(8,128)(2,1)S(1)} %copy-done.15), channel_id=1, source_target_pairs={{0,8},{1,9},{2,10},{3,11},{4,12},{5,13},{6,14},{7,15},{8,0},{9,1},... | collective-permute-start | bytes 552968 | tf_op jit(solution)/shard_map/ppermute | solution.py:24
  31.1 14.7 %collective-permute-start.14 = (bf16[240,384]{1,0:T(8,128)(2,1)S(1)}, bf16[240,384]{1,0:T(8,128)(2,1)S(1)}, u32[]{:S(2)}, u32[]{:S(2)}) collective-permute-start(bf16[240,384]{1,0:T(8,128)(2,1)S(1)} %copy-done.15), channel_id=1, source_target_pairs={{0,4},{1,5},{2,6},{3,7},{4,0},{5,1},{6,2},{7,3},{8,12},{9,13},{10,... | collective-permute-start | bytes 552968 | tf_op jit(solution)/shard_map/ppermute | solution.py:24
  48.8 24.7 %collective-permute-start.28 = (bf16[192,384]{1,0:T(8,128)(2,1)S(1)}, bf16[192,384]{1,0:T(8,128)(2,1)S(1)}, u32[]{:S(2)}, u32[]{:S(2)}) collective-permute-start(bf16[192,384]{1,0:T(8,128)(2,1)S(1)} %copy-done.16), channel_id=1, source_target_pairs={{0,12},{1,13},{2,14},{3,15},{4,8},{5,9},{6,10},{7,11},{8,4},{9,5},... | collective-permute-start | bytes 442376 | tf_op jit(solution)/shard_map/ppermute | solution.py:24
  50.0 23.6 %collective-permute-start.27 = (bf16[192,384]{1,0:T(8,128)(2,1)S(1)}, bf16[192,384]{1,0:T(8,128)(2,1)S(1)}, u32[]{:S(2)}, u32[]{:S(2)}) collective-permute-start(bf16[192,384]{1,0:T(8,128)(2,1)S(1)} %copy-done.16), channel_id=1, source_target_pairs={{0,8},{1,9},{2,10},{3,11},{4,12},{5,13},{6,14},{7,15},{8,0},{9,1},... | collective-permute-start | bytes 442376 | tf_op jit(solution)/shard_map/ppermute | solution.py:24
  50.0 24.1 %collective-permute-start.26 = (bf16[192,384]{1,0:T(8,128)(2,1)S(1)}, bf16[192,384]{1,0:T(8,128)(2,1)S(1)}, u32[]{:S(2)}, u32[]{:S(2)}) collective-permute-start(bf16[192,384]{1,0:T(8,128)(2,1)S(1)} %copy-done.16), channel_id=1, source_target_pairs={{0,4},{1,5},{2,6},{3,7},{4,0},{5,1},{6,2},{7,3},{8,12},{9,13},{10,... | collective-permute-start | bytes 442376 | tf_op jit(solution)/shard_map/ppermute | solution.py:24
  53.2 17.6 %collective-permute-start.18 = (bf16[4,240,384]{2,1,0:T(8,128)(2,1)S(1)}, bf16[4,240,384]{2,1,0:T(8,128)(2,1)S(1)}, u32[]{:S(2)}, u32[]{:S(2)}) collective-permute-start(bf16[4,240,384]{2,1,0:T(8,128)(2,1)S(1)} %pad_maximum_fusion.1.refs_0_), channel_id=1, source_target_pairs={{0,2},{1,3},{2,0},{3,1},{4,6},{5,7},{6,4},{7,5},{8,10},{9,11},{10,... | collective-permute-start | bytes 2211848 | tf_op jit(solution)/shard_map/ppermute | solution.py:24
  53.8 17.3 %collective-permute-start.17 = (bf16[4,240,384]{2,1,0:T(8,128)(2,1)S(1)}, bf16[4,240,384]{2,1,0:T(8,128)(2,1)S(1)}, u32[]{:S(2)}, u32[]{:S(2)}) collective-permute-start(bf16[4,240,384]{2,1,0:T(8,128)(2,1)S(1)} %pad_maximum_fusion.1.refs_0_), channel_id=1, source_target_pairs={{0,1},{1,0},{2,3},{3,2},{4,5},{5,4},{6,7},{7,6},{8,9},{9,8},{10,11... | collective-permute-start | bytes 2211848 | tf_op jit(solution)/shard_map/ppermute | solution.py:24
  72.0 9.2 %collective-permute-start.19 = (bf16[2,240,384]{2,1,0:T(8,128)(2,1)S(1)}, bf16[2,240,384]{2,1,0:T(8,128)(2,1)}, u32[]{:S(2)}, u32[]{:S(2)}) collective-permute-start(bf16[2,240,384]{2,1,0:T(8,128)(2,1)S(1)} %slice.279), channel_id=1, source_target_pairs={{0,2},{1,3},{2,0},{3,1},{4,6},{5,7},{6,4},{7,5},{8,10},{9,11},{10,... | collective-permute-start | bytes 1105928 | tf_op jit(solution)/shard_map/ppermute | solution.py:24
  73.6 11.5 %collective-permute-start.22 = (bf16[4,240,384]{2,1,0:T(8,128)(2,1)S(1)}, bf16[4,240,384]{2,1,0:T(8,128)(2,1)}, u32[]{:S(2)}, u32[]{:S(2)}) collective-permute-start(bf16[4,240,384]{2,1,0:T(8,128)(2,1)S(1)} %collective-permute-done.17.refs_1_), channel_id=1, source_target_pairs={{0,16},{16,0},{1,17},{17,1},{2,18},{18,2},{3,19},{19,3},{4,20},{20... | collective-permute-start | bytes 2211848 | tf_op jit(solution)/shard_map/ppermute | solution.py:24
  74.2 10.8 %collective-permute-start.23 = (bf16[4,240,384]{2,1,0:T(8,128)(2,1)S(1)}, bf16[4,240,384]{2,1,0:T(8,128)(2,1)}, u32[]{:S(2)}, u32[]{:S(2)}) collective-permute-start(bf16[4,240,384]{2,1,0:T(8,128)(2,1)S(1)} %collective-permute-done.18.refs_2_), channel_id=1, source_target_pairs={{0,16},{16,0},{1,17},{17,1},{2,18},{18,2},{3,19},{19,3},{4,20},{20... | collective-permute-start | bytes 2211848 | tf_op jit(solution)/shard_map/ppermute | solution.py:24
  82.4 27.3 %collective-permute-start.33 = (bf16[4,192,384]{2,1,0:T(8,128)(2,1)S(1)}, bf16[4,192,384]{2,1,0:T(8,128)(2,1)S(1)}, u32[]{:S(2)}, u32[]{:S(2)}) collective-permute-start(bf16[4,192,384]{2,1,0:T(8,128)(2,1)S(1)} %pad_maximum_fusion.3.refs_0_), channel_id=1, source_target_pairs={{0,16},{16,0},{1,17},{17,1},{2,18},{18,2},{3,19},{19,3},{4,20},{20... | collective-permute-start | bytes 1769480 | tf_op jit(solution)/shard_map/ppermute | solution.py:24
  83.0 15.8 %collective-permute-start.30 = (bf16[4,192,384]{2,1,0:T(8,128)(2,1)S(1)}, bf16[4,192,384]{2,1,0:T(8,128)(2,1)S(1)}, u32[]{:S(2)}, u32[]{:S(2)}) collective-permute-start(bf16[4,192,384]{2,1,0:T(8,128)(2,1)S(1)} %pad_maximum_fusion.3.refs_0_), channel_id=1, source_target_pairs={{0,2},{1,3},{2,0},{3,1},{4,6},{5,7},{6,4},{7,5},{8,10},{9,11},{10,... | collective-permute-start | bytes 1769480 | tf_op jit(solution)/shard_map/ppermute | solution.py:24
  84.2 15.0 %collective-permute-start.29 = (bf16[4,192,384]{2,1,0:T(8,128)(2,1)S(1)}, bf16[4,192,384]{2,1,0:T(8,128)(2,1)S(1)}, u32[]{:S(2)}, u32[]{:S(2)}) collective-permute-start(bf16[4,192,384]{2,1,0:T(8,128)(2,1)S(1)} %pad_maximum_fusion.3.refs_0_), channel_id=1, source_target_pairs={{0,1},{1,0},{2,3},{3,2},{4,5},{5,4},{6,7},{7,6},{8,9},{9,8},{10,11... | collective-permute-start | bytes 1769480 | tf_op jit(solution)/shard_map/ppermute | solution.py:24
  99.3 10.5 %collective-permute-start.34 = (bf16[4,192,384]{2,1,0:T(8,128)(2,1)S(1)}, bf16[4,192,384]{2,1,0:T(8,128)(2,1)S(1)}, u32[]{:S(2)}, u32[]{:S(2)}) collective-permute-start(bf16[4,192,384]{2,1,0:T(8,128)(2,1)S(1)} %collective-permute-done.29.refs_1_), channel_id=1, source_target_pairs={{0,16},{16,0},{1,17},{17,1},{2,18},{18,2},{3,19},{19,3},{4,20},{20... | collective-permute-start | bytes 1769480 | tf_op jit(solution)/shard_map/ppermute | solution.py:24
  99.4 9.5 %collective-permute-start.32 = (bf16[2,192,384]{2,1,0:T(8,128)(2,1)S(1)}, bf16[2,192,384]{2,1,0:T(8,128)(2,1)S(1)}, u32[]{:S(2)}, u32[]{:S(2)}) collective-permute-start(bf16[2,192,384]{2,1,0:T(8,128)(2,1)S(1)} %slice.282), channel_id=1, source_target_pairs={{0,1},{1,0},{2,3},{3,2},{4,5},{5,4},{6,7},{7,6},{8,9},{9,8},{10,11... | collective-permute-start | bytes 884744 | tf_op jit(solution)/shard_map/ppermute | solution.py:24
  100.3 9.5 %collective-permute-start.35 = (bf16[4,192,384]{2,1,0:T(8,128)(2,1)S(1)}, bf16[4,192,384]{2,1,0:T(8,128)(2,1)S(1)}, u32[]{:S(2)}, u32[]{:S(2)}) collective-permute-start(bf16[4,192,384]{2,1,0:T(8,128)(2,1)S(1)} %collective-permute-done.30.refs_2_), channel_id=1, source_target_pairs={{0,16},{16,0},{1,17},{17,1},{2,18},{18,2},{3,19},{19,3},{4,20},{20... | collective-permute-start | bytes 1769480 | tf_op jit(solution)/shard_map/ppermute | solution.py:24
  100.6 9.2 %collective-permute-start.31 = (bf16[2,192,384]{2,1,0:T(8,128)(2,1)S(1)}, bf16[2,192,384]{2,1,0:T(8,128)(2,1)S(1)}, u32[]{:S(2)}, u32[]{:S(2)}) collective-permute-start(bf16[2,192,384]{2,1,0:T(8,128)(2,1)S(1)} %slice.281), channel_id=1, source_target_pairs={{0,2},{1,3},{2,0},{3,1},{4,6},{5,7},{6,4},{7,5},{8,10},{9,11},{10,... | collective-permute-start | bytes 884744 | tf_op jit(solution)/shard_map/ppermute | solution.py:24
  138.9 11.7 %collective-permute-start.42 = (bf16[3,4,96,768]{3,2,1,0:T(8,128)(2,1)}, bf16[3,4,96,768]{3,2,1,0:T(8,128)(2,1)S(1)}, u32[]{:S(2)}, u32[]{:S(2)}) collective-permute-start(bf16[3,4,96,768]{3,2,1,0:T(8,128)(2,1)} %get-tuple-element.173), channel_id=1, source_target_pairs={{0,16},{16,0},{1,17},{17,1},{2,18},{18,2},{3,19},{19,3},{4,20},{20... | collective-permute-start | bytes 5308424 | tf_op jit(solution)/shard_map/ppermute | solution.py:24
  140.4 10.2 %collective-permute-start.41 = (bf16[2,96,768]{2,1,0:T(8,128)(2,1)S(1)}, bf16[2,96,768]{2,1,0:T(8,128)(2,1)S(1)}, u32[]{:S(2)}, u32[]{:S(2)}) collective-permute-start(bf16[2,96,768]{2,1,0:T(8,128)(2,1)S(1)} %get-tuple-element.250), channel_id=1, source_target_pairs={{0,2},{1,3},{2,0},{3,1},{4,6},{5,7},{6,4},{7,5},{8,10},{9,11},{10,... | collective-permute-start | bytes 884744 | tf_op jit(solution)/shard_map/ppermute | solution.py:24
  141.3 9.3 %collective-permute-start.40 = (bf16[2,96,768]{2,1,0:T(8,128)(2,1)S(1)}, bf16[2,96,768]{2,1,0:T(8,128)(2,1)S(1)}, u32[]{:S(2)}, u32[]{:S(2)}) collective-permute-start(bf16[2,96,768]{2,1,0:T(8,128)(2,1)S(1)} %get-tuple-element.251), channel_id=1, source_target_pairs={{0,1},{1,0},{2,3},{3,2},{4,5},{5,4},{6,7},{7,6},{8,9},{9,8},{10,11... | collective-permute-start | bytes 884744 | tf_op jit(solution)/shard_map/ppermute | solution.py:24
  151.8 20.0 %collective-permute-start.45 = (bf16[4,96,768]{2,1,0:T(8,128)(2,1)S(1)}, bf16[4,96,768]{2,1,0:T(8,128)(2,1)S(1)}, u32[]{:S(2)}, u32[]{:S(2)}) collective-permute-start(bf16[4,96,768]{2,1,0:T(8,128)(2,1)S(1)} %get-tuple-element.244), channel_id=1, source_target_pairs={{0,2},{1,3},{2,0},{3,1},{4,6},{5,7},{6,4},{7,5},{8,10},{9,11},{10,... | collective-permute-start | bytes 1769480 | tf_op jit(solution)/shard_map/ppermute | solution.py:24
  153.0 18.8 %collective-permute-start.44 = (bf16[4,96,768]{2,1,0:T(8,128)(2,1)S(1)}, bf16[4,96,768]{2,1,0:T(8,128)(2,1)S(1)}, u32[]{:S(2)}, u32[]{:S(2)}) collective-permute-start(bf16[4,96,768]{2,1,0:T(8,128)(2,1)S(1)} %get-tuple-element.245), channel_id=1, source_target_pairs={{0,1},{1,0},{2,3},{3,2},{4,5},{5,4},{6,7},{7,6},{8,9},{9,8},{10,11... | collective-permute-start | bytes 1769480 | tf_op jit(solution)/shard_map/ppermute | solution.py:24
  174.3 14.0 %collective-permute-start.49 = (bf16[3,4,24,3840]{3,2,1,0:T(8,128)(2,1)}, bf16[3,4,24,3840]{3,2,1,0:T(8,128)(2,1)S(1)}, u32[]{:S(2)}, u32[]{:S(2)}) collective-permute-start(bf16[3,4,24,3840]{3,2,1,0:T(8,128)(2,1)} %get-tuple-element.189), channel_id=1, source_target_pairs={{0,16},{16,0},{1,17},{17,1},{2,18},{18,2},{3,19},{19,3},{4,20},{20... | collective-permute-start | bytes 6635528 | tf_op jit(solution)/shard_map/ppermute | solution.py:24
  177.1 10.7 %collective-permute-start.48 = (bf16[2,24,3840]{2,1,0:T(8,128)(2,1)S(1)}, bf16[2,24,3840]{2,1,0:T(8,128)(2,1)S(1)}, u32[]{:S(2)}, u32[]{:S(2)}) collective-permute-start(bf16[2,24,3840]{2,1,0:T(8,128)(2,1)S(1)} %get-tuple-element.246), channel_id=1, source_target_pairs={{0,2},{1,3},{2,0},{3,1},{4,6},{5,7},{6,4},{7,5},{8,10},{9,11},{10,... | collective-permute-start | bytes 1105928 | tf_op jit(solution)/shard_map/ppermute | solution.py:24
  178.0 10.4 %collective-permute-start.47 = (bf16[2,24,3840]{2,1,0:T(8,128)(2,1)S(1)}, bf16[2,24,3840]{2,1,0:T(8,128)(2,1)S(1)}, u32[]{:S(2)}, u32[]{:S(2)}) collective-permute-start(bf16[2,24,3840]{2,1,0:T(8,128)(2,1)S(1)} %get-tuple-element.247), channel_id=1, source_target_pairs={{0,1},{1,0},{2,3},{3,2},{4,5},{5,4},{6,7},{7,6},{8,9},{9,8},{10,11... | collective-permute-start | bytes 1105928 | tf_op jit(solution)/shard_map/ppermute | solution.py:24
  180.8 23.1 %collective-permute-start.54 = (bf16[96,768]{1,0:T(8,128)(2,1)S(1)}, bf16[96,768]{1,0:T(8,128)(2,1)}, u32[]{:S(2)}, u32[]{:S(2)}) collective-permute-start(bf16[96,768]{1,0:T(8,128)(2,1)S(1)} %get-tuple-element.236), channel_id=1, source_target_pairs={{0,12},{1,13},{2,14},{3,15},{4,8},{5,9},{6,10},{7,11},{8,4},{9,5},... | collective-permute-start | bytes 442376 | tf_op jit(solution)/shard_map/ppermute | solution.py:24
  182.0 22.8 %collective-permute-start.53 = (bf16[96,768]{1,0:T(8,128)(2,1)S(1)}, bf16[96,768]{1,0:T(8,128)(2,1)S(1)}, u32[]{:S(2)}, u32[]{:S(2)}) collective-permute-start(bf16[96,768]{1,0:T(8,128)(2,1)S(1)} %get-tuple-element.237), channel_id=1, source_target_pairs={{0,8},{1,9},{2,10},{3,11},{4,12},{5,13},{6,14},{7,15},{8,0},{9,1},... | collective-permute-start | bytes 442376 | tf_op jit(solution)/shard_map/ppermute | solution.py:24
  187.8 17.1 %collective-permute-start.52 = (bf16[96,768]{1,0:T(8,128)(2,1)S(1)}, bf16[96,768]{1,0:T(8,128)(2,1)S(1)}, u32[]{:S(2)}, u32[]{:S(2)}) collective-permute-start(bf16[96,768]{1,0:T(8,128)(2,1)S(1)} %get-tuple-element.238), channel_id=1, source_target_pairs={{0,4},{1,5},{2,6},{3,7},{4,0},{5,1},{6,2},{7,3},{8,12},{9,13},{10,... | collective-permute-start | bytes 442376 | tf_op jit(solution)/shard_map/ppermute | solution.py:24
  189.8 17.5 %collective-permute-start.51 = (bf16[4,24,3840]{2,1,0:T(8,128)(2,1)S(1)}, bf16[4,24,3840]{2,1,0:T(8,128)(2,1)S(1)}, u32[]{:S(2)}, u32[]{:S(2)}) collective-permute-start(bf16[4,24,3840]{2,1,0:T(8,128)(2,1)S(1)} %get-tuple-element.239), channel_id=1, source_target_pairs={{0,2},{1,3},{2,0},{3,1},{4,6},{5,7},{6,4},{7,5},{8,10},{9,11},{10,... | collective-permute-start | bytes 2211848 | tf_op jit(solution)/shard_map/ppermute | solution.py:24
  191.0 17.3 %collective-permute-start.50 = (bf16[4,24,3840]{2,1,0:T(8,128)(2,1)S(1)}, bf16[4,24,3840]{2,1,0:T(8,128)(2,1)}, u32[]{:S(2)}, u32[]{:S(2)}) collective-permute-start(bf16[4,24,3840]{2,1,0:T(8,128)(2,1)S(1)} %get-tuple-element.240), channel_id=1, source_target_pairs={{0,1},{1,0},{2,3},{3,2},{4,5},{5,4},{6,7},{7,6},{8,9},{9,8},{10,11... | collective-permute-start | bytes 2211848 | tf_op jit(solution)/shard_map/ppermute | solution.py:24
  204.0 23.1 %collective-permute-start.58 = (f32[16,2304]{1,0:T(8,128)S(1)}, f32[16,2304]{1,0:T(8,128)S(1)}, u32[]{:S(2)}, u32[]{:S(2)}) collective-permute-start(f32[16,2304]{1,0:T(8,128)S(1)} %fusion.35), channel_id=1, source_target_pairs={{0,4},{1,5},{2,6},{3,7},{4,0},{5,1},{6,2},{7,3},{8,12},{9,13},{10,... | collective-permute-start | bytes 442376 | tf_op jit(solution)/shard_map/ppermute | solution.py:24
  209.9 17.2 %collective-permute-start.57 = (bf16[24,3840]{1,0:T(8,128)(2,1)S(1)}, bf16[24,3840]{1,0:T(8,128)(2,1)S(1)}, u32[]{:S(2)}, u32[]{:S(2)}) collective-permute-start(bf16[24,3840]{1,0:T(8,128)(2,1)S(1)} %get-tuple-element.233), channel_id=1, source_target_pairs={{0,12},{1,13},{2,14},{3,15},{4,8},{5,9},{6,10},{7,11},{8,4},{9,5},... | collective-permute-start | bytes 552968 | tf_op jit(solution)/shard_map/ppermute | solution.py:24
  211.4 15.7 %collective-permute-start.56 = (bf16[24,3840]{1,0:T(8,128)(2,1)S(1)}, bf16[24,3840]{1,0:T(8,128)(2,1)S(1)}, u32[]{:S(2)}, u32[]{:S(2)}) collective-permute-start(bf16[24,3840]{1,0:T(8,128)(2,1)S(1)} %get-tuple-element.234), channel_id=1, source_target_pairs={{0,8},{1,9},{2,10},{3,11},{4,12},{5,13},{6,14},{7,15},{8,0},{9,1},... | collective-permute-start | bytes 552968 | tf_op jit(solution)/shard_map/ppermute | solution.py:24
  212.5 14.6 %collective-permute-start.55 = (bf16[24,3840]{1,0:T(8,128)(2,1)S(1)}, bf16[24,3840]{1,0:T(8,128)(2,1)}, u32[]{:S(2)}, u32[]{:S(2)}) collective-permute-start(bf16[24,3840]{1,0:T(8,128)(2,1)S(1)} %get-tuple-element.235), channel_id=1, source_target_pairs={{0,4},{1,5},{2,6},{3,7},{4,0},{5,1},{6,2},{7,3},{8,12},{9,13},{10,... | collective-permute-start | bytes 552968 | tf_op jit(solution)/shard_map/ppermute | solution.py:24
  229.9 10.3 %collective-permute-start.63 = (bf16[3,4,24,2432]{3,2,1,0:T(8,128)(2,1)}, bf16[3,4,24,2432]{3,2,1,0:T(8,128)(2,1)}, u32[]{:S(2)}, u32[]{:S(2)}) collective-permute-start(bf16[3,4,24,2432]{3,2,1,0:T(8,128)(2,1)} %get-tuple-element.206), channel_id=1, source_target_pairs={{0,16},{16,0},{1,17},{17,1},{2,18},{18,2},{3,19},{19,3},{4,20},{20... | collective-permute-start | bytes 4202504 | tf_op jit(solution)/shard_map/ppermute | solution.py:24
  235.7 11.2 %collective-permute-start.69 = (f32[16,2304]{1,0:T(8,128)S(1)}, f32[16,2304]{1,0:T(8,128)S(1)}, u32[]{:S(2)}, u32[]{:S(2)}) collective-permute-start(f32[16,2304]{1,0:T(8,128)S(1)} %add.513), channel_id=1, source_target_pairs={{0,8},{1,9},{2,10},{3,11},{4,12},{5,13},{6,14},{7,15},{8,0},{9,1},... | collective-permute-start | bytes 442376 | tf_op jit(solution)/shard_map/ppermute | solution.py:24
  240.2 21.1 %collective-permute-start.62 = (bf16[8,128,768]{2,1,0:T(8,128)(2,1)}, bf16[8,128,768]{2,1,0:T(8,128)(2,1)S(1)}, u32[]{:S(2)}, u32[]{:S(2)}) collective-permute-start(bf16[8,128,768]{2,1,0:T(8,128)(2,1)} %get-tuple-element.204), channel_id=1, source_target_pairs={{0,16},{16,0},{1,17},{17,1},{2,18},{18,2},{3,19},{19,3},{4,20},{20... | collective-permute-start | bytes 4718600 | tf_op jit(solution)/shard_map/ppermute | solution.py:24
  241.7 13.6 %collective-permute-start.64 = (bf16[4,24,2432]{2,1,0:T(8,128)(2,1)S(1)}, bf16[4,24,2432]{2,1,0:T(8,128)(2,1)S(1)}, u32[]{:S(2)}, u32[]{:S(2)}) collective-permute-start(bf16[4,24,2432]{2,1,0:T(8,128)(2,1)S(1)} %get-tuple-element.248), channel_id=1, source_target_pairs={{0,1},{1,0},{2,3},{3,2},{4,5},{5,4},{6,7},{7,6},{8,9},{9,8},{10,11... | collective-permute-start | bytes 1400840 | tf_op jit(solution)/shard_map/ppermute | solution.py:24
  242.8 12.8 %collective-permute-start.65 = (bf16[4,24,2432]{2,1,0:T(8,128)(2,1)S(1)}, bf16[4,24,2432]{2,1,0:T(8,128)(2,1)S(1)}, u32[]{:S(2)}, u32[]{:S(2)}) collective-permute-start(bf16[4,24,2432]{2,1,0:T(8,128)(2,1)S(1)} %get-tuple-element.249), channel_id=1, source_target_pairs={{0,2},{1,3},{2,0},{3,1},{4,6},{5,7},{6,4},{7,5},{8,10},{9,11},{10,... | collective-permute-start | bytes 1400840 | tf_op jit(solution)/shard_map/ppermute | solution.py:24
  247.0 16.3 %collective-permute-start.70 = (f32[16,2304]{1,0:T(8,128)S(1)}, f32[16,2304]{1,0:T(8,128)S(1)}, u32[]{:S(2)}, u32[]{:S(2)}) collective-permute-start(f32[16,2304]{1,0:T(8,128)S(1)} %add.514), channel_id=1, source_target_pairs={{0,1},{1,0},{2,3},{3,2},{4,5},{5,4},{6,7},{7,6},{8,9},{9,8},{10,11... | collective-permute-start | bytes 442376 | tf_op jit(solution)/shard_map/ppermute | solution.py:24
  258.7 10.6 %collective-permute-start.67 = (bf16[24,2432]{1,0:T(8,128)(2,1)S(1)}, bf16[24,2432]{1,0:T(8,128)(2,1)S(1)}, u32[]{:S(2)}, u32[]{:S(2)}) collective-permute-start(bf16[24,2432]{1,0:T(8,128)(2,1)S(1)} %get-tuple-element.242), channel_id=1, source_target_pairs={{0,8},{1,9},{2,10},{3,11},{4,12},{5,13},{6,14},{7,15},{8,0},{9,1},... | collective-permute-start | bytes 350216 | tf_op jit(solution)/shard_map/ppermute | solution.py:24
  259.0 10.3 %collective-permute-start.66 = (bf16[24,2432]{1,0:T(8,128)(2,1)S(1)}, bf16[24,2432]{1,0:T(8,128)(2,1)S(1)}, u32[]{:S(2)}, u32[]{:S(2)}) collective-permute-start(bf16[24,2432]{1,0:T(8,128)(2,1)S(1)} %get-tuple-element.243), channel_id=1, source_target_pairs={{0,4},{1,5},{2,6},{3,7},{4,0},{5,1},{6,2},{7,3},{8,12},{9,13},{10,... | collective-permute-start | bytes 350216 | tf_op jit(solution)/shard_map/ppermute | solution.py:24
  (71 other events, 513.4 us)

commit v4 on v3

--- a/solution.py
+++ b/solution.py
@@ -192,6 +192,27 @@
     return jnp.concatenate([fn(x[:half]), fn(x[half:])], 0)
 
 
+def pair_lanes(base, p):
+    at = base + p * PAIR
+    return slice(at, at + PAIR) if isinstance(p, int) else pl.ds(pl.multiple_of(at, PAIR), PAIR)
+
+
+def pair_rows(p, size):
+    return slice(p * size, (p + 1) * size) if isinstance(p, int) else pl.ds(pl.multiple_of(p * size, PAIR), size)
+
+
+def over_pairs(count, looped, step):
+    def one(g, _):
+        step(g * GROUP)
+        return 0
+
+    if looped:
+        lax.fori_loop(0, count // GROUP, one, 0)
+    else:
+        for first in range(0, count, GROUP):
+            step(first)
+
+
 def by_length(lens, count, seq, step):
     def one(b, _):
         @pl.when(lens[b] > seq // 2)
@@ -241,29 +262,28 @@
 
 
 def fetch(place, pieces, targets, sems):
-    copies = []
-    for side in range(2):
-        tower = place[0] if side == 0 else 1 - place[0]
-        block, by_one, by_two, low, high = pieces[5 * side : 5 * side + 5]
-        half = FAR // 2
-        spots = ((block, 0, 0, FAR), (by_one, 1, 0, FAR), (by_two, 2, 0, FAR), (low, 3, 0, half), (high, 3, half, half))
-        for piece, k, far, size in spots:
-            at = 0
-            for weight, rows in targets:
-                cols = weight.shape[2] // 2
+    copies, at = [], 0
+    half = FAR // 2
+    for weight, rows in targets:
+        cols = weight.shape[2] // 2
+        for side in range(2):
+            tower = place[0] if side == 0 else 1 - place[0]
+            block, by_one, by_two, low, high = pieces[5 * side : 5 * side + 5]
+            spots = (
+                (block, 0, 0, FAR), (by_one, 1, 0, FAR), (by_two, 2, 0, FAR), (low, 3, 0, half), (high, 3, half, half)
+            )
+            for piece, k, far, size in spots:
                 for c in range(cols // CHUNK):
                     row = pl.multiple_of((place[1] ^ k) * rows, PACK)
                     col = pl.multiple_of(tower * cols + c * CHUNK, 128)
                     copies.append(
                         pltpu.make_async_copy(
-                            piece.at[:, pl.ds(at, rows), :],
+                            piece.at[:, pl.ds(at + c * rows, rows), :],
                             weight.at[pl.ds(far, size), pl.ds(row, rows), pl.ds(col, CHUNK)],
                             sems.at[len(copies)],
                         )
                     )
-                    at += rows
-    for copy in copies:
-        copy.start()
+        at += cols // CHUNK * rows
     return copies
 
 
@@ -278,9 +298,13 @@
         side = place[0] if own else 1 - place[0]
         for k in range(4):
             target = mine.at[k] if own else first if k == 3 else rest.at[k]
-            for j in range(FAR):
+
+            def block(j, _):
                 at = (side * 4 * FAR + (place[2] ^ j) * 4 + (place[1] ^ k)) * rows
                 target[j, :, base : base + cols] = acc[pl.ds(pl.multiple_of(at, 8), rows), :].astype(b16)
+                return 0
+
+            lax.fori_loop(0, FAR, block, 0)
 
 
 def flat_of(weight, cols=slice(None)):
@@ -288,48 +312,60 @@
     return block.reshape(block.shape[0] * block.shape[1], block.shape[2])
 
 
-def attend_kernel(n_pieces, lens, offs, tiles, place, homes, x_ref, y_ref, vec, *refs):
+def attend_kernel(n_pieces, lens, offs, tiles, place, homes, vec, x_h, y_h, *refs):
     pieces, refs = refs[:n_pieces], refs[n_pieces:]
     if n_pieces:
-        sinks, refs = refs[:5], refs[5:]
-        wqkv, xs, qkv, probs, ctx, got, sent = refs
+        wqkv_h, *sinks, x, xs, qkv, probs, ctx, sems, wqkv, got = refs
         copies = fetch(place, pieces, ((wqkv, wqkv.shape[1] // 4),), got)
+        for copy in copies:
+            copy.start()
     else:
-        wqkv = refs[0]
-        sinks, refs = refs[1:5], refs[5:]
-        xs, qkv, probs, ctx, sent = refs
+        wqkv, *sinks, x, xs, qkv, probs, ctx, sems = refs
         copies = []
-    held = (wqkv, xs, qkv, probs, ctx)[5 - len(sinks) :]
-    count, seq, width = x_ref.shape
-    leaving = []
-
-    def leave(*which):
-        for ref in which:
-            for i, own in enumerate(held):
-                if own is ref:
-                    copy = pltpu.make_async_copy(ref, sinks[i], sent.at[i])
-                    copy.start()
-                    leaving.append(copy)
-
+    xs_h, qkv_h, probs_h, ctx_h = sinks
+    count, seq, width = x.shape
+
+    def tokens(b, size, do):
+        for side, source in enumerate((x_h, y_h)):
+
+            @pl.when(homes[b] == side)
+            def _():
+                at = pl.ds(0, size)
+                do(pltpu.make_async_copy(source.at[homes[count + b], at], x.at[b, at], sems.at[0, b]))
+
+    by_length(lens, count, seq, lambda b, size: tokens(b, size, lambda copy: copy.start()))
     xs[...] = jnp.zeros_like(xs)
     ctx[...] = jnp.zeros_like(ctx)
+    by_length(lens, count, seq, lambda b, size: tokens(b, size, lambda copy: copy.wait()))
 
     def pack(b, _):
-        blocks = (lens[b] + PACK - 1) // PACK
-        for side, source in enumerate((x_ref, y_ref)):
-
-            def block(i, _):
-                at = pl.multiple_of(offs[b] + i * PACK, PACK)
-                xs[pl.ds(at, PACK), :] = source[homes[count + b], pl.ds(pl.multiple_of(i * PACK, PACK), PACK), :]
-                return 0
-
-            lax.fori_loop(0, jnp.where(homes[b] == side, blocks, 0), block, 0)
-        return 0
+        def block(i, _):
+            at = pl.multiple_of(offs[b] + i * PACK, PACK)
+            xs[pl.ds(at, PACK), :] = x[b, pl.ds(pl.multiple_of(i * PACK, PACK), PACK), :]
+            return 0
+
+        return lax.fori_loop(0, (lens[b] + PACK - 1) // PACK, block, 0)
 
     lax.fori_loop(0, count, pack, 0)
+
+    def leave(source, target, which, do):
+        def one(i, _):
+            at = pl.ds(pl.multiple_of(i * seq, seq), seq)
+            do(pltpu.make_async_copy(source.at[at], target.at[at], sems.at[which, i]))
+            return 0
+
+        lax.fori_loop(0, tiles[0] * (TILE // seq) + 1, one, 0)
+
+    def probs_of(b, size):
+        at = pl.ds(0, HEADS * size)
+        return pltpu.make_async_copy(probs.at[b, at], probs_h.at[b, at], sems.at[4, b])
+
+    leave(xs, xs_h, 1, lambda copy: copy.start())
     for copy in copies:
         copy.wait()
-    leave(wqkv, xs)
+    if n_pieces:
+        out = pltpu.make_async_copy(wqkv, wqkv_h, sems.at[5, 0])
+        out.start()
 
     def project(t, _):
         x = xs[tile_at(t), :]
@@ -345,7 +381,7 @@
 
     lax.fori_loop(0, tiles[0], project, 0)
     qkv[pl.ds(pl.multiple_of(tiles[0] * TILE, TILE), seq), :] = jnp.zeros((seq, 3 * width), b16)
-    leave(qkv)
+    leave(qkv, qkv_h, 2, lambda copy: copy.start())
 
     def attend(b, size):
         rows, key_rows = sentence_rows(offs, b, seq), sentence_rows(offs, b, size)
@@ -356,24 +392,29 @@
             e = jnp.exp(s - jnp.max(s, axis=0, keepdims=True))
             return (e * (1.0 / jnp.sum(e, axis=0, keepdims=True))).astype(b16)
 
-        for group in range(0, width // PAIR, GROUP):
-            pairs = range(group, group + GROUP)
-            cols = [slice(p * PAIR, (p + 1) * PAIR) for p in pairs]
-            queries = [qkv[rows, c] for c in cols]
-            keys = [split_heads(qkv[key_rows, width + c.start : width + c.stop]) for c in cols]
-            vals = [split_heads(qkv[key_rows, 2 * width + c.start : 2 * width + c.stop]) for c in cols]
+        def pairs(group):
+            spots = range(GROUP)
+            queries = [qkv[rows, pair_lanes(0, group + i)] for i in spots]
+            keys = [split_heads(qkv[key_rows, pair_lanes(width, group + i)]) for i in spots]
+            vals = [split_heads(qkv[key_rows, pair_lanes(2 * width, group + i)]) for i in spots]
             scores = [dot_nt(k, q) for k, q in zip(keys, queries)]
             lows = [by_head(softmax, s) for s in scores]
             outs = [dot_tn(low, v).astype(b16) for low, v in zip(lows, vals)]
-            for p, c, low, out in zip(pairs, cols, lows, outs):
-                probs[b, p * 2 * size : (p + 1) * 2 * size, :] = low
-                ctx[rows, c] = out
+            for i, low, out in zip(spots, lows, outs):
+                probs[b, pair_rows(group + i, 2 * size), :] = low
+                ctx[rows, pair_lanes(0, group + i)] = out
+
+        over_pairs(width // PAIR, size == seq, pairs)
+        probs_of(b, size).start()
 
     by_length(lens, count, seq, attend)
-    leave(probs, ctx)
-
-    for copy in leaving:
-        copy.wait()
+    leave(ctx, ctx_h, 3, lambda copy: copy.start())
+    leave(xs, xs_h, 1, lambda copy: copy.wait())
+    leave(qkv, qkv_h, 2, lambda copy: copy.wait())
+    leave(ctx, ctx_h, 3, lambda copy: copy.wait())
+    by_length(lens, count, seq, lambda b, size: probs_of(b, size).wait())
+    if n_pieces:
+        out.wait()
 
 
 def inside(offs, lens, b, t):
@@ -383,17 +424,28 @@
 
 def take_weights(step, place, pieces, refs, count, rows):
     if not pieces:
-        return refs[:count], refs[count:], lambda: None
+        return refs[:count], refs[count:], lambda: None, lambda: None
     sinks, refs = refs[:count], refs[count:]
     held, got, sent, refs = refs[-count - 2 : -2], refs[-2], refs[-1], refs[: -count - 2]
     leave = [pltpu.make_async_copy(a, b, sent.at[i]) for i, (a, b) in enumerate(zip(held, sinks))]
 
+    copies = fetch(place, pieces, [(weight, rows) for weight in held], got)
+    first = held[0].shape[2] // CHUNK * 5
+
     @pl.when(step == 0)
     def _():
-        for copy in fetch(place, pieces, [(weight, rows) for weight in held], got):
+        for copy in copies:
+            copy.start()
+        for copy in copies[:first]:
             copy.wait()
-        for copy in leave:
-            copy.start()
+
+    def others():
+        @pl.when(step == 0)
+        def _():
+            for copy in copies[first:]:
+                copy.wait()
+            for copy in leave:
+                copy.start()
 
     def finish():
         @pl.when(step == pl.num_programs(0) - 1)
@@ -401,13 +453,13 @@
             for copy in leave:
                 copy.wait()
 
-    return held, refs, finish
+    return held, refs, others, finish
 
 
 def up_kernel(n_pieces, rows, lens, offs, tiles, place, ctx, xs, vec, ups, *refs):
     t = pl.program_id(0)
     pieces, refs = refs[:n_pieces], refs[n_pieces:]
-    (wout, wup), (act, slope, n1, inv1), finish = take_weights(t, place, pieces, refs, 2, rows)
+    (wout, wup), (act, slope, n1, inv1), others, finish = take_weights(t, place, pieces, refs, 2, rows)
     width = n1.shape[1]
 
     @pl.when(t < tiles[0])
@@ -417,12 +469,17 @@
         n1[...] = normal
         inv1[...] = jnp.broadcast_to(inverse, (TILE, 128))
         low = (normal * row_of(vec, GAIN_1) + row_of(vec, SHIFT_1)).astype(b16)
-        for c in range(ups.shape[0]):
-            cols = slice(c * width, (c + 1) * width)
-            pre = dot(low, flat_of(wup, cols)) + row_of(ups, c)
+        others()
+
+        def chunk(c, _):
+            cols = pl.ds(pl.multiple_of(c * width, width), width)
+            pre = dot(low, flat_of(wup, cols)) + ups[pl.ds(c, 1), :]
             half = 0.5 * (1.0 + lax.erf(pre * (0.5 ** 0.5)))
             act[:, cols] = (pre * half).astype(b16)
             slope[:, cols] = (half + pre * (jnp.exp(-0.5 * pre * pre) * 0.3989422804014327)).astype(b16)
+            return 0
+
+        lax.fori_loop(0, ups.shape[0], chunk, 0)
 
     finish()
 
@@ -430,7 +487,8 @@
 def down_kernel(n_pieces, rows, lens, offs, tiles, place, n1, act, vec, *refs):
     t = pl.program_id(0)
     pieces, refs = refs[:n_pieces], refs[n_pieces:]
-    (wdown,), (n2, inv2, pooled), finish = take_weights(t, place, pieces, refs, 1, rows)
+    (wdown,), (n2, inv2, pooled), others, finish = take_weights(t, place, pieces, refs, 1, rows)
+    others()
     width = n1.shape[1]
     count = pooled.shape[0]
 
@@ -612,7 +670,7 @@
         deal(place, acc, outs)
 
 
-def attend_back_kernel(lens, offs, tiles, place, qkv_h, probs_h, ctx_grad_h, grad, sums, qkv, probs, ctx_grad, sems):
+def attend_back_kernel(lens, offs, tiles, place, qkv_h, probs_h, ctx_grad_h, grad_h, sums, grad, qkv, probs, ctx_grad, sems):
     width = ctx_grad.shape[1]
     count, seq = probs.shape[0], probs.shape[2]
     blocks = qkv.shape[0] // seq
@@ -644,14 +702,13 @@
         def spread(x):
             return jnp.broadcast_to(jnp.sum(x, axis=0, keepdims=True), x.shape)
 
-        for group in range(0, width // PAIR, GROUP):
-            pairs = range(group, group + GROUP)
-            cols = [slice(p * PAIR, (p + 1) * PAIR) for p in pairs]
-            ups = [jnp.where(real, ctx_grad[rows, c], jnp.zeros((), b16)) for c in cols]
-            queries = [qkv[rows, c] for c in cols]
-            keys = [split_heads(qkv[key_rows, width + c.start : width + c.stop]) for c in cols]
-            vals = [split_heads(qkv[key_rows, 2 * width + c.start : 2 * width + c.stop]) for c in cols]
-            lows = [probs[b, p * 2 * size : (p + 1) * 2 * size, :] for p in pairs]
+        def pairs(group):
+            spots = range(GROUP)
+            ups = [jnp.where(real, ctx_grad[rows, pair_lanes(0, group + i)], jnp.zeros((), b16)) for i in spots]
+            queries = [qkv[rows, pair_lanes(0, group + i)] for i in spots]
+            keys = [split_heads(qkv[key_rows, pair_lanes(width, group + i)]) for i in spots]
+            vals = [split_heads(qkv[key_rows, pair_lanes(2 * width, group + i)]) for i in spots]
+            lows = [probs[b, pair_rows(group + i, 2 * size), :] for i in spots]
             prob_grads = [dot_nt(v, up) for v, up in zip(vals, ups)]
             val_grads = [join_heads(dot(low, up)).astype(b16) for low, up in zip(lows, ups)]
             scores = []
@@ -660,19 +717,31 @@
                 scores.append((pr * (pg - by_head(spread, pg * pr))).astype(b16))
             query_grads = [(dot_tn(s, k) * (HEAD_DIM ** -0.5)).astype(b16) for s, k in zip(scores, keys)]
             key_grads = [join_heads(dot(s, q)).astype(b16) for s, q in zip(scores, queries)]
-            for i, c in enumerate(cols):
-                grad[rows, c] = query_grads[i]
-                grad[key_rows, width + c.start : width + c.stop] = key_grads[i]
-                grad[key_rows, 2 * width + c.start : 2 * width + c.stop] = val_grads[i]
+            for i in spots:
+                grad[rows, pair_lanes(0, group + i)] = query_grads[i]
+                grad[key_rows, pair_lanes(width, group + i)] = key_grads[i]
+                grad[key_rows, pair_lanes(2 * width, group + i)] = val_grads[i]
+
+        over_pairs(width // PAIR, size == seq, pairs)
 
     by_length(lens, count, seq, attend)
 
+    def result(t):
+        return pltpu.make_async_copy(grad.at[tile_at(t)], grad_h.at[tile_at(t)], sems.at[2 * blocks + count + t])
+
     def total(t, _):
+        result(t).start()
         for c in (0, 2):
             add_row(sums, c // 2, grad[tile_at(t), c * width : (c + 1) * width].astype(f32))
         return 0
 
+    def finish(t, _):
+        result(t).wait()
+        return 0
+
     lax.fori_loop(0, tiles[0], total, 0)
+    lax.fori_loop(0, tiles[0], finish, 0)
+
 
 def input_kernel(lens, offs, tiles, place, homes, grad, mid, xs, biases, wqkv_h, gx, gy, *refs):
     *outs, buf, acc, tail, wqkv, sems = refs
@@ -893,21 +962,23 @@
         Flat(shape(b16, ext, width)), Flat(shape(b16, ext, 3 * width)),
         Flat(shape(b16, count, HEADS * seq_len, seq_len)), Flat(shape(b16, ext, width)),
     ]
+    scratch = [pltpu.VMEM((count, seq_len, width), b16)]
+    scratch += [pltpu.VMEM(o.array.shape, o.array.dtype) for o in sinks]
+    scratch.append(pltpu.SemaphoreType.DMA((6, max(ext // seq_len, count))))
     if quick:
         both = [Flat(shape(b16, *full[0]))] + sinks
         pieces_first = after(pieces_first, block_up)
         proj_qkv, xs, qkv, probs, ctx = call(
             partial(attend_kernel, 10), meta,
-            (Scalars(homes), embeddings[0], other_tokens, vec, *map(Flat, pieces_first)), both,
-            [pltpu.VMEM(o.array.shape, o.array.dtype) for o in both]
-            + [pltpu.SemaphoreType.DMA((30,)), pltpu.SemaphoreType.DMA((5,))],
+            (Scalars(homes), vec, Flat(embeddings[0]), Flat(other_tokens), *map(Flat, pieces_first)), both,
+            scratch + [pltpu.VMEM(full[0], b16), pltpu.SemaphoreType.DMA((30,))],
             micros=16,
         )
     else:
         (proj_qkv,) = pieces_first
         xs, qkv, probs, ctx = call(
-            partial(attend_kernel, 0), meta, (Scalars(homes), embeddings[0], other_tokens, vec, proj_qkv), sinks,
-            [pltpu.VMEM(o.array.shape, o.array.dtype) for o in sinks] + [pltpu.SemaphoreType.DMA((5,))],
+            partial(attend_kernel, 0), meta, (Scalars(homes), vec, Flat(embeddings[0]), Flat(other_tokens), proj_qkv), sinks,
+            scratch,
             micros=16,
         )
 
@@ -990,10 +1061,10 @@
         up.sides()
         ctx_grad = after(ctx_grad, came, *up.corner, *up.sent)
     qkv_grad, sums_in = call(
-        attend_back_kernel, meta, (Flat(qkv), Flat(probs), Flat(ctx_grad)), [shape(b16, ext, 3 * width), sums_of],
+        attend_back_kernel, meta, (Flat(qkv), Flat(probs), Flat(ctx_grad)), [Flat(shape(b16, ext, 3 * width)), sums_of],
         [
-            pltpu.VMEM(qkv.shape, b16), pltpu.VMEM(probs.shape, b16), pltpu.VMEM(ctx_grad.shape, b16),
-            pltpu.SemaphoreType.DMA((2 * (ext // seq_len) + count,)),
+            pltpu.VMEM(qkv.shape, b16), pltpu.VMEM(qkv.shape, b16), pltpu.VMEM(probs.shape, b16), pltpu.VMEM(ctx_grad.shape, b16),
+            pltpu.SemaphoreType.DMA((2 * (ext // seq_len) + count + steps,)),
         ],
         micros=14,
     )

time: 279 us -> 275 us (0.986); the launches traced: 274 us -> 275 us
  transfers between devices with their start and end apart: 72 -> 72, of which waited for: 27 -> 26; matrix products, arithmetic and copies ran while one was open for 12% -> 12% of each run, Pallas kernels for 30% -> 30%
where the time goes in v4:
time: 275 us
  Pallas kernels  105 us (38%)
  waiting for transfers between devices  67.1 us (24%)
  starting transfers between devices  60.2 us (22%)
  other arithmetic  27.3 us (10%)
  local copies, waits for them, and re-layouts  12.6 us (5%)
    pallas_call x9, Pallas kernels, call(): pl.pallas_call(kernel, out_shape=[bare(o) for o in outs], grid_spec=pltpu...  103 us
    ppermute x72, waiting for transfers between devices, swap(): lax.ppermute(x, axis, [(i, i ^ k) for i in range(lax.axis_size(axis))])  67.1 us
    ppermute x72, starting transfers between devices, swap(): lax.ppermute(x, axis, [(i, i ^ k) for i in range(lax.axis_size(axis))])  60.2 us
    unnamed x96, local copies, waits for them, and re-layouts  5.62 us
  transfers between devices with their start and end apart: 72, of which 26 were waited for; matrix products, arithmetic and copies ran while one was open for 12% of the time, Pallas kernels for 30%

profile of v4, /device:TPU:0, one launch (start us, length us, event | category | flops | bytes accessed | tf_op | source)
XLA Modules:
  0.0 274.5 jit_solution(17445803680439426932)
XLA Ops:
  4.3 2.7 shard_map.305
  7.0 4.6 %collective-permute-start.3 = (bf16[152,384]{1,0:T(8,128)(2,1)}, bf16[152,384]{1,0:T(8,128)(2,1)S(1)}, u32[]{:S(2)}, u32[]{:S(2)}) collective-permute-start(bf16[152,384]{1,0:T(8,128)(2,1)} %get-tuple-element.123), channel_id=1, source_target_pairs={{0,12},{1,13},{2,14},{3,15},{4,8},{5,9},{6,10},{7,11},{8,4},{9,5},... | collective-permute-start | bytes 350216 | tf_op jit(solution)/shard_map/ppermute | solution.py:24
  15.9 6.3 %collective-permute-done.2 = bf16[152,384]{1,0:T(8,128)(2,1)S(1)} collective-permute-done((bf16[152,384]{1,0:T(8,128)(2,1)}, bf16[152,384]{1,0:T(8,128)(2,1)S(1)}, u32[]{:S(2)}, u32[]{:S(2)}) %collective-permute-start.2) | collective-permute-done | bytes 116768 | tf_op jit(solution)/shard_map/ppermute | solution.py:24
  23.6 1.6 collective-permute-start.6
  25.2 1.5 collective-permute-start.5
  28.6 2.5 collective-permute-start.16
  31.1 1.9 collective-permute-start.14
  33.0 2.9 %collective-permute-done.6.refs_2_ = bf16[4,152,384]{2,1,0:T(8,128)(2,1)S(1)} collective-permute-done((bf16[4,152,384]{2,1,0:T(8,128)(2,1)S(1)}, bf16[4,152,384]{2,1,0:T(8,128)(2,1)S(1)}, u32[]{:S(2)}, u32[]{:S(2)}) %collective-permute-start.6) | collective-permute-done | bytes 466976 | tf_op jit(solution)/shard_map/ppermute | solution.py:24
  37.2 1.6 collective-permute-start.8
  39.4 6.3 %collective-permute-done.15 = bf16[240,384]{1,0:T(8,128)(2,1)S(1)} collective-permute-done((bf16[240,384]{1,0:T(8,128)(2,1)S(1)}, bf16[240,384]{1,0:T(8,128)(2,1)S(1)}, u32[]{:S(2)}, u32[]{:S(2)}) %collective-permute-start.15) | collective-permute-done | bytes 184352 | tf_op jit(solution)/shard_map/ppermute | solution.py:24
  50.0 3.2 %collective-permute-start.26 = (bf16[192,384]{1,0:T(8,128)(2,1)S(1)}, bf16[192,384]{1,0:T(8,128)(2,1)S(1)}, u32[]{:S(2)}, u32[]{:S(2)}) collective-permute-start(bf16[192,384]{1,0:T(8,128)(2,1)S(1)} %copy-done.16), channel_id=1, source_target_pairs={{0,4},{1,5},{2,6},{3,7},{4,0},{5,1},{6,2},{7,3},{8,12},{9,13},{10,... | collective-permute-start | bytes 442376 | tf_op jit(solution)/shard_map/ppermute | solution.py:24
  54.3 14.3 %shard_map.306 = (bf16[4,192,2304]{2,1,0:T(8,128)(2,1)}, bf16[1152,768]{1,0:T(8,128)(2,1)}, bf16[1152,2304]{1,0:T(8,128)(2,1)}, bf16[8,1536,128]{2,1,0:T(8,128)(2,1)}, bf16[1152,768]{1,0:T(8,128)(2,1)}) custom-call(s32[8]{0:T(128)} %copy-done.32, s32[8]{0:T(128)} %select_reduce_fusion.1.offs, s32[1]{0:T(128)S(6)} %select_n.135.tiles, s32[3]{0:T(128)} %pad_add_fusion.place, ...), custom_call_target="tpu_custom_call" | custom-call | flops 18400000000 | bytes 22438080 | tf_op jit(solution)/shard_map/pallas_call | solution.py:849
  68.6 2.2 collective-permute-done.18.refs_2_
  71.7 1.6 collective-permute-start.19
  75.4 4.4 %collective-permute-done.20.refs_4_ = bf16[2,240,384]{2,1,0:T(8,128)(2,1)} collective-permute-done((bf16[2,240,384]{2,1,0:T(8,128)(2,1)S(1)}, bf16[2,240,384]{2,1,0:T(8,128)(2,1)}, u32[]{:S(2)}, u32[]{:S(2)}) %collective-permute-start.20) | collective-permute-done | bytes 368672 | tf_op jit(solution)/shard_map/ppermute | solution.py:24
  82.0 1.5 collective-permute-start.30
  83.5 1.5 collective-permute-start.29
  85.0 13.9 %shard_map.307 = (bf16[4,192,768]{2,1,0:T(8,128)(2,1)}, bf16[4,192,3072]{2,1,0:T(8,128)(2,1)}, bf16[1024,3072]{1,0:T(8,128)(2,1)}, bf16[1024,3072]{1,0:T(8,128)(...) custom-call(s32[8]{0:T(128)} %copy-done.32, s32[8]{0:T(128)} %select_reduce_fusion.1.offs, s32[1]{0:T(128)S(6)} %select_n.135.tiles, ...), custom_call_target="tpu_custom_call" | custom-call | flops 16099999744 | bytes 31625216 | tf_op jit(solution)/shard_map/pallas_call | solution.py:849
  101.0 7.5 %collective-permute-done.32.refs_4_ = bf16[2,192,384]{2,1,0:T(8,128)(2,1)S(1)} collective-permute-done((bf16[2,192,384]{2,1,0:T(8,128)(2,1)S(1)}, bf16[2,192,384]{2,1,0:T(8,128)(2,1)S(1)}, u32[]{:S(2)}, u32[]{:S(2)}) %collective-permute-start.32) | collective-permute-done | bytes 294944 | tf_op jit(solution)/shard_map/ppermute | solution.py:24
  112.0 10.7 %shard_map.308 = (bf16[4,768,768]{2,1,0:T(8,128)(2,1)}, f32[1024,768]{1,0:T(8,128)}, f32[1024,128]{1,0:T(8,128)}, f32[8,768]{1,0:T(8,128)}) custom-call(s32[8]{0:T(128)} %copy-done.32, s32[8]{0:T(128)} %select_reduce_fusion.1.offs, s32[1]{0:T(128)S(6)} %select_n.135.tiles, s32[3]{0:T(128)} %pad_add_fusion.place, f32[1024,768]{1,0:T(8,128)} %get-tuple-element.149.n1, ...), custom_call_target="tpu_custom_call" | custom-call | flops 11500000256 | bytes 22593536 | tf_op jit(solution)/shard_map/pallas_call | solution.py:849
  125.5 11.2 %shard_map.309 = (f32[1024,768]{1,0:T(8,128)}, bf16[4,4,96,768]{3,2,1,0:T(8,128)(2,1)}, bf16[4,96,768]{2,1,0:T(8,128)(2,1)}, bf16[3,4,96,768]{3,2,1,0:T(8,128)(2...) custom-call(s32[8]{0:T(128)} %copy-done.32, s32[8]{0:T(128)} %select_reduce_fusion.1.offs, ...), custom_call_target="tpu_custom_call" | custom-call | flops 12650000384 | bytes 18050284 | tf_op jit(solution)/shard_map/pallas_call | solution.py:849
  137.1 1.8 collective-permute-done.39
  142.0 8.3 %shard_map.310 = (bf16[1024,3072]{1,0:T(8,128)(2,1)}, f32[8,768]{1,0:T(8,128)}) custom-call(s32[8]{0:T(128)} %copy-done.32, s32[8]{0:T(128)} %select_reduce_fusion.1.offs, s32[1]{0:T(128)S(6)} %select_n.135.tiles, s32[3]{0:T(128)} %pad_add_fusion.place, f32[1024,768]{1,0:T(8,128)} %get-tuple-element.167.sum_grad, ...), custom_call_target="tpu_custom_call" | custom-call | flops 9200000000 | bytes 20471808 | tf_op jit(solution)/shard_map/pallas_call | solution.py:849
  151.6 1.5 collective-permute-start.45
  154.2 18.0 %shard_map.311 = (f32[1024,768]{1,0:T(8,128)}, bf16[1152,768]{1,0:T(8,128)(2,1)}, bf16[4,4,24,3840]{3,2,1,0:T(8,128)(2,1)}, bf16[4,24,3840]{2,1,0:T(8,128)(2,1)}...) custom-call(s32[8]{0:T(128)} %copy-done.32, s32[8]{0:T(128)} %select_reduce_fusion.1.offs, s32[1]{0:T(128)S(6)} %select_n.135.tiles, ...), custom_call_target="tpu_custom_call" | custom-call | flops 23000000512 | bytes 31637504 | tf_op jit(solution)/shard_map/pallas_call | solution.py:849
  172.3 2.4 collective-permute-done.46
  179.3 1.6 fusion.21
  183.1 5.1 %collective-permute-done.48 = bf16[2,24,3840]{2,1,0:T(8,128)(2,1)S(1)} collective-permute-done((bf16[2,24,3840]{2,1,0:T(8,128)(2,1)S(1)}, bf16[2,24,3840]{2,1,0:T(8,128)(2,1)S(1)}, u32[]{:S(2)}, u32[]{:S(2)}) %collective-permute-start.48) | collective-permute-done | bytes 368672 | tf_op jit(solution)/shard_map/ppermute | solution.py:24
  192.3 11.4 %shard_map.312 = (bf16[1152,2304]{1,0:T(8,128)(2,1)}, f32[8,768]{1,0:T(8,128)}) custom-call(s32[8]{0:T(128)} %copy-done.32, s32[8]{0:T(128)} %select_reduce_fusion.1.offs, s32[1]{0:T(128)S(6)} %select_n.135.tiles, s32[3]{0:T(128)} %pad_add_fusion.place, bf16[1152,2304]{1,0:T(8,128)(2,1)} %get-tuple-element.163.qkv_h, ...), custom_call_target="tpu_custom_call" | custom-call | flops 16099999744 | bytes 15556608 | tf_op jit(solution)/shard_map/pallas_call | solution.py:849
  203.7 1.6 collective-permute-start.58
  205.3 2.5 collective-permute-done.51
  208.7 1.6 fusion.15
  212.7 2.0 collective-permute-start.55
  214.7 13.0 %shard_map.313 = (f32[8,128,768]{2,1,0:T(8,128)}, bf16[8,128,768]{2,1,0:T(8,128)(2,1)}, bf16[4,4,24,2432]{3,2,1,0:T(8,128)(2,1)}, bf16[4,24,2432]{2,1,0:T(8,128)(2,1)}, bf16[3,4,24,2432]{3,2,1,0:T(8,128)(2,1)}) custom-call(s32[8]{0:T(128)} %copy-done.32, s32[8]{0:T(128)} %select_reduce_fusion.1.offs, s32[1]{0:T(128)S(6)} %select_n.135.tiles, ...), custom_call_target="tpu_custom_call" | custom-call | flops 18400000000 | bytes 22241472 | tf_op jit(solution)/shard_map/pallas_call | solution.py:849
  228.4 2.2 collective-permute-done.59
  230.8 1.5 fusion.10
  233.9 2.1 fusion.20
  236.7 3.6 %collective-permute-done.61 = bf16[2,24,2432]{2,1,0:T(8,128)(2,1)S(1)} collective-permute-done((bf16[2,24,2432]{2,1,0:T(8,128)(2,1)S(1)}, bf16[2,24,2432]{2,1,0:T(8,128)(2,1)S(1)}, u32[]{:S(2)}, u32[]{:S(2)}) %collective-permute-start.61) | collective-permute-done | bytes 233504 | tf_op jit(solution)/shard_map/ppermute | solution.py:24
  241.0 1.5 fusion.5
  243.1 1.4 collective-permute-start.65
  244.5 1.5 fusion.14
  248.6 7.4 %collective-permute-done.64 = bf16[4,24,2432]{2,1,0:T(8,128)(2,1)S(1)} collective-permute-done((bf16[4,24,2432]{2,1,0:T(8,128)(2,1)S(1)}, bf16[4,24,2432]{2,1,0:T(8,128)(2,1)S(1)}, u32[]{:S(2)}, u32[]{:S(2)}) %collective-permute-start.64) | collective-permute-done | bytes 466976 | tf_op jit(solution)/shard_map/ppermute | solution.py:24
  257.2 1.8 collective-permute-start.68
  259.5 2.2 collective-permute-start.66
  261.7 2.0 convert_add_fusion
  263.7 1.4 collective-permute-start.71
  265.2 4.5 %collective-permute-done.67 = bf16[24,2432]{1,0:T(8,128)(2,1)S(1)} collective-permute-done((bf16[24,2432]{1,0:T(8,128)(2,1)S(1)}, bf16[24,2432]{1,0:T(8,128)(2,1)S(1)}, u32[]{:S(2)}, u32[]{:S(2)}) %collective-permute-start.67) | collective-permute-done | bytes 116768 | tf_op jit(solution)/shard_map/ppermute | solution.py:24
  272.8 1.7 shard_map.314
  (275 shorter events, 62.6 us)
Async XLA Ops:
  0.7 21.6 %collective-permute-start.4 = (bf16[8,128,768]{2,1,0:T(8,128)(2,1)}, bf16[8,128,768]{2,1,0:T(8,128)(2,1)S(1)}, u32[]{:S(2)}, u32[]{:S(2)}) collective-permute-start(bf16[8,128,768]{2,1,0:T(8,128)(2,1)} %bitcast.252), channel_id=1, source_target_pairs={{0,16},{16,0},{1,17},{17,1},{2,18},{18,2},{3,19},{19,3},{4,20},{20... | collective-permute-start | bytes 4718600 | tf_op jit(solution)/shard_map/ppermute | solution.py:24
  11.6 10.7 %collective-permute-start.2 = (bf16[152,384]{1,0:T(8,128)(2,1)}, bf16[152,384]{1,0:T(8,128)(2,1)S(1)}, u32[]{:S(2)}, u32[]{:S(2)}) collective-permute-start(bf16[152,384]{1,0:T(8,128)(2,1)} %get-tuple-element.123), channel_id=1, source_target_pairs={{0,8},{1,9},{2,10},{3,11},{4,12},{5,13},{6,14},{7,15},{8,0},{9,1},... | collective-permute-start | bytes 350216 | tf_op jit(solution)/shard_map/ppermute | solution.py:24
  11.6 10.7 %collective-permute-start.1 = (bf16[152,384]{1,0:T(8,128)(2,1)}, bf16[152,384]{1,0:T(8,128)(2,1)S(1)}, u32[]{:S(2)}, u32[]{:S(2)}) collective-permute-start(bf16[152,384]{1,0:T(8,128)(2,1)} %get-tuple-element.123), channel_id=1, source_target_pairs={{0,4},{1,5},{2,6},{3,7},{4,0},{5,1},{6,2},{7,3},{8,12},{9,13},{10,... | collective-permute-start | bytes 350216 | tf_op jit(solution)/shard_map/ppermute | solution.py:24
  23.6 12.4 %collective-permute-start.6 = (bf16[4,152,384]{2,1,0:T(8,128)(2,1)S(1)}, bf16[4,152,384]{2,1,0:T(8,128)(2,1)S(1)}, u32[]{:S(2)}, u32[]{:S(2)}) collective-permute-start(bf16[4,152,384]{2,1,0:T(8,128)(2,1)S(1)} %pad_maximum_fusion.5.refs_0_), channel_id=1, source_target_pairs={{0,2},{1,3},{2,0},{3,1},{4,6},{5,7},{6,4},{7,5},{8,10},{9,11},{10,... | collective-permute-start | bytes 1400840 | tf_op jit(solution)/shard_map/ppermute | solution.py:24
  25.2 12.0 %collective-permute-start.5 = (bf16[4,152,384]{2,1,0:T(8,128)(2,1)S(1)}, bf16[4,152,384]{2,1,0:T(8,128)(2,1)S(1)}, u32[]{:S(2)}, u32[]{:S(2)}) collective-permute-start(bf16[4,152,384]{2,1,0:T(8,128)(2,1)S(1)} %pad_maximum_fusion.5.refs_0_), channel_id=1, source_target_pairs={{0,1},{1,0},{2,3},{3,2},{4,5},{5,4},{6,7},{7,6},{8,9},{9,8},{10,11... | collective-permute-start | bytes 1400840 | tf_op jit(solution)/shard_map/ppermute | solution.py:24
  28.6 10.7 %collective-permute-start.16 = (bf16[240,384]{1,0:T(8,128)(2,1)S(1)}, bf16[240,384]{1,0:T(8,128)(2,1)S(1)}, u32[]{:S(2)}, u32[]{:S(2)}) collective-permute-start(bf16[240,384]{1,0:T(8,128)(2,1)S(1)} %copy-done.15), channel_id=1, source_target_pairs={{0,12},{1,13},{2,14},{3,15},{4,8},{5,9},{6,10},{7,11},{8,4},{9,5},... | collective-permute-start | bytes 552968 | tf_op jit(solution)/shard_map/ppermute | solution.py:24
  31.1 14.7 %collective-permute-start.15 = (bf16[240,384]{1,0:T(8,128)(2,1)S(1)}, bf16[240,384]{1,0:T(8,128)(2,1)S(1)}, u32[]{:S(2)}, u32[]{:S(2)}) collective-permute-start(bf16[240,384]{1,0:T(8,128)(2,1)S(1)} %copy-done.15), channel_id=1, source_target_pairs={{0,8},{1,9},{2,10},{3,11},{4,12},{5,13},{6,14},{7,15},{8,0},{9,1},... | collective-permute-start | bytes 552968 | tf_op jit(solution)/shard_map/ppermute | solution.py:24
  31.1 14.7 %collective-permute-start.14 = (bf16[240,384]{1,0:T(8,128)(2,1)S(1)}, bf16[240,384]{1,0:T(8,128)(2,1)S(1)}, u32[]{:S(2)}, u32[]{:S(2)}) collective-permute-start(bf16[240,384]{1,0:T(8,128)(2,1)S(1)} %copy-done.15), channel_id=1, source_target_pairs={{0,4},{1,5},{2,6},{3,7},{4,0},{5,1},{6,2},{7,3},{8,12},{9,13},{10,... | collective-permute-start | bytes 552968 | tf_op jit(solution)/shard_map/ppermute | solution.py:24
  37.2 9.0 %collective-permute-start.8 = (bf16[2,152,384]{2,1,0:T(8,128)(2,1)S(1)}, bf16[2,152,384]{2,1,0:T(8,128)(2,1)S(1)}, u32[]{:S(2)}, u32[]{:S(2)}) collective-permute-start(bf16[2,152,384]{2,1,0:T(8,128)(2,1)S(1)} %slice.275), channel_id=1, source_target_pairs={{0,1},{1,0},{2,3},{3,2},{4,5},{5,4},{6,7},{7,6},{8,9},{9,8},{10,11... | collective-permute-start | bytes 700424 | tf_op jit(solution)/shard_map/ppermute | solution.py:24
  48.8 24.5 %collective-permute-start.28 = (bf16[192,384]{1,0:T(8,128)(2,1)S(1)}, bf16[192,384]{1,0:T(8,128)(2,1)S(1)}, u32[]{:S(2)}, u32[]{:S(2)}) collective-permute-start(bf16[192,384]{1,0:T(8,128)(2,1)S(1)} %copy-done.16), channel_id=1, source_target_pairs={{0,12},{1,13},{2,14},{3,15},{4,8},{5,9},{6,10},{7,11},{8,4},{9,5},... | collective-permute-start | bytes 442376 | tf_op jit(solution)/shard_map/ppermute | solution.py:24
  50.0 23.3 %collective-permute-start.27 = (bf16[192,384]{1,0:T(8,128)(2,1)S(1)}, bf16[192,384]{1,0:T(8,128)(2,1)S(1)}, u32[]{:S(2)}, u32[]{:S(2)}) collective-permute-start(bf16[192,384]{1,0:T(8,128)(2,1)S(1)} %copy-done.16), channel_id=1, source_target_pairs={{0,8},{1,9},{2,10},{3,11},{4,12},{5,13},{6,14},{7,15},{8,0},{9,1},... | collective-permute-start | bytes 442376 | tf_op jit(solution)/shard_map/ppermute | solution.py:24
  50.0 23.8 %collective-permute-start.26 = (bf16[192,384]{1,0:T(8,128)(2,1)S(1)}, bf16[192,384]{1,0:T(8,128)(2,1)S(1)}, u32[]{:S(2)}, u32[]{:S(2)}) collective-permute-start(bf16[192,384]{1,0:T(8,128)(2,1)S(1)} %copy-done.16), channel_id=1, source_target_pairs={{0,4},{1,5},{2,6},{3,7},{4,0},{5,1},{6,2},{7,3},{8,12},{9,13},{10,... | collective-permute-start | bytes 442376 | tf_op jit(solution)/shard_map/ppermute | solution.py:24
  53.2 17.6 %collective-permute-start.18 = (bf16[4,240,384]{2,1,0:T(8,128)(2,1)S(1)}, bf16[4,240,384]{2,1,0:T(8,128)(2,1)S(1)}, u32[]{:S(2)}, u32[]{:S(2)}) collective-permute-start(bf16[4,240,384]{2,1,0:T(8,128)(2,1)S(1)} %pad_maximum_fusion.1.refs_0_), channel_id=1, source_target_pairs={{0,2},{1,3},{2,0},{3,1},{4,6},{5,7},{6,4},{7,5},{8,10},{9,11},{10,... | collective-permute-start | bytes 2211848 | tf_op jit(solution)/shard_map/ppermute | solution.py:24
  53.8 17.3 %collective-permute-start.17 = (bf16[4,240,384]{2,1,0:T(8,128)(2,1)S(1)}, bf16[4,240,384]{2,1,0:T(8,128)(2,1)S(1)}, u32[]{:S(2)}, u32[]{:S(2)}) collective-permute-start(bf16[4,240,384]{2,1,0:T(8,128)(2,1)S(1)} %pad_maximum_fusion.1.refs_0_), channel_id=1, source_target_pairs={{0,1},{1,0},{2,3},{3,2},{4,5},{5,4},{6,7},{7,6},{8,9},{9,8},{10,11... | collective-permute-start | bytes 2211848 | tf_op jit(solution)/shard_map/ppermute | solution.py:24
  73.4 11.6 %collective-permute-start.22 = (bf16[4,240,384]{2,1,0:T(8,128)(2,1)S(1)}, bf16[4,240,384]{2,1,0:T(8,128)(2,1)}, u32[]{:S(2)}, u32[]{:S(2)}) collective-permute-start(bf16[4,240,384]{2,1,0:T(8,128)(2,1)S(1)} %collective-permute-done.17.refs_1_), channel_id=1, source_target_pairs={{0,16},{16,0},{1,17},{17,1},{2,18},{18,2},{3,19},{19,3},{4,20},{20... | collective-permute-start | bytes 2211848 | tf_op jit(solution)/shard_map/ppermute | solution.py:24
  74.0 11.0 %collective-permute-start.23 = (bf16[4,240,384]{2,1,0:T(8,128)(2,1)S(1)}, bf16[4,240,384]{2,1,0:T(8,128)(2,1)}, u32[]{:S(2)}, u32[]{:S(2)}) collective-permute-start(bf16[4,240,384]{2,1,0:T(8,128)(2,1)S(1)} %collective-permute-done.18.refs_2_), channel_id=1, source_target_pairs={{0,16},{16,0},{1,17},{17,1},{2,18},{18,2},{3,19},{19,3},{4,20},{20... | collective-permute-start | bytes 2211848 | tf_op jit(solution)/shard_map/ppermute | solution.py:24
  81.6 28.1 %collective-permute-start.33 = (bf16[4,192,384]{2,1,0:T(8,128)(2,1)S(1)}, bf16[4,192,384]{2,1,0:T(8,128)(2,1)S(1)}, u32[]{:S(2)}, u32[]{:S(2)}) collective-permute-start(bf16[4,192,384]{2,1,0:T(8,128)(2,1)S(1)} %pad_maximum_fusion.3.refs_0_), channel_id=1, source_target_pairs={{0,16},{16,0},{1,17},{17,1},{2,18},{18,2},{3,19},{19,3},{4,20},{20... | collective-permute-start | bytes 1769480 | tf_op jit(solution)/shard_map/ppermute | solution.py:24
  82.0 16.9 %collective-permute-start.30 = (bf16[4,192,384]{2,1,0:T(8,128)(2,1)S(1)}, bf16[4,192,384]{2,1,0:T(8,128)(2,1)S(1)}, u32[]{:S(2)}, u32[]{:S(2)}) collective-permute-start(bf16[4,192,384]{2,1,0:T(8,128)(2,1)S(1)} %pad_maximum_fusion.3.refs_0_), channel_id=1, source_target_pairs={{0,2},{1,3},{2,0},{3,1},{4,6},{5,7},{6,4},{7,5},{8,10},{9,11},{10,... | collective-permute-start | bytes 1769480 | tf_op jit(solution)/shard_map/ppermute | solution.py:24
  83.5 15.4 %collective-permute-start.29 = (bf16[4,192,384]{2,1,0:T(8,128)(2,1)S(1)}, bf16[4,192,384]{2,1,0:T(8,128)(2,1)S(1)}, u32[]{:S(2)}, u32[]{:S(2)}) collective-permute-start(bf16[4,192,384]{2,1,0:T(8,128)(2,1)S(1)} %pad_maximum_fusion.3.refs_0_), channel_id=1, source_target_pairs={{0,1},{1,0},{2,3},{3,2},{4,5},{5,4},{6,7},{7,6},{8,9},{9,8},{10,11... | collective-permute-start | bytes 1769480 | tf_op jit(solution)/shard_map/ppermute | solution.py:24
  99.0 10.7 %collective-permute-start.34 = (bf16[4,192,384]{2,1,0:T(8,128)(2,1)S(1)}, bf16[4,192,384]{2,1,0:T(8,128)(2,1)S(1)}, u32[]{:S(2)}, u32[]{:S(2)}) collective-permute-start(bf16[4,192,384]{2,1,0:T(8,128)(2,1)S(1)} %collective-permute-done.29.refs_1_), channel_id=1, source_target_pairs={{0,16},{16,0},{1,17},{17,1},{2,18},{18,2},{3,19},{19,3},{4,20},{20... | collective-permute-start | bytes 1769480 | tf_op jit(solution)/shard_map/ppermute | solution.py:24
  99.1 9.5 %collective-permute-start.32 = (bf16[2,192,384]{2,1,0:T(8,128)(2,1)S(1)}, bf16[2,192,384]{2,1,0:T(8,128)(2,1)S(1)}, u32[]{:S(2)}, u32[]{:S(2)}) collective-permute-start(bf16[2,192,384]{2,1,0:T(8,128)(2,1)S(1)} %slice.282), channel_id=1, source_target_pairs={{0,1},{1,0},{2,3},{3,2},{4,5},{5,4},{6,7},{7,6},{8,9},{9,8},{10,11... | collective-permute-start | bytes 884744 | tf_op jit(solution)/shard_map/ppermute | solution.py:24
  100.3 9.5 %collective-permute-start.35 = (bf16[4,192,384]{2,1,0:T(8,128)(2,1)S(1)}, bf16[4,192,384]{2,1,0:T(8,128)(2,1)S(1)}, u32[]{:S(2)}, u32[]{:S(2)}) collective-permute-start(bf16[4,192,384]{2,1,0:T(8,128)(2,1)S(1)} %collective-permute-done.30.refs_2_), channel_id=1, source_target_pairs={{0,16},{16,0},{1,17},{17,1},{2,18},{18,2},{3,19},{19,3},{4,20},{20... | collective-permute-start | bytes 1769480 | tf_op jit(solution)/shard_map/ppermute | solution.py:24
  100.5 9.2 %collective-permute-start.31 = (bf16[2,192,384]{2,1,0:T(8,128)(2,1)S(1)}, bf16[2,192,384]{2,1,0:T(8,128)(2,1)S(1)}, u32[]{:S(2)}, u32[]{:S(2)}) collective-permute-start(bf16[2,192,384]{2,1,0:T(8,128)(2,1)S(1)} %slice.281), channel_id=1, source_target_pairs={{0,2},{1,3},{2,0},{3,1},{4,6},{5,7},{6,4},{7,5},{8,10},{9,11},{10,... | collective-permute-start | bytes 884744 | tf_op jit(solution)/shard_map/ppermute | solution.py:24
  138.9 11.4 %collective-permute-start.42 = (bf16[3,4,96,768]{3,2,1,0:T(8,128)(2,1)}, bf16[3,4,96,768]{3,2,1,0:T(8,128)(2,1)S(1)}, u32[]{:S(2)}, u32[]{:S(2)}) collective-permute-start(bf16[3,4,96,768]{3,2,1,0:T(8,128)(2,1)} %get-tuple-element.173), channel_id=1, source_target_pairs={{0,16},{16,0},{1,17},{17,1},{2,18},{18,2},{3,19},{19,3},{4,20},{20... | collective-permute-start | bytes 5308424 | tf_op jit(solution)/shard_map/ppermute | solution.py:24
  140.5 9.9 %collective-permute-start.41 = (bf16[2,96,768]{2,1,0:T(8,128)(2,1)S(1)}, bf16[2,96,768]{2,1,0:T(8,128)(2,1)S(1)}, u32[]{:S(2)}, u32[]{:S(2)}) collective-permute-start(bf16[2,96,768]{2,1,0:T(8,128)(2,1)S(1)} %get-tuple-element.250), channel_id=1, source_target_pairs={{0,2},{1,3},{2,0},{3,1},{4,6},{5,7},{6,4},{7,5},{8,10},{9,11},{10,... | collective-permute-start | bytes 884744 | tf_op jit(solution)/shard_map/ppermute | solution.py:24
  141.1 9.2 %collective-permute-start.40 = (bf16[2,96,768]{2,1,0:T(8,128)(2,1)S(1)}, bf16[2,96,768]{2,1,0:T(8,128)(2,1)S(1)}, u32[]{:S(2)}, u32[]{:S(2)}) collective-permute-start(bf16[2,96,768]{2,1,0:T(8,128)(2,1)S(1)} %get-tuple-element.251), channel_id=1, source_target_pairs={{0,1},{1,0},{2,3},{3,2},{4,5},{5,4},{6,7},{7,6},{8,9},{9,8},{10,11... | collective-permute-start | bytes 884744 | tf_op jit(solution)/shard_map/ppermute | solution.py:24
  151.6 20.6 %collective-permute-start.45 = (bf16[4,96,768]{2,1,0:T(8,128)(2,1)S(1)}, bf16[4,96,768]{2,1,0:T(8,128)(2,1)S(1)}, u32[]{:S(2)}, u32[]{:S(2)}) collective-permute-start(bf16[4,96,768]{2,1,0:T(8,128)(2,1)S(1)} %get-tuple-element.244), channel_id=1, source_target_pairs={{0,2},{1,3},{2,0},{3,1},{4,6},{5,7},{6,4},{7,5},{8,10},{9,11},{10,... | collective-permute-start | bytes 1769480 | tf_op jit(solution)/shard_map/ppermute | solution.py:24
  153.1 19.2 %collective-permute-start.44 = (bf16[4,96,768]{2,1,0:T(8,128)(2,1)S(1)}, bf16[4,96,768]{2,1,0:T(8,128)(2,1)S(1)}, u32[]{:S(2)}, u32[]{:S(2)}) collective-permute-start(bf16[4,96,768]{2,1,0:T(8,128)(2,1)S(1)} %get-tuple-element.245), channel_id=1, source_target_pairs={{0,1},{1,0},{2,3},{3,2},{4,5},{5,4},{6,7},{7,6},{8,9},{9,8},{10,11... | collective-permute-start | bytes 1769480 | tf_op jit(solution)/shard_map/ppermute | solution.py:24
  174.7 14.1 %collective-permute-start.49 = (bf16[3,4,24,3840]{3,2,1,0:T(8,128)(2,1)}, bf16[3,4,24,3840]{3,2,1,0:T(8,128)(2,1)S(1)}, u32[]{:S(2)}, u32[]{:S(2)}) collective-permute-start(bf16[3,4,24,3840]{3,2,1,0:T(8,128)(2,1)} %get-tuple-element.189), channel_id=1, source_target_pairs={{0,16},{16,0},{1,17},{17,1},{2,18},{18,2},{3,19},{19,3},{4,20},{20... | collective-permute-start | bytes 6635528 | tf_op jit(solution)/shard_map/ppermute | solution.py:24
  177.5 10.7 %collective-permute-start.48 = (bf16[2,24,3840]{2,1,0:T(8,128)(2,1)S(1)}, bf16[2,24,3840]{2,1,0:T(8,128)(2,1)S(1)}, u32[]{:S(2)}, u32[]{:S(2)}) collective-permute-start(bf16[2,24,3840]{2,1,0:T(8,128)(2,1)S(1)} %get-tuple-element.246), channel_id=1, source_target_pairs={{0,2},{1,3},{2,0},{3,1},{4,6},{5,7},{6,4},{7,5},{8,10},{9,11},{10,... | collective-permute-start | bytes 1105928 | tf_op jit(solution)/shard_map/ppermute | solution.py:24
  178.1 10.7 %collective-permute-start.47 = (bf16[2,24,3840]{2,1,0:T(8,128)(2,1)S(1)}, bf16[2,24,3840]{2,1,0:T(8,128)(2,1)S(1)}, u32[]{:S(2)}, u32[]{:S(2)}) collective-permute-start(bf16[2,24,3840]{2,1,0:T(8,128)(2,1)S(1)} %get-tuple-element.247), channel_id=1, source_target_pairs={{0,1},{1,0},{2,3},{3,2},{4,5},{5,4},{6,7},{7,6},{8,9},{9,8},{10,11... | collective-permute-start | bytes 1105928 | tf_op jit(solution)/shard_map/ppermute | solution.py:24
  180.9 22.8 %collective-permute-start.54 = (bf16[96,768]{1,0:T(8,128)(2,1)S(1)}, bf16[96,768]{1,0:T(8,128)(2,1)}, u32[]{:S(2)}, u32[]{:S(2)}) collective-permute-start(bf16[96,768]{1,0:T(8,128)(2,1)S(1)} %get-tuple-element.236), channel_id=1, source_target_pairs={{0,12},{1,13},{2,14},{3,15},{4,8},{5,9},{6,10},{7,11},{8,4},{9,5},... | collective-permute-start | bytes 442376 | tf_op jit(solution)/shard_map/ppermute | solution.py:24
  182.1 23.2 %collective-permute-start.53 = (bf16[96,768]{1,0:T(8,128)(2,1)S(1)}, bf16[96,768]{1,0:T(8,128)(2,1)S(1)}, u32[]{:S(2)}, u32[]{:S(2)}) collective-permute-start(bf16[96,768]{1,0:T(8,128)(2,1)S(1)} %get-tuple-element.237), channel_id=1, source_target_pairs={{0,8},{1,9},{2,10},{3,11},{4,12},{5,13},{6,14},{7,15},{8,0},{9,1},... | collective-permute-start | bytes 442376 | tf_op jit(solution)/shard_map/ppermute | solution.py:24
  188.2 17.1 %collective-permute-start.52 = (bf16[96,768]{1,0:T(8,128)(2,1)S(1)}, bf16[96,768]{1,0:T(8,128)(2,1)S(1)}, u32[]{:S(2)}, u32[]{:S(2)}) collective-permute-start(bf16[96,768]{1,0:T(8,128)(2,1)S(1)} %get-tuple-element.238), channel_id=1, source_target_pairs={{0,4},{1,5},{2,6},{3,7},{4,0},{5,1},{6,2},{7,3},{8,12},{9,13},{10,... | collective-permute-start | bytes 442376 | tf_op jit(solution)/shard_map/ppermute | solution.py:24
  190.3 17.5 %collective-permute-start.51 = (bf16[4,24,3840]{2,1,0:T(8,128)(2,1)S(1)}, bf16[4,24,3840]{2,1,0:T(8,128)(2,1)S(1)}, u32[]{:S(2)}, u32[]{:S(2)}) collective-permute-start(bf16[4,24,3840]{2,1,0:T(8,128)(2,1)S(1)} %get-tuple-element.239), channel_id=1, source_target_pairs={{0,2},{1,3},{2,0},{3,1},{4,6},{5,7},{6,4},{7,5},{8,10},{9,11},{10,... | collective-permute-start | bytes 2211848 | tf_op jit(solution)/shard_map/ppermute | solution.py:24
  191.4 17.3 %collective-permute-start.50 = (bf16[4,24,3840]{2,1,0:T(8,128)(2,1)S(1)}, bf16[4,24,3840]{2,1,0:T(8,128)(2,1)}, u32[]{:S(2)}, u32[]{:S(2)}) collective-permute-start(bf16[4,24,3840]{2,1,0:T(8,128)(2,1)S(1)} %get-tuple-element.240), channel_id=1, source_target_pairs={{0,1},{1,0},{2,3},{3,2},{4,5},{5,4},{6,7},{7,6},{8,9},{9,8},{10,11... | collective-permute-start | bytes 2211848 | tf_op jit(solution)/shard_map/ppermute | solution.py:24
  203.7 24.1 %collective-permute-start.58 = (f32[16,2304]{1,0:T(8,128)S(1)}, f32[16,2304]{1,0:T(8,128)S(1)}, u32[]{:S(2)}, u32[]{:S(2)}) collective-permute-start(f32[16,2304]{1,0:T(8,128)S(1)} %fusion.35), channel_id=1, source_target_pairs={{0,4},{1,5},{2,6},{3,7},{4,0},{5,1},{6,2},{7,3},{8,12},{9,13},{10,... | collective-permute-start | bytes 442376 | tf_op jit(solution)/shard_map/ppermute | solution.py:24
  210.3 17.5 %collective-permute-start.57 = (bf16[24,3840]{1,0:T(8,128)(2,1)S(1)}, bf16[24,3840]{1,0:T(8,128)(2,1)S(1)}, u32[]{:S(2)}, u32[]{:S(2)}) collective-permute-start(bf16[24,3840]{1,0:T(8,128)(2,1)S(1)} %get-tuple-element.233), channel_id=1, source_target_pairs={{0,12},{1,13},{2,14},{3,15},{4,8},{5,9},{6,10},{7,11},{8,4},{9,5},... | collective-permute-start | bytes 552968 | tf_op jit(solution)/shard_map/ppermute | solution.py:24
  211.5 16.3 %collective-permute-start.56 = (bf16[24,3840]{1,0:T(8,128)(2,1)S(1)}, bf16[24,3840]{1,0:T(8,128)(2,1)S(1)}, u32[]{:S(2)}, u32[]{:S(2)}) collective-permute-start(bf16[24,3840]{1,0:T(8,128)(2,1)S(1)} %get-tuple-element.234), channel_id=1, source_target_pairs={{0,8},{1,9},{2,10},{3,11},{4,12},{5,13},{6,14},{7,15},{8,0},{9,1},... | collective-permute-start | bytes 552968 | tf_op jit(solution)/shard_map/ppermute | solution.py:24
  212.7 15.1 %collective-permute-start.55 = (bf16[24,3840]{1,0:T(8,128)(2,1)S(1)}, bf16[24,3840]{1,0:T(8,128)(2,1)}, u32[]{:S(2)}, u32[]{:S(2)}) collective-permute-start(bf16[24,3840]{1,0:T(8,128)(2,1)S(1)} %get-tuple-element.235), channel_id=1, source_target_pairs={{0,4},{1,5},{2,6},{3,7},{4,0},{5,1},{6,2},{7,3},{8,12},{9,13},{10,... | collective-permute-start | bytes 552968 | tf_op jit(solution)/shard_map/ppermute | solution.py:24
  230.6 10.4 %collective-permute-start.63 = (bf16[3,4,24,2432]{3,2,1,0:T(8,128)(2,1)}, bf16[3,4,24,2432]{3,2,1,0:T(8,128)(2,1)}, u32[]{:S(2)}, u32[]{:S(2)}) collective-permute-start(bf16[3,4,24,2432]{3,2,1,0:T(8,128)(2,1)} %get-tuple-element.206), channel_id=1, source_target_pairs={{0,16},{16,0},{1,17},{17,1},{2,18},{18,2},{3,19},{19,3},{4,20},{20... | collective-permute-start | bytes 4202504 | tf_op jit(solution)/shard_map/ppermute | solution.py:24
  236.1 11.4 %collective-permute-start.69 = (f32[16,2304]{1,0:T(8,128)S(1)}, f32[16,2304]{1,0:T(8,128)S(1)}, u32[]{:S(2)}, u32[]{:S(2)}) collective-permute-start(f32[16,2304]{1,0:T(8,128)S(1)} %add.513), channel_id=1, source_target_pairs={{0,8},{1,9},{2,10},{3,11},{4,12},{5,13},{6,14},{7,15},{8,0},{9,1},... | collective-permute-start | bytes 442376 | tf_op jit(solution)/shard_map/ppermute | solution.py:24
  241.0 20.7 %collective-permute-start.62 = (bf16[8,128,768]{2,1,0:T(8,128)(2,1)}, bf16[8,128,768]{2,1,0:T(8,128)(2,1)S(1)}, u32[]{:S(2)}, u32[]{:S(2)}) collective-permute-start(bf16[8,128,768]{2,1,0:T(8,128)(2,1)} %get-tuple-element.204), channel_id=1, source_target_pairs={{0,16},{16,0},{1,17},{17,1},{2,18},{18,2},{3,19},{19,3},{4,20},{20... | collective-permute-start | bytes 4718600 | tf_op jit(solution)/shard_map/ppermute | solution.py:24
  242.5 13.6 %collective-permute-start.64 = (bf16[4,24,2432]{2,1,0:T(8,128)(2,1)S(1)}, bf16[4,24,2432]{2,1,0:T(8,128)(2,1)S(1)}, u32[]{:S(2)}, u32[]{:S(2)}) collective-permute-start(bf16[4,24,2432]{2,1,0:T(8,128)(2,1)S(1)} %get-tuple-element.248), channel_id=1, source_target_pairs={{0,1},{1,0},{2,3},{3,2},{4,5},{5,4},{6,7},{7,6},{8,9},{9,8},{10,11... | collective-permute-start | bytes 1400840 | tf_op jit(solution)/shard_map/ppermute | solution.py:24
  243.1 12.9 %collective-permute-start.65 = (bf16[4,24,2432]{2,1,0:T(8,128)(2,1)S(1)}, bf16[4,24,2432]{2,1,0:T(8,128)(2,1)S(1)}, u32[]{:S(2)}, u32[]{:S(2)}) collective-permute-start(bf16[4,24,2432]{2,1,0:T(8,128)(2,1)S(1)} %get-tuple-element.249), channel_id=1, source_target_pairs={{0,2},{1,3},{2,0},{3,1},{4,6},{5,7},{6,4},{7,5},{8,10},{9,11},{10,... | collective-permute-start | bytes 1400840 | tf_op jit(solution)/shard_map/ppermute | solution.py:24
  247.5 16.2 %collective-permute-start.70 = (f32[16,2304]{1,0:T(8,128)S(1)}, f32[16,2304]{1,0:T(8,128)S(1)}, u32[]{:S(2)}, u32[]{:S(2)}) collective-permute-start(f32[16,2304]{1,0:T(8,128)S(1)} %add.514), channel_id=1, source_target_pairs={{0,1},{1,0},{2,3},{3,2},{4,5},{5,4},{6,7},{7,6},{8,9},{9,8},{10,11... | collective-permute-start | bytes 442376 | tf_op jit(solution)/shard_map/ppermute | solution.py:24
  259.0 10.7 %collective-permute-start.67 = (bf16[24,2432]{1,0:T(8,128)(2,1)S(1)}, bf16[24,2432]{1,0:T(8,128)(2,1)S(1)}, u32[]{:S(2)}, u32[]{:S(2)}) collective-permute-start(bf16[24,2432]{1,0:T(8,128)(2,1)S(1)} %get-tuple-element.242), channel_id=1, source_target_pairs={{0,8},{1,9},{2,10},{3,11},{4,12},{5,13},{6,14},{7,15},{8,0},{9,1},... | collective-permute-start | bytes 350216 | tf_op jit(solution)/shard_map/ppermute | solution.py:24
  259.5 10.3 %collective-permute-start.66 = (bf16[24,2432]{1,0:T(8,128)(2,1)S(1)}, bf16[24,2432]{1,0:T(8,128)(2,1)S(1)}, u32[]{:S(2)}, u32[]{:S(2)}) collective-permute-start(bf16[24,2432]{1,0:T(8,128)(2,1)S(1)} %get-tuple-element.243), channel_id=1, source_target_pairs={{0,4},{1,5},{2,6},{3,7},{4,0},{5,1},{6,2},{7,3},{8,12},{9,13},{10,... | collective-permute-start | bytes 350216 | tf_op jit(solution)/shard_map/ppermute | solution.py:24
  (71 other events, 512.2 us)

commit v5 on v4

--- a/solution.py
+++ b/solution.py
@@ -151,7 +151,7 @@
 TILE = 256
 PACK = 16
 PAIR = 2 * HEAD_DIM
-GROUP = 3
+GROUP = 6
 Q_BIAS, V_BIAS, O_BIAS, GAIN_1, SHIFT_1, D_BIAS, GAIN_2, SHIFT_2 = range(8)
 
 
@@ -972,14 +972,14 @@
             partial(attend_kernel, 10), meta,
             (Scalars(homes), vec, Flat(embeddings[0]), Flat(other_tokens), *map(Flat, pieces_first)), both,
             scratch + [pltpu.VMEM(full[0], b16), pltpu.SemaphoreType.DMA((30,))],
-            micros=16,
+            micros=4,
         )
     else:
         (proj_qkv,) = pieces_first
         xs, qkv, probs, ctx = call(
             partial(attend_kernel, 0), meta, (Scalars(homes), vec, Flat(embeddings[0]), Flat(other_tokens), proj_qkv), sinks,
             scratch,
-            micros=16,
+            micros=4,
         )
 
     wide, slim, thin = shape(b16, rows, hidden), shape(f32, rows, width), shape(f32, rows, 128)

time: 275 us -> 273 us (level)
    unnamed x96 -> x90, local copies, waits for them, and re-layouts: 5.62 us -> 5.48 us
  transfers between devices with their start and end apart: 72 -> 72, of which waited for: 26 -> 28; matrix products, arithmetic and copies ran while one was open for 12% -> 13% of each run, Pallas kernels for 30% -> 29%
where the time goes in v5:
time: 273 us; the launch traced here: 272 us
  Pallas kernels  103 us (38%)
  waiting for transfers between devices  65.2 us (24%)
  starting transfers between devices  60 us (22%)
  other arithmetic  27.3 us (10%)
  local copies, waits for them, and re-layouts  14.1 us (5%)
    pallas_call x9, Pallas kernels, call(): pl.pallas_call(kernel, out_shape=[bare(o) for o in outs], grid_spec=pltpu...  101 us
    ppermute x72, waiting for transfers between devices, swap(): lax.ppermute(x, axis, [(i, i ^ k) for i in range(lax.axis_size(axis))])  65.2 us
    ppermute x72, starting transfers between devices, swap(): lax.ppermute(x, axis, [(i, i ^ k) for i in range(lax.axis_size(axis))])  60 us
    unnamed x90, local copies, waits for them, and re-layouts  5.48 us
  transfers between devices with their start and end apart: 72, of which 28 were waited for; matrix products, arithmetic and copies ran while one was open for 13% of the time, Pallas kernels for 29%

profile of v5, /device:TPU:0, one launch (start us, length us, event | category | flops | bytes accessed | tf_op | source)
XLA Modules:
  0.0 271.6 jit_solution(15157804402118248163)
XLA Ops:
  4.3 2.7 shard_map.305
  7.0 4.6 %collective-permute-start.3 = (bf16[152,384]{1,0:T(8,128)(2,1)}, bf16[152,384]{1,0:T(8,128)(2,1)S(1)}, u32[]{:S(2)}, u32[]{:S(2)}) collective-permute-start(bf16[152,384]{1,0:T(8,128)(2,1)} %get-tuple-element.123), channel_id=1, source_target_pairs={{0,12},{1,13},{2,14},{3,15},{4,8},{5,9},{6,10},{7,11},{8,4},{9,5},... | collective-permute-start | bytes 350216 | tf_op jit(solution)/shard_map/ppermute | solution.py:24
  15.9 6.3 %collective-permute-done.2 = bf16[152,384]{1,0:T(8,128)(2,1)S(1)} collective-permute-done((bf16[152,384]{1,0:T(8,128)(2,1)}, bf16[152,384]{1,0:T(8,128)(2,1)S(1)}, u32[]{:S(2)}, u32[]{:S(2)}) %collective-permute-start.2) | collective-permute-done | bytes 116768 | tf_op jit(solution)/shard_map/ppermute | solution.py:24
  23.6 1.6 collective-permute-start.6
  25.2 1.5 collective-permute-start.5
  28.6 2.5 collective-permute-start.16
  31.1 1.9 collective-permute-start.14
  33.0 2.9 %collective-permute-done.6.refs_2_ = bf16[4,152,384]{2,1,0:T(8,128)(2,1)S(1)} collective-permute-done((bf16[4,152,384]{2,1,0:T(8,128)(2,1)S(1)}, bf16[4,152,384]{2,1,0:T(8,128)(2,1)S(1)}, u32[]{:S(2)}, u32[]{:S(2)}) %collective-permute-start.6) | collective-permute-done | bytes 466976 | tf_op jit(solution)/shard_map/ppermute | solution.py:24
  38.3 1.6 collective-permute-start.8
  41.2 4.5 %collective-permute-done.15 = bf16[240,384]{1,0:T(8,128)(2,1)S(1)} collective-permute-done((bf16[240,384]{1,0:T(8,128)(2,1)S(1)}, bf16[240,384]{1,0:T(8,128)(2,1)S(1)}, u32[]{:S(2)}, u32[]{:S(2)}) %collective-permute-start.15) | collective-permute-done | bytes 184352 | tf_op jit(solution)/shard_map/ppermute | solution.py:24
  50.2 1.5 collective-permute-start.28
  51.7 2.9 %collective-permute-start.26 = (bf16[192,384]{1,0:T(8,128)(2,1)S(1)}, bf16[192,384]{1,0:T(8,128)(2,1)S(1)}, u32[]{:S(2)}, u32[]{:S(2)}) collective-permute-start(bf16[192,384]{1,0:T(8,128)(2,1)S(1)} %copy-done.16), channel_id=1, source_target_pairs={{0,4},{1,5},{2,6},{3,7},{4,0},{5,1},{6,2},{7,3},{8,12},{9,13},{10,... | collective-permute-start | bytes 442376 | tf_op jit(solution)/shard_map/ppermute | solution.py:24
  54.6 12.8 %shard_map.306 = (bf16[4,192,2304]{2,1,0:T(8,128)(2,1)}, bf16[1152,768]{1,0:T(8,128)(2,1)}, bf16[1152,2304]{1,0:T(8,128)(2,1)}, bf16[8,1536,128]{2,1,0:T(8,128)(2,1)}, bf16[1152,768]{1,0:T(8,128)(2,1)}) custom-call(s32[8]{0:T(128)} %copy-done.31, s32[8]{0:T(128)} %select_reduce_fusion.1.offs, s32[1]{0:T(128)S(6)} %select_n.135.tiles, s32[3]{0:T(128)} %pad_add_fusion.place, ...), custom_call_target="tpu_custom_call" | custom-call | flops 4600000000 | bytes 22438080 | tf_op jit(solution)/shard_map/pallas_call | solution.py:849
  68.1 1.6 collective-permute-start.19
  71.8 5.9 %collective-permute-done.20.refs_4_ = bf16[2,240,384]{2,1,0:T(8,128)(2,1)} collective-permute-done((bf16[2,240,384]{2,1,0:T(8,128)(2,1)S(1)}, bf16[2,240,384]{2,1,0:T(8,128)(2,1)}, u32[]{:S(2)}, u32[]{:S(2)}) %collective-permute-start.20) | collective-permute-done | bytes 368672 | tf_op jit(solution)/shard_map/ppermute | solution.py:24
  81.8 13.9 %shard_map.307 = (bf16[4,192,768]{2,1,0:T(8,128)(2,1)}, bf16[4,192,3072]{2,1,0:T(8,128)(2,1)}, bf16[1024,3072]{1,0:T(8,128)(2,1)}, bf16[1024,3072]{1,0:T(8,128)(...) custom-call(s32[8]{0:T(128)} %copy-done.31, s32[8]{0:T(128)} %select_reduce_fusion.1.offs, s32[1]{0:T(128)S(6)} %select_n.135.tiles, ...), custom_call_target="tpu_custom_call" | custom-call | flops 16099999744 | bytes 31625216 | tf_op jit(solution)/shard_map/pallas_call | solution.py:849
  97.5 1.4 collective-permute-start.31
  98.9 6.8 %collective-permute-done.32.refs_4_ = bf16[2,192,384]{2,1,0:T(8,128)(2,1)S(1)} collective-permute-done((bf16[2,192,384]{2,1,0:T(8,128)(2,1)S(1)}, bf16[2,192,384]{2,1,0:T(8,128)(2,1)S(1)}, u32[]{:S(2)}, u32[]{:S(2)}) %collective-permute-start.32) | collective-permute-done | bytes 294944 | tf_op jit(solution)/shard_map/ppermute | solution.py:24
  109.0 10.7 %shard_map.308 = (bf16[4,768,768]{2,1,0:T(8,128)(2,1)}, f32[1024,768]{1,0:T(8,128)}, f32[1024,128]{1,0:T(8,128)}, f32[8,768]{1,0:T(8,128)}) custom-call(s32[8]{0:T(128)} %copy-done.31, s32[8]{0:T(128)} %select_reduce_fusion.1.offs, s32[1]{0:T(128)S(6)} %select_n.135.tiles, s32[3]{0:T(128)} %pad_add_fusion.place, f32[1024,768]{1,0:T(8,128)} %get-tuple-element.149.n1, ...), custom_call_target="tpu_custom_call" | custom-call | flops 11500000256 | bytes 22593536 | tf_op jit(solution)/shard_map/pallas_call | solution.py:849
  122.5 11.2 %shard_map.309 = (f32[1024,768]{1,0:T(8,128)}, bf16[4,4,96,768]{3,2,1,0:T(8,128)(2,1)}, bf16[4,96,768]{2,1,0:T(8,128)(2,1)}, bf16[3,4,96,768]{3,2,1,0:T(8,128)(2...) custom-call(s32[8]{0:T(128)} %copy-done.31, s32[8]{0:T(128)} %select_reduce_fusion.1.offs, ...), custom_call_target="tpu_custom_call" | custom-call | flops 12650000384 | bytes 18050284 | tf_op jit(solution)/shard_map/pallas_call | solution.py:849
  134.1 1.8 collective-permute-done.39
  137.5 1.5 collective-permute-start.41
  139.9 8.3 %shard_map.310 = (bf16[1024,3072]{1,0:T(8,128)(2,1)}, f32[8,768]{1,0:T(8,128)}) custom-call(s32[8]{0:T(128)} %copy-done.31, s32[8]{0:T(128)} %select_reduce_fusion.1.offs, s32[1]{0:T(128)S(6)} %select_n.135.tiles, s32[3]{0:T(128)} %pad_add_fusion.place, f32[1024,768]{1,0:T(8,128)} %get-tuple-element.167.sum_grad, ...), custom_call_target="tpu_custom_call" | custom-call | flops 9200000000 | bytes 20471808 | tf_op jit(solution)/shard_map/pallas_call | solution.py:849
  151.2 18.1 %shard_map.311 = (f32[1024,768]{1,0:T(8,128)}, bf16[1152,768]{1,0:T(8,128)(2,1)}, bf16[4,4,24,3840]{3,2,1,0:T(8,128)(2,1)}, bf16[4,24,3840]{2,1,0:T(8,128)(2,1)}...) custom-call(s32[8]{0:T(128)} %copy-done.31, s32[8]{0:T(128)} %select_reduce_fusion.1.offs, s32[1]{0:T(128)S(6)} %select_n.135.tiles, ...), custom_call_target="tpu_custom_call" | custom-call | flops 23000000512 | bytes 31637504 | tf_op jit(solution)/shard_map/pallas_call | solution.py:849
  169.4 2.4 collective-permute-done.46
  173.2 1.4 fusion.6
  174.6 1.5 collective-permute-start.48
  177.1 1.6 fusion.21
  178.7 1.8 collective-permute-start.54
  180.5 4.8 %collective-permute-done.48 = bf16[2,24,3840]{2,1,0:T(8,128)(2,1)S(1)} collective-permute-done((bf16[2,24,3840]{2,1,0:T(8,128)(2,1)S(1)}, bf16[2,24,3840]{2,1,0:T(8,128)(2,1)S(1)}, u32[]{:S(2)}, u32[]{:S(2)}) %collective-permute-start.48) | collective-permute-done | bytes 368672 | tf_op jit(solution)/shard_map/ppermute | solution.py:24
  189.2 10.4 %shard_map.312 = (bf16[1152,2304]{1,0:T(8,128)(2,1)}, f32[8,768]{1,0:T(8,128)}) custom-call(s32[8]{0:T(128)} %copy-done.31, s32[8]{0:T(128)} %select_reduce_fusion.1.offs, s32[1]{0:T(128)S(6)} %select_n.135.tiles, s32[3]{0:T(128)} %pad_add_fusion.place, bf16[1152,2304]{1,0:T(8,128)(2,1)} %get-tuple-element.163.qkv_h, ...), custom_call_target="tpu_custom_call" | custom-call | flops 16099999744 | bytes 15556608 | tf_op jit(solution)/shard_map/pallas_call | solution.py:849
  199.6 1.8 collective-permute-start.58
  201.4 3.9 %collective-permute-done.51 = bf16[4,24,3840]{2,1,0:T(8,128)(2,1)S(1)} collective-permute-done((bf16[4,24,3840]{2,1,0:T(8,128)(2,1)S(1)}, bf16[4,24,3840]{2,1,0:T(8,128)(2,1)S(1)}, u32[]{:S(2)}, u32[]{:S(2)}) %collective-permute-start.51) | collective-permute-done | bytes 737312 | tf_op jit(solution)/shard_map/ppermute | solution.py:24
  205.8 1.6 fusion.15
  207.4 2.5 collective-permute-start.57
  211.8 13.1 %shard_map.313 = (f32[8,128,768]{2,1,0:T(8,128)}, bf16[8,128,768]{2,1,0:T(8,128)(2,1)}, bf16[4,4,24,2432]{3,2,1,0:T(8,128)(2,1)}, bf16[4,24,2432]{2,1,0:T(8,128)(2,1)}, bf16[3,4,24,2432]{3,2,1,0:T(8,128)(2,1)}) custom-call(s32[8]{0:T(128)} %copy-done.31, s32[8]{0:T(128)} %select_reduce_fusion.1.offs, s32[1]{0:T(128)S(6)} %select_n.135.tiles, ...), custom_call_target="tpu_custom_call" | custom-call | flops 18400000000 | bytes 22241472 | tf_op jit(solution)/shard_map/pallas_call | solution.py:849
  225.6 2.2 collective-permute-done.59
  227.9 1.5 fusion.10
  231.8 2.1 fusion.20
  235.1 2.3 collective-permute-done.61
  238.5 1.5 fusion.5
  241.6 1.5 fusion.14
  245.8 7.8 %collective-permute-done.64 = bf16[4,24,2432]{2,1,0:T(8,128)(2,1)S(1)} collective-permute-done((bf16[4,24,2432]{2,1,0:T(8,128)(2,1)S(1)}, bf16[4,24,2432]{2,1,0:T(8,128)(2,1)S(1)}, u32[]{:S(2)}, u32[]{:S(2)}) %collective-permute-start.64) | collective-permute-done | bytes 466976 | tf_op jit(solution)/shard_map/ppermute | solution.py:24
  255.0 1.9 collective-permute-start.68
  256.9 2.6 collective-permute-start.66
  259.5 2.0 convert_add_fusion
  263.0 3.9 %collective-permute-done.67 = bf16[24,2432]{1,0:T(8,128)(2,1)S(1)} collective-permute-done((bf16[24,2432]{1,0:T(8,128)(2,1)S(1)}, bf16[24,2432]{1,0:T(8,128)(2,1)S(1)}, u32[]{:S(2)}, u32[]{:S(2)}) %collective-permute-start.67) | collective-permute-done | bytes 116768 | tf_op jit(solution)/shard_map/ppermute | solution.py:24
  269.9 1.7 shard_map.314
  (269 shorter events, 63.2 us)
Async XLA Ops:
  0.7 21.6 %collective-permute-start.4 = (bf16[8,128,768]{2,1,0:T(8,128)(2,1)}, bf16[8,128,768]{2,1,0:T(8,128)(2,1)S(1)}, u32[]{:S(2)}, u32[]{:S(2)}) collective-permute-start(bf16[8,128,768]{2,1,0:T(8,128)(2,1)} %bitcast.252), channel_id=1, source_target_pairs={{0,16},{16,0},{1,17},{17,1},{2,18},{18,2},{3,19},{19,3},{4,20},{20... | collective-permute-start | bytes 4718600 | tf_op jit(solution)/shard_map/ppermute | solution.py:24
  11.6 10.7 %collective-permute-start.2 = (bf16[152,384]{1,0:T(8,128)(2,1)}, bf16[152,384]{1,0:T(8,128)(2,1)S(1)}, u32[]{:S(2)}, u32[]{:S(2)}) collective-permute-start(bf16[152,384]{1,0:T(8,128)(2,1)} %get-tuple-element.123), channel_id=1, source_target_pairs={{0,8},{1,9},{2,10},{3,11},{4,12},{5,13},{6,14},{7,15},{8,0},{9,1},... | collective-permute-start | bytes 350216 | tf_op jit(solution)/shard_map/ppermute | solution.py:24
  11.6 10.7 %collective-permute-start.1 = (bf16[152,384]{1,0:T(8,128)(2,1)}, bf16[152,384]{1,0:T(8,128)(2,1)S(1)}, u32[]{:S(2)}, u32[]{:S(2)}) collective-permute-start(bf16[152,384]{1,0:T(8,128)(2,1)} %get-tuple-element.123), channel_id=1, source_target_pairs={{0,4},{1,5},{2,6},{3,7},{4,0},{5,1},{6,2},{7,3},{8,12},{9,13},{10,... | collective-permute-start | bytes 350216 | tf_op jit(solution)/shard_map/ppermute | solution.py:24
  23.6 12.4 %collective-permute-start.6 = (bf16[4,152,384]{2,1,0:T(8,128)(2,1)S(1)}, bf16[4,152,384]{2,1,0:T(8,128)(2,1)S(1)}, u32[]{:S(2)}, u32[]{:S(2)}) collective-permute-start(bf16[4,152,384]{2,1,0:T(8,128)(2,1)S(1)} %pad_maximum_fusion.5.refs_0_), channel_id=1, source_target_pairs={{0,2},{1,3},{2,0},{3,1},{4,6},{5,7},{6,4},{7,5},{8,10},{9,11},{10,... | collective-permute-start | bytes 1400840 | tf_op jit(solution)/shard_map/ppermute | solution.py:24
  25.2 12.1 %collective-permute-start.5 = (bf16[4,152,384]{2,1,0:T(8,128)(2,1)S(1)}, bf16[4,152,384]{2,1,0:T(8,128)(2,1)}, u32[]{:S(2)}, u32[]{:S(2)}) collective-permute-start(bf16[4,152,384]{2,1,0:T(8,128)(2,1)S(1)} %pad_maximum_fusion.5.refs_0_), channel_id=1, source_target_pairs={{0,1},{1,0},{2,3},{3,2},{4,5},{5,4},{6,7},{7,6},{8,9},{9,8},{10,11... | collective-permute-start | bytes 1400840 | tf_op jit(solution)/shard_map/ppermute | solution.py:24
  28.6 12.5 %collective-permute-start.16 = (bf16[240,384]{1,0:T(8,128)(2,1)S(1)}, bf16[240,384]{1,0:T(8,128)(2,1)S(1)}, u32[]{:S(2)}, u32[]{:S(2)}) collective-permute-start(bf16[240,384]{1,0:T(8,128)(2,1)S(1)} %copy-done.15), channel_id=1, source_target_pairs={{0,12},{1,13},{2,14},{3,15},{4,8},{5,9},{6,10},{7,11},{8,4},{9,5},... | collective-permute-start | bytes 552968 | tf_op jit(solution)/shard_map/ppermute | solution.py:24
  31.1 14.7 %collective-permute-start.15 = (bf16[240,384]{1,0:T(8,128)(2,1)S(1)}, bf16[240,384]{1,0:T(8,128)(2,1)S(1)}, u32[]{:S(2)}, u32[]{:S(2)}) collective-permute-start(bf16[240,384]{1,0:T(8,128)(2,1)S(1)} %copy-done.15), channel_id=1, source_target_pairs={{0,8},{1,9},{2,10},{3,11},{4,12},{5,13},{6,14},{7,15},{8,0},{9,1},... | collective-permute-start | bytes 552968 | tf_op jit(solution)/shard_map/ppermute | solution.py:24
  31.1 14.7 %collective-permute-start.14 = (bf16[240,384]{1,0:T(8,128)(2,1)S(1)}, bf16[240,384]{1,0:T(8,128)(2,1)S(1)}, u32[]{:S(2)}, u32[]{:S(2)}) collective-permute-start(bf16[240,384]{1,0:T(8,128)(2,1)S(1)} %copy-done.15), channel_id=1, source_target_pairs={{0,4},{1,5},{2,6},{3,7},{4,0},{5,1},{6,2},{7,3},{8,12},{9,13},{10,... | collective-permute-start | bytes 552968 | tf_op jit(solution)/shard_map/ppermute | solution.py:24
  46.8 20.7 %collective-permute-start.18 = (bf16[4,240,384]{2,1,0:T(8,128)(2,1)S(1)}, bf16[4,240,384]{2,1,0:T(8,128)(2,1)S(1)}, u32[]{:S(2)}, u32[]{:S(2)}) collective-permute-start(bf16[4,240,384]{2,1,0:T(8,128)(2,1)S(1)} %pad_maximum_fusion.1.refs_0_), channel_id=1, source_target_pairs={{0,2},{1,3},{2,0},{3,1},{4,6},{5,7},{6,4},{7,5},{8,10},{9,11},{10,... | collective-permute-start | bytes 2211848 | tf_op jit(solution)/shard_map/ppermute | solution.py:24
  47.4 20.1 %collective-permute-start.17 = (bf16[4,240,384]{2,1,0:T(8,128)(2,1)S(1)}, bf16[4,240,384]{2,1,0:T(8,128)(2,1)S(1)}, u32[]{:S(2)}, u32[]{:S(2)}) collective-permute-start(bf16[4,240,384]{2,1,0:T(8,128)(2,1)S(1)} %pad_maximum_fusion.1.refs_0_), channel_id=1, source_target_pairs={{0,1},{1,0},{2,3},{3,2},{4,5},{5,4},{6,7},{7,6},{8,9},{9,8},{10,11... | collective-permute-start | bytes 2211848 | tf_op jit(solution)/shard_map/ppermute | solution.py:24
  50.2 19.5 %collective-permute-start.28 = (bf16[192,384]{1,0:T(8,128)(2,1)S(1)}, bf16[192,384]{1,0:T(8,128)(2,1)S(1)}, u32[]{:S(2)}, u32[]{:S(2)}) collective-permute-start(bf16[192,384]{1,0:T(8,128)(2,1)S(1)} %copy-done.16), channel_id=1, source_target_pairs={{0,12},{1,13},{2,14},{3,15},{4,8},{5,9},{6,10},{7,11},{8,4},{9,5},... | collective-permute-start | bytes 442376 | tf_op jit(solution)/shard_map/ppermute | solution.py:24
  51.7 18.0 %collective-permute-start.27 = (bf16[192,384]{1,0:T(8,128)(2,1)S(1)}, bf16[192,384]{1,0:T(8,128)(2,1)S(1)}, u32[]{:S(2)}, u32[]{:S(2)}) collective-permute-start(bf16[192,384]{1,0:T(8,128)(2,1)S(1)} %copy-done.16), channel_id=1, source_target_pairs={{0,8},{1,9},{2,10},{3,11},{4,12},{5,13},{6,14},{7,15},{8,0},{9,1},... | collective-permute-start | bytes 442376 | tf_op jit(solution)/shard_map/ppermute | solution.py:24
  51.7 18.6 %collective-permute-start.26 = (bf16[192,384]{1,0:T(8,128)(2,1)S(1)}, bf16[192,384]{1,0:T(8,128)(2,1)S(1)}, u32[]{:S(2)}, u32[]{:S(2)}) collective-permute-start(bf16[192,384]{1,0:T(8,128)(2,1)S(1)} %copy-done.16), channel_id=1, source_target_pairs={{0,4},{1,5},{2,6},{3,7},{4,0},{5,1},{6,2},{7,3},{8,12},{9,13},{10,... | collective-permute-start | bytes 442376 | tf_op jit(solution)/shard_map/ppermute | solution.py:24
  67.5 10.1 %collective-permute-start.20 = (bf16[2,240,384]{2,1,0:T(8,128)(2,1)S(1)}, bf16[2,240,384]{2,1,0:T(8,128)(2,1)}, u32[]{:S(2)}, u32[]{:S(2)}) collective-permute-start(bf16[2,240,384]{2,1,0:T(8,128)(2,1)S(1)} %slice.280), channel_id=1, source_target_pairs={{0,1},{1,0},{2,3},{3,2},{4,5},{5,4},{6,7},{7,6},{8,9},{9,8},{10,11... | collective-permute-start | bytes 1105928 | tf_op jit(solution)/shard_map/ppermute | solution.py:24
  68.1 9.6 %collective-permute-start.19 = (bf16[2,240,384]{2,1,0:T(8,128)(2,1)S(1)}, bf16[2,240,384]{2,1,0:T(8,128)(2,1)}, u32[]{:S(2)}, u32[]{:S(2)}) collective-permute-start(bf16[2,240,384]{2,1,0:T(8,128)(2,1)S(1)} %slice.279), channel_id=1, source_target_pairs={{0,2},{1,3},{2,0},{3,1},{4,6},{5,7},{6,4},{7,5},{8,10},{9,11},{10,... | collective-permute-start | bytes 1105928 | tf_op jit(solution)/shard_map/ppermute | solution.py:24
  69.7 9.7 %collective-permute-start.21 = (bf16[4,240,384]{2,1,0:T(8,128)(2,1)S(1)}, bf16[4,240,384]{2,1,0:T(8,128)(2,1)}, u32[]{:S(2)}, u32[]{:S(2)}) collective-permute-start(bf16[4,240,384]{2,1,0:T(8,128)(2,1)S(1)} %pad_maximum_fusion.1.refs_0_), channel_id=1, source_target_pairs={{0,16},{16,0},{1,17},{17,1},{2,18},{18,2},{3,19},{19,3},{4,20},{20... | collective-permute-start | bytes 2211848 | tf_op jit(solution)/shard_map/ppermute | solution.py:24
  69.8 11.9 %collective-permute-start.22 = (bf16[4,240,384]{2,1,0:T(8,128)(2,1)S(1)}, bf16[4,240,384]{2,1,0:T(8,128)(2,1)}, u32[]{:S(2)}, u32[]{:S(2)}) collective-permute-start(bf16[4,240,384]{2,1,0:T(8,128)(2,1)S(1)} %collective-permute-done.17.refs_1_), channel_id=1, source_target_pairs={{0,16},{16,0},{1,17},{17,1},{2,18},{18,2},{3,19},{19,3},{4,20},{20... | collective-permute-start | bytes 2211848 | tf_op jit(solution)/shard_map/ppermute | solution.py:24
  70.4 11.3 %collective-permute-start.23 = (bf16[4,240,384]{2,1,0:T(8,128)(2,1)S(1)}, bf16[4,240,384]{2,1,0:T(8,128)(2,1)}, u32[]{:S(2)}, u32[]{:S(2)}) collective-permute-start(bf16[4,240,384]{2,1,0:T(8,128)(2,1)S(1)} %collective-permute-done.18.refs_2_), channel_id=1, source_target_pairs={{0,16},{16,0},{1,17},{17,1},{2,18},{18,2},{3,19},{19,3},{4,20},{20... | collective-permute-start | bytes 2211848 | tf_op jit(solution)/shard_map/ppermute | solution.py:24
  79.5 27.2 %collective-permute-start.33 = (bf16[4,192,384]{2,1,0:T(8,128)(2,1)S(1)}, bf16[4,192,384]{2,1,0:T(8,128)(2,1)S(1)}, u32[]{:S(2)}, u32[]{:S(2)}) collective-permute-start(bf16[4,192,384]{2,1,0:T(8,128)(2,1)S(1)} %pad_maximum_fusion.3.refs_0_), channel_id=1, source_target_pairs={{0,16},{16,0},{1,17},{17,1},{2,18},{18,2},{3,19},{19,3},{4,20},{20... | collective-permute-start | bytes 1769480 | tf_op jit(solution)/shard_map/ppermute | solution.py:24
  79.7 16.0 %collective-permute-start.30 = (bf16[4,192,384]{2,1,0:T(8,128)(2,1)S(1)}, bf16[4,192,384]{2,1,0:T(8,128)(2,1)S(1)}, u32[]{:S(2)}, u32[]{:S(2)}) collective-permute-start(bf16[4,192,384]{2,1,0:T(8,128)(2,1)S(1)} %pad_maximum_fusion.3.refs_0_), channel_id=1, source_target_pairs={{0,2},{1,3},{2,0},{3,1},{4,6},{5,7},{6,4},{7,5},{8,10},{9,11},{10,... | collective-permute-start | bytes 1769480 | tf_op jit(solution)/shard_map/ppermute | solution.py:24
  81.1 15.0 %collective-permute-start.29 = (bf16[4,192,384]{2,1,0:T(8,128)(2,1)S(1)}, bf16[4,192,384]{2,1,0:T(8,128)(2,1)S(1)}, u32[]{:S(2)}, u32[]{:S(2)}) collective-permute-start(bf16[4,192,384]{2,1,0:T(8,128)(2,1)S(1)} %pad_maximum_fusion.3.refs_0_), channel_id=1, source_target_pairs={{0,1},{1,0},{2,3},{3,2},{4,5},{5,4},{6,7},{7,6},{8,9},{9,8},{10,11... | collective-permute-start | bytes 1769480 | tf_op jit(solution)/shard_map/ppermute | solution.py:24
  96.1 10.6 %collective-permute-start.34 = (bf16[4,192,384]{2,1,0:T(8,128)(2,1)S(1)}, bf16[4,192,384]{2,1,0:T(8,128)(2,1)S(1)}, u32[]{:S(2)}, u32[]{:S(2)}) collective-permute-start(bf16[4,192,384]{2,1,0:T(8,128)(2,1)S(1)} %collective-permute-done.29.refs_1_), channel_id=1, source_target_pairs={{0,16},{16,0},{1,17},{17,1},{2,18},{18,2},{3,19},{19,3},{4,20},{20... | collective-permute-start | bytes 1769480 | tf_op jit(solution)/shard_map/ppermute | solution.py:24
  96.2 9.5 %collective-permute-start.32 = (bf16[2,192,384]{2,1,0:T(8,128)(2,1)S(1)}, bf16[2,192,384]{2,1,0:T(8,128)(2,1)S(1)}, u32[]{:S(2)}, u32[]{:S(2)}) collective-permute-start(bf16[2,192,384]{2,1,0:T(8,128)(2,1)S(1)} %slice.282), channel_id=1, source_target_pairs={{0,1},{1,0},{2,3},{3,2},{4,5},{5,4},{6,7},{7,6},{8,9},{9,8},{10,11... | collective-permute-start | bytes 884744 | tf_op jit(solution)/shard_map/ppermute | solution.py:24
  97.3 9.5 %collective-permute-start.35 = (bf16[4,192,384]{2,1,0:T(8,128)(2,1)S(1)}, bf16[4,192,384]{2,1,0:T(8,128)(2,1)S(1)}, u32[]{:S(2)}, u32[]{:S(2)}) collective-permute-start(bf16[4,192,384]{2,1,0:T(8,128)(2,1)S(1)} %collective-permute-done.30.refs_2_), channel_id=1, source_target_pairs={{0,16},{16,0},{1,17},{17,1},{2,18},{18,2},{3,19},{19,3},{4,20},{20... | collective-permute-start | bytes 1769480 | tf_op jit(solution)/shard_map/ppermute | solution.py:24
  135.9 12.4 %collective-permute-start.42 = (bf16[3,4,96,768]{3,2,1,0:T(8,128)(2,1)}, bf16[3,4,96,768]{3,2,1,0:T(8,128)(2,1)S(1)}, u32[]{:S(2)}, u32[]{:S(2)}) collective-permute-start(bf16[3,4,96,768]{3,2,1,0:T(8,128)(2,1)} %get-tuple-element.173), channel_id=1, source_target_pairs={{0,16},{16,0},{1,17},{17,1},{2,18},{18,2},{3,19},{19,3},{4,20},{20... | collective-permute-start | bytes 5308424 | tf_op jit(solution)/shard_map/ppermute | solution.py:24
  137.5 10.8 %collective-permute-start.41 = (bf16[2,96,768]{2,1,0:T(8,128)(2,1)S(1)}, bf16[2,96,768]{2,1,0:T(8,128)(2,1)S(1)}, u32[]{:S(2)}, u32[]{:S(2)}) collective-permute-start(bf16[2,96,768]{2,1,0:T(8,128)(2,1)S(1)} %get-tuple-element.250), channel_id=1, source_target_pairs={{0,2},{1,3},{2,0},{3,1},{4,6},{5,7},{6,4},{7,5},{8,10},{9,11},{10,... | collective-permute-start | bytes 884744 | tf_op jit(solution)/shard_map/ppermute | solution.py:24
  149.5 19.8 %collective-permute-start.45 = (bf16[4,96,768]{2,1,0:T(8,128)(2,1)S(1)}, bf16[4,96,768]{2,1,0:T(8,128)(2,1)S(1)}, u32[]{:S(2)}, u32[]{:S(2)}) collective-permute-start(bf16[4,96,768]{2,1,0:T(8,128)(2,1)S(1)} %get-tuple-element.244), channel_id=1, source_target_pairs={{0,2},{1,3},{2,0},{3,1},{4,6},{5,7},{6,4},{7,5},{8,10},{9,11},{10,... | collective-permute-start | bytes 1769480 | tf_op jit(solution)/shard_map/ppermute | solution.py:24
  149.9 19.4 %collective-permute-start.44 = (bf16[4,96,768]{2,1,0:T(8,128)(2,1)S(1)}, bf16[4,96,768]{2,1,0:T(8,128)(2,1)S(1)}, u32[]{:S(2)}, u32[]{:S(2)}) collective-permute-start(bf16[4,96,768]{2,1,0:T(8,128)(2,1)S(1)} %get-tuple-element.245), channel_id=1, source_target_pairs={{0,1},{1,0},{2,3},{3,2},{4,5},{5,4},{6,7},{7,6},{8,9},{9,8},{10,11... | collective-permute-start | bytes 1769480 | tf_op jit(solution)/shard_map/ppermute | solution.py:24
  171.8 14.6 %collective-permute-start.49 = (bf16[3,4,24,3840]{3,2,1,0:T(8,128)(2,1)}, bf16[3,4,24,3840]{3,2,1,0:T(8,128)(2,1)S(1)}, u32[]{:S(2)}, u32[]{:S(2)}) collective-permute-start(bf16[3,4,24,3840]{3,2,1,0:T(8,128)(2,1)} %get-tuple-element.189), channel_id=1, source_target_pairs={{0,16},{16,0},{1,17},{17,1},{2,18},{18,2},{3,19},{19,3},{4,20},{20... | collective-permute-start | bytes 6635528 | tf_op jit(solution)/shard_map/ppermute | solution.py:24
  174.6 10.7 %collective-permute-start.48 = (bf16[2,24,3840]{2,1,0:T(8,128)(2,1)S(1)}, bf16[2,24,3840]{2,1,0:T(8,128)(2,1)S(1)}, u32[]{:S(2)}, u32[]{:S(2)}) collective-permute-start(bf16[2,24,3840]{2,1,0:T(8,128)(2,1)S(1)} %get-tuple-element.246), channel_id=1, source_target_pairs={{0,2},{1,3},{2,0},{3,1},{4,6},{5,7},{6,4},{7,5},{8,10},{9,11},{10,... | collective-permute-start | bytes 1105928 | tf_op jit(solution)/shard_map/ppermute | solution.py:24
  176.1 10.3 %collective-permute-start.47 = (bf16[2,24,3840]{2,1,0:T(8,128)(2,1)S(1)}, bf16[2,24,3840]{2,1,0:T(8,128)(2,1)S(1)}, u32[]{:S(2)}, u32[]{:S(2)}) collective-permute-start(bf16[2,24,3840]{2,1,0:T(8,128)(2,1)S(1)} %get-tuple-element.247), channel_id=1, source_target_pairs={{0,1},{1,0},{2,3},{3,2},{4,5},{5,4},{6,7},{7,6},{8,9},{9,8},{10,11... | collective-permute-start | bytes 1105928 | tf_op jit(solution)/shard_map/ppermute | solution.py:24
  178.7 20.9 %collective-permute-start.54 = (bf16[96,768]{1,0:T(8,128)(2,1)S(1)}, bf16[96,768]{1,0:T(8,128)(2,1)}, u32[]{:S(2)}, u32[]{:S(2)}) collective-permute-start(bf16[96,768]{1,0:T(8,128)(2,1)S(1)} %get-tuple-element.236), channel_id=1, source_target_pairs={{0,12},{1,13},{2,14},{3,15},{4,8},{5,9},{6,10},{7,11},{8,4},{9,5},... | collective-permute-start | bytes 442376 | tf_op jit(solution)/shard_map/ppermute | solution.py:24
  180.5 20.9 %collective-permute-start.53 = (bf16[96,768]{1,0:T(8,128)(2,1)S(1)}, bf16[96,768]{1,0:T(8,128)(2,1)S(1)}, u32[]{:S(2)}, u32[]{:S(2)}) collective-permute-start(bf16[96,768]{1,0:T(8,128)(2,1)S(1)} %get-tuple-element.237), channel_id=1, source_target_pairs={{0,8},{1,9},{2,10},{3,11},{4,12},{5,13},{6,14},{7,15},{8,0},{9,1},... | collective-permute-start | bytes 442376 | tf_op jit(solution)/shard_map/ppermute | solution.py:24
  185.3 16.1 %collective-permute-start.52 = (bf16[96,768]{1,0:T(8,128)(2,1)S(1)}, bf16[96,768]{1,0:T(8,128)(2,1)S(1)}, u32[]{:S(2)}, u32[]{:S(2)}) collective-permute-start(bf16[96,768]{1,0:T(8,128)(2,1)S(1)} %get-tuple-element.238), channel_id=1, source_target_pairs={{0,4},{1,5},{2,6},{3,7},{4,0},{5,1},{6,2},{7,3},{8,12},{9,13},{10,... | collective-permute-start | bytes 442376 | tf_op jit(solution)/shard_map/ppermute | solution.py:24
  187.9 17.5 %collective-permute-start.51 = (bf16[4,24,3840]{2,1,0:T(8,128)(2,1)S(1)}, bf16[4,24,3840]{2,1,0:T(8,128)(2,1)S(1)}, u32[]{:S(2)}, u32[]{:S(2)}) collective-permute-start(bf16[4,24,3840]{2,1,0:T(8,128)(2,1)S(1)} %get-tuple-element.239), channel_id=1, source_target_pairs={{0,2},{1,3},{2,0},{3,1},{4,6},{5,7},{6,4},{7,5},{8,10},{9,11},{10,... | collective-permute-start | bytes 2211848 | tf_op jit(solution)/shard_map/ppermute | solution.py:24
  188.4 17.3 %collective-permute-start.50 = (bf16[4,24,3840]{2,1,0:T(8,128)(2,1)S(1)}, bf16[4,24,3840]{2,1,0:T(8,128)(2,1)}, u32[]{:S(2)}, u32[]{:S(2)}) collective-permute-start(bf16[4,24,3840]{2,1,0:T(8,128)(2,1)S(1)} %get-tuple-element.240), channel_id=1, source_target_pairs={{0,1},{1,0},{2,3},{3,2},{4,5},{5,4},{6,7},{7,6},{8,9},{9,8},{10,11... | collective-permute-start | bytes 2211848 | tf_op jit(solution)/shard_map/ppermute | solution.py:24
  199.6 25.3 %collective-permute-start.58 = (f32[16,2304]{1,0:T(8,128)S(1)}, f32[16,2304]{1,0:T(8,128)S(1)}, u32[]{:S(2)}, u32[]{:S(2)}) collective-permute-start(f32[16,2304]{1,0:T(8,128)S(1)} %fusion.35), channel_id=1, source_target_pairs={{0,4},{1,5},{2,6},{3,7},{4,0},{5,1},{6,2},{7,3},{8,12},{9,13},{10,... | collective-permute-start | bytes 442376 | tf_op jit(solution)/shard_map/ppermute | solution.py:24
  207.4 17.6 %collective-permute-start.57 = (bf16[24,3840]{1,0:T(8,128)(2,1)S(1)}, bf16[24,3840]{1,0:T(8,128)(2,1)S(1)}, u32[]{:S(2)}, u32[]{:S(2)}) collective-permute-start(bf16[24,3840]{1,0:T(8,128)(2,1)S(1)} %get-tuple-element.233), channel_id=1, source_target_pairs={{0,12},{1,13},{2,14},{3,15},{4,8},{5,9},{6,10},{7,11},{8,4},{9,5},... | collective-permute-start | bytes 552968 | tf_op jit(solution)/shard_map/ppermute | solution.py:24
  209.8 15.1 %collective-permute-start.56 = (bf16[24,3840]{1,0:T(8,128)(2,1)S(1)}, bf16[24,3840]{1,0:T(8,128)(2,1)S(1)}, u32[]{:S(2)}, u32[]{:S(2)}) collective-permute-start(bf16[24,3840]{1,0:T(8,128)(2,1)S(1)} %get-tuple-element.234), channel_id=1, source_target_pairs={{0,8},{1,9},{2,10},{3,11},{4,12},{5,13},{6,14},{7,15},{8,0},{9,1},... | collective-permute-start | bytes 552968 | tf_op jit(solution)/shard_map/ppermute | solution.py:24
  210.6 14.3 %collective-permute-start.55 = (bf16[24,3840]{1,0:T(8,128)(2,1)S(1)}, bf16[24,3840]{1,0:T(8,128)(2,1)}, u32[]{:S(2)}, u32[]{:S(2)}) collective-permute-start(bf16[24,3840]{1,0:T(8,128)(2,1)S(1)} %get-tuple-element.235), channel_id=1, source_target_pairs={{0,4},{1,5},{2,6},{3,7},{4,0},{5,1},{6,2},{7,3},{8,12},{9,13},{10,... | collective-permute-start | bytes 552968 | tf_op jit(solution)/shard_map/ppermute | solution.py:24
  227.8 10.8 %collective-permute-start.63 = (bf16[3,4,24,2432]{3,2,1,0:T(8,128)(2,1)}, bf16[3,4,24,2432]{3,2,1,0:T(8,128)(2,1)}, u32[]{:S(2)}, u32[]{:S(2)}) collective-permute-start(bf16[3,4,24,2432]{3,2,1,0:T(8,128)(2,1)} %get-tuple-element.206), channel_id=1, source_target_pairs={{0,16},{16,0},{1,17},{17,1},{2,18},{18,2},{3,19},{19,3},{4,20},{20... | collective-permute-start | bytes 4202504 | tf_op jit(solution)/shard_map/ppermute | solution.py:24
  233.9 10.6 %collective-permute-start.69 = (f32[16,2304]{1,0:T(8,128)S(1)}, f32[16,2304]{1,0:T(8,128)S(1)}, u32[]{:S(2)}, u32[]{:S(2)}) collective-permute-start(f32[16,2304]{1,0:T(8,128)S(1)} %add.513), channel_id=1, source_target_pairs={{0,8},{1,9},{2,10},{3,11},{4,12},{5,13},{6,14},{7,15},{8,0},{9,1},... | collective-permute-start | bytes 442376 | tf_op jit(solution)/shard_map/ppermute | solution.py:24
  238.5 21.0 %collective-permute-start.62 = (bf16[8,128,768]{2,1,0:T(8,128)(2,1)}, bf16[8,128,768]{2,1,0:T(8,128)(2,1)S(1)}, u32[]{:S(2)}, u32[]{:S(2)}) collective-permute-start(bf16[8,128,768]{2,1,0:T(8,128)(2,1)} %get-tuple-element.204), channel_id=1, source_target_pairs={{0,16},{16,0},{1,17},{17,1},{2,18},{18,2},{3,19},{19,3},{4,20},{20... | collective-permute-start | bytes 4718600 | tf_op jit(solution)/shard_map/ppermute | solution.py:24
  240.0 13.6 %collective-permute-start.64 = (bf16[4,24,2432]{2,1,0:T(8,128)(2,1)S(1)}, bf16[4,24,2432]{2,1,0:T(8,128)(2,1)S(1)}, u32[]{:S(2)}, u32[]{:S(2)}) collective-permute-start(bf16[4,24,2432]{2,1,0:T(8,128)(2,1)S(1)} %get-tuple-element.248), channel_id=1, source_target_pairs={{0,1},{1,0},{2,3},{3,2},{4,5},{5,4},{6,7},{7,6},{8,9},{9,8},{10,11... | collective-permute-start | bytes 1400840 | tf_op jit(solution)/shard_map/ppermute | solution.py:24
  241.0 12.8 %collective-permute-start.65 = (bf16[4,24,2432]{2,1,0:T(8,128)(2,1)S(1)}, bf16[4,24,2432]{2,1,0:T(8,128)(2,1)S(1)}, u32[]{:S(2)}, u32[]{:S(2)}) collective-permute-start(bf16[4,24,2432]{2,1,0:T(8,128)(2,1)S(1)} %get-tuple-element.249), channel_id=1, source_target_pairs={{0,2},{1,3},{2,0},{3,1},{4,6},{5,7},{6,4},{7,5},{8,10},{9,11},{10,... | collective-permute-start | bytes 1400840 | tf_op jit(solution)/shard_map/ppermute | solution.py:24
  244.5 17.0 %collective-permute-start.70 = (f32[16,2304]{1,0:T(8,128)S(1)}, f32[16,2304]{1,0:T(8,128)S(1)}, u32[]{:S(2)}, u32[]{:S(2)}) collective-permute-start(f32[16,2304]{1,0:T(8,128)S(1)} %add.514), channel_id=1, source_target_pairs={{0,1},{1,0},{2,3},{3,2},{4,5},{5,4},{6,7},{7,6},{8,9},{9,8},{10,11... | collective-permute-start | bytes 442376 | tf_op jit(solution)/shard_map/ppermute | solution.py:24
  256.9 9.9 %collective-permute-start.67 = (bf16[24,2432]{1,0:T(8,128)(2,1)S(1)}, bf16[24,2432]{1,0:T(8,128)(2,1)S(1)}, u32[]{:S(2)}, u32[]{:S(2)}) collective-permute-start(bf16[24,2432]{1,0:T(8,128)(2,1)S(1)} %get-tuple-element.242), channel_id=1, source_target_pairs={{0,8},{1,9},{2,10},{3,11},{4,12},{5,13},{6,14},{7,15},{8,0},{9,1},... | collective-permute-start | bytes 350216 | tf_op jit(solution)/shard_map/ppermute | solution.py:24
  256.9 9.9 %collective-permute-start.66 = (bf16[24,2432]{1,0:T(8,128)(2,1)S(1)}, bf16[24,2432]{1,0:T(8,128)(2,1)S(1)}, u32[]{:S(2)}, u32[]{:S(2)}) collective-permute-start(bf16[24,2432]{1,0:T(8,128)(2,1)S(1)} %get-tuple-element.243), channel_id=1, source_target_pairs={{0,4},{1,5},{2,6},{3,7},{4,0},{5,1},{6,2},{7,3},{8,12},{9,13},{10,... | collective-permute-start | bytes 350216 | tf_op jit(solution)/shard_map/ppermute | solution.py:24
  (68 other events, 487.9 us)

commit v6 on v5

--- a/solution.py
+++ b/solution.py
@@ -287,7 +287,7 @@
     return copies
 
 
-def deal(place, acc, outs, base=0):
+def deal(place, acc, outs, base=0, looped=True):
     cols = acc.shape[1]
     if len(outs) == 1:
         outs[0][:, base : base + cols] = acc[...].astype(b16)
@@ -304,7 +304,11 @@
                 target[j, :, base : base + cols] = acc[pl.ds(pl.multiple_of(at, 8), rows), :].astype(b16)
                 return 0
 
-            lax.fori_loop(0, FAR, block, 0)
+            if looped:
+                lax.fori_loop(0, FAR, block, 0)
+            else:
+                for j in range(FAR):
+                    block(j, 0)
 
 
 def flat_of(weight, cols=slice(None)):
@@ -776,7 +780,7 @@
             return 0
 
         lax.fori_loop(0, count, unpack, 0)
-        deal(place, acc, outs)
+        deal(place, acc, outs, looped=False)
         if len(outs) > 1:
             cols, lanes = acc.shape[1], tail.shape[1]
             each = biases.shape[1] // lanes

time: 273 us -> 273 us (level)
  Pallas kernels: 103 us -> 82.7 us
  starting transfers between devices: 60 us -> 73.1 us
  waiting for transfers between devices: 65.2 us -> 72.8 us
    pallas_call x9, Pallas kernels: 101 us -> 81.1 us  [call(): pl.pallas_call(kernel, out_shape=[bare(o) for o in outs], grid_spec=pltpu...]
    ppermute x72, starting transfers between devices: 60 us -> 73.1 us  [swap(): lax.ppermute(x, axis, [(i, i ^ k) for i in range(lax.axis_size(axis))])]
    ppermute x72, waiting for transfers between devices: 65.2 us -> 72.8 us  [swap(): lax.ppermute(x, axis, [(i, i ^ k) for i in range(lax.axis_size(axis))])]
  transfers between devices with their start and end apart: 72 -> 72, of which waited for: 28 -> 32; matrix products, arithmetic and copies ran while one was open for 13% -> 13% of each run, Pallas kernels for 29% -> 24%
where the time goes in v6:
time: 273 us; the launch traced here: 271 us
  Pallas kernels  82.7 us (30%)
  starting transfers between devices  73.1 us (27%)
  waiting for transfers between devices  72.8 us (27%)
  other arithmetic  27.3 us (10%)
  local copies, waits for them, and re-layouts  13.4 us (5%)
    pallas_call x9, Pallas kernels, call(): pl.pallas_call(kernel, out_shape=[bare(o) for o in outs], grid_spec=pltpu...  81.1 us
    ppermute x72, starting transfers between devices, swap(): lax.ppermute(x, axis, [(i, i ^ k) for i in range(lax.axis_size(axis))])  73.1 us
    ppermute x72, waiting for transfers between devices, swap(): lax.ppermute(x, axis, [(i, i ^ k) for i in range(lax.axis_size(axis))])  72.8 us
  transfers between devices with their start and end apart: 72, of which 32 were waited for; matrix products, arithmetic and copies ran while one was open for 13% of the time, Pallas kernels for 24%

profile of v6, /device:TPU:0, one launch (start us, length us, event | category | flops | bytes accessed | tf_op | source)
XLA Modules:
  0.0 271.5 jit_solution(9832185131802946413)
XLA Ops:
  4.3 2.7 shard_map.305
  7.0 4.6 %collective-permute-start.3 = (bf16[152,384]{1,0:T(8,128)(2,1)}, bf16[152,384]{1,0:T(8,128)(2,1)S(1)}, u32[]{:S(2)}, u32[]{:S(2)}) collective-permute-start(bf16[152,384]{1,0:T(8,128)(2,1)} %get-tuple-element.123), channel_id=1, source_target_pairs={{0,12},{1,13},{2,14},{3,15},{4,8},{5,9},{6,10},{7,11},{8,4},{9,5},... | collective-permute-start | bytes 350216 | tf_op jit(solution)/shard_map/ppermute | solution.py:24
  15.9 6.3 %collective-permute-done.2 = bf16[152,384]{1,0:T(8,128)(2,1)S(1)} collective-permute-done((bf16[152,384]{1,0:T(8,128)(2,1)}, bf16[152,384]{1,0:T(8,128)(2,1)S(1)}, u32[]{:S(2)}, u32[]{:S(2)}) %collective-permute-start.2) | collective-permute-done | bytes 116768 | tf_op jit(solution)/shard_map/ppermute | solution.py:24
  23.6 1.6 collective-permute-start.6
  28.6 2.5 collective-permute-start.16
  31.1 1.9 collective-permute-start.14
  33.0 2.9 %collective-permute-done.6.refs_2_ = bf16[4,152,384]{2,1,0:T(8,128)(2,1)S(1)} collective-permute-done((bf16[4,152,384]{2,1,0:T(8,128)(2,1)S(1)}, bf16[4,152,384]{2,1,0:T(8,128)(2,1)S(1)}, u32[]{:S(2)}, u32[]{:S(2)}) %collective-permute-start.6) | collective-permute-done | bytes 466976 | tf_op jit(solution)/shard_map/ppermute | solution.py:24
  38.3 1.6 collective-permute-start.8
  41.2 4.5 %collective-permute-done.15 = bf16[240,384]{1,0:T(8,128)(2,1)S(1)} collective-permute-done((bf16[240,384]{1,0:T(8,128)(2,1)S(1)}, bf16[240,384]{1,0:T(8,128)(2,1)S(1)}, u32[]{:S(2)}, u32[]{:S(2)}) %collective-permute-start.15) | collective-permute-done | bytes 184352 | tf_op jit(solution)/shard_map/ppermute | solution.py:24
  51.7 2.9 %collective-permute-start.26 = (bf16[192,384]{1,0:T(8,128)(2,1)S(1)}, bf16[192,384]{1,0:T(8,128)(2,1)S(1)}, u32[]{:S(2)}, u32[]{:S(2)}) collective-permute-start(bf16[192,384]{1,0:T(8,128)(2,1)S(1)} %copy-done.16), channel_id=1, source_target_pairs={{0,4},{1,5},{2,6},{3,7},{4,0},{5,1},{6,2},{7,3},{8,12},{9,13},{10,... | collective-permute-start | bytes 442376 | tf_op jit(solution)/shard_map/ppermute | solution.py:24
  54.6 11.2 %shard_map.306 = (bf16[4,192,2304]{2,1,0:T(8,128)(2,1)}, bf16[1152,768]{1,0:T(8,128)(2,1)}, bf16[1152,2304]{1,0:T(8,128)(2,1)}, bf16[8,1536,128]{2,1,0:T(8,128)(2,1)}, bf16[1152,768]{1,0:T(8,128)(2,1)}) custom-call(s32[8]{0:T(128)} %copy-done.31, s32[8]{0:T(128)} %select_reduce_fusion.1.offs, s32[1]{0:T(128)S(6)} %select_n.135.tiles, s32[3]{0:T(128)} %pad_add_fusion.place, ...), custom_call_target="tpu_custom_call" | custom-call | flops 4600000000 | bytes 22438080 | tf_op jit(solution)/shard_map/pallas_call | solution.py:853
  66.1 2.0 collective-permute-start.20
  68.1 1.6 collective-permute-start.19
  71.8 5.3 %collective-permute-done.20.refs_4_ = bf16[2,240,384]{2,1,0:T(8,128)(2,1)} collective-permute-done((bf16[2,240,384]{2,1,0:T(8,128)(2,1)S(1)}, bf16[2,240,384]{2,1,0:T(8,128)(2,1)}, u32[]{:S(2)}, u32[]{:S(2)}) %collective-permute-start.20) | collective-permute-done | bytes 368672 | tf_op jit(solution)/shard_map/ppermute | solution.py:24
  82.0 10.5 %shard_map.307 = (bf16[4,192,768]{2,1,0:T(8,128)(2,1)}, bf16[4,192,3072]{2,1,0:T(8,128)(2,1)}, bf16[1024,3072]{1,0:T(8,128)(2,1)}, bf16[1024,3072]{1,0:T(8,128)(...) custom-call(s32[8]{0:T(128)} %copy-done.31, s32[8]{0:T(128)} %select_reduce_fusion.1.offs, s32[1]{0:T(128)S(6)} %select_n.135.tiles, ...), custom_call_target="tpu_custom_call" | custom-call | flops 16099999744 | bytes 31625216 | tf_op jit(solution)/shard_map/pallas_call | solution.py:853
  92.5 2.7 collective-permute-done.30.refs_2_
  98.3 7.4 %collective-permute-done.32.refs_4_ = bf16[2,192,384]{2,1,0:T(8,128)(2,1)S(1)} collective-permute-done((bf16[2,192,384]{2,1,0:T(8,128)(2,1)S(1)}, bf16[2,192,384]{2,1,0:T(8,128)(2,1)S(1)}, u32[]{:S(2)}, u32[]{:S(2)}) %collective-permute-start.32) | collective-permute-done | bytes 294944 | tf_op jit(solution)/shard_map/ppermute | solution.py:24
  109.0 8.3 %shard_map.308 = (bf16[4,768,768]{2,1,0:T(8,128)(2,1)}, f32[1024,768]{1,0:T(8,128)}, f32[1024,128]{1,0:T(8,128)}, f32[8,768]{1,0:T(8,128)}) custom-call(s32[8]{0:T(128)} %copy-done.31, s32[8]{0:T(128)} %select_reduce_fusion.1.offs, s32[1]{0:T(128)S(6)} %select_n.135.tiles, s32[3]{0:T(128)} %pad_add_fusion.place, f32[1024,768]{1,0:T(8,128)} %get-tuple-element.149.n1, ...), custom_call_target="tpu_custom_call" | custom-call | flops 11500000256 | bytes 22593536 | tf_op jit(solution)/shard_map/pallas_call | solution.py:853
  117.3 2.6 collective-permute-start.38
  122.5 8.7 %shard_map.309 = (f32[1024,768]{1,0:T(8,128)}, bf16[4,4,96,768]{3,2,1,0:T(8,128)(2,1)}, bf16[4,96,768]{2,1,0:T(8,128)(2,1)}, bf16[3,4,96,768]{3,2,1,0:T(8,128)(2...) custom-call(s32[8]{0:T(128)} %copy-done.31, s32[8]{0:T(128)} %select_reduce_fusion.1.offs, ...), custom_call_target="tpu_custom_call" | custom-call | flops 12650000384 | bytes 18050284 | tf_op jit(solution)/shard_map/pallas_call | solution.py:853
  131.2 2.6 collective-permute-start.39
  133.8 1.8 collective-permute-done.39
  139.5 7.0 %shard_map.310 = (bf16[1024,3072]{1,0:T(8,128)(2,1)}, f32[8,768]{1,0:T(8,128)}) custom-call(s32[8]{0:T(128)} %copy-done.31, s32[8]{0:T(128)} %select_reduce_fusion.1.offs, s32[1]{0:T(128)S(6)} %select_n.135.tiles, s32[3]{0:T(128)} %pad_add_fusion.place, f32[1024,768]{1,0:T(8,128)} %get-tuple-element.167.sum_grad, ...), custom_call_target="tpu_custom_call" | custom-call | flops 9200000000 | bytes 20471808 | tf_op jit(solution)/shard_map/pallas_call | solution.py:853
  148.4 1.8 collective-permute-start.45
  150.9 13.5 %shard_map.311 = (f32[1024,768]{1,0:T(8,128)}, bf16[1152,768]{1,0:T(8,128)(2,1)}, bf16[4,4,24,3840]{3,2,1,0:T(8,128)(2,1)}, bf16[4,24,3840]{2,1,0:T(8,128)(2,1)}...) custom-call(s32[8]{0:T(128)} %copy-done.31, s32[8]{0:T(128)} %select_reduce_fusion.1.offs, s32[1]{0:T(128)S(6)} %select_n.135.tiles, ...), custom_call_target="tpu_custom_call" | custom-call | flops 23000000512 | bytes 31637504 | tf_op jit(solution)/shard_map/pallas_call | solution.py:853
  164.8 3.3 %collective-permute-start.46 = (bf16[4,24,3840]{2,1,0:T(8,128)(2,1)}, bf16[4,24,3840]{2,1,0:T(8,128)(2,1)S(1)}, u32[]{:S(2)}, u32[]{:S(2)}) collective-permute-start(bf16[4,24,3840]{2,1,0:T(8,128)(2,1)} %get-tuple-element.187), channel_id=1, source_target_pairs={{0,16},{16,0},{1,17},{17,1},{2,18},{18,2},{3,19},{19,3},{4,20},{20... | collective-permute-start | bytes 2211848 | tf_op jit(solution)/shard_map/ppermute | solution.py:24
  168.1 2.1 collective-permute-done.46
  172.9 2.6 collective-permute-start.48
  176.0 1.6 fusion.21
  177.6 2.6 collective-permute-start.54
  180.2 4.2 %collective-permute-done.48 = bf16[2,24,3840]{2,1,0:T(8,128)(2,1)S(1)} collective-permute-done((bf16[2,24,3840]{2,1,0:T(8,128)(2,1)S(1)}, bf16[2,24,3840]{2,1,0:T(8,128)(2,1)S(1)}, u32[]{:S(2)}, u32[]{:S(2)}) %collective-permute-start.48) | collective-permute-done | bytes 368672 | tf_op jit(solution)/shard_map/ppermute | solution.py:24
  189.5 9.2 %shard_map.312 = (bf16[1152,2304]{1,0:T(8,128)(2,1)}, f32[8,768]{1,0:T(8,128)}) custom-call(s32[8]{0:T(128)} %copy-done.31, s32[8]{0:T(128)} %select_reduce_fusion.1.offs, s32[1]{0:T(128)S(6)} %select_n.135.tiles, s32[3]{0:T(128)} %pad_add_fusion.place, bf16[1152,2304]{1,0:T(8,128)(2,1)} %get-tuple-element.163.qkv_h, ...), custom_call_target="tpu_custom_call" | custom-call | flops 16099999744 | bytes 15556608 | tf_op jit(solution)/shard_map/pallas_call | solution.py:853
  198.8 1.8 collective-permute-start.58
  200.6 4.4 %collective-permute-done.51 = bf16[4,24,3840]{2,1,0:T(8,128)(2,1)S(1)} collective-permute-done((bf16[4,24,3840]{2,1,0:T(8,128)(2,1)S(1)}, bf16[4,24,3840]{2,1,0:T(8,128)(2,1)S(1)}, u32[]{:S(2)}, u32[]{:S(2)}) %collective-permute-start.51) | collective-permute-done | bytes 737312 | tf_op jit(solution)/shard_map/ppermute | solution.py:24
  205.4 1.6 fusion.15
  207.0 2.4 collective-permute-start.57
  211.5 10.1 %shard_map.313 = (f32[8,128,768]{2,1,0:T(8,128)}, bf16[8,128,768]{2,1,0:T(8,128)(2,1)}, bf16[4,4,24,2432]{3,2,1,0:T(8,128)(2,1)}, bf16[4,24,2432]{2,1,0:T(8,128)(2,1)}, bf16[3,4,24,2432]{3,2,1,0:T(8,128)(2,1)}) custom-call(s32[8]{0:T(128)} %copy-done.31, s32[8]{0:T(128)} %select_reduce_fusion.1.offs, s32[1]{0:T(128)S(6)} %select_n.135.tiles, ...), custom_call_target="tpu_custom_call" | custom-call | flops 18400000000 | bytes 22241472 | tf_op jit(solution)/shard_map/pallas_call | solution.py:853
  221.6 2.7 %collective-permute-done.56 = bf16[24,3840]{1,0:T(8,128)(2,1)S(1)} collective-permute-done((bf16[24,3840]{1,0:T(8,128)(2,1)S(1)}, bf16[24,3840]{1,0:T(8,128)(2,1)S(1)}, u32[]{:S(2)}, u32[]{:S(2)}) %collective-permute-start.56) | collective-permute-done | bytes 184352 | tf_op jit(solution)/shard_map/ppermute | solution.py:24
  224.4 2.2 collective-permute-done.59
  228.2 1.9 collective-permute-start.61
  231.1 2.1 fusion.20
  234.4 1.9 collective-permute-done.61
  244.7 8.1 %collective-permute-done.64 = bf16[4,24,2432]{2,1,0:T(8,128)(2,1)S(1)} collective-permute-done((bf16[4,24,2432]{2,1,0:T(8,128)(2,1)S(1)}, bf16[4,24,2432]{2,1,0:T(8,128)(2,1)S(1)}, u32[]{:S(2)}, u32[]{:S(2)}) %collective-permute-start.64) | collective-permute-done | bytes 466976 | tf_op jit(solution)/shard_map/ppermute | solution.py:24
  254.4 1.8 collective-permute-start.68
  256.4 2.4 collective-permute-start.66
  258.9 2.0 convert_add_fusion
  262.4 4.3 %collective-permute-done.67 = bf16[24,2432]{1,0:T(8,128)(2,1)S(1)} collective-permute-done((bf16[24,2432]{1,0:T(8,128)(2,1)S(1)}, bf16[24,2432]{1,0:T(8,128)(2,1)S(1)}, u32[]{:S(2)}, u32[]{:S(2)}) %collective-permute-start.67) | collective-permute-done | bytes 116768 | tf_op jit(solution)/shard_map/ppermute | solution.py:24
  269.7 1.7 shard_map.314
  (269 shorter events, 73.8 us)
Async XLA Ops:
  0.7 21.6 %collective-permute-start.4 = (bf16[8,128,768]{2,1,0:T(8,128)(2,1)}, bf16[8,128,768]{2,1,0:T(8,128)(2,1)S(1)}, u32[]{:S(2)}, u32[]{:S(2)}) collective-permute-start(bf16[8,128,768]{2,1,0:T(8,128)(2,1)} %bitcast.252), channel_id=1, source_target_pairs={{0,16},{16,0},{1,17},{17,1},{2,18},{18,2},{3,19},{19,3},{4,20},{20... | collective-permute-start | bytes 4718600 | tf_op jit(solution)/shard_map/ppermute | solution.py:24
  11.6 10.7 %collective-permute-start.2 = (bf16[152,384]{1,0:T(8,128)(2,1)}, bf16[152,384]{1,0:T(8,128)(2,1)S(1)}, u32[]{:S(2)}, u32[]{:S(2)}) collective-permute-start(bf16[152,384]{1,0:T(8,128)(2,1)} %get-tuple-element.123), channel_id=1, source_target_pairs={{0,8},{1,9},{2,10},{3,11},{4,12},{5,13},{6,14},{7,15},{8,0},{9,1},... | collective-permute-start | bytes 350216 | tf_op jit(solution)/shard_map/ppermute | solution.py:24
  11.6 10.7 %collective-permute-start.1 = (bf16[152,384]{1,0:T(8,128)(2,1)}, bf16[152,384]{1,0:T(8,128)(2,1)S(1)}, u32[]{:S(2)}, u32[]{:S(2)}) collective-permute-start(bf16[152,384]{1,0:T(8,128)(2,1)} %get-tuple-element.123), channel_id=1, source_target_pairs={{0,4},{1,5},{2,6},{3,7},{4,0},{5,1},{6,2},{7,3},{8,12},{9,13},{10,... | collective-permute-start | bytes 350216 | tf_op jit(solution)/shard_map/ppermute | solution.py:24
  23.6 12.4 %collective-permute-start.6 = (bf16[4,152,384]{2,1,0:T(8,128)(2,1)S(1)}, bf16[4,152,384]{2,1,0:T(8,128)(2,1)S(1)}, u32[]{:S(2)}, u32[]{:S(2)}) collective-permute-start(bf16[4,152,384]{2,1,0:T(8,128)(2,1)S(1)} %pad_maximum_fusion.5.refs_0_), channel_id=1, source_target_pairs={{0,2},{1,3},{2,0},{3,1},{4,6},{5,7},{6,4},{7,5},{8,10},{9,11},{10,... | collective-permute-start | bytes 1400840 | tf_op jit(solution)/shard_map/ppermute | solution.py:24
  25.2 12.1 %collective-permute-start.5 = (bf16[4,152,384]{2,1,0:T(8,128)(2,1)S(1)}, bf16[4,152,384]{2,1,0:T(8,128)(2,1)}, u32[]{:S(2)}, u32[]{:S(2)}) collective-permute-start(bf16[4,152,384]{2,1,0:T(8,128)(2,1)S(1)} %pad_maximum_fusion.5.refs_0_), channel_id=1, source_target_pairs={{0,1},{1,0},{2,3},{3,2},{4,5},{5,4},{6,7},{7,6},{8,9},{9,8},{10,11... | collective-permute-start | bytes 1400840 | tf_op jit(solution)/shard_map/ppermute | solution.py:24
  28.6 12.5 %collective-permute-start.16 = (bf16[240,384]{1,0:T(8,128)(2,1)S(1)}, bf16[240,384]{1,0:T(8,128)(2,1)S(1)}, u32[]{:S(2)}, u32[]{:S(2)}) collective-permute-start(bf16[240,384]{1,0:T(8,128)(2,1)S(1)} %copy-done.15), channel_id=1, source_target_pairs={{0,12},{1,13},{2,14},{3,15},{4,8},{5,9},{6,10},{7,11},{8,4},{9,5},... | collective-permute-start | bytes 552968 | tf_op jit(solution)/shard_map/ppermute | solution.py:24
  31.1 14.7 %collective-permute-start.15 = (bf16[240,384]{1,0:T(8,128)(2,1)S(1)}, bf16[240,384]{1,0:T(8,128)(2,1)S(1)}, u32[]{:S(2)}, u32[]{:S(2)}) collective-permute-start(bf16[240,384]{1,0:T(8,128)(2,1)S(1)} %copy-done.15), channel_id=1, source_target_pairs={{0,8},{1,9},{2,10},{3,11},{4,12},{5,13},{6,14},{7,15},{8,0},{9,1},... | collective-permute-start | bytes 552968 | tf_op jit(solution)/shard_map/ppermute | solution.py:24
  31.1 14.7 %collective-permute-start.14 = (bf16[240,384]{1,0:T(8,128)(2,1)S(1)}, bf16[240,384]{1,0:T(8,128)(2,1)S(1)}, u32[]{:S(2)}, u32[]{:S(2)}) collective-permute-start(bf16[240,384]{1,0:T(8,128)(2,1)S(1)} %copy-done.15), channel_id=1, source_target_pairs={{0,4},{1,5},{2,6},{3,7},{4,0},{5,1},{6,2},{7,3},{8,12},{9,13},{10,... | collective-permute-start | bytes 552968 | tf_op jit(solution)/shard_map/ppermute | solution.py:24
  46.8 19.0 %collective-permute-start.18 = (bf16[4,240,384]{2,1,0:T(8,128)(2,1)S(1)}, bf16[4,240,384]{2,1,0:T(8,128)(2,1)S(1)}, u32[]{:S(2)}, u32[]{:S(2)}) collective-permute-start(bf16[4,240,384]{2,1,0:T(8,128)(2,1)S(1)} %pad_maximum_fusion.1.refs_0_), channel_id=1, source_target_pairs={{0,2},{1,3},{2,0},{3,1},{4,6},{5,7},{6,4},{7,5},{8,10},{9,11},{10,... | collective-permute-start | bytes 2211848 | tf_op jit(solution)/shard_map/ppermute | solution.py:24
  47.4 18.7 %collective-permute-start.17 = (bf16[4,240,384]{2,1,0:T(8,128)(2,1)S(1)}, bf16[4,240,384]{2,1,0:T(8,128)(2,1)S(1)}, u32[]{:S(2)}, u32[]{:S(2)}) collective-permute-start(bf16[4,240,384]{2,1,0:T(8,128)(2,1)S(1)} %pad_maximum_fusion.1.refs_0_), channel_id=1, source_target_pairs={{0,1},{1,0},{2,3},{3,2},{4,5},{5,4},{6,7},{7,6},{8,9},{9,8},{10,11... | collective-permute-start | bytes 2211848 | tf_op jit(solution)/shard_map/ppermute | solution.py:24
  50.2 19.5 %collective-permute-start.28 = (bf16[192,384]{1,0:T(8,128)(2,1)S(1)}, bf16[192,384]{1,0:T(8,128)(2,1)S(1)}, u32[]{:S(2)}, u32[]{:S(2)}) collective-permute-start(bf16[192,384]{1,0:T(8,128)(2,1)S(1)} %copy-done.16), channel_id=1, source_target_pairs={{0,12},{1,13},{2,14},{3,15},{4,8},{5,9},{6,10},{7,11},{8,4},{9,5},... | collective-permute-start | bytes 442376 | tf_op jit(solution)/shard_map/ppermute | solution.py:24
  51.7 18.0 %collective-permute-start.27 = (bf16[192,384]{1,0:T(8,128)(2,1)S(1)}, bf16[192,384]{1,0:T(8,128)(2,1)S(1)}, u32[]{:S(2)}, u32[]{:S(2)}) collective-permute-start(bf16[192,384]{1,0:T(8,128)(2,1)S(1)} %copy-done.16), channel_id=1, source_target_pairs={{0,8},{1,9},{2,10},{3,11},{4,12},{5,13},{6,14},{7,15},{8,0},{9,1},... | collective-permute-start | bytes 442376 | tf_op jit(solution)/shard_map/ppermute | solution.py:24
  51.7 18.5 %collective-permute-start.26 = (bf16[192,384]{1,0:T(8,128)(2,1)S(1)}, bf16[192,384]{1,0:T(8,128)(2,1)S(1)}, u32[]{:S(2)}, u32[]{:S(2)}) collective-permute-start(bf16[192,384]{1,0:T(8,128)(2,1)S(1)} %copy-done.16), channel_id=1, source_target_pairs={{0,4},{1,5},{2,6},{3,7},{4,0},{5,1},{6,2},{7,3},{8,12},{9,13},{10,... | collective-permute-start | bytes 442376 | tf_op jit(solution)/shard_map/ppermute | solution.py:24
  66.1 11.0 %collective-permute-start.20 = (bf16[2,240,384]{2,1,0:T(8,128)(2,1)S(1)}, bf16[2,240,384]{2,1,0:T(8,128)(2,1)}, u32[]{:S(2)}, u32[]{:S(2)}) collective-permute-start(bf16[2,240,384]{2,1,0:T(8,128)(2,1)S(1)} %slice.280), channel_id=1, source_target_pairs={{0,1},{1,0},{2,3},{3,2},{4,5},{5,4},{6,7},{7,6},{8,9},{9,8},{10,11... | collective-permute-start | bytes 1105928 | tf_op jit(solution)/shard_map/ppermute | solution.py:24
  68.1 9.9 %collective-permute-start.19 = (bf16[2,240,384]{2,1,0:T(8,128)(2,1)S(1)}, bf16[2,240,384]{2,1,0:T(8,128)(2,1)}, u32[]{:S(2)}, u32[]{:S(2)}) collective-permute-start(bf16[2,240,384]{2,1,0:T(8,128)(2,1)S(1)} %slice.279), channel_id=1, source_target_pairs={{0,2},{1,3},{2,0},{3,1},{4,6},{5,7},{6,4},{7,5},{8,10},{9,11},{10,... | collective-permute-start | bytes 1105928 | tf_op jit(solution)/shard_map/ppermute | solution.py:24
  69.7 9.6 %collective-permute-start.21 = (bf16[4,240,384]{2,1,0:T(8,128)(2,1)S(1)}, bf16[4,240,384]{2,1,0:T(8,128)(2,1)}, u32[]{:S(2)}, u32[]{:S(2)}) collective-permute-start(bf16[4,240,384]{2,1,0:T(8,128)(2,1)S(1)} %pad_maximum_fusion.1.refs_0_), channel_id=1, source_target_pairs={{0,16},{16,0},{1,17},{17,1},{2,18},{18,2},{3,19},{19,3},{4,20},{20... | collective-permute-start | bytes 2211848 | tf_op jit(solution)/shard_map/ppermute | solution.py:24
  69.8 12.2 %collective-permute-start.22 = (bf16[4,240,384]{2,1,0:T(8,128)(2,1)S(1)}, bf16[4,240,384]{2,1,0:T(8,128)(2,1)}, u32[]{:S(2)}, u32[]{:S(2)}) collective-permute-start(bf16[4,240,384]{2,1,0:T(8,128)(2,1)S(1)} %collective-permute-done.17.refs_1_), channel_id=1, source_target_pairs={{0,16},{16,0},{1,17},{17,1},{2,18},{18,2},{3,19},{19,3},{4,20},{20... | collective-permute-start | bytes 2211848 | tf_op jit(solution)/shard_map/ppermute | solution.py:24
  70.4 11.6 %collective-permute-start.23 = (bf16[4,240,384]{2,1,0:T(8,128)(2,1)S(1)}, bf16[4,240,384]{2,1,0:T(8,128)(2,1)}, u32[]{:S(2)}, u32[]{:S(2)}) collective-permute-start(bf16[4,240,384]{2,1,0:T(8,128)(2,1)S(1)} %collective-permute-done.18.refs_2_), channel_id=1, source_target_pairs={{0,16},{16,0},{1,17},{17,1},{2,18},{18,2},{3,19},{19,3},{4,20},{20... | collective-permute-start | bytes 2211848 | tf_op jit(solution)/shard_map/ppermute | solution.py:24
  79.3 27.4 %collective-permute-start.33 = (bf16[4,192,384]{2,1,0:T(8,128)(2,1)S(1)}, bf16[4,192,384]{2,1,0:T(8,128)(2,1)S(1)}, u32[]{:S(2)}, u32[]{:S(2)}) collective-permute-start(bf16[4,192,384]{2,1,0:T(8,128)(2,1)S(1)} %pad_maximum_fusion.3.refs_0_), channel_id=1, source_target_pairs={{0,16},{16,0},{1,17},{17,1},{2,18},{18,2},{3,19},{19,3},{4,20},{20... | collective-permute-start | bytes 1769480 | tf_op jit(solution)/shard_map/ppermute | solution.py:24
  79.9 15.3 %collective-permute-start.30 = (bf16[4,192,384]{2,1,0:T(8,128)(2,1)S(1)}, bf16[4,192,384]{2,1,0:T(8,128)(2,1)S(1)}, u32[]{:S(2)}, u32[]{:S(2)}) collective-permute-start(bf16[4,192,384]{2,1,0:T(8,128)(2,1)S(1)} %pad_maximum_fusion.3.refs_0_), channel_id=1, source_target_pairs={{0,2},{1,3},{2,0},{3,1},{4,6},{5,7},{6,4},{7,5},{8,10},{9,11},{10,... | collective-permute-start | bytes 1769480 | tf_op jit(solution)/shard_map/ppermute | solution.py:24
  81.1 15.0 %collective-permute-start.29 = (bf16[4,192,384]{2,1,0:T(8,128)(2,1)S(1)}, bf16[4,192,384]{2,1,0:T(8,128)(2,1)S(1)}, u32[]{:S(2)}, u32[]{:S(2)}) collective-permute-start(bf16[4,192,384]{2,1,0:T(8,128)(2,1)S(1)} %pad_maximum_fusion.3.refs_0_), channel_id=1, source_target_pairs={{0,1},{1,0},{2,3},{3,2},{4,5},{5,4},{6,7},{7,6},{8,9},{9,8},{10,11... | collective-permute-start | bytes 1769480 | tf_op jit(solution)/shard_map/ppermute | solution.py:24
  96.1 10.6 %collective-permute-start.34 = (bf16[4,192,384]{2,1,0:T(8,128)(2,1)S(1)}, bf16[4,192,384]{2,1,0:T(8,128)(2,1)S(1)}, u32[]{:S(2)}, u32[]{:S(2)}) collective-permute-start(bf16[4,192,384]{2,1,0:T(8,128)(2,1)S(1)} %collective-permute-done.29.refs_1_), channel_id=1, source_target_pairs={{0,16},{16,0},{1,17},{17,1},{2,18},{18,2},{3,19},{19,3},{4,20},{20... | collective-permute-start | bytes 1769480 | tf_op jit(solution)/shard_map/ppermute | solution.py:24
  96.3 9.5 %collective-permute-start.32 = (bf16[2,192,384]{2,1,0:T(8,128)(2,1)S(1)}, bf16[2,192,384]{2,1,0:T(8,128)(2,1)S(1)}, u32[]{:S(2)}, u32[]{:S(2)}) collective-permute-start(bf16[2,192,384]{2,1,0:T(8,128)(2,1)S(1)} %slice.282), channel_id=1, source_target_pairs={{0,1},{1,0},{2,3},{3,2},{4,5},{5,4},{6,7},{7,6},{8,9},{9,8},{10,11... | collective-permute-start | bytes 884744 | tf_op jit(solution)/shard_map/ppermute | solution.py:24
  97.3 9.5 %collective-permute-start.35 = (bf16[4,192,384]{2,1,0:T(8,128)(2,1)S(1)}, bf16[4,192,384]{2,1,0:T(8,128)(2,1)S(1)}, u32[]{:S(2)}, u32[]{:S(2)}) collective-permute-start(bf16[4,192,384]{2,1,0:T(8,128)(2,1)S(1)} %collective-permute-done.30.refs_2_), channel_id=1, source_target_pairs={{0,16},{16,0},{1,17},{17,1},{2,18},{18,2},{3,19},{19,3},{4,20},{20... | collective-permute-start | bytes 1769480 | tf_op jit(solution)/shard_map/ppermute | solution.py:24
  135.6 11.6 %collective-permute-start.42 = (bf16[3,4,96,768]{3,2,1,0:T(8,128)(2,1)}, bf16[3,4,96,768]{3,2,1,0:T(8,128)(2,1)S(1)}, u32[]{:S(2)}, u32[]{:S(2)}) collective-permute-start(bf16[3,4,96,768]{3,2,1,0:T(8,128)(2,1)} %get-tuple-element.173), channel_id=1, source_target_pairs={{0,16},{16,0},{1,17},{17,1},{2,18},{18,2},{3,19},{19,3},{4,20},{20... | collective-permute-start | bytes 5308424 | tf_op jit(solution)/shard_map/ppermute | solution.py:24
  137.2 9.3 %collective-permute-start.41 = (bf16[2,96,768]{2,1,0:T(8,128)(2,1)S(1)}, bf16[2,96,768]{2,1,0:T(8,128)(2,1)S(1)}, u32[]{:S(2)}, u32[]{:S(2)}) collective-permute-start(bf16[2,96,768]{2,1,0:T(8,128)(2,1)S(1)} %get-tuple-element.250), channel_id=1, source_target_pairs={{0,2},{1,3},{2,0},{3,1},{4,6},{5,7},{6,4},{7,5},{8,10},{9,11},{10,... | collective-permute-start | bytes 884744 | tf_op jit(solution)/shard_map/ppermute | solution.py:24
  148.4 16.0 %collective-permute-start.45 = (bf16[4,96,768]{2,1,0:T(8,128)(2,1)S(1)}, bf16[4,96,768]{2,1,0:T(8,128)(2,1)S(1)}, u32[]{:S(2)}, u32[]{:S(2)}) collective-permute-start(bf16[4,96,768]{2,1,0:T(8,128)(2,1)S(1)} %get-tuple-element.244), channel_id=1, source_target_pairs={{0,2},{1,3},{2,0},{3,1},{4,6},{5,7},{6,4},{7,5},{8,10},{9,11},{10,... | collective-permute-start | bytes 1769480 | tf_op jit(solution)/shard_map/ppermute | solution.py:24
  150.3 14.5 %collective-permute-start.44 = (bf16[4,96,768]{2,1,0:T(8,128)(2,1)S(1)}, bf16[4,96,768]{2,1,0:T(8,128)(2,1)S(1)}, u32[]{:S(2)}, u32[]{:S(2)}) collective-permute-start(bf16[4,96,768]{2,1,0:T(8,128)(2,1)S(1)} %get-tuple-element.245), channel_id=1, source_target_pairs={{0,1},{1,0},{2,3},{3,2},{4,5},{5,4},{6,7},{7,6},{8,9},{9,8},{10,11... | collective-permute-start | bytes 1769480 | tf_op jit(solution)/shard_map/ppermute | solution.py:24
  170.2 15.8 %collective-permute-start.49 = (bf16[3,4,24,3840]{3,2,1,0:T(8,128)(2,1)}, bf16[3,4,24,3840]{3,2,1,0:T(8,128)(2,1)S(1)}, u32[]{:S(2)}, u32[]{:S(2)}) collective-permute-start(bf16[3,4,24,3840]{3,2,1,0:T(8,128)(2,1)} %get-tuple-element.189), channel_id=1, source_target_pairs={{0,16},{16,0},{1,17},{17,1},{2,18},{18,2},{3,19},{19,3},{4,20},{20... | collective-permute-start | bytes 6635528 | tf_op jit(solution)/shard_map/ppermute | solution.py:24
  172.9 11.5 %collective-permute-start.48 = (bf16[2,24,3840]{2,1,0:T(8,128)(2,1)S(1)}, bf16[2,24,3840]{2,1,0:T(8,128)(2,1)S(1)}, u32[]{:S(2)}, u32[]{:S(2)}) collective-permute-start(bf16[2,24,3840]{2,1,0:T(8,128)(2,1)S(1)} %get-tuple-element.246), channel_id=1, source_target_pairs={{0,2},{1,3},{2,0},{3,1},{4,6},{5,7},{6,4},{7,5},{8,10},{9,11},{10,... | collective-permute-start | bytes 1105928 | tf_op jit(solution)/shard_map/ppermute | solution.py:24
  175.5 10.4 %collective-permute-start.47 = (bf16[2,24,3840]{2,1,0:T(8,128)(2,1)S(1)}, bf16[2,24,3840]{2,1,0:T(8,128)(2,1)S(1)}, u32[]{:S(2)}, u32[]{:S(2)}) collective-permute-start(bf16[2,24,3840]{2,1,0:T(8,128)(2,1)S(1)} %get-tuple-element.247), channel_id=1, source_target_pairs={{0,1},{1,0},{2,3},{3,2},{4,5},{5,4},{6,7},{7,6},{8,9},{9,8},{10,11... | collective-permute-start | bytes 1105928 | tf_op jit(solution)/shard_map/ppermute | solution.py:24
  177.6 21.2 %collective-permute-start.54 = (bf16[96,768]{1,0:T(8,128)(2,1)S(1)}, bf16[96,768]{1,0:T(8,128)(2,1)}, u32[]{:S(2)}, u32[]{:S(2)}) collective-permute-start(bf16[96,768]{1,0:T(8,128)(2,1)S(1)} %get-tuple-element.236), channel_id=1, source_target_pairs={{0,12},{1,13},{2,14},{3,15},{4,8},{5,9},{6,10},{7,11},{8,4},{9,5},... | collective-permute-start | bytes 442376 | tf_op jit(solution)/shard_map/ppermute | solution.py:24
  180.2 20.3 %collective-permute-start.53 = (bf16[96,768]{1,0:T(8,128)(2,1)S(1)}, bf16[96,768]{1,0:T(8,128)(2,1)S(1)}, u32[]{:S(2)}, u32[]{:S(2)}) collective-permute-start(bf16[96,768]{1,0:T(8,128)(2,1)S(1)} %get-tuple-element.237), channel_id=1, source_target_pairs={{0,8},{1,9},{2,10},{3,11},{4,12},{5,13},{6,14},{7,15},{8,0},{9,1},... | collective-permute-start | bytes 442376 | tf_op jit(solution)/shard_map/ppermute | solution.py:24
  184.4 16.1 %collective-permute-start.52 = (bf16[96,768]{1,0:T(8,128)(2,1)S(1)}, bf16[96,768]{1,0:T(8,128)(2,1)S(1)}, u32[]{:S(2)}, u32[]{:S(2)}) collective-permute-start(bf16[96,768]{1,0:T(8,128)(2,1)S(1)} %get-tuple-element.238), channel_id=1, source_target_pairs={{0,4},{1,5},{2,6},{3,7},{4,0},{5,1},{6,2},{7,3},{8,12},{9,13},{10,... | collective-permute-start | bytes 442376 | tf_op jit(solution)/shard_map/ppermute | solution.py:24
  187.4 17.5 %collective-permute-start.51 = (bf16[4,24,3840]{2,1,0:T(8,128)(2,1)S(1)}, bf16[4,24,3840]{2,1,0:T(8,128)(2,1)S(1)}, u32[]{:S(2)}, u32[]{:S(2)}) collective-permute-start(bf16[4,24,3840]{2,1,0:T(8,128)(2,1)S(1)} %get-tuple-element.239), channel_id=1, source_target_pairs={{0,2},{1,3},{2,0},{3,1},{4,6},{5,7},{6,4},{7,5},{8,10},{9,11},{10,... | collective-permute-start | bytes 2211848 | tf_op jit(solution)/shard_map/ppermute | solution.py:24
  188.0 17.4 %collective-permute-start.50 = (bf16[4,24,3840]{2,1,0:T(8,128)(2,1)S(1)}, bf16[4,24,3840]{2,1,0:T(8,128)(2,1)}, u32[]{:S(2)}, u32[]{:S(2)}) collective-permute-start(bf16[4,24,3840]{2,1,0:T(8,128)(2,1)S(1)} %get-tuple-element.240), channel_id=1, source_target_pairs={{0,1},{1,0},{2,3},{3,2},{4,5},{5,4},{6,7},{7,6},{8,9},{9,8},{10,11... | collective-permute-start | bytes 2211848 | tf_op jit(solution)/shard_map/ppermute | solution.py:24
  198.8 22.8 %collective-permute-start.58 = (f32[16,2304]{1,0:T(8,128)S(1)}, f32[16,2304]{1,0:T(8,128)S(1)}, u32[]{:S(2)}, u32[]{:S(2)}) collective-permute-start(f32[16,2304]{1,0:T(8,128)S(1)} %fusion.35), channel_id=1, source_target_pairs={{0,4},{1,5},{2,6},{3,7},{4,0},{5,1},{6,2},{7,3},{8,12},{9,13},{10,... | collective-permute-start | bytes 442376 | tf_op jit(solution)/shard_map/ppermute | solution.py:24
  207.0 14.6 %collective-permute-start.57 = (bf16[24,3840]{1,0:T(8,128)(2,1)S(1)}, bf16[24,3840]{1,0:T(8,128)(2,1)S(1)}, u32[]{:S(2)}, u32[]{:S(2)}) collective-permute-start(bf16[24,3840]{1,0:T(8,128)(2,1)S(1)} %get-tuple-element.233), channel_id=1, source_target_pairs={{0,12},{1,13},{2,14},{3,15},{4,8},{5,9},{6,10},{7,11},{8,4},{9,5},... | collective-permute-start | bytes 552968 | tf_op jit(solution)/shard_map/ppermute | solution.py:24
  209.5 14.9 %collective-permute-start.56 = (bf16[24,3840]{1,0:T(8,128)(2,1)S(1)}, bf16[24,3840]{1,0:T(8,128)(2,1)S(1)}, u32[]{:S(2)}, u32[]{:S(2)}) collective-permute-start(bf16[24,3840]{1,0:T(8,128)(2,1)S(1)} %get-tuple-element.234), channel_id=1, source_target_pairs={{0,8},{1,9},{2,10},{3,11},{4,12},{5,13},{6,14},{7,15},{8,0},{9,1},... | collective-permute-start | bytes 552968 | tf_op jit(solution)/shard_map/ppermute | solution.py:24
  210.1 14.3 %collective-permute-start.55 = (bf16[24,3840]{1,0:T(8,128)(2,1)S(1)}, bf16[24,3840]{1,0:T(8,128)(2,1)}, u32[]{:S(2)}, u32[]{:S(2)}) collective-permute-start(bf16[24,3840]{1,0:T(8,128)(2,1)S(1)} %get-tuple-element.235), channel_id=1, source_target_pairs={{0,4},{1,5},{2,6},{3,7},{4,0},{5,1},{6,2},{7,3},{8,12},{9,13},{10,... | collective-permute-start | bytes 552968 | tf_op jit(solution)/shard_map/ppermute | solution.py:24
  226.5 11.2 %collective-permute-start.63 = (bf16[3,4,24,2432]{3,2,1,0:T(8,128)(2,1)}, bf16[3,4,24,2432]{3,2,1,0:T(8,128)(2,1)}, u32[]{:S(2)}, u32[]{:S(2)}) collective-permute-start(bf16[3,4,24,2432]{3,2,1,0:T(8,128)(2,1)} %get-tuple-element.206), channel_id=1, source_target_pairs={{0,16},{16,0},{1,17},{17,1},{2,18},{18,2},{3,19},{19,3},{4,20},{20... | collective-permute-start | bytes 4202504 | tf_op jit(solution)/shard_map/ppermute | solution.py:24
  233.3 11.0 %collective-permute-start.69 = (f32[16,2304]{1,0:T(8,128)S(1)}, f32[16,2304]{1,0:T(8,128)S(1)}, u32[]{:S(2)}, u32[]{:S(2)}) collective-permute-start(f32[16,2304]{1,0:T(8,128)S(1)} %add.513), channel_id=1, source_target_pairs={{0,8},{1,9},{2,10},{3,11},{4,12},{5,13},{6,14},{7,15},{8,0},{9,1},... | collective-permute-start | bytes 442376 | tf_op jit(solution)/shard_map/ppermute | solution.py:24
  237.8 21.1 %collective-permute-start.62 = (bf16[8,128,768]{2,1,0:T(8,128)(2,1)}, bf16[8,128,768]{2,1,0:T(8,128)(2,1)S(1)}, u32[]{:S(2)}, u32[]{:S(2)}) collective-permute-start(bf16[8,128,768]{2,1,0:T(8,128)(2,1)} %get-tuple-element.204), channel_id=1, source_target_pairs={{0,16},{16,0},{1,17},{17,1},{2,18},{18,2},{3,19},{19,3},{4,20},{20... | collective-permute-start | bytes 4718600 | tf_op jit(solution)/shard_map/ppermute | solution.py:24
  239.3 13.6 %collective-permute-start.64 = (bf16[4,24,2432]{2,1,0:T(8,128)(2,1)S(1)}, bf16[4,24,2432]{2,1,0:T(8,128)(2,1)S(1)}, u32[]{:S(2)}, u32[]{:S(2)}) collective-permute-start(bf16[4,24,2432]{2,1,0:T(8,128)(2,1)S(1)} %get-tuple-element.248), channel_id=1, source_target_pairs={{0,1},{1,0},{2,3},{3,2},{4,5},{5,4},{6,7},{7,6},{8,9},{9,8},{10,11... | collective-permute-start | bytes 1400840 | tf_op jit(solution)/shard_map/ppermute | solution.py:24
  240.4 12.8 %collective-permute-start.65 = (bf16[4,24,2432]{2,1,0:T(8,128)(2,1)S(1)}, bf16[4,24,2432]{2,1,0:T(8,128)(2,1)S(1)}, u32[]{:S(2)}, u32[]{:S(2)}) collective-permute-start(bf16[4,24,2432]{2,1,0:T(8,128)(2,1)S(1)} %get-tuple-element.249), channel_id=1, source_target_pairs={{0,2},{1,3},{2,0},{3,1},{4,6},{5,7},{6,4},{7,5},{8,10},{9,11},{10,... | collective-permute-start | bytes 1400840 | tf_op jit(solution)/shard_map/ppermute | solution.py:24
  244.3 16.5 %collective-permute-start.70 = (f32[16,2304]{1,0:T(8,128)S(1)}, f32[16,2304]{1,0:T(8,128)S(1)}, u32[]{:S(2)}, u32[]{:S(2)}) collective-permute-start(f32[16,2304]{1,0:T(8,128)S(1)} %add.514), channel_id=1, source_target_pairs={{0,1},{1,0},{2,3},{3,2},{4,5},{5,4},{6,7},{7,6},{8,9},{9,8},{10,11... | collective-permute-start | bytes 442376 | tf_op jit(solution)/shard_map/ppermute | solution.py:24
  256.2 10.5 %collective-permute-start.67 = (bf16[24,2432]{1,0:T(8,128)(2,1)S(1)}, bf16[24,2432]{1,0:T(8,128)(2,1)S(1)}, u32[]{:S(2)}, u32[]{:S(2)}) collective-permute-start(bf16[24,2432]{1,0:T(8,128)(2,1)S(1)} %get-tuple-element.242), channel_id=1, source_target_pairs={{0,8},{1,9},{2,10},{3,11},{4,12},{5,13},{6,14},{7,15},{8,0},{9,1},... | collective-permute-start | bytes 350216 | tf_op jit(solution)/shard_map/ppermute | solution.py:24
  256.4 10.3 %collective-permute-start.66 = (bf16[24,2432]{1,0:T(8,128)(2,1)S(1)}, bf16[24,2432]{1,0:T(8,128)(2,1)S(1)}, u32[]{:S(2)}, u32[]{:S(2)}) collective-permute-start(bf16[24,2432]{1,0:T(8,128)(2,1)S(1)} %get-tuple-element.243), channel_id=1, source_target_pairs={{0,4},{1,5},{2,6},{3,7},{4,0},{5,1},{6,2},{7,3},{8,12},{9,13},{10,... | collective-permute-start | bytes 350216 | tf_op jit(solution)/shard_map/ppermute | solution.py:24
  (68 other events, 505.1 us)
